TPU v7x, 256 devices: a whole 4x4x8 slice. The times are simulated.
256 devices in a mesh: blk: 64 (over z, y, x_lo), feat: 4 (over x_hi, core).
Axes of the slice: x: 4 (x_hi: 2, x_lo: 2; x = x_hi * 2 + x_lo), y: 4, z: 8, core: 2. Of those that a mesh axis runs over, the one named last changes fastest.
Arguments:
- x_t: bfloat16 [256, 262144], P('feat', 'blk'), may hold values from -6 to 6
- weight: bfloat16 [256, 256], P('feat'), may hold values from -0.375 to 0.375
- cotangent: bfloat16 [256, 262144], P('feat', 'blk'), may hold values from -6 to 6
- tile_row: int32 [18432], P('blk'), may hold values from 0 to 31
- tile_col: int32 [18432], P('blk'), may hold values from 0 to 31
- tile_off: int32 [18432], P('blk'), may hold values from -4 to 4, as said below
- tile_vals: bfloat16 [18432, 128, 128], P('blk'), may hold values from -0.625 to 0.625
- tile_count: int32 [64], P('blk'), may hold values from 72 to 288, as said below
Outputs:
- out_t: bfloat16 [256, 262144], P('feat', 'blk')
- grad_x_t: bfloat16 [256, 262144], P('feat', 'blk')
- grad_weight: float32 [256, 256], P('feat')
Inputs may be any that keep to these rules, and one draw needn't show every extreme that they name: `tile_off`: slots 0 to 8 of every partition name each offset once; slots may repeat a tile position, and repeated tiles add. `tile_count`: some partition lists 288 live tiles and some 288 // 4.
All inputs are finite; a program needn't handle non-finite values.
Results may differ from a plain program's by a relative error of at most 0.0062.
Values may be sent and summed in bfloat16 or wider, within the bound.
No kernel may reach another device: no remote copies, remote signals or barrier semaphores. Data moves between devices by JAX's collectives and lax.ppermute only.
A program may use at most 128 MiB of HBM per device.

v0:
```python
import math

import jax
import jax.numpy as jnp
from jax import lax
from jax.sharding import PartitionSpec as P

REACH = 4


def shifted(block, axis, distance):
    devices = range(lax.axis_size(axis))
    route = [((i - distance) % len(devices), i) for i in devices]
    return lax.ppermute(block, axis, route)


def silu_slope(value):
    sig = jax.nn.sigmoid(value)
    return sig * (1.0 + value * (1.0 - sig))


def per_device(x_t, weight, cotangent, tile_row, tile_col, tile_off, tile_vals, tile_count):
    feat_rows = x_t.shape[0]
    nodes = x_t.shape[1]
    tile = tile_vals.shape[1]
    tiles = nodes // tile
    slots = tile_row.shape[0]
    span = 2 * REACH + 1
    w_cols = weight
    proj = lax.psum_scatter(
        lax.dot_general(w_cols, x_t, (((0,), (0,)), ((), ())), preferred_element_type=jnp.float32),
        "feat",
        scatter_dimension=0,
        tiled=True,
    ).astype(jnp.bfloat16)
    slab = proj.reshape(feat_rows, tiles, tile)
    fetched = {0: slab}
    for offset in range(-REACH, REACH + 1):
        if offset != 0:
            fetched[offset] = shifted(slab, "blk", -offset)
    stacked = jnp.concatenate([fetched[offset] for offset in range(-REACH, REACH + 1)], axis=1)
    live = (jnp.arange(slots, dtype=jnp.int32) < tile_count[0]).astype(jnp.float32)
    source_index = (tile_off + REACH) * tiles + tile_col
    pieces = jnp.take(stacked, source_index, axis=1)
    product = jnp.einsum("hsk,srk->hsr", pieces, tile_vals, preferred_element_type=jnp.float32)
    row_hot = (tile_row[:, None] == jnp.arange(tiles, dtype=jnp.int32)[None, :]).astype(
        jnp.float32
    ) * live[:, None]
    summed = jnp.einsum("hsr,st->htr", product, row_hot, precision=lax.Precision.HIGHEST)
    pre_t = summed.reshape(feat_rows, nodes)
    out_t = jax.nn.silu(pre_t).astype(jnp.bfloat16)
    grad_pre = (cotangent.astype(jnp.float32) * silu_slope(pre_t)).astype(jnp.bfloat16)
    grad_pieces = jnp.take(grad_pre.reshape(feat_rows, tiles, tile), tile_row, axis=1)
    contrib = jnp.einsum("hsr,srk->hsk", grad_pieces, tile_vals, preferred_element_type=jnp.float32)
    dest_hot = (source_index[:, None] == jnp.arange(span * tiles, dtype=jnp.int32)[None, :]).astype(
        jnp.float32
    ) * live[:, None]
    buffers = jnp.einsum("hsk,sd->hdk", contrib, dest_hot, precision=lax.Precision.HIGHEST)

    def bound_for(offset):
        return buffers[:, (offset + REACH) * tiles : (offset + REACH + 1) * tiles, :]

    gathered_sum = bound_for(0)
    for offset in range(-REACH, REACH + 1):
        if offset != 0:
            gathered_sum = gathered_sum + shifted(bound_for(offset), "blk", offset)
    grad_proj = gathered_sum.reshape(feat_rows, nodes).astype(jnp.bfloat16)
    piece = lax.all_gather(grad_proj, "feat", axis=0, tiled=True)
    block = lax.dot_general(
        x_t, piece, (((1,), (1,)), ((), ())), preferred_element_type=jnp.float32
    )
    weight_grad = block
    w_cols = weight
    input_grad = jnp.dot(w_cols, piece, preferred_element_type=jnp.float32)
    weight_grad, input_grad = (weight_grad, input_grad)
    factor = 1.0 / math.sqrt(nodes * lax.axis_size("blk"))
    weight_grad = lax.psum(weight_grad * factor, "blk")
    return (out_t, input_grad.astype(jnp.bfloat16), weight_grad)


def solution(mesh):
    placed = (
        P("feat", "blk"),
        P("feat", None),
        P("feat", "blk"),
        P("blk"),
        P("blk"),
        P("blk"),
        P("blk", None, None),
        P("blk"),
    )
    return jax.shard_map(
        per_device,
        mesh=mesh,
        in_specs=placed,
        out_specs=(P("feat", "blk"), P("feat", "blk"), P("feat", None)),
        check_vma=False,
    )
```

profile of v0, /device:TPU:4, one launch (start us, length us, event | category | flops | bytes accessed | tf_op | source)
XLA Modules:
  0.0 1055.9 jit_solution(13803362977749975269)
XLA Ops:
  8.2 3.4 fusion.58
  11.8 56.9 %reduce-scatter.2.cloned.1.call-done = f32[64,4096]{1,0:T(8,128)} async-done(((f32[256,4096]{1,0:T(8,128)}), f32[64,4096]{1,0:T(8,128)}) %reduce-scatter.2.cloned.1.call-update) | async-done | bytes 1048592 | tf_op jit(solution)/shard_map/reduce_scatter | solution.py:30
  68.7 1.4 copy_bitcast_fusion.2
  70.1 3.3 collective-permute-start.1
  73.4 2.7 collective-permute-start
  78.6 6.0 collective-permute-start.6
  84.7 26.6 %collective-permute-done = bf16[64,32,128]{2,0,1:T(8,128)(2,1)S(1)} collective-permute-done((bf16[64,32,128]{2,0,1:T(8,128)(2,1)S(1)}, bf16[64,32,128]{2,0,1:T(8,128)(2,1)S(1)}, u32[]{:S(2)}, u32[]{:S(2)}) %collective-permute-start) | collective-permute-done | bytes 524320 | tf_op jit(solution)/shard_map/ppermute | solution.py:14
  111.3 14.4 %collective-permute-start.5 = (bf16[64,32,128]{2,0,1:T(8,128)(2,1)S(1)}, bf16[64,32,128]{2,0,1:T(8,128)(2,1)S(1)}, u32[]{:S(2)}, u32[]{:S(2)}) collective-permute-start(bf16[64,32,128]{2,0,1:T(8,128)(2,1)S(1)} %copy_bitcast_fusion.2), channel_id=1, source_target_pairs={{8,0},{12,4},{16,8},{20,12},{24,16},{28,20},{32,24},{36,28},{40,32... | collective-permute-start | bytes 1572872 | tf_op jit(solution)/shard_map/ppermute | solution.py:14
  128.3 6.6 collective-permute-done.3
  136.7 19.0 %collective-permute-done.4 = bf16[64,32,128]{2,0,1:T(8,128)(2,1)S(1)} collective-permute-done((bf16[64,32,128]{2,0,1:T(8,128)(2,1)S(1)}, bf16[64,32,128]{2,0,1:T(8,128)(2,1)S(1)}, u32[]{:S(2)}, u32[]{:S(2)}) %collective-permute-start.4) | collective-permute-done | bytes 524320 | tf_op jit(solution)/shard_map/ppermute | solution.py:14
  158.2 7.8 collective-permute-done.7
  166.9 5.9 gather_fusion
  172.7 15.2 %fusion.16 = f32[64,288,128]{2,0,1:T(8,128)} fusion(bf16[288,128,128]{2,1,0:T(8,128)(2,1)} %param.14, bf16[288,64,128]{2,1,0:T(8,128)(2,1)} %gather_fusion, pred[288]{0:T(512)(128)(4,1)S(1)} %get-tuple-element.3), kind=kOutput, calls=%fused_computation.17 | convolution fusion | flops 606339072 | bytes 23593248 | tf_op jit(solution)/shard_map/hsk,srk->hsr/dot_general | solution.py:45
  187.9 15.2 %fusion.2 = f32[32,64,128]{2,0,1:T(8,128)S(1)} fusion(f32[64,288,128]{2,0,1:T(8,128)} %fusion.16, f32[288]{0:T(512)S(1)} %fusion.52, s32[288]{0:T(512)S(1)} %copy-done.4), kind=kOutput, calls=%fused_computation.4 | convolution fusion | flops 905988096 | bytes 10488064 | tf_op jit(solution)/shard_map/hsr,st->htr/dot_general | solution.py:49
  203.2 1.8 fusion.41
  205.1 13.3 %gather_fusion.1 = bf16[288,64,128]{2,1,0:T(8,128)(2,1)} fusion(bf16[64,32,128]{2,0,1:T(8,128)(2,1)S(1)} %bitcast.81, s32[1024]{0:T(1024)S(1)} %pad_clamp_fusion), kind=kCustom, calls=%fused_computation.1 | custom fusion | bytes 9438336 | tf_op jit(solution)/shard_map/jit(_take)/gather | solution.py:53
  218.4 7.0 fusion.19
  225.4 20.5 %fusion.13 = f32[64,288,128]{2,1,0:T(8,128)S(1)} fusion(f32[64,288,128]{2,0,1:T(8,128)S(1)} %fusion.19, f32[288]{0:T(512)S(1)} %fusion.52, s32[288]{0:T(512)S(1)} %get-tuple-element.4), kind=kOutput, calls=%fused_computation.16 | convolution fusion | flops 8153892864 | bytes 18876672 | tf_op jit(solution)/shard_map/hsk,sd->hdk/dot_general | solution.py:58
  246.0 1.6 fusion.57
  247.5 6.2 collective-permute-start.8
  253.9 5.8 collective-permute-start.12
  259.7 112.2 %collective-permute-done.8 = f32[64,32,128]{2,1,0:T(8,128)S(1)} collective-permute-done((f32[64,32,128]{2,1,0:T(8,128)S(1)}, f32[64,32,128]{2,1,0:T(8,128)S(1)}, u32[]{:S(2)}, u32[]{:S(2)}) %collective-permute-start.8) | collective-permute-done | bytes 1048608 | tf_op jit(solution)/shard_map/ppermute | solution.py:14
  372.4 6.2 collective-permute-done.13
  378.6 54.1 %collective-permute-done.11 = f32[64,32,128]{2,1,0:T(8,128)S(1)} collective-permute-done((f32[64,32,128]{2,1,0:T(8,128)S(1)}, f32[64,32,128]{2,1,0:T(8,128)S(1)}, u32[]{:S(2)}, u32[]{:S(2)}) %collective-permute-start.11) | collective-permute-done | bytes 1048608 | tf_op jit(solution)/shard_map/ppermute | solution.py:14
  432.7 34.5 %collective-permute-done.10 = f32[64,32,128]{2,1,0:T(8,128)S(1)} collective-permute-done((f32[64,32,128]{2,1,0:T(8,128)S(1)}, f32[64,32,128]{2,1,0:T(8,128)S(1)}, u32[]{:S(2)}, u32[]{:S(2)}) %collective-permute-start.10) | collective-permute-done | bytes 1048608 | tf_op jit(solution)/shard_map/ppermute | solution.py:14
  467.2 18.8 %collective-permute-done.9 = f32[64,32,128]{2,1,0:T(8,128)S(1)} collective-permute-done((f32[64,32,128]{2,1,0:T(8,128)S(1)}, f32[64,32,128]{2,1,0:T(8,128)S(1)}, u32[]{:S(2)}, u32[]{:S(2)}) %collective-permute-start.9) | collective-permute-done | bytes 1048608 | tf_op jit(solution)/shard_map/ppermute | solution.py:14
  486.0 1.2 fusion.40
  488.2 25.8 %all-gather.2.cloned.1.call-done = bf16[256,4096]{1,0:T(8,128)(2,1)} async-done(((bf16[64,4096]{1,0:T(8,128)(2,1)}), bf16[256,4096]{1,0:T(8,128)(2,1)}) %all-gather.2.cloned.1.call-update) | async-done | bytes 2097168 | tf_op jit(solution)/shard_map/all_gather | solution.py:68
  514.0 3.0 fusion.24
  517.0 2.9 fusion.12
  519.9 527.8 %all-reduce.2.cloned.1.call-done = f32[64,256]{1,0:T(8,128)} async-done(((f32[64,256]{1,0:T(8,128)}), f32[64,256]{1,0:T(8,128)}) %all-reduce.2.cloned.1.call-update) | async-done | bytes 65552 | tf_op jit(solution)/shard_map/psum | solution.py:77
  1047.7 1.5 copy.63
  (55 shorter events, 12.5 us)
Async XLA Ops:
  7.2 1.0 copy-start
  7.2 4.6 copy-start.4
  7.2 4.6 copy-start.6
  7.2 4.6 copy-start.5
  7.2 61.5 %reduce-scatter.2.cloned.1.call-start = ((), (), s32[]{:S(2)}) async-start(), calls=%async_computation.1 | async-start | bytes 5242880 | tf_op jit(solution)/shard_map/reduce_scatter | solution.py:30
  11.7 502.3 %all-gather.2.cloned.1.call-start = ((), (), s32[]{:S(2)}) async-start(), calls=%async_computation.2 | async-start | bytes 2621440 | tf_op jit(solution)/shard_map/all_gather | solution.py:68
  68.7 67.1 %copy-start.1 = (f32[64,4096]{1,0:T(8,128)S(1)}, f32[64,4096]{1,0:T(8,128)}, u32[]{:S(2)}) copy-start(f32[64,4096]{1,0:T(8,128)} %reduce-scatter.2.cloned.1.call-done) | copy-start | bytes 3145732
  70.1 56.4 %collective-permute-start.1 = (bf16[64,32,128]{2,0,1:T(8,128)(2,1)S(1)}, bf16[64,32,128]{2,0,1:T(8,128)(2,1)S(1)}, u32[]{:S(2)}, u32[]{:S(2)}) collective-permute-start(bf16[64,32,128]{2,0,1:T(8,128)(2,1)S(1)} %copy_bitcast_fusion.2), channel_id=1, source_target_pairs={{244,0},{248,4},{252,8},{0,12},{4,16},{8,20},{12,24},{16,28},{20,3... | collective-permute-start | bytes 1572872 | tf_op jit(solution)/shard_map/ppermute | solution.py:14
  73.4 37.8 %collective-permute-start = (bf16[64,32,128]{2,0,1:T(8,128)(2,1)S(1)}, bf16[64,32,128]{2,0,1:T(8,128)(2,1)S(1)}, u32[]{:S(2)}, u32[]{:S(2)}) collective-permute-start(bf16[64,32,128]{2,0,1:T(8,128)(2,1)S(1)} %copy_bitcast_fusion.2), channel_id=1, source_target_pairs={{240,0},{244,4},{248,8},{252,12},{0,16},{4,20},{8,24},{12,28},{16,... | collective-permute-start | bytes 1572872 | tf_op jit(solution)/shard_map/ppermute | solution.py:14
  76.1 51.2 %collective-permute-start.2 = (bf16[64,32,128]{2,0,1:T(8,128)(2,1)S(1)}, bf16[64,32,128]{2,0,1:T(8,128)(2,1)S(1)}, u32[]{:S(2)}, u32[]{:S(2)}) collective-permute-start(bf16[64,32,128]{2,0,1:T(8,128)(2,1)S(1)} %copy_bitcast_fusion.2), channel_id=1, source_target_pairs={{248,0},{252,4},{0,8},{4,12},{8,16},{12,20},{16,24},{20,28},{24,32... | collective-permute-start | bytes 1572872 | tf_op jit(solution)/shard_map/ppermute | solution.py:14
  77.7 57.2 %collective-permute-start.3 = (bf16[64,32,128]{2,0,1:T(8,128)(2,1)S(1)}, bf16[64,32,128]{2,0,1:T(8,128)(2,1)S(1)}, u32[]{:S(2)}, u32[]{:S(2)}) collective-permute-start(bf16[64,32,128]{2,0,1:T(8,128)(2,1)S(1)} %copy_bitcast_fusion.2), channel_id=1, source_target_pairs={{252,0},{0,4},{4,8},{8,12},{12,16},{16,20},{20,24},{24,28},{28,32}... | collective-permute-start | bytes 1572872 | tf_op jit(solution)/shard_map/ppermute | solution.py:14
  78.6 78.8 %collective-permute-start.6 = (bf16[64,32,128]{2,0,1:T(8,128)(2,1)S(1)}, bf16[64,32,128]{2,0,1:T(8,128)(2,1)S(1)}, u32[]{:S(2)}, u32[]{:S(2)}) collective-permute-start(bf16[64,32,128]{2,0,1:T(8,128)(2,1)S(1)} %copy_bitcast_fusion.2), channel_id=1, source_target_pairs={{12,0},{16,4},{20,8},{24,12},{28,16},{32,20},{36,24},{40,28},{44,3... | collective-permute-start | bytes 1572872 | tf_op jit(solution)/shard_map/ppermute | solution.py:14
  111.3 45.3 %collective-permute-start.5 = (bf16[64,32,128]{2,0,1:T(8,128)(2,1)S(1)}, bf16[64,32,128]{2,0,1:T(8,128)(2,1)S(1)}, u32[]{:S(2)}, u32[]{:S(2)}) collective-permute-start(bf16[64,32,128]{2,0,1:T(8,128)(2,1)S(1)} %copy_bitcast_fusion.2), channel_id=1, source_target_pairs={{8,0},{12,4},{16,8},{20,12},{24,16},{28,20},{32,24},{36,28},{40,32... | collective-permute-start | bytes 1572872 | tf_op jit(solution)/shard_map/ppermute | solution.py:14
  126.5 29.2 %collective-permute-start.4 = (bf16[64,32,128]{2,0,1:T(8,128)(2,1)S(1)}, bf16[64,32,128]{2,0,1:T(8,128)(2,1)S(1)}, u32[]{:S(2)}, u32[]{:S(2)}) collective-permute-start(bf16[64,32,128]{2,0,1:T(8,128)(2,1)S(1)} %copy_bitcast_fusion.2), channel_id=1, source_target_pairs={{4,0},{8,4},{12,8},{16,12},{20,16},{24,20},{28,24},{32,28},{36,32}... | collective-permute-start | bytes 1572872 | tf_op jit(solution)/shard_map/ppermute | solution.py:14
  127.3 38.7 %collective-permute-start.7 = (bf16[64,32,128]{2,0,1:T(8,128)(2,1)S(1)}, bf16[64,32,128]{2,0,1:T(8,128)(2,1)S(1)}, u32[]{:S(2)}, u32[]{:S(2)}) collective-permute-start(bf16[64,32,128]{2,0,1:T(8,128)(2,1)S(1)} %copy_bitcast_fusion.2), channel_id=1, source_target_pairs={{16,0},{20,4},{24,8},{28,12},{32,16},{36,20},{40,24},{44,28},{48,3... | collective-permute-start | bytes 1572872 | tf_op jit(solution)/shard_map/ppermute | solution.py:14
  187.9 15.2 %copy-start.2 = (bf16[64,4096]{1,0:T(8,128)(2,1)S(1)}, bf16[64,4096]{1,0:T(8,128)(2,1)}, u32[]{:S(2)}) copy-start(bf16[64,4096]{1,0:T(8,128)(2,1)} %param.10) | copy-start | bytes 1572868
  247.5 124.4 %collective-permute-start.8 = (f32[64,32,128]{2,1,0:T(8,128)S(1)}, f32[64,32,128]{2,1,0:T(8,128)S(1)}, u32[]{:S(2)}, u32[]{:S(2)}) collective-permute-start(f32[64,32,128]{2,1,0:T(8,128)S(1)} %get-tuple-element.5), channel_id=1, source_target_pairs={{16,0},{20,4},{24,8},{28,12},{32,16},{36,20},{40,24},{44,28},{48,3... | collective-permute-start | bytes 3145736 | tf_op jit(solution)/shard_map/ppermute | solution.py:14
  253.7 118.4 %collective-permute-start.15 = (f32[64,32,128]{2,1,0:T(8,128)S(1)}, f32[64,32,128]{2,1,0:T(8,128)S(1)}, u32[]{:S(2)}, u32[]{:S(2)}) collective-permute-start(f32[64,32,128]{2,1,0:T(8,128)S(1)} %get-tuple-element.6), channel_id=1, source_target_pairs={{240,0},{244,4},{248,8},{252,12},{0,16},{4,20},{8,24},{12,28},{16,... | collective-permute-start | bytes 3145736 | tf_op jit(solution)/shard_map/ppermute | solution.py:14
  253.9 118.3 %collective-permute-start.14 = (f32[64,32,128]{2,1,0:T(8,128)S(1)}, f32[64,32,128]{2,1,0:T(8,128)S(1)}, u32[]{:S(2)}, u32[]{:S(2)}) collective-permute-start(f32[64,32,128]{2,1,0:T(8,128)S(1)} %get-tuple-element.7), channel_id=1, source_target_pairs={{244,0},{248,4},{252,8},{0,12},{4,16},{8,20},{12,24},{16,28},{20,3... | collective-permute-start | bytes 3145736 | tf_op jit(solution)/shard_map/ppermute | solution.py:14
  253.9 124.7 %collective-permute-start.13 = (f32[64,32,128]{2,1,0:T(8,128)S(1)}, f32[64,32,128]{2,1,0:T(8,128)S(1)}, u32[]{:S(2)}, u32[]{:S(2)}) collective-permute-start(f32[64,32,128]{2,1,0:T(8,128)S(1)} %get-tuple-element.8), channel_id=1, source_target_pairs={{248,0},{252,4},{0,8},{4,12},{8,16},{12,20},{16,24},{20,28},{24,32... | collective-permute-start | bytes 3145736 | tf_op jit(solution)/shard_map/ppermute | solution.py:14
  253.9 124.7 %collective-permute-start.12 = (f32[64,32,128]{2,1,0:T(8,128)S(1)}, f32[64,32,128]{2,1,0:T(8,128)S(1)}, u32[]{:S(2)}, u32[]{:S(2)}) collective-permute-start(f32[64,32,128]{2,1,0:T(8,128)S(1)} %get-tuple-element.9), channel_id=1, source_target_pairs={{252,0},{0,4},{4,8},{8,12},{12,16},{16,20},{20,24},{24,28},{28,32}... | collective-permute-start | bytes 3145736 | tf_op jit(solution)/shard_map/ppermute | solution.py:14
  371.9 60.8 %collective-permute-start.11 = (f32[64,32,128]{2,1,0:T(8,128)S(1)}, f32[64,32,128]{2,1,0:T(8,128)S(1)}, u32[]{:S(2)}, u32[]{:S(2)}) collective-permute-start(f32[64,32,128]{2,1,0:T(8,128)S(1)} %get-tuple-element.10), channel_id=1, source_target_pairs={{4,0},{8,4},{12,8},{16,12},{20,16},{24,20},{28,24},{32,28},{36,32}... | collective-permute-start | bytes 3145736 | tf_op jit(solution)/shard_map/ppermute | solution.py:14
  372.1 95.0 %collective-permute-start.10 = (f32[64,32,128]{2,1,0:T(8,128)S(1)}, f32[64,32,128]{2,1,0:T(8,128)S(1)}, u32[]{:S(2)}, u32[]{:S(2)}) collective-permute-start(f32[64,32,128]{2,1,0:T(8,128)S(1)} %get-tuple-element.11), channel_id=1, source_target_pairs={{8,0},{12,4},{16,8},{20,12},{24,16},{28,20},{32,24},{36,28},{40,32... | collective-permute-start | bytes 3145736 | tf_op jit(solution)/shard_map/ppermute | solution.py:14
  372.3 144.8 %copy-start.3 = (bf16[64,256]{1,0:T(8,128)(2,1)S(1)}, bf16[64,256]{1,0:T(8,128)(2,1)}, u32[]{:S(2)}) copy-start(bf16[64,256]{1,0:T(8,128)(2,1)} %param.9) | copy-start | bytes 98308
  372.3 113.7 %collective-permute-start.9 = (f32[64,32,128]{2,1,0:T(8,128)S(1)}, f32[64,32,128]{2,1,0:T(8,128)S(1)}, u32[]{:S(2)}, u32[]{:S(2)}) collective-permute-start(f32[64,32,128]{2,1,0:T(8,128)S(1)} %get-tuple-element.12), channel_id=1, source_target_pairs={{12,0},{16,4},{20,8},{24,12},{28,16},{32,20},{36,24},{40,28},{44,3... | collective-permute-start | bytes 3145736 | tf_op jit(solution)/shard_map/ppermute | solution.py:14
  488.2 559.5 %all-reduce.2.cloned.1.call-start = ((), (), s32[]{:S(2)}) async-start(), calls=%async_computation.3 | async-start | bytes 131072 | tf_op jit(solution)/shard_map/psum | solution.py:77
Sparse Core Ops, SparseCore 0:
  11.8 56.8 reduce-scatter.1
  488.3 25.6 all-gather.1
  517.4 530.2 all-reduce.1
where the time goes:
time: 1060 us
  waiting for transfers between devices  896 us (85%)
  matrix products  67.2 us (6%)
  starting transfers between devices  41.1 us (4%)
  local copies, waits for them, and re-layouts  31.1 us (3%)
  between operations  14.9 us (1%)
    psum x1, waiting for transfers between devices, per_device(): weight_grad = lax.psum(weight_grad * factor, 'blk')  528 us
    ppermute x16, waiting for transfers between devices, shifted(): return lax.ppermute(block, axis, route)  286 us
    reduce_scatter x1, waiting for transfers between devices, per_device(): lax.psum_scatter(lax.dot_general(w_cols, x_t, (((0,), (0,)), ((), ())), p...  56.9 us
    ppermute x16, starting transfers between devices, shifted(): return lax.ppermute(block, axis, route)  40.9 us
    all_gather x1, waiting for transfers between devices, per_device(): piece = lax.all_gather(grad_proj, 'feat', axis=0, tiled=True)  25.8 us
  transfers between devices with their start and end apart: 19, of which 12 were waited for; matrix products, arithmetic and copies ran while one was open for 1% of the time, Pallas kernels for 0%

commit v1 on v0

v1 whole, which is shorter than its diff:
```python
import functools
import math

import jax
import jax.numpy as jnp
from jax import lax
from jax.experimental import pallas as pl
from jax.experimental.pallas import tpu as pltpu
from jax.sharding import PartitionSpec as P

REACH = 4
SPAN = 2 * REACH + 1
UNROLL = 4
RING = 16
OFFSETS = [0] + [s * d for d in range(1, REACH + 1) for s in (1, -1)]


def shifted(block, distance):
    count = lax.axis_size("blk")
    route = [((i - distance) % count, i) for i in range(count)]
    return lax.ppermute(block, "blk", route)


def flipped(block, axis, bit):
    return lax.ppermute(block, axis, [(i, i ^ bit) for i in range(lax.axis_size(axis))])


def exchanged_columns(array, place):
    q = array.shape[1] // 4
    b = [array[:, i * q : (i + 1) * q] for i in range(4)]
    swapped = jnp.concatenate([b[1], b[0], b[3], b[2]], axis=1)
    array = jnp.where(place % 2 == 1, swapped, array)
    halves = jnp.concatenate([array[:, 2 * q :], array[:, : 2 * q]], axis=1)
    return jnp.where(place // 2 == 1, halves, array)


def plan_body(row_ref, col_ref, off_ref, count_ref, order_ref, src_ref, dst_ref, start_ref, fill):
    live = count_ref[0]

    def key_of(s):
        o = off_ref[s]
        return 2 * jnp.abs(o) - (o > 0).astype(jnp.int32)

    for k in range(16):
        fill[k] = 0

    def tally(s, c):
        k = key_of(s)
        fill[k] = fill[k] + 1
        return c

    lax.fori_loop(0, live, tally, 0)
    total = jnp.int32(0)
    for k in range(16):
        n = fill[k]
        start_ref[k] = total
        fill[k] = total
        total = total + n

    def place(s, c):
        k = key_of(s)
        at = fill[k]
        fill[k] = at + 1
        order_ref[at] = s
        src_ref[at] = k * 32 + col_ref[s]
        dst_ref[at] = row_ref[s]
        return c

    lax.fori_loop(0, live, place, 0)


def plan(tile_row, tile_col, tile_off, tile_count):
    slots = tile_row.shape[0]
    smem = pl.BlockSpec(memory_space=pltpu.SMEM)
    ints = jax.ShapeDtypeStruct((slots,), jnp.int32)
    return pl.pallas_call(
        plan_body,
        out_shape=(ints, ints, ints, jax.ShapeDtypeStruct((16,), jnp.int32)),
        in_specs=[smem] * 4,
        out_specs=(smem,) * 4,
        scratch_shapes=[pltpu.SMEM((16,), jnp.int32)],
        name="plan",
    )(tile_row, tile_col, tile_off, tile_count)


def tile_loop(begin, end, order_ref, vals_ref, ring, sems, multiply):
    n = end - begin

    def copy(i):
        slot = lax.rem(i, RING)
        return pltpu.make_async_copy(vals_ref.at[order_ref[begin + i]], ring.at[slot], sems.at[slot])

    def prime(i, c):
        copy(i).start()
        return c

    lax.fori_loop(0, jnp.minimum(n, RING), prime, 0)

    def step(first, width):
        for u in range(width):
            copy(first + u).wait()
        base = lax.rem(first, RING)
        multiply([begin + first + u for u in range(width)], [ring[base + u] for u in range(width)])
        for u in range(width):
            nxt = first + u + RING

            @pl.when(nxt < n)
            def _():
                copy(nxt).start()

    groups = n // UNROLL

    def group(g, c):
        step(g * UNROLL, UNROLL)
        return c

    lax.fori_loop(0, groups, group, 0)

    def single(i, c):
        step(i, 1)
        return c

    lax.fori_loop(groups * UNROLL, n, single, 0)


def forward_body(first, last, seeded, narrow, *refs):
    order_ref, src_ref, dst_ref, start_ref, vals_ref = refs[:5]
    slabs = refs[5 : 5 + last - first]
    rest = refs[5 + last - first :]
    if seeded:
        seed_ref, rest = rest[0], rest[1:]
    out_ref, acc, held, ring, sems, slab_sems = rest
    copies = [
        pltpu.make_async_copy(slab, held.at[j], slab_sems.at[j]) for j, slab in enumerate(slabs)
    ]
    for c in copies:
        c.start()
    if seeded:
        acc[...] = seed_ref[...]
    else:
        acc[...] = jnp.zeros_like(acc)
    for c in copies:
        c.wait()

    def multiply(positions, tiles):
        parts = []
        for at, tile in zip(positions, tiles):
            src = src_ref[at]
            lane = pl.multiple_of((src % 32) * 128, 128)
            piece = held[src // 32 - first, :, pl.ds(lane, 128)]
            parts.append(
                lax.dot_general(
                    piece, tile, (((1,), (1,)), ((), ())), preferred_element_type=jnp.float32
                )
            )
        for at, part in zip(positions, parts):
            lane = pl.multiple_of(dst_ref[at] * 128, 128)
            acc[:, pl.ds(lane, 128)] += part

    tile_loop(start_ref[first], start_ref[last], order_ref, vals_ref, ring, sems, multiply)
    out_ref[...] = acc[...].astype(out_ref.dtype)


def forward(first, last, listed, vals, slabs, seed, dtype):
    feats, nodes = slabs[0].shape
    smem = pl.BlockSpec(memory_space=pltpu.SMEM)
    hbm = pl.BlockSpec(memory_space=pl.ANY)
    vmem = pl.BlockSpec(memory_space=pltpu.VMEM)
    n = last - first
    return pl.pallas_call(
        functools.partial(forward_body, first, last, seed is not None, dtype),
        out_shape=jax.ShapeDtypeStruct((feats, nodes), dtype),
        in_specs=[smem] * 4 + [hbm] * (1 + n) + ([vmem] if seed is not None else []),
        out_specs=vmem,
        scratch_shapes=[
            pltpu.VMEM((feats, nodes), jnp.float32),
            pltpu.VMEM((n, feats, nodes), slabs[0].dtype),
            pltpu.VMEM((RING, 128, 128), vals.dtype),
            pltpu.SemaphoreType.DMA((RING,)),
            pltpu.SemaphoreType.DMA((n,)),
        ],
        name=f"forward_{first}_{last}",
    )(*listed, vals, *slabs, *(() if seed is None else (seed,)))


def backward_body(first, last, *refs):
    order_ref, src_ref, dst_ref, start_ref, vals_ref, grad_ref = refs[:6]
    outs = refs[6 : 6 + last - first]
    acc, ring, sems = refs[6 + last - first :]
    acc[...] = jnp.zeros_like(acc)

    def multiply(positions, tiles):
        parts = []
        for at, tile in zip(positions, tiles):
            lane = pl.multiple_of(dst_ref[at] * 128, 128)
            piece = grad_ref[:, pl.ds(lane, 128)]
            parts.append(jnp.dot(piece, tile, preferred_element_type=jnp.float32))
        for at, part in zip(positions, parts):
            src = src_ref[at]
            lane = pl.multiple_of((src % 32) * 128, 128)
            acc[src // 32 - first, :, pl.ds(lane, 128)] += part

    tile_loop(start_ref[first], start_ref[last], order_ref, vals_ref, ring, sems, multiply)
    for j, out in enumerate(outs):
        out[...] = acc[j].astype(out.dtype)


def backward(first, last, listed, vals, grad, dtypes):
    feats, nodes = grad.shape
    smem = pl.BlockSpec(memory_space=pltpu.SMEM)
    hbm = pl.BlockSpec(memory_space=pl.ANY)
    vmem = pl.BlockSpec(memory_space=pltpu.VMEM)
    n = last - first
    return pl.pallas_call(
        functools.partial(backward_body, first, last),
        out_shape=tuple(jax.ShapeDtypeStruct((feats, nodes), d) for d in dtypes),
        in_specs=[smem] * 4 + [hbm, vmem],
        out_specs=(vmem,) * n,
        scratch_shapes=[
            pltpu.VMEM((n, feats, nodes), jnp.float32),
            pltpu.VMEM((RING, 128, 128), vals.dtype),
            pltpu.SemaphoreType.DMA((RING,)),
        ],
        name=f"backward_{first}_{last}",
    )(*listed, vals, grad)


def middle_body(*refs):
    ys, cots, ws = refs[0:4], refs[4:8], refs[8:12]
    out_ref, grad_ref, wgrad_ref, turned = refs[12:]
    step = pl.program_id(0)
    feats = ys[0].shape[0]

    @pl.when(step == 0)
    def _():
        rows = []
        for k in range(4):
            w = ws[k][...]
            rows.append(
                jnp.concatenate(
                    [w[:, (j ^ k) * feats : ((j ^ k) + 1) * feats] for j in range(4)], axis=1
                )
            )
        turned[...] = jnp.concatenate(rows, axis=0).T
        wgrad_ref[...] = jnp.zeros_like(wgrad_ref)

    y = jnp.concatenate([r[...] for r in ys], axis=0)
    pre = jnp.dot(turned[...], y, preferred_element_type=jnp.float32)
    sig = jax.nn.sigmoid(pre)
    out_ref[...] = (pre[:feats] * sig[:feats]).astype(out_ref.dtype)
    cot = jnp.concatenate([r[...] for r in cots], axis=0).astype(jnp.float32)
    grad_pre = (cot * (sig * (1.0 + pre * (1.0 - sig)))).astype(jnp.bfloat16)
    grad_ref[...] = jnp.dot(
        ws[0][...], grad_pre, preferred_element_type=jnp.float32
    ).astype(grad_ref.dtype)
    wgrad_ref[...] += lax.dot_general(
        ys[0][...], grad_pre, (((1,), (1,)), ((), ())), preferred_element_type=jnp.float32
    )


def middle(ys, packed):
    feats, nodes = ys[0].shape
    hidden = 4 * feats
    chunk = 512
    piece = pl.BlockSpec((feats, chunk), lambda i: (0, i))
    w_spec = pl.BlockSpec((feats, hidden), lambda i: (0, nodes // hidden))
    whole = pl.BlockSpec((feats, hidden), lambda i: (0, 0))
    return pl.pallas_call(
        middle_body,
        grid=(nodes // chunk,),
        out_shape=(
            jax.ShapeDtypeStruct((feats, nodes), jnp.bfloat16),
            jax.ShapeDtypeStruct((feats, nodes), jnp.bfloat16),
            jax.ShapeDtypeStruct((feats, hidden), jnp.float32),
        ),
        in_specs=[piece] * 8 + [w_spec] * 4,
        out_specs=(piece, piece, whole),
        scratch_shapes=[pltpu.VMEM((hidden, hidden), jnp.bfloat16)],
        name="middle",
    )(*ys, *packed, *packed)


def per_device(x_t, weight, cotangent, tile_row, tile_col, tile_off, tile_vals, tile_count):
    nodes = x_t.shape[1]
    place = lax.axis_index("feat")
    slabs = {o: (shifted(x_t, -o) if o else x_t) for o in OFFSETS}
    own = jnp.concatenate([cotangent, exchanged_columns(weight, place)], axis=1)
    far = flipped(own, "feat", 2)
    packed = [own, flipped(own, "feat", 1), far, flipped(far, "feat", 1)]
    listed = plan(tile_row, tile_col, tile_off, tile_count)
    near = forward(0, 5, listed, tile_vals, [slabs[o] for o in OFFSETS[:5]], None, jnp.float32)
    y = forward(5, 9, listed, tile_vals, [slabs[o] for o in OFFSETS[5:]], near, jnp.bfloat16)
    y_far = flipped(y, "feat", 2)
    ys = [y, flipped(y, "feat", 1), y_far, flipped(y_far, "feat", 1)]
    out_t, grad, wgrad = middle(ys, packed)
    bf16 = jnp.bfloat16
    sent = dict(zip(OFFSETS[5:], backward(5, 9, listed, tile_vals, grad, [bf16] * 4)))
    total, *nearer = backward(0, 5, listed, tile_vals, grad, [jnp.float32] + [bf16] * 4)
    sent.update(zip(OFFSETS[1:5], nearer))
    for o in OFFSETS[::-1][:-1]:
        total = total + shifted(sent[o], o).astype(jnp.float32)
    wgrad = wgrad * (1.0 / math.sqrt(nodes * lax.axis_size("blk")))
    bit = 1
    while bit < lax.axis_size("blk"):
        wgrad = wgrad + flipped(wgrad, "blk", bit)
        bit *= 2
    return (out_t, total.astype(bf16), exchanged_columns(wgrad, place))


def solution(mesh):
    placed = (
        P("feat", "blk"),
        P("feat", None),
        P("feat", "blk"),
        P("blk"),
        P("blk"),
        P("blk"),
        P("blk", None, None),
        P("blk"),
    )
    return jax.shard_map(
        per_device,
        mesh=mesh,
        in_specs=placed,
        out_specs=(P("feat", "blk"), P("feat", "blk"), P("feat", None)),
        check_vma=False,
    )
```

time: 1060 us -> 276 us (0.26)
  the two profiles are of different devices: /device:TPU:4 before, /device:TPU:112 now
where the time goes in v1:
time: 276 us; the launch traced here: 273 us
  starting transfers between devices  131 us (47%)
  waiting for transfers between devices  95.4 us (35%)
  Pallas kernels  36.3 us (13%)
  other arithmetic  5.91 us (2%)
    ppermute x16, starting transfers between devices, shifted(): return lax.ppermute(block, 'blk', route)  89.9 us
    ppermute x16, waiting for transfers between devices, shifted(): return lax.ppermute(block, 'blk', route)  59.4 us
    ppermute x12, starting transfers between devices, flipped(): lax.ppermute(block, axis, [(i, i ^ bit) for i in range(lax.axis_size(axis...  40.7 us
    ppermute x12, waiting for transfers between devices, flipped(): lax.ppermute(block, axis, [(i, i ^ bit) for i in range(lax.axis_size(axis...  36 us
    pallas_call x2, Pallas kernels, forward(): pl.pallas_call(functools.partial(forward_body, first, last, seed is not N...  13.3 us
    pallas_call x2, Pallas kernels, backward(): pl.pallas_call(functools.partial(backward_body, first, last), out_shape=t...  11.9 us
    pallas_call x1, Pallas kernels, middle(): pl.pallas_call(middle_body, grid=(nodes // chunk,), out_shape=(jax.ShapeD...  7.82 us
  transfers between devices with their start and end apart: 28, of which 10 were waited for; matrix products, arithmetic and copies ran while one was open for 1% of the time, Pallas kernels for 10%

profile of v1, /device:TPU:112, one launch (start us, length us, event | category | flops | bytes accessed | tf_op | source)
XLA Modules:
  0.0 272.7 jit_solution(7685730528860550137)
XLA Ops:
  1.2 1.5 collective-permute-start.5
  4.1 8.3 %collective-permute-start.3 = (bf16[64,4096]{1,0:T(8,128)(2,1)}, bf16[64,4096]{1,0:T(8,128)(2,1)S(1)}, u32[]{:S(2)}, u32[]{:S(2)}) collective-permute-start(bf16[64,4096]{1,0:T(8,128)(2,1)} %refs_5_.1), channel_id=1, source_target_pairs={{240,0},{244,4},{248,8},{252,12},{0,16},{4,20},{8,24},{12,28},{16,... | collective-permute-start | bytes 1572872 | tf_op jit(solution)/shard_map/ppermute | solution.py:21
  14.2 12.8 %collective-permute-done.6.refs_8_ = bf16[64,4096]{1,0:T(8,128)(2,1)S(1)} collective-permute-done((bf16[64,4096]{1,0:T(8,128)(2,1)}, bf16[64,4096]{1,0:T(8,128)(2,1)S(1)}, u32[]{:S(2)}, u32[]{:S(2)}) %collective-permute-start.6) | collective-permute-done | bytes 524320 | tf_op jit(solution)/shard_map/ppermute | solution.py:21
  27.0 28.5 %collective-permute-start = (bf16[64,4096]{1,0:T(8,128)(2,1)}, bf16[64,4096]{1,0:T(8,128)(2,1)}, u32[]{:S(2)}, u32[]{:S(2)}) collective-permute-start(bf16[64,4096]{1,0:T(8,128)(2,1)} %refs_5_.1), channel_id=1, source_target_pairs={{12,0},{16,4},{20,8},{24,12},{28,16},{32,20},{36,24},{40,28},{44,3... | collective-permute-start | bytes 1572872 | tf_op jit(solution)/shard_map/ppermute | solution.py:21
  55.5 3.3 %collective-permute-start.7 = (bf16[64,4096]{1,0:T(8,128)(2,1)}, bf16[64,4096]{1,0:T(8,128)(2,1)S(1)}, u32[]{:S(2)}, u32[]{:S(2)}) collective-permute-start(bf16[64,4096]{1,0:T(8,128)(2,1)} %refs_5_.1), channel_id=1, source_target_pairs={{248,0},{252,4},{0,8},{4,12},{8,16},{12,20},{16,24},{20,28},{24,32... | collective-permute-start | bytes 1572872 | tf_op jit(solution)/shard_map/ppermute | solution.py:21
  59.9 12.1 %collective-permute-done.7.refs_9_ = bf16[64,4096]{1,0:T(8,128)(2,1)S(1)} collective-permute-done((bf16[64,4096]{1,0:T(8,128)(2,1)}, bf16[64,4096]{1,0:T(8,128)(2,1)S(1)}, u32[]{:S(2)}, u32[]{:S(2)}) %collective-permute-start.7) | collective-permute-done | bytes 524320 | tf_op jit(solution)/shard_map/ppermute | solution.py:21
  72.9 2.7 %collective-permute-start.12 = (bf16[64,4352]{1,0:T(8,128)(2,1)S(1)}, bf16[64,4352]{1,0:T(8,128)(2,1)S(1)}, u32[]{:S(2)}, u32[]{:S(2)}) collective-permute-start(bf16[64,4352]{1,0:T(8,128)(2,1)S(1)} %pad_maximum_fusion.refs_4_.refs_8_), channel_id=1, source_target_pairs={{0,2},{1,3},{2,0},{3,1},{4,6},{5,7},{6,4},{7,5},{8,10},{9,11},{10,... | collective-permute-start | bytes 1671176 | tf_op jit(solution)/shard_map/ppermute | solution.py:25
  76.2 3.3 %plan.1 = (s32[288]{0:T(512)}, s32[288]{0:T(512)}, s32[288]{0:T(512)}, s32[16]{0:T(128)}) custom-call(s32[288]{0:T(512)} %row_ref.1, s32[288]{0:T(512)} %col_ref.1, s32[288]{0:T(512)} %off_ref.1, s32[1]{0:T(128)S(6)} %copy.11.count_ref), custom_call_target="tpu_custom_call" | custom-call | tf_op jit(solution)/shard_map/plan/pallas_call | solution.py:76
  79.6 6.7 %forward_0_5.1.refs_9_ = f32[64,4096]{1,0:T(8,128)} custom-call(s32[288]{0:T(512)} %get-tuple-element.19.refs_0_, s32[288]{0:T(512)} %get-tuple-element.20.refs_1_, s32[288]{0:T(512)} %get-tuple-element.21.refs_2_, s32[16]{0:T(128)} %get-tuple-element.22.refs_3_, bf16[288,128,128]{2,1,0:T(8,128)(2,1)} %refs_4_.7, bf16[64,4096]{1,0:T(8,128)(2,1)} %refs_5_.1, ...), custom_call_target="tpu_custom_call" | custom-call | tf_op jit(solution)/shard_map/forward_0_5/pallas_call | solution.py:170
  87.3 6.6 %forward_5_9.1.refs_0_ = bf16[64,4096]{1,0:T(8,128)(2,1)} custom-call(s32[288]{0:T(512)} %get-tuple-element.19.refs_0_, s32[288]{0:T(512)} %get-tuple-element.20.refs_1_, s32[288]{0:T(512)} %get-tuple-element.21.refs_2_, s32[16]{0:T(128)} %get-tuple-element.22.refs_3_, bf16[288,128,128]{2,1,0:T(8,128)(2,1)} %refs_4_.7, ...), custom_call_target="tpu_custom_call" | custom-call | tf_op jit(solution)/shard_map/forward_5_9/pallas_call | solution.py:170
  95.4 11.8 %collective-permute-done.9.refs_2_ = bf16[64,4096]{1,0:T(8,128)(2,1)S(1)} collective-permute-done((bf16[64,4096]{1,0:T(8,128)(2,1)}, bf16[64,4096]{1,0:T(8,128)(2,1)S(1)}, u32[]{:S(2)}, u32[]{:S(2)}) %collective-permute-start.9) | collective-permute-done | bytes 524320 | tf_op jit(solution)/shard_map/ppermute | solution.py:25
  107.3 2.0 collective-permute-done.10.refs_3_
  109.3 7.8 %middle.1 = (bf16[64,4096]{1,0:T(8,128)(2,1)}, bf16[64,4096]{1,0:T(8,128)(2,1)}, f32[64,256]{1,0:T(8,128)}) custom-call(bf16[64,4096]{1,0:T(8,128)(2,1)} %forward_5_9.1.refs_0_, bf16[64,4096]{1,0:T(8,128)(2,1)} %copy-done.6, bf16[64,4096]{1,0:T(8,128)(2,1)} %copy-done.5, bf16[64,4096]{1,0:T(8,128)(2,1)} %collective-permute-done.10.refs_3_, ...), custom_call_target="tpu_custom_call" | custom-call | tf_op jit(solution)/shard_map/middle/pallas_call | solution.py:268
  118.0 16.7 %collective-permute-start.22 = (f32[64,256]{1,0:T(8,128)S(1)}, f32[64,256]{1,0:T(8,128)S(1)}, u32[]{:S(2)}, u32[]{:S(2)}) collective-permute-start(f32[64,256]{1,0:T(8,128)S(1)} %broadcast_multiply_fusion), channel_id=1, source_target_pairs={{0,4},{4,0},{8,12},{12,8},{16,20},{20,16},{24,28},{28,24},{32,36},... | collective-permute-start | bytes 196616 | tf_op jit(solution)/shard_map/ppermute | solution.py:25
  134.7 2.4 collective-permute-done.22
  137.9 3.2 %collective-permute-start.23 = (f32[64,256]{1,0:T(8,128)S(1)}, f32[64,256]{1,0:T(8,128)S(1)}, u32[]{:S(2)}, u32[]{:S(2)}) collective-permute-start(f32[64,256]{1,0:T(8,128)S(1)} %fusion), channel_id=1, source_target_pairs={{0,8},{4,12},{8,0},{12,4},{16,24},{20,28},{24,16},{28,20},{32,40},... | collective-permute-start | bytes 196616 | tf_op jit(solution)/shard_map/ppermute | solution.py:25
  141.1 5.6 %backward_5_9.1 = (bf16[64,4096]{1,0:T(8,128)(2,1)}, bf16[64,4096]{1,0:T(8,128)(2,1)}, bf16[64,4096]{1,0:T(8,128)(2,1)}, bf16[64,4096]{1,0:T(8,128)(2,1)}) custom-call(s32[288]{0:T(512)} %get-tuple-element.19.refs_0_, s32[288]{0:T(512)} %get-tuple-element.20.refs_1_, s32[288]{0:T(512)} %get-tuple-element.21.refs_2_, s32[16]{0:T(128)} %get-tuple-element.22.refs_3_, ...), custom_call_target="tpu_custom_call" | custom-call | tf_op jit(solution)/shard_map/backward_5_9/pallas_call | solution.py:214
  146.8 12.2 %collective-permute-start.15 = (bf16[64,4096]{1,0:T(8,128)(2,1)}, bf16[64,4096]{1,0:T(8,128)(2,1)S(1)}, u32[]{:S(2)}, u32[]{:S(2)}) collective-permute-start(bf16[64,4096]{1,0:T(8,128)(2,1)} %get-tuple-element.27), channel_id=1, source_target_pairs={{240,0},{244,4},{248,8},{252,12},{0,16},{4,20},{8,24},{12,28},{16,... | collective-permute-start | bytes 1572872 | tf_op jit(solution)/shard_map/ppermute | solution.py:21
  159.1 14.8 %collective-permute-done.24 = f32[64,256]{1,0:T(8,128)S(1)} collective-permute-done((f32[64,256]{1,0:T(8,128)S(1)}, f32[64,256]{1,0:T(8,128)S(1)}, u32[]{:S(2)}, u32[]{:S(2)}) %collective-permute-start.24) | collective-permute-done | bytes 65568 | tf_op jit(solution)/shard_map/ppermute | solution.py:25
  173.8 1.5 collective-permute-start.25
  175.4 2.8 %collective-permute-done.25 = f32[64,256]{1,0:T(8,128)S(1)} collective-permute-done((f32[64,256]{1,0:T(8,128)S(1)}, f32[64,256]{1,0:T(8,128)S(1)}, u32[]{:S(2)}, u32[]{:S(2)}) %collective-permute-start.25) | collective-permute-done | bytes 65568 | tf_op jit(solution)/shard_map/ppermute | solution.py:25
  178.2 8.3 %collective-permute-start.26 = (f32[64,256]{1,0:T(8,128)S(1)}, f32[64,256]{1,0:T(8,128)S(1)}, u32[]{:S(2)}, u32[]{:S(2)}) collective-permute-start(f32[64,256]{1,0:T(8,128)S(1)} %add.60), channel_id=1, source_target_pairs={{0,64},{4,68},{8,72},{12,76},{16,80},{20,84},{24,88},{28,92},{32,9... | collective-permute-start | bytes 196616 | tf_op jit(solution)/shard_map/ppermute | solution.py:25
  186.5 2.2 collective-permute-done.26
  188.8 6.7 %collective-permute-start.27 = (f32[64,256]{1,0:T(8,128)S(1)}, f32[64,256]{1,0:T(8,128)S(1)}, u32[]{:S(2)}, u32[]{:S(2)}) collective-permute-start(f32[64,256]{1,0:T(8,128)S(1)} %add.61), channel_id=1, source_target_pairs={{0,128},{4,132},{8,136},{12,140},{16,144},{20,148},{24,152},{28,15... | collective-permute-start | bytes 196616 | tf_op jit(solution)/shard_map/ppermute | solution.py:25
  195.5 6.2 %backward_0_5.1 = (f32[64,4096]{1,0:T(8,128)}, bf16[64,4096]{1,0:T(8,128)(2,1)}, bf16[64,4096]{1,0:T(8,128)(2,1)}, bf16[64,4096]{1,0:T(8,128)(2,1)}, bf16[64,4096]{1,0:T(8,128)(2,1)}) custom-call(s32[288]{0:T(512)} %get-tuple-element.19.refs_0_, s32[288]{0:T(512)} %get-tuple-element.20.refs_1_, s32[288]{0:T(512)} %get-tuple-element.21.refs_2_, ...), custom_call_target="tpu_custom_call" | custom-call | tf_op jit(solution)/shard_map/backward_0_5/pallas_call | solution.py:214
  201.8 16.9 %collective-permute-start.17 = (bf16[64,4096]{1,0:T(8,128)(2,1)S(1)}, bf16[64,4096]{1,0:T(8,128)(2,1)S(1)}, u32[]{:S(2)}, u32[]{:S(2)}) collective-permute-start(bf16[64,4096]{1,0:T(8,128)(2,1)S(1)} %copy-done.13), channel_id=1, source_target_pairs={{244,0},{248,4},{252,8},{0,12},{4,16},{8,20},{12,24},{16,28},{20,3... | collective-permute-start | bytes 1572872 | tf_op jit(solution)/shard_map/ppermute | solution.py:21
  218.7 6.5 %collective-permute-start.18 = (bf16[64,4096]{1,0:T(8,128)(2,1)}, bf16[64,4096]{1,0:T(8,128)(2,1)S(1)}, u32[]{:S(2)}, u32[]{:S(2)}) collective-permute-start(bf16[64,4096]{1,0:T(8,128)(2,1)} %get-tuple-element.30), channel_id=1, source_target_pairs={{8,0},{12,4},{16,8},{20,12},{24,16},{28,20},{32,24},{36,28},{40,32... | collective-permute-start | bytes 1572872 | tf_op jit(solution)/shard_map/ppermute | solution.py:21
  225.3 6.3 %collective-permute-start.19 = (bf16[64,4096]{1,0:T(8,128)(2,1)}, bf16[64,4096]{1,0:T(8,128)(2,1)S(1)}, u32[]{:S(2)}, u32[]{:S(2)}) collective-permute-start(bf16[64,4096]{1,0:T(8,128)(2,1)} %get-tuple-element.31), channel_id=1, source_target_pairs={{248,0},{252,4},{0,8},{4,12},{8,16},{12,20},{16,24},{20,28},{24,32... | collective-permute-start | bytes 1572872 | tf_op jit(solution)/shard_map/ppermute | solution.py:21
  231.7 4.3 %collective-permute-start.20 = (bf16[64,4096]{1,0:T(8,128)(2,1)}, bf16[64,4096]{1,0:T(8,128)(2,1)S(1)}, u32[]{:S(2)}, u32[]{:S(2)}) collective-permute-start(bf16[64,4096]{1,0:T(8,128)(2,1)} %get-tuple-element.32), channel_id=1, source_target_pairs={{4,0},{8,4},{12,8},{16,12},{20,16},{24,20},{28,24},{32,28},{36,32}... | collective-permute-start | bytes 1572872 | tf_op jit(solution)/shard_map/ppermute | solution.py:21
  236.7 12.1 %collective-permute-done.18 = bf16[64,4096]{1,0:T(8,128)(2,1)S(1)} collective-permute-done((bf16[64,4096]{1,0:T(8,128)(2,1)}, bf16[64,4096]{1,0:T(8,128)(2,1)S(1)}, u32[]{:S(2)}, u32[]{:S(2)}) %collective-permute-start.18) | collective-permute-done | bytes 524320 | tf_op jit(solution)/shard_map/ppermute | solution.py:21
  248.8 22.4 %collective-permute-done.21 = bf16[64,4096]{1,0:T(8,128)(2,1)S(1)} collective-permute-done((bf16[64,4096]{1,0:T(8,128)(2,1)}, bf16[64,4096]{1,0:T(8,128)(2,1)S(1)}, u32[]{:S(2)}, u32[]{:S(2)}) %collective-permute-start.21) | collective-permute-done | bytes 524320 | tf_op jit(solution)/shard_map/ppermute | solution.py:21
  271.2 1.5 add_convert_fusion
  (75 shorter events, 10.8 us)
Async XLA Ops:
  0.6 26.3 %collective-permute-start.6 = (bf16[64,4096]{1,0:T(8,128)(2,1)}, bf16[64,4096]{1,0:T(8,128)(2,1)S(1)}, u32[]{:S(2)}, u32[]{:S(2)}) collective-permute-start(bf16[64,4096]{1,0:T(8,128)(2,1)} %refs_5_.1), channel_id=1, source_target_pairs={{8,0},{12,4},{16,8},{20,12},{24,16},{28,20},{32,24},{36,28},{40,32... | collective-permute-start | bytes 1572872 | tf_op jit(solution)/shard_map/ppermute | solution.py:21
  1.2 25.8 %collective-permute-start.5 = (bf16[64,4096]{1,0:T(8,128)(2,1)}, bf16[64,4096]{1,0:T(8,128)(2,1)S(1)}, u32[]{:S(2)}, u32[]{:S(2)}) collective-permute-start(bf16[64,4096]{1,0:T(8,128)(2,1)} %refs_5_.1), channel_id=1, source_target_pairs={{252,0},{0,4},{4,8},{8,12},{12,16},{16,20},{20,24},{24,28},{28,32}... | collective-permute-start | bytes 1572872 | tf_op jit(solution)/shard_map/ppermute | solution.py:21
  2.6 52.8 %collective-permute-start.4 = (bf16[64,4096]{1,0:T(8,128)(2,1)}, bf16[64,4096]{1,0:T(8,128)(2,1)S(1)}, u32[]{:S(2)}, u32[]{:S(2)}) collective-permute-start(bf16[64,4096]{1,0:T(8,128)(2,1)} %refs_5_.1), channel_id=1, source_target_pairs={{4,0},{8,4},{12,8},{16,12},{20,16},{24,20},{28,24},{32,28},{36,32}... | collective-permute-start | bytes 1572872 | tf_op jit(solution)/shard_map/ppermute | solution.py:21
  4.1 82.2 %collective-permute-start.3 = (bf16[64,4096]{1,0:T(8,128)(2,1)}, bf16[64,4096]{1,0:T(8,128)(2,1)S(1)}, u32[]{:S(2)}, u32[]{:S(2)}) collective-permute-start(bf16[64,4096]{1,0:T(8,128)(2,1)} %refs_5_.1), channel_id=1, source_target_pairs={{240,0},{244,4},{248,8},{252,12},{0,16},{4,20},{8,24},{12,28},{16,... | collective-permute-start | bytes 1572872 | tf_op jit(solution)/shard_map/ppermute | solution.py:21
  12.4 73.9 %collective-permute-start.2 = (bf16[64,4096]{1,0:T(8,128)(2,1)}, bf16[64,4096]{1,0:T(8,128)(2,1)S(1)}, u32[]{:S(2)}, u32[]{:S(2)}) collective-permute-start(bf16[64,4096]{1,0:T(8,128)(2,1)} %refs_5_.1), channel_id=1, source_target_pairs={{16,0},{20,4},{24,8},{28,12},{32,16},{36,20},{40,24},{44,28},{48,3... | collective-permute-start | bytes 1572872 | tf_op jit(solution)/shard_map/ppermute | solution.py:21
  27.0 52.6 %copy-start.9 = (bf16[64,4096]{1,0:T(8,128)(2,1)}, bf16[64,4096]{1,0:T(8,128)(2,1)S(1)}, u32[]{:S(2)}) copy-start(bf16[64,4096]{1,0:T(8,128)(2,1)S(1)} %collective-permute-done.6.refs_8_) | copy-start | bytes 1572868
  27.0 59.4 %collective-permute-start.1 = (bf16[64,4096]{1,0:T(8,128)(2,1)}, bf16[64,4096]{1,0:T(8,128)(2,1)}, u32[]{:S(2)}, u32[]{:S(2)}) collective-permute-start(bf16[64,4096]{1,0:T(8,128)(2,1)} %refs_5_.1), channel_id=1, source_target_pairs={{244,0},{248,4},{252,8},{0,12},{4,16},{8,20},{12,24},{16,28},{20,3... | collective-permute-start | bytes 1572872 | tf_op jit(solution)/shard_map/ppermute | solution.py:21
  27.0 52.6 %copy-start.10 = (bf16[64,4096]{1,0:T(8,128)(2,1)}, bf16[64,4096]{1,0:T(8,128)(2,1)S(1)}, u32[]{:S(2)}) copy-start(bf16[64,4096]{1,0:T(8,128)(2,1)S(1)} %collective-permute-done.5.refs_7_) | copy-start | bytes 1572868
  27.0 59.4 %collective-permute-start = (bf16[64,4096]{1,0:T(8,128)(2,1)}, bf16[64,4096]{1,0:T(8,128)(2,1)}, u32[]{:S(2)}, u32[]{:S(2)}) collective-permute-start(bf16[64,4096]{1,0:T(8,128)(2,1)} %refs_5_.1), channel_id=1, source_target_pairs={{12,0},{16,4},{20,8},{24,12},{28,16},{32,20},{36,24},{40,28},{44,3... | collective-permute-start | bytes 1572872 | tf_op jit(solution)/shard_map/ppermute | solution.py:21
  55.5 16.6 %collective-permute-start.7 = (bf16[64,4096]{1,0:T(8,128)(2,1)}, bf16[64,4096]{1,0:T(8,128)(2,1)S(1)}, u32[]{:S(2)}, u32[]{:S(2)}) collective-permute-start(bf16[64,4096]{1,0:T(8,128)(2,1)} %refs_5_.1), channel_id=1, source_target_pairs={{248,0},{252,4},{0,8},{4,12},{8,16},{12,20},{16,24},{20,28},{24,32... | collective-permute-start | bytes 1572872 | tf_op jit(solution)/shard_map/ppermute | solution.py:21
  59.9 34.9 %copy-start = (bf16[64,4352]{1,0:T(8,128)(2,1)}, bf16[64,4352]{1,0:T(8,128)(2,1)S(1)}, u32[]{:S(2)}) copy-start(bf16[64,4352]{1,0:T(8,128)(2,1)S(1)} %pad_maximum_fusion.refs_4_.refs_8_) | copy-start | bytes 1671172
  72.9 22.0 %collective-permute-start.12 = (bf16[64,4352]{1,0:T(8,128)(2,1)S(1)}, bf16[64,4352]{1,0:T(8,128)(2,1)S(1)}, u32[]{:S(2)}, u32[]{:S(2)}) collective-permute-start(bf16[64,4352]{1,0:T(8,128)(2,1)S(1)} %pad_maximum_fusion.refs_4_.refs_8_), channel_id=1, source_target_pairs={{0,2},{1,3},{2,0},{3,1},{4,6},{5,7},{6,4},{7,5},{8,10},{9,11},{10,... | collective-permute-start | bytes 1671176 | tf_op jit(solution)/shard_map/ppermute | solution.py:25
  93.9 13.3 %collective-permute-start.9 = (bf16[64,4096]{1,0:T(8,128)(2,1)}, bf16[64,4096]{1,0:T(8,128)(2,1)S(1)}, u32[]{:S(2)}, u32[]{:S(2)}) collective-permute-start(bf16[64,4096]{1,0:T(8,128)(2,1)} %forward_5_9.1.refs_0_), channel_id=1, source_target_pairs={{0,2},{1,3},{2,0},{3,1},{4,6},{5,7},{6,4},{7,5},{8,10},{9,11},{10,... | collective-permute-start | bytes 1572872 | tf_op jit(solution)/shard_map/ppermute | solution.py:25
  94.8 12.4 %collective-permute-start.11 = (bf16[64,4352]{1,0:T(8,128)(2,1)S(1)}, bf16[64,4352]{1,0:T(8,128)(2,1)S(1)}, u32[]{:S(2)}, u32[]{:S(2)}) collective-permute-start(bf16[64,4352]{1,0:T(8,128)(2,1)S(1)} %pad_maximum_fusion.refs_4_.refs_8_), channel_id=1, source_target_pairs={{0,1},{1,0},{2,3},{3,2},{4,5},{5,4},{6,7},{7,6},{8,9},{9,8},{10,11... | collective-permute-start | bytes 1671176 | tf_op jit(solution)/shard_map/ppermute | solution.py:25
  94.8 12.5 %collective-permute-start.13 = (bf16[64,4352]{1,0:T(8,128)(2,1)S(1)}, bf16[64,4352]{1,0:T(8,128)(2,1)S(1)}, u32[]{:S(2)}, u32[]{:S(2)}) collective-permute-start(bf16[64,4352]{1,0:T(8,128)(2,1)S(1)} %collective-permute-done.12.refs_6_.refs_10_), channel_id=1, source_target_pairs={{0,1},{1,0},{2,3},{3,2},{4,5},{5,4},{6,7},{7,6},{8,9},{9,8},{10,11... | collective-permute-start | bytes 1671176 | tf_op jit(solution)/shard_map/ppermute | solution.py:25
  95.3 11.9 %collective-permute-start.8 = (bf16[64,4096]{1,0:T(8,128)(2,1)}, bf16[64,4096]{1,0:T(8,128)(2,1)S(1)}, u32[]{:S(2)}, u32[]{:S(2)}) collective-permute-start(bf16[64,4096]{1,0:T(8,128)(2,1)} %forward_5_9.1.refs_0_), channel_id=1, source_target_pairs={{0,1},{1,0},{2,3},{3,2},{4,5},{5,4},{6,7},{7,6},{8,9},{9,8},{10,11... | collective-permute-start | bytes 1572872 | tf_op jit(solution)/shard_map/ppermute | solution.py:25
  107.3 2.0 collective-permute-start.10
  118.0 19.1 %collective-permute-start.22 = (f32[64,256]{1,0:T(8,128)S(1)}, f32[64,256]{1,0:T(8,128)S(1)}, u32[]{:S(2)}, u32[]{:S(2)}) collective-permute-start(f32[64,256]{1,0:T(8,128)S(1)} %broadcast_multiply_fusion), channel_id=1, source_target_pairs={{0,4},{4,0},{8,12},{12,8},{16,20},{20,16},{24,28},{28,24},{32,36},... | collective-permute-start | bytes 196616 | tf_op jit(solution)/shard_map/ppermute | solution.py:25
  137.9 21.0 %collective-permute-start.23 = (f32[64,256]{1,0:T(8,128)S(1)}, f32[64,256]{1,0:T(8,128)S(1)}, u32[]{:S(2)}, u32[]{:S(2)}) collective-permute-start(f32[64,256]{1,0:T(8,128)S(1)} %fusion), channel_id=1, source_target_pairs={{0,8},{4,12},{8,0},{12,4},{16,24},{20,28},{24,16},{28,20},{32,40},... | collective-permute-start | bytes 196616 | tf_op jit(solution)/shard_map/ppermute | solution.py:25
  146.7 78.6 %collective-permute-start.14 = (bf16[64,4096]{1,0:T(8,128)(2,1)}, bf16[64,4096]{1,0:T(8,128)(2,1)S(1)}, u32[]{:S(2)}, u32[]{:S(2)}) collective-permute-start(bf16[64,4096]{1,0:T(8,128)(2,1)} %get-tuple-element.26), channel_id=1, source_target_pairs={{16,0},{20,4},{24,8},{28,12},{32,16},{36,20},{40,24},{44,28},{48,3... | collective-permute-start | bytes 1572872 | tf_op jit(solution)/shard_map/ppermute | solution.py:21
  146.8 84.9 %collective-permute-start.15 = (bf16[64,4096]{1,0:T(8,128)(2,1)}, bf16[64,4096]{1,0:T(8,128)(2,1)S(1)}, u32[]{:S(2)}, u32[]{:S(2)}) collective-permute-start(bf16[64,4096]{1,0:T(8,128)(2,1)} %get-tuple-element.27), channel_id=1, source_target_pairs={{240,0},{244,4},{248,8},{252,12},{0,16},{4,20},{8,24},{12,28},{16,... | collective-permute-start | bytes 1572872 | tf_op jit(solution)/shard_map/ppermute | solution.py:21
  158.9 77.0 %collective-permute-start.16 = (bf16[64,4096]{1,0:T(8,128)(2,1)}, bf16[64,4096]{1,0:T(8,128)(2,1)S(1)}, u32[]{:S(2)}, u32[]{:S(2)}) collective-permute-start(bf16[64,4096]{1,0:T(8,128)(2,1)} %get-tuple-element.28), channel_id=1, source_target_pairs={{12,0},{16,4},{20,8},{24,12},{28,16},{32,20},{36,24},{40,28},{44,3... | collective-permute-start | bytes 1572872 | tf_op jit(solution)/shard_map/ppermute | solution.py:21
  159.0 14.9 %collective-permute-start.24 = (f32[64,256]{1,0:T(8,128)S(1)}, f32[64,256]{1,0:T(8,128)S(1)}, u32[]{:S(2)}, u32[]{:S(2)}) collective-permute-start(f32[64,256]{1,0:T(8,128)S(1)} %add.58), channel_id=1, source_target_pairs={{0,16},{4,20},{8,24},{12,28},{16,0},{20,4},{24,8},{28,12},{32,48},... | collective-permute-start | bytes 196616 | tf_op jit(solution)/shard_map/ppermute | solution.py:25
  173.8 4.4 %collective-permute-start.25 = (f32[64,256]{1,0:T(8,128)S(1)}, f32[64,256]{1,0:T(8,128)S(1)}, u32[]{:S(2)}, u32[]{:S(2)}) collective-permute-start(f32[64,256]{1,0:T(8,128)S(1)} %add.59), channel_id=1, source_target_pairs={{0,32},{4,36},{8,40},{12,44},{16,48},{20,52},{24,56},{28,60},{32,0... | collective-permute-start | bytes 196616 | tf_op jit(solution)/shard_map/ppermute | solution.py:25
  178.2 10.6 %collective-permute-start.26 = (f32[64,256]{1,0:T(8,128)S(1)}, f32[64,256]{1,0:T(8,128)S(1)}, u32[]{:S(2)}, u32[]{:S(2)}) collective-permute-start(f32[64,256]{1,0:T(8,128)S(1)} %add.60), channel_id=1, source_target_pairs={{0,64},{4,68},{8,72},{12,76},{16,80},{20,84},{24,88},{28,92},{32,9... | collective-permute-start | bytes 196616 | tf_op jit(solution)/shard_map/ppermute | solution.py:25
  188.8 29.9 %collective-permute-start.27 = (f32[64,256]{1,0:T(8,128)S(1)}, f32[64,256]{1,0:T(8,128)S(1)}, u32[]{:S(2)}, u32[]{:S(2)}) collective-permute-start(f32[64,256]{1,0:T(8,128)S(1)} %add.61), channel_id=1, source_target_pairs={{0,128},{4,132},{8,136},{12,140},{16,144},{20,148},{24,152},{28,15... | collective-permute-start | bytes 196616 | tf_op jit(solution)/shard_map/ppermute | solution.py:25
  201.8 69.4 %copy-start.4 = (f32[64,4096]{1,0:T(8,128)S(1)}, f32[64,4096]{1,0:T(8,128)}, u32[]{:S(2)}) copy-start(f32[64,4096]{1,0:T(8,128)} %get-tuple-element.25) | copy-start | bytes 3145732
  201.8 34.9 %collective-permute-start.17 = (bf16[64,4096]{1,0:T(8,128)(2,1)S(1)}, bf16[64,4096]{1,0:T(8,128)(2,1)S(1)}, u32[]{:S(2)}, u32[]{:S(2)}) collective-permute-start(bf16[64,4096]{1,0:T(8,128)(2,1)S(1)} %copy-done.13), channel_id=1, source_target_pairs={{244,0},{248,4},{252,8},{0,12},{4,16},{8,20},{12,24},{16,28},{20,3... | collective-permute-start | bytes 1572872 | tf_op jit(solution)/shard_map/ppermute | solution.py:21
  218.7 30.0 %collective-permute-start.18 = (bf16[64,4096]{1,0:T(8,128)(2,1)}, bf16[64,4096]{1,0:T(8,128)(2,1)S(1)}, u32[]{:S(2)}, u32[]{:S(2)}) collective-permute-start(bf16[64,4096]{1,0:T(8,128)(2,1)} %get-tuple-element.30), channel_id=1, source_target_pairs={{8,0},{12,4},{16,8},{20,12},{24,16},{28,20},{32,24},{36,28},{40,32... | collective-permute-start | bytes 1572872 | tf_op jit(solution)/shard_map/ppermute | solution.py:21
  225.3 23.4 %collective-permute-start.19 = (bf16[64,4096]{1,0:T(8,128)(2,1)}, bf16[64,4096]{1,0:T(8,128)(2,1)S(1)}, u32[]{:S(2)}, u32[]{:S(2)}) collective-permute-start(bf16[64,4096]{1,0:T(8,128)(2,1)} %get-tuple-element.31), channel_id=1, source_target_pairs={{248,0},{252,4},{0,8},{4,12},{8,16},{12,20},{16,24},{20,28},{24,32... | collective-permute-start | bytes 1572872 | tf_op jit(solution)/shard_map/ppermute | solution.py:21
  231.7 17.1 %collective-permute-start.20 = (bf16[64,4096]{1,0:T(8,128)(2,1)}, bf16[64,4096]{1,0:T(8,128)(2,1)S(1)}, u32[]{:S(2)}, u32[]{:S(2)}) collective-permute-start(bf16[64,4096]{1,0:T(8,128)(2,1)} %get-tuple-element.32), channel_id=1, source_target_pairs={{4,0},{8,4},{12,8},{16,12},{20,16},{24,20},{28,24},{32,28},{36,32}... | collective-permute-start | bytes 1572872 | tf_op jit(solution)/shard_map/ppermute | solution.py:21
  235.9 35.3 %collective-permute-start.21 = (bf16[64,4096]{1,0:T(8,128)(2,1)}, bf16[64,4096]{1,0:T(8,128)(2,1)S(1)}, u32[]{:S(2)}, u32[]{:S(2)}) collective-permute-start(bf16[64,4096]{1,0:T(8,128)(2,1)} %get-tuple-element.33), channel_id=1, source_target_pairs={{252,0},{0,4},{4,8},{8,12},{12,16},{16,20},{20,24},{24,28},{28,32}... | collective-permute-start | bytes 1572872 | tf_op jit(solution)/shard_map/ppermute | solution.py:21
  (10 other events, 42.6 us)

commit v2 on v0

v2 whole, which is shorter than its diff:
```python
import functools
import math

import jax
import jax.numpy as jnp
from jax import lax
from jax.experimental import pallas as pl
from jax.experimental.pallas import tpu as pltpu
from jax.sharding import PartitionSpec as P

REACH = 4
GROUP = 8
WAVES = [[0, 1, 2, -2], [4, -4], [3, -1, -3]]
MIB = 1 << 20


def stepped(block, forth):
    count = lax.axis_size("blk")
    route = [((i + (2 if forth == (i % 2 == 0) else -2)) % count, i) for i in range(count)]
    return lax.ppermute(block, "blk", route)


def flipped(block, axis, bit):
    return lax.ppermute(block, axis, [(i, i ^ bit) for i in range(lax.axis_size(axis))])


def exchanged_columns(array, place):
    q = array.shape[1] // 4
    b = [array[:, i * q : (i + 1) * q] for i in range(4)]
    swapped = jnp.concatenate([b[1], b[0], b[3], b[2]], axis=1)
    array = jnp.where(place % 2 == 1, swapped, array)
    halves = jnp.concatenate([array[:, 2 * q :], array[:, : 2 * q]], axis=1)
    return jnp.where(place // 2 == 1, halves, array)


COST = pl.CostEstimate(flops=0, transcendentals=0, bytes_accessed=24_000_000)
SMEM = pl.BlockSpec(memory_space=pltpu.SMEM)
VMEM = pl.BlockSpec(memory_space=pltpu.VMEM)


def near(array):
    return pltpu.with_memory_space_constraint(array, pltpu.VMEM)


def kept(mib):
    return pltpu.CompilerParams(vmem_limit_bytes=mib * MIB)


def plan_body(cap, row_ref, col_ref, off_ref, count_ref, sign_ref, list_ref, fill, home):
    sign = sign_ref[0]
    for w, wave in enumerate(WAVES):
        fill[w] = 0
        for j, offset in enumerate(wave):
            home[offset + REACH] = w + 16 * j

    def place(s, c):
        at_home = home[off_ref[s] * sign + REACH]
        wave = at_home & 15
        n = fill[wave]
        fill[wave] = n + 1
        list_ref[wave * cap + n] = (
            s + (row_ref[s] << 9) + (col_ref[s] << 15) + ((at_home >> 4) << 20)
        )
        return c

    lax.fori_loop(0, count_ref[0], place, 0)
    for w in range(len(WAVES)):
        n = fill[w]
        groups = (n + GROUP - 1) >> 3

        def pad(i, c):
            list_ref[w * cap + i] = 32 << 9
            return c

        lax.fori_loop(n, groups * GROUP, pad, 0)
        list_ref[len(WAVES) * cap + w] = groups


def plan(tile_row, tile_col, tile_off, tile_count, sign):
    cap = tile_row.shape[0] + GROUP
    return pl.pallas_call(
        functools.partial(plan_body, cap),
        out_shape=jax.ShapeDtypeStruct((len(WAVES) * cap + 16,), jnp.int32),
        in_specs=[SMEM] * 5,
        out_specs=SMEM,
        scratch_shapes=[pltpu.SMEM((16,), jnp.int32)] * 2,
        cost_estimate=COST,
        compiler_params=kept(2),
        name="plan",
    )(tile_row, tile_col, tile_off, tile_count, sign)


def tile_loop(wave, list_ref, vals_ref, multiply):
    cap = (list_ref.shape[0] - 16) // len(WAVES)

    def body(g, c):
        entries = [list_ref[wave * cap + g * GROUP + u] for u in range(GROUP)]
        multiply(entries, [vals_ref[e & 511] for e in entries])
        return c

    lax.fori_loop(0, list_ref[len(WAVES) * cap + wave], body, 0)


def column(tile):
    return pl.ds(pl.multiple_of(tile * 128, 128), 128)


def paired(first, second):
    zero = jnp.zeros_like(first)
    return jnp.concatenate(
        [jnp.concatenate([first, zero], axis=1), jnp.concatenate([zero, second], axis=1)], axis=0
    )


def forward_body(wave, seeded, *refs):
    n = len(WAVES[wave])
    list_ref, vals_ref = refs[:2]
    slabs, rest = refs[2 : 2 + n], refs[2 + n :]
    if seeded:
        seed_ref, rest = rest[0], rest[1:]
    out_ref, held = rest[:2]
    acc = rest[2] if len(rest) > 2 else out_ref
    acc[...] = seed_ref[...] if seeded else jnp.zeros_like(acc)
    for j, slab in enumerate(slabs):
        held[j] = slab[...]
    feats = acc.shape[0]
    held[n, :, 0:128] = jnp.zeros((feats, 128), held.dtype)

    def multiply(entries, tiles):
        pieces = [
            held[(e >> 20) + ((e >> 14) & 1) * n, :, column((e >> 15) & 31)] for e in entries
        ]
        products = [
            lax.dot_general(
                paired(pieces[u], pieces[u + 1]),
                jnp.concatenate([tiles[u], tiles[u + 1]], axis=1),
                (((1,), (1,)), ((), ())),
                preferred_element_type=jnp.float32,
            )
            for u in range(0, GROUP, 2)
        ]
        for u, e in enumerate(entries):
            half = products[u // 2][u % 2 * feats : (u % 2 + 1) * feats]
            acc[:, column((e >> 9) & 31)] += half

    tile_loop(wave, list_ref, vals_ref, multiply)
    if acc is not out_ref:
        out_ref[...] = acc[...].astype(out_ref.dtype)


def forward(wave, listed, vals, slabs, seed, dtype):
    feats, nodes = slabs[0].shape
    wide = dtype == jnp.float32
    return pl.pallas_call(
        functools.partial(forward_body, wave, seed is not None),
        out_shape=pltpu.VMEM((feats, nodes), dtype),
        in_specs=[SMEM] + [VMEM] * (1 + len(slabs) + (seed is not None)),
        out_specs=VMEM,
        scratch_shapes=[pltpu.VMEM((len(slabs) + 1, feats, nodes), slabs[0].dtype)]
        + ([] if wide else [pltpu.VMEM((feats, nodes), jnp.float32)]),
        cost_estimate=COST,
        compiler_params=kept(8),
        name=f"forward_{wave}",
    )(listed, near(vals), *map(near, slabs), *(() if seed is None else (near(seed),)))


def backward_body(wave, *refs):
    n = len(WAVES[wave])
    list_ref, vals_ref, grad_ref = refs[:3]
    outs, acc = refs[3:-1], refs[-1]
    acc[0:n] = jnp.zeros((n,) + acc.shape[1:], acc.dtype)
    feats = acc.shape[1]

    def multiply(entries, tiles):
        pieces = [grad_ref[:, column((e >> 9) & 31)] for e in entries]
        products = [
            jnp.dot(
                paired(pieces[u], pieces[u + 1]),
                jnp.concatenate([tiles[u], tiles[u + 1]], axis=0),
                preferred_element_type=jnp.float32,
            )
            for u in range(0, GROUP, 2)
        ]
        for u, e in enumerate(entries):
            half = products[u // 2][u % 2 * feats : (u % 2 + 1) * feats]
            acc[(e >> 20) + ((e >> 14) & 1) * n, :, column((e >> 15) & 31)] += half

    tile_loop(wave, list_ref, vals_ref, multiply)
    for j, out in enumerate(outs):
        out[...] = acc[j].astype(out.dtype)


def backward(wave, listed, vals, grad, dtypes):
    n = len(dtypes)
    return pl.pallas_call(
        functools.partial(backward_body, wave),
        out_shape=tuple(pltpu.VMEM(grad.shape, d) for d in dtypes),
        in_specs=[SMEM, VMEM, VMEM],
        out_specs=(VMEM,) * n,
        scratch_shapes=[pltpu.VMEM((n + 1,) + grad.shape, jnp.float32)],
        cost_estimate=COST,
        compiler_params=kept(8),
        name=f"backward_{wave}",
    )(listed, near(vals), near(grad))


def middle_body(*refs):
    ys, packed, (out_ref, grad_ref, wgrad_ref) = refs[0:4], refs[4:8], refs[8:]
    feats, nodes = ys[0].shape
    hidden = 4 * feats
    chunk = 512
    rows = []
    for k in range(4):
        w = packed[k][:, nodes:]
        rows.append(
            jnp.concatenate(
                [w[:, (j ^ k) * feats : ((j ^ k) + 1) * feats] for j in range(4)], axis=1
            )
        )
    own_rows = rows[0]
    turned = jnp.concatenate(rows, axis=0).T
    wgrad = jnp.zeros((feats, hidden), jnp.float32)
    for start in range(0, nodes, chunk):
        here = slice(start, start + chunk)
        y = jnp.concatenate([r[:, here] for r in ys], axis=0)
        pre = jnp.dot(turned, y, preferred_element_type=jnp.float32)
        sig = jax.nn.sigmoid(pre)
        out_ref[:, here] = (pre[:feats] * sig[:feats]).astype(out_ref.dtype)
        cot = jnp.concatenate([r[:, here] for r in packed], axis=0).astype(jnp.float32)
        grad_pre = (cot * (sig * (1.0 + pre * (1.0 - sig)))).astype(jnp.bfloat16)
        grad_ref[:, here] = jnp.dot(
            own_rows, grad_pre, preferred_element_type=jnp.float32
        ).astype(grad_ref.dtype)
        wgrad += lax.dot_general(
            ys[0][:, here], grad_pre, (((1,), (1,)), ((), ())), preferred_element_type=jnp.float32
        )
    wgrad_ref[...] = wgrad


def middle(ys, packed):
    feats, nodes = ys[0].shape
    return pl.pallas_call(
        middle_body,
        out_shape=(
            jax.ShapeDtypeStruct((feats, nodes), jnp.bfloat16),
            pltpu.VMEM((feats, nodes), jnp.bfloat16),
            pltpu.VMEM((feats, 4 * feats), jnp.float32),
        ),
        in_specs=[VMEM] * 8,
        out_specs=(VMEM,) * 3,
        cost_estimate=COST,
        compiler_params=kept(10),
        name="middle",
    )(*map(near, ys), *map(near, packed))


def fenced(*groups):
    return lax.optimization_barrier(groups)


def summed(value, radix_bits):
    low, high = radix_bits
    return [flipped(value, "blk", low), flipped(value, "blk", high), flipped(value, "blk", low | high)]


def per_device(x_t, weight, cotangent, tile_row, tile_col, tile_off, tile_vals, tile_count):
    nodes = x_t.shape[1]
    f32, bf16 = jnp.float32, jnp.bfloat16
    place = lax.axis_index("feat")
    sign = (1 - 2 * (lax.axis_index("blk") % 2)).astype(jnp.int32).reshape(1)
    own = jnp.concatenate([cotangent, exchanged_columns(weight, place)], axis=1)

    x, u, v = flipped(x_t, "blk", 1), stepped(x_t, True), stepped(x_t, False)
    listed = plan(tile_row, tile_col, tile_off, tile_count, sign)
    x, u, v, listed, own = fenced(x, u, v, listed, own)
    m, n, far = stepped(u, True), stepped(v, False), flipped(own, "feat", 2)
    y = forward(0, listed, tile_vals, [x_t, x, u, v], None, f32)
    m, n, y, x = fenced(m, n, y, x)
    mx, xu, xv = flipped(m, "blk", 1), stepped(x, True), stepped(x, False)
    y = forward(1, listed, tile_vals, [m, n], y, f32)
    xu, xv, mx, y, far, own = fenced(xu, xv, mx, y, far, own)
    packed = [own, flipped(own, "feat", 1), far, flipped(far, "feat", 1)]
    y = forward(2, listed, tile_vals, [xu, xv, mx], y, bf16)
    y_far = flipped(y, "feat", 2)
    out_t, grad, wgrad = middle([y, flipped(y, "feat", 1), y_far, flipped(y_far, "feat", 1)], packed)

    to_xu, to_xv, to_mx = backward(2, listed, tile_vals, grad, [bf16] * 3)
    from_mx = flipped(to_mx, "blk", 1)
    from_xu, from_xv = stepped(to_xu, False), stepped(to_xv, True)
    to_m, to_n = backward(1, listed, tile_vals, grad, [f32, bf16])
    wgrad = exchanged_columns(wgrad, place) * (1.0 / math.sqrt(nodes * lax.axis_size("blk")))
    parts = summed(wgrad, (1, 2))
    from_mx, to_m, grad = fenced(from_mx, to_m, grad)
    from_m = stepped((to_m + from_mx.astype(f32)).astype(bf16), False)
    from_n = stepped(to_n, True)
    total, to_x, to_u, to_v = backward(0, listed, tile_vals, grad, [f32] * 4)
    wgrad, parts, to_x = fenced(wgrad, parts, to_x)
    wgrad = (wgrad + parts[0]) + (parts[1] + parts[2])
    parts = summed(wgrad, (4, 8))
    from_x = flipped((to_x + from_xu.astype(f32) + from_xv.astype(f32)).astype(bf16), "blk", 1)
    from_v = stepped((to_v + from_n.astype(f32)).astype(bf16), True)
    from_u = stepped((to_u + from_m.astype(f32)).astype(bf16), False)
    wgrad = (wgrad + parts[0]) + (parts[1] + parts[2])
    parts = summed(wgrad, (16, 32))
    wgrad = (wgrad + parts[0]) + (parts[1] + parts[2])
    total = total + from_u.astype(f32) + from_v.astype(f32) + from_x.astype(f32)
    return (out_t, total.astype(bf16), wgrad)


def solution(mesh):
    placed = (
        P("feat", "blk"),
        P("feat", None),
        P("feat", "blk"),
        P("blk"),
        P("blk"),
        P("blk"),
        P("blk", None, None),
        P("blk"),
    )
    return jax.shard_map(
        per_device,
        mesh=mesh,
        in_specs=placed,
        out_specs=(P("feat", "blk"), P("feat", "blk"), P("feat", None)),
        check_vma=False,
    )
```

time: 1060 us -> 156 us (0.15)
  the two profiles are of different devices: /device:TPU:4 before, /device:TPU:6 now
where the time goes in v2:
time: 156 us; the launch traced here: 155 us
  waiting for transfers between devices  68.4 us (44%)
  starting transfers between devices  52.6 us (34%)
  Pallas kernels  21.1 us (14%)
  local copies, waits for them, and re-layouts  6.71 us (4%)
  other arithmetic  4.27 us (3%)
  between operations  1.58 us (1%)
    ppermute x12, waiting for transfers between devices, stepped(): return lax.ppermute(block, 'blk', route)  39.8 us
    ppermute x19, starting transfers between devices, flipped(): lax.ppermute(block, axis, [(i, i ^ bit) for i in range(lax.axis_size(axis...  31.1 us
    ppermute x19, waiting for transfers between devices, flipped(): lax.ppermute(block, axis, [(i, i ^ bit) for i in range(lax.axis_size(axis...  28.7 us
    ppermute x12, starting transfers between devices, stepped(): return lax.ppermute(block, 'blk', route)  21.5 us
    pallas_call x3, Pallas kernels, backward(): pl.pallas_call(functools.partial(backward_body, wave), out_shape=tuple((p...  7.43 us
    pallas_call x3, Pallas kernels, forward(): pl.pallas_call(functools.partial(forward_body, wave, seed is not None), o...  7.06 us
    unnamed x16, local copies, waits for them, and re-layouts  5.74 us
    pallas_call x1, Pallas kernels, middle(): pl.pallas_call(middle_body, out_shape=(jax.ShapeDtypeStruct((feats, nodes...  3.37 us
  transfers between devices with their start and end apart: 31, of which 14 were waited for; matrix products, arithmetic and copies ran while one was open for 3% of the time, Pallas kernels for 8%

profile of v2, /device:TPU:6, one launch (start us, length us, event | category | flops | bytes accessed | tf_op | source)
XLA Modules:
  0.0 154.7 jit_solution(18240083055421723131)
XLA Ops:
  0.6 1.7 %collective-permute-start.1 = (bf16[64,4096]{1,0:T(8,128)(2,1)}, bf16[64,4096]{1,0:T(8,128)(2,1)S(1)}, u32[]{:S(2)}, u32[]{:S(2)}) collective-permute-start(bf16[64,4096]{1,0:T(8,128)(2,1)} %refs_2_.1), channel_id=1, source_target_pairs={{8,0},{252,4},{16,8},{4,12},{24,16},{12,20},{32,24},{20,28},{40,32... | collective-permute-start | bytes 1572872 | tf_op jit(solution)/shard_map/ppermute | solution.py:20
  2.3 7.6 %collective-permute-start = (bf16[64,4096]{1,0:T(8,128)(2,1)}, bf16[64,4096]{1,0:T(8,128)(2,1)S(1)}, u32[]{:S(2)}, u32[]{:S(2)}) collective-permute-start(bf16[64,4096]{1,0:T(8,128)(2,1)} %refs_2_.1), channel_id=1, source_target_pairs={{0,4},{4,0},{8,12},{12,8},{16,20},{20,16},{24,28},{28,24},{32,36},... | collective-permute-start | bytes 1572872 | tf_op jit(solution)/shard_map/ppermute | solution.py:24
  15.1 3.2 %plan.1.refs_0_ = s32[904]{0:T(1024)S(1)} custom-call(s32[288]{0:T(512)S(1)} %copy-done.2, s32[288]{0:T(512)S(1)} %copy-done.3, s32[288]{0:T(512)S(1)} %copy-done.4, s32[1]{0:T(128)S(6)} %copy.11.count_ref, s32[1]{0:T(128)} %bitcast.sign_ref), custom_call_target="tpu_custom_call" | custom-call | bytes 24000000 | tf_op jit(solution)/shard_map/plan/pallas_call | solution.py:81
  19.4 1.8 %collective-permute-done.1.refs_4_ = bf16[64,4096]{1,0:T(8,128)(2,1)S(1)} collective-permute-done((bf16[64,4096]{1,0:T(8,128)(2,1)}, bf16[64,4096]{1,0:T(8,128)(2,1)S(1)}, u32[]{:S(2)}, u32[]{:S(2)}) %collective-permute-start.1) | collective-permute-done | bytes 524320 | tf_op jit(solution)/shard_map/ppermute | solution.py:20
  23.2 5.3 %collective-permute-start.4 = (bf16[64,4096]{1,0:T(8,128)(2,1)S(1)}, bf16[64,4096]{1,0:T(8,128)(2,1)S(1)}, u32[]{:S(2)}, u32[]{:S(2)}) collective-permute-start(bf16[64,4096]{1,0:T(8,128)(2,1)S(1)} %collective-permute-done.2.refs_5_), channel_id=1, source_target_pairs={{248,0},{12,4},{0,8},{20,12},{8,16},{28,20},{16,24},{36,28},{24,32... | collective-permute-start | bytes 1572872 | tf_op jit(solution)/shard_map/ppermute | solution.py:20
  29.6 3.7 %copy-done = bf16[288,128,128]{2,1,0:T(8,128)(2,1)S(1)} copy-done((bf16[288,128,128]{2,1,0:T(8,128)(2,1)S(1)}, bf16[288,128,128]{2,1,0:T(8,128)(2,1)}, u32[]{:S(2)}) %copy-start) | copy-done | bytes 9437208
  33.3 2.8 %forward_0.1.refs_4_ = f32[64,4096]{1,0:T(8,128)S(1)} custom-call(s32[904]{0:T(1024)S(1)} %plan.1.refs_0_, bf16[288,128,128]{2,1,0:T(8,128)(2,1)S(1)} %copy-done, bf16[64,4096]{1,0:T(8,128)(2,1)S(1)} %copy-done.1, bf16[64,4096]{1,0:T(8,128)(2,1)S(1)} %collective-permute-done.refs_3_, bf16[64,4096]{1,0:T(8,128)(2,1)S(1)} %collective-permute-done.1.refs_4_, ...), custom_call_target="tpu_custom_call" | custom-call | bytes 24000000 | tf_op jit(solution)/shard_map/forward_0/pallas_call | solution.py:154
  36.1 2.6 %collective-permute-done.3.refs_2_ = bf16[64,4096]{1,0:T(8,128)(2,1)S(1)} collective-permute-done((bf16[64,4096]{1,0:T(8,128)(2,1)S(1)}, bf16[64,4096]{1,0:T(8,128)(2,1)S(1)}, u32[]{:S(2)}, u32[]{:S(2)}) %collective-permute-start.3) | collective-permute-done | bytes 524320 | tf_op jit(solution)/shard_map/ppermute | solution.py:20
  38.7 5.1 %collective-permute-start.6 = (bf16[64,4096]{1,0:T(8,128)(2,1)S(1)}, bf16[64,4096]{1,0:T(8,128)(2,1)S(1)}, u32[]{:S(2)}, u32[]{:S(2)}) collective-permute-start(bf16[64,4096]{1,0:T(8,128)(2,1)S(1)} %collective-permute-done.refs_3_), channel_id=1, source_target_pairs={{248,0},{12,4},{0,8},{20,12},{8,16},{28,20},{16,24},{36,28},{24,32... | collective-permute-start | bytes 1572872 | tf_op jit(solution)/shard_map/ppermute | solution.py:20
  43.7 4.5 %collective-permute-start.7 = (bf16[64,4096]{1,0:T(8,128)(2,1)S(1)}, bf16[64,4096]{1,0:T(8,128)(2,1)S(1)}, u32[]{:S(2)}, u32[]{:S(2)}) collective-permute-start(bf16[64,4096]{1,0:T(8,128)(2,1)S(1)} %collective-permute-done.3.refs_2_), channel_id=1, source_target_pairs={{0,4},{4,0},{8,12},{12,8},{16,20},{20,16},{24,28},{28,24},{32,36},... | collective-permute-start | bytes 1572872 | tf_op jit(solution)/shard_map/ppermute | solution.py:24
  48.2 1.7 %forward_1.1.refs_5_ = f32[64,4096]{1,0:T(8,128)S(1)} custom-call(s32[904]{0:T(1024)S(1)} %plan.1.refs_0_, bf16[288,128,128]{2,1,0:T(8,128)(2,1)S(1)} %copy-done, bf16[64,4096]{1,0:T(8,128)(2,1)S(1)} %collective-permute-done.3.refs_2_, bf16[64,4096]{1,0:T(8,128)(2,1)S(1)} %collective-permute-done.4.refs_3_, f32[64,4096]{1,0:T(8,128)S(1)} %forward_0.1.refs_4_), custom_call_target="tpu_custom_call" | custom-call | bytes 24000000 | tf_op jit(solution)/shard_map/forward_1/pallas_call | solution.py:154
  50.0 2.2 %collective-permute-done.6.refs_3_ = bf16[64,4096]{1,0:T(8,128)(2,1)S(1)} collective-permute-done((bf16[64,4096]{1,0:T(8,128)(2,1)S(1)}, bf16[64,4096]{1,0:T(8,128)(2,1)S(1)}, u32[]{:S(2)}, u32[]{:S(2)}) %collective-permute-start.6) | collective-permute-done | bytes 524320 | tf_op jit(solution)/shard_map/ppermute | solution.py:20
  52.2 5.5 %collective-permute-done.5.refs_2_ = bf16[64,4096]{1,0:T(8,128)(2,1)S(1)} collective-permute-done((bf16[64,4096]{1,0:T(8,128)(2,1)S(1)}, bf16[64,4096]{1,0:T(8,128)(2,1)S(1)}, u32[]{:S(2)}, u32[]{:S(2)}) %collective-permute-start.5) | collective-permute-done | bytes 524320 | tf_op jit(solution)/shard_map/ppermute | solution.py:20
  57.8 2.6 %forward_2.1.refs_0_ = bf16[64,4096]{1,0:T(8,128)(2,1)S(1)} custom-call(s32[904]{0:T(1024)S(1)} %plan.1.refs_0_, bf16[288,128,128]{2,1,0:T(8,128)(2,1)S(1)} %copy-done, bf16[64,4096]{1,0:T(8,128)(2,1)S(1)} %collective-permute-done.5.refs_2_, bf16[64,4096]{1,0:T(8,128)(2,1)S(1)} %collective-permute-done.6.refs_3_, ...), custom_call_target="tpu_custom_call" | custom-call | bytes 24000000 | tf_op jit(solution)/shard_map/forward_2/pallas_call | solution.py:154
  62.0 10.0 %collective-permute-done.10.refs_2_ = bf16[64,4096]{1,0:T(8,128)(2,1)S(1)} collective-permute-done((bf16[64,4096]{1,0:T(8,128)(2,1)S(1)}, bf16[64,4096]{1,0:T(8,128)(2,1)S(1)}, u32[]{:S(2)}, u32[]{:S(2)}) %collective-permute-start.10) | collective-permute-done | bytes 524320 | tf_op jit(solution)/shard_map/ppermute | solution.py:24
  72.1 1.9 %collective-permute-done.11.refs_3_ = bf16[64,4096]{1,0:T(8,128)(2,1)S(1)} collective-permute-done((bf16[64,4096]{1,0:T(8,128)(2,1)S(1)}, bf16[64,4096]{1,0:T(8,128)(2,1)S(1)}, u32[]{:S(2)}, u32[]{:S(2)}) %collective-permute-start.11) | collective-permute-done | bytes 524320 | tf_op jit(solution)/shard_map/ppermute | solution.py:24
  74.0 3.4 %middle.1 = (bf16[64,4096]{1,0:T(8,128)(2,1)}, bf16[64,4096]{1,0:T(8,128)(2,1)S(1)}, f32[64,256]{1,0:T(8,128)S(1)}) custom-call(bf16[64,4096]{1,0:T(8,128)(2,1)S(1)} %forward_2.1.refs_0_, bf16[64,4096]{1,0:T(8,128)(2,1)S(1)} %collective-permute-done.9.refs_1_, bf16[64,4096]{1,0:T(8,128)(2,1)S(1)} %collective-permute-done.10.refs_2_, ...), custom_call_target="tpu_custom_call" | custom-call | bytes 24000000 | tf_op jit(solution)/shard_map/middle/pallas_call | solution.py:242
  77.5 2.6 %backward_2.1 = (bf16[64,4096]{1,0:T(8,128)(2,1)S(1)}, bf16[64,4096]{1,0:T(8,128)(2,1)S(1)}, bf16[64,4096]{1,0:T(8,128)(2,1)S(1)}) custom-call(s32[904]{0:T(1024)S(1)} %plan.1.refs_0_, bf16[288,128,128]{2,1,0:T(8,128)(2,1)S(1)} %bitcast.2, bf16[64,4096]{1,0:T(8,128)(2,1)S(1)} %get-tuple-element.57.refs_2_), custom_call_target="tpu_custom_call" | custom-call | bytes 24000000 | tf_op jit(solution)/shard_map/backward_2/pallas_call | solution.py:195
  80.1 3.5 %collective-permute-start.14 = (bf16[64,4096]{1,0:T(8,128)(2,1)S(1)}, bf16[64,4096]{1,0:T(8,128)(2,1)S(1)}, u32[]{:S(2)}, u32[]{:S(2)}) collective-permute-start(bf16[64,4096]{1,0:T(8,128)(2,1)S(1)} %get-tuple-element.55), channel_id=1, source_target_pairs={{0,4},{4,0},{8,12},{12,8},{16,20},{20,16},{24,28},{28,24},{32,36},... | collective-permute-start | bytes 1572872 | tf_op jit(solution)/shard_map/ppermute | solution.py:24
  85.3 2.0 %collective-permute-start.19 = (f32[64,256]{1,0:T(8,128)S(1)}, f32[64,256]{1,0:T(8,128)S(1)}, u32[]{:S(2)}, u32[]{:S(2)}) collective-permute-start(f32[64,256]{1,0:T(8,128)S(1)} %fusion), channel_id=1, source_target_pairs={{0,4},{4,0},{8,12},{12,8},{16,20},{20,16},{24,28},{28,24},{32,36},... | collective-permute-start | bytes 196616 | tf_op jit(solution)/shard_map/ppermute | solution.py:24
  87.3 1.8 %backward_1.1 = (f32[64,4096]{1,0:T(8,128)S(1)}, bf16[64,4096]{1,0:T(8,128)(2,1)S(1)}) custom-call(s32[904]{0:T(1024)S(1)} %plan.1.refs_0_, bf16[288,128,128]{2,1,0:T(8,128)(2,1)S(1)} %bitcast.2, bf16[64,4096]{1,0:T(8,128)(2,1)S(1)} %get-tuple-element.57.refs_2_), custom_call_target="tpu_custom_call" | custom-call | bytes 24000000 | tf_op jit(solution)/shard_map/backward_1/pallas_call | solution.py:195
  89.1 2.5 %collective-permute-start.22 = (bf16[64,4096]{1,0:T(8,128)(2,1)S(1)}, bf16[64,4096]{1,0:T(8,128)(2,1)S(1)}, u32[]{:S(2)}, u32[]{:S(2)}) collective-permute-start(bf16[64,4096]{1,0:T(8,128)(2,1)S(1)} %get-tuple-element.67), channel_id=1, source_target_pairs={{248,0},{12,4},{0,8},{20,12},{8,16},{28,20},{16,24},{36,28},{24,32... | collective-permute-start | bytes 1572872 | tf_op jit(solution)/shard_map/ppermute | solution.py:20
  91.6 4.7 %collective-permute-done.14 = bf16[64,4096]{1,0:T(8,128)(2,1)S(1)} collective-permute-done((bf16[64,4096]{1,0:T(8,128)(2,1)S(1)}, bf16[64,4096]{1,0:T(8,128)(2,1)S(1)}, u32[]{:S(2)}, u32[]{:S(2)}) %collective-permute-start.14) | collective-permute-done | bytes 524320 | tf_op jit(solution)/shard_map/ppermute | solution.py:24
  96.3 3.0 %backward_0.1 = (f32[64,4096]{1,0:T(8,128)S(1)}, f32[64,4096]{1,0:T(8,128)S(1)}, f32[64,4096]{1,0:T(8,128)S(1)}, f32[64,4096]{1,0:T(8,128)S(1)}) custom-call(s32[904]{0:T(1024)S(1)} %plan.1.refs_0_, bf16[288,128,128]{2,1,0:T(8,128)(2,1)S(1)} %bitcast.2, bf16[64,4096]{1,0:T(8,128)(2,1)S(1)} %get-tuple-element.57.refs_2_), custom_call_target="tpu_custom_call" | custom-call | bytes 24000000 | tf_op jit(solution)/shard_map/backward_0/pallas_call | solution.py:195
  100.2 5.3 %collective-permute-done.22 = bf16[64,4096]{1,0:T(8,128)(2,1)S(1)} collective-permute-done((bf16[64,4096]{1,0:T(8,128)(2,1)S(1)}, bf16[64,4096]{1,0:T(8,128)(2,1)S(1)}, u32[]{:S(2)}, u32[]{:S(2)}) %collective-permute-start.22) | collective-permute-done | bytes 524320 | tf_op jit(solution)/shard_map/ppermute | solution.py:20
  105.5 10.9 %collective-permute-done.23 = bf16[64,4096]{1,0:T(8,128)(2,1)S(1)} collective-permute-done((bf16[64,4096]{1,0:T(8,128)(2,1)S(1)}, bf16[64,4096]{1,0:T(8,128)(2,1)S(1)}, u32[]{:S(2)}, u32[]{:S(2)}) %collective-permute-start.23) | collective-permute-done | bytes 524320 | tf_op jit(solution)/shard_map/ppermute | solution.py:20
  116.6 10.0 %collective-permute-done.17 = bf16[64,4096]{1,0:T(8,128)(2,1)S(1)} collective-permute-done((bf16[64,4096]{1,0:T(8,128)(2,1)S(1)}, bf16[64,4096]{1,0:T(8,128)(2,1)S(1)}, u32[]{:S(2)}, u32[]{:S(2)}) %collective-permute-start.17) | collective-permute-done | bytes 524320 | tf_op jit(solution)/shard_map/ppermute | solution.py:20
  127.2 5.4 %collective-permute-start.16 = (bf16[64,4096]{1,0:T(8,128)(2,1)S(1)}, bf16[64,4096]{1,0:T(8,128)(2,1)S(1)}, u32[]{:S(2)}, u32[]{:S(2)}) collective-permute-start(bf16[64,4096]{1,0:T(8,128)(2,1)S(1)} %add_convert_fusion.3), channel_id=1, source_target_pairs={{248,0},{12,4},{0,8},{20,12},{8,16},{28,20},{16,24},{36,28},{24,32... | collective-permute-start | bytes 1572872 | tf_op jit(solution)/shard_map/ppermute | solution.py:20
  132.7 4.4 %collective-permute-start.29 = (f32[64,256]{1,0:T(8,128)S(1)}, f32[64,256]{1,0:T(8,128)S(1)}, u32[]{:S(2)}, u32[]{:S(2)}) collective-permute-start(f32[64,256]{1,0:T(8,128)S(1)} %add_add_fusion.1), channel_id=1, source_target_pairs={{0,128},{4,132},{8,136},{12,140},{16,144},{20,148},{24,152},{28,15... | collective-permute-start | bytes 196616 | tf_op jit(solution)/shard_map/ppermute | solution.py:24
  137.1 9.2 %collective-permute-done.30 = f32[64,256]{1,0:T(8,128)S(1)} collective-permute-done((f32[64,256]{1,0:T(8,128)S(1)}, f32[64,256]{1,0:T(8,128)S(1)}, u32[]{:S(2)}, u32[]{:S(2)}) %collective-permute-start.30) | collective-permute-done | bytes 65568 | tf_op jit(solution)/shard_map/ppermute | solution.py:24
  146.3 4.5 %collective-permute-start.28 = (f32[64,256]{1,0:T(8,128)S(1)}, f32[64,256]{1,0:T(8,128)S(1)}, u32[]{:S(2)}, u32[]{:S(2)}) collective-permute-start(f32[64,256]{1,0:T(8,128)S(1)} %add_add_fusion.1), channel_id=1, source_target_pairs={{0,64},{4,68},{8,72},{12,76},{16,80},{20,84},{24,88},{28,92},{32,9... | collective-permute-start | bytes 196616 | tf_op jit(solution)/shard_map/ppermute | solution.py:24
  150.7 2.2 %collective-permute-done.28 = f32[64,256]{1,0:T(8,128)S(1)} collective-permute-done((f32[64,256]{1,0:T(8,128)S(1)}, f32[64,256]{1,0:T(8,128)S(1)}, u32[]{:S(2)}, u32[]{:S(2)}) %collective-permute-start.28) | collective-permute-done | bytes 65568 | tf_op jit(solution)/shard_map/ppermute | solution.py:24
  (72 shorter events, 15.6 us)
Async XLA Ops:
  0.6 20.5 %collective-permute-start.1 = (bf16[64,4096]{1,0:T(8,128)(2,1)}, bf16[64,4096]{1,0:T(8,128)(2,1)S(1)}, u32[]{:S(2)}, u32[]{:S(2)}) collective-permute-start(bf16[64,4096]{1,0:T(8,128)(2,1)} %refs_2_.1), channel_id=1, source_target_pairs={{8,0},{252,4},{16,8},{4,12},{24,16},{12,20},{32,24},{20,28},{40,32... | collective-permute-start | bytes 1572872 | tf_op jit(solution)/shard_map/ppermute | solution.py:20
  2.3 19.4 %collective-permute-start = (bf16[64,4096]{1,0:T(8,128)(2,1)}, bf16[64,4096]{1,0:T(8,128)(2,1)S(1)}, u32[]{:S(2)}, u32[]{:S(2)}) collective-permute-start(bf16[64,4096]{1,0:T(8,128)(2,1)} %refs_2_.1), channel_id=1, source_target_pairs={{0,4},{4,0},{8,12},{12,8},{16,20},{20,16},{24,28},{28,24},{32,36},... | collective-permute-start | bytes 1572872 | tf_op jit(solution)/shard_map/ppermute | solution.py:24
  9.9 13.3 %collective-permute-start.2 = (bf16[64,4096]{1,0:T(8,128)(2,1)}, bf16[64,4096]{1,0:T(8,128)(2,1)S(1)}, u32[]{:S(2)}, u32[]{:S(2)}) collective-permute-start(bf16[64,4096]{1,0:T(8,128)(2,1)} %refs_2_.1), channel_id=1, source_target_pairs={{248,0},{12,4},{0,8},{20,12},{8,16},{28,20},{16,24},{36,28},{24,32... | collective-permute-start | bytes 1572872 | tf_op jit(solution)/shard_map/ppermute | solution.py:20
  23.2 15.5 %collective-permute-start.3 = (bf16[64,4096]{1,0:T(8,128)(2,1)S(1)}, bf16[64,4096]{1,0:T(8,128)(2,1)S(1)}, u32[]{:S(2)}, u32[]{:S(2)}) collective-permute-start(bf16[64,4096]{1,0:T(8,128)(2,1)S(1)} %collective-permute-done.1.refs_4_), channel_id=1, source_target_pairs={{8,0},{252,4},{16,8},{4,12},{24,16},{12,20},{32,24},{20,28},{40,32... | collective-permute-start | bytes 1572872 | tf_op jit(solution)/shard_map/ppermute | solution.py:20
  23.2 15.5 %collective-permute-start.4 = (bf16[64,4096]{1,0:T(8,128)(2,1)S(1)}, bf16[64,4096]{1,0:T(8,128)(2,1)S(1)}, u32[]{:S(2)}, u32[]{:S(2)}) collective-permute-start(bf16[64,4096]{1,0:T(8,128)(2,1)S(1)} %collective-permute-done.2.refs_5_), channel_id=1, source_target_pairs={{248,0},{12,4},{0,8},{20,12},{8,16},{28,20},{16,24},{36,28},{24,32... | collective-permute-start | bytes 1572872 | tf_op jit(solution)/shard_map/ppermute | solution.py:20
  28.5 21.5 %collective-permute-start.8 = (bf16[64,4352]{1,0:T(8,128)(2,1)S(1)}, bf16[64,4352]{1,0:T(8,128)(2,1)S(1)}, u32[]{:S(2)}, u32[]{:S(2)}) collective-permute-start(bf16[64,4352]{1,0:T(8,128)(2,1)S(1)} %pad_maximum_fusion.refs_4_), channel_id=1, source_target_pairs={{0,2},{1,3},{2,0},{3,1},{4,6},{5,7},{6,4},{7,5},{8,10},{9,11},{10,... | collective-permute-start | bytes 1671176 | tf_op jit(solution)/shard_map/ppermute | solution.py:24
  38.7 13.6 %collective-permute-start.6 = (bf16[64,4096]{1,0:T(8,128)(2,1)S(1)}, bf16[64,4096]{1,0:T(8,128)(2,1)S(1)}, u32[]{:S(2)}, u32[]{:S(2)}) collective-permute-start(bf16[64,4096]{1,0:T(8,128)(2,1)S(1)} %collective-permute-done.refs_3_), channel_id=1, source_target_pairs={{248,0},{12,4},{0,8},{20,12},{8,16},{28,20},{16,24},{36,28},{24,32... | collective-permute-start | bytes 1572872 | tf_op jit(solution)/shard_map/ppermute | solution.py:20
  43.7 14.0 %collective-permute-start.5 = (bf16[64,4096]{1,0:T(8,128)(2,1)S(1)}, bf16[64,4096]{1,0:T(8,128)(2,1)S(1)}, u32[]{:S(2)}, u32[]{:S(2)}) collective-permute-start(bf16[64,4096]{1,0:T(8,128)(2,1)S(1)} %collective-permute-done.refs_3_), channel_id=1, source_target_pairs={{8,0},{252,4},{16,8},{4,12},{24,16},{12,20},{32,24},{20,28},{40,32... | collective-permute-start | bytes 1572872 | tf_op jit(solution)/shard_map/ppermute | solution.py:20
  43.7 14.0 %collective-permute-start.7 = (bf16[64,4096]{1,0:T(8,128)(2,1)S(1)}, bf16[64,4096]{1,0:T(8,128)(2,1)S(1)}, u32[]{:S(2)}, u32[]{:S(2)}) collective-permute-start(bf16[64,4096]{1,0:T(8,128)(2,1)S(1)} %collective-permute-done.3.refs_2_), channel_id=1, source_target_pairs={{0,4},{4,0},{8,12},{12,8},{16,20},{20,16},{24,28},{28,24},{32,36},... | collective-permute-start | bytes 1572872 | tf_op jit(solution)/shard_map/ppermute | solution.py:24
  48.2 29.2 %slice-start.1 = ((s8[9437184]{0:T(1024)(128)(4,1)}), s8[4194304]{0:T(1024)(128)(4,1)S(1)}, s32[]{:S(2)}) async-start(s8[9437184]{0:T(1024)(128)(4,1)} %bitcast.1), calls=%async_computation.1 | async-start | bytes 8388608
  60.3 11.7 %collective-permute-start.10 = (bf16[64,4096]{1,0:T(8,128)(2,1)S(1)}, bf16[64,4096]{1,0:T(8,128)(2,1)S(1)}, u32[]{:S(2)}, u32[]{:S(2)}) collective-permute-start(bf16[64,4096]{1,0:T(8,128)(2,1)S(1)} %forward_2.1.refs_0_), channel_id=1, source_target_pairs={{0,2},{1,3},{2,0},{3,1},{4,6},{5,7},{6,4},{7,5},{8,10},{9,11},{10,... | collective-permute-start | bytes 1572872 | tf_op jit(solution)/shard_map/ppermute | solution.py:24
  61.5 10.6 %collective-permute-start.12 = (bf16[64,4352]{1,0:T(8,128)(2,1)S(1)}, bf16[64,4352]{1,0:T(8,128)(2,1)S(1)}, u32[]{:S(2)}, u32[]{:S(2)}) collective-permute-start(bf16[64,4352]{1,0:T(8,128)(2,1)S(1)} %pad_maximum_fusion.refs_4_), channel_id=1, source_target_pairs={{0,1},{1,0},{2,3},{3,2},{4,5},{5,4},{6,7},{7,6},{8,9},{9,8},{10,11... | collective-permute-start | bytes 1671176 | tf_op jit(solution)/shard_map/ppermute | solution.py:24
  61.5 10.6 %collective-permute-start.13 = (bf16[64,4352]{1,0:T(8,128)(2,1)S(1)}, bf16[64,4352]{1,0:T(8,128)(2,1)S(1)}, u32[]{:S(2)}, u32[]{:S(2)}) collective-permute-start(bf16[64,4352]{1,0:T(8,128)(2,1)S(1)} %collective-permute-done.8.refs_6_), channel_id=1, source_target_pairs={{0,1},{1,0},{2,3},{3,2},{4,5},{5,4},{6,7},{7,6},{8,9},{9,8},{10,11... | collective-permute-start | bytes 1671176 | tf_op jit(solution)/shard_map/ppermute | solution.py:24
  62.0 10.0 %collective-permute-start.9 = (bf16[64,4096]{1,0:T(8,128)(2,1)S(1)}, bf16[64,4096]{1,0:T(8,128)(2,1)S(1)}, u32[]{:S(2)}, u32[]{:S(2)}) collective-permute-start(bf16[64,4096]{1,0:T(8,128)(2,1)S(1)} %forward_2.1.refs_0_), channel_id=1, source_target_pairs={{0,1},{1,0},{2,3},{3,2},{4,5},{5,4},{6,7},{7,6},{8,9},{9,8},{10,11... | collective-permute-start | bytes 1572872 | tf_op jit(solution)/shard_map/ppermute | solution.py:24
  72.1 1.9 %collective-permute-start.11 = (bf16[64,4096]{1,0:T(8,128)(2,1)S(1)}, bf16[64,4096]{1,0:T(8,128)(2,1)S(1)}, u32[]{:S(2)}, u32[]{:S(2)}) collective-permute-start(bf16[64,4096]{1,0:T(8,128)(2,1)S(1)} %collective-permute-done.10.refs_2_), channel_id=1, source_target_pairs={{0,1},{1,0},{2,3},{3,2},{4,5},{5,4},{6,7},{7,6},{8,9},{9,8},{10,11... | collective-permute-start | bytes 1572872 | tf_op jit(solution)/shard_map/ppermute | solution.py:24
  80.1 16.2 %collective-permute-start.14 = (bf16[64,4096]{1,0:T(8,128)(2,1)S(1)}, bf16[64,4096]{1,0:T(8,128)(2,1)S(1)}, u32[]{:S(2)}, u32[]{:S(2)}) collective-permute-start(bf16[64,4096]{1,0:T(8,128)(2,1)S(1)} %get-tuple-element.55), channel_id=1, source_target_pairs={{0,4},{4,0},{8,12},{12,8},{16,20},{20,16},{24,28},{28,24},{32,36},... | collective-permute-start | bytes 1572872 | tf_op jit(solution)/shard_map/ppermute | solution.py:24
  83.7 15.6 %collective-permute-start.21 = (f32[64,256]{1,0:T(8,128)S(1)}, f32[64,256]{1,0:T(8,128)S(1)}, u32[]{:S(2)}, u32[]{:S(2)}) collective-permute-start(f32[64,256]{1,0:T(8,128)S(1)} %fusion), channel_id=1, source_target_pairs={{0,12},{4,8},{8,4},{12,0},{16,28},{20,24},{24,20},{28,16},{32,44},... | collective-permute-start | bytes 196616 | tf_op jit(solution)/shard_map/ppermute | solution.py:24
  83.8 16.1 %collective-permute-start.20 = (f32[64,256]{1,0:T(8,128)S(1)}, f32[64,256]{1,0:T(8,128)S(1)}, u32[]{:S(2)}, u32[]{:S(2)}) collective-permute-start(f32[64,256]{1,0:T(8,128)S(1)} %fusion), channel_id=1, source_target_pairs={{0,8},{4,12},{8,0},{12,4},{16,24},{20,28},{24,16},{28,20},{32,40},... | collective-permute-start | bytes 196616 | tf_op jit(solution)/shard_map/ppermute | solution.py:24
  85.3 14.6 %collective-permute-start.19 = (f32[64,256]{1,0:T(8,128)S(1)}, f32[64,256]{1,0:T(8,128)S(1)}, u32[]{:S(2)}, u32[]{:S(2)}) collective-permute-start(f32[64,256]{1,0:T(8,128)S(1)} %fusion), channel_id=1, source_target_pairs={{0,4},{4,0},{8,12},{12,8},{16,20},{20,16},{24,28},{28,24},{32,36},... | collective-permute-start | bytes 196616 | tf_op jit(solution)/shard_map/ppermute | solution.py:24
  89.1 16.4 %collective-permute-start.22 = (bf16[64,4096]{1,0:T(8,128)(2,1)S(1)}, bf16[64,4096]{1,0:T(8,128)(2,1)S(1)}, u32[]{:S(2)}, u32[]{:S(2)}) collective-permute-start(bf16[64,4096]{1,0:T(8,128)(2,1)S(1)} %get-tuple-element.67), channel_id=1, source_target_pairs={{248,0},{12,4},{0,8},{20,12},{8,16},{28,20},{16,24},{36,28},{24,32... | collective-permute-start | bytes 1572872 | tf_op jit(solution)/shard_map/ppermute | solution.py:20
  96.3 20.2 %collective-permute-start.23 = (bf16[64,4096]{1,0:T(8,128)(2,1)S(1)}, bf16[64,4096]{1,0:T(8,128)(2,1)S(1)}, u32[]{:S(2)}, u32[]{:S(2)}) collective-permute-start(bf16[64,4096]{1,0:T(8,128)(2,1)S(1)} %get-tuple-element.68), channel_id=1, source_target_pairs={{8,0},{252,4},{16,8},{4,12},{24,16},{12,20},{32,24},{20,28},{40,32... | collective-permute-start | bytes 1572872 | tf_op jit(solution)/shard_map/ppermute | solution.py:20
  99.3 27.3 %collective-permute-start.17 = (bf16[64,4096]{1,0:T(8,128)(2,1)S(1)}, bf16[64,4096]{1,0:T(8,128)(2,1)S(1)}, u32[]{:S(2)}, u32[]{:S(2)}) collective-permute-start(bf16[64,4096]{1,0:T(8,128)(2,1)S(1)} %get-tuple-element.63), channel_id=1, source_target_pairs={{8,0},{252,4},{16,8},{4,12},{24,16},{12,20},{32,24},{20,28},{40,32... | collective-permute-start | bytes 1572872 | tf_op jit(solution)/shard_map/ppermute | solution.py:20
  99.9 27.3 %collective-permute-start.27 = (f32[64,256]{1,0:T(8,128)S(1)}, f32[64,256]{1,0:T(8,128)S(1)}, u32[]{:S(2)}, u32[]{:S(2)}) collective-permute-start(f32[64,256]{1,0:T(8,128)S(1)} %add_add_fusion.2), channel_id=1, source_target_pairs={{0,48},{4,52},{8,56},{12,60},{16,32},{20,36},{24,40},{28,44},{32,1... | collective-permute-start | bytes 196616 | tf_op jit(solution)/shard_map/ppermute | solution.py:24
  100.0 32.6 %collective-permute-start.26 = (f32[64,256]{1,0:T(8,128)S(1)}, f32[64,256]{1,0:T(8,128)S(1)}, u32[]{:S(2)}, u32[]{:S(2)}) collective-permute-start(f32[64,256]{1,0:T(8,128)S(1)} %add_add_fusion.2), channel_id=1, source_target_pairs={{0,32},{4,36},{8,40},{12,44},{16,48},{20,52},{24,56},{28,60},{32,0... | collective-permute-start | bytes 196616 | tf_op jit(solution)/shard_map/ppermute | solution.py:24
  105.5 27.1 %collective-permute-start.25 = (f32[64,256]{1,0:T(8,128)S(1)}, f32[64,256]{1,0:T(8,128)S(1)}, u32[]{:S(2)}, u32[]{:S(2)}) collective-permute-start(f32[64,256]{1,0:T(8,128)S(1)} %add_add_fusion.2), channel_id=1, source_target_pairs={{0,16},{4,20},{8,24},{12,28},{16,0},{20,4},{24,8},{28,12},{32,48},... | collective-permute-start | bytes 196616 | tf_op jit(solution)/shard_map/ppermute | solution.py:24
  116.4 10.3 %collective-permute-start.15 = (bf16[64,4096]{1,0:T(8,128)(2,1)S(1)}, bf16[64,4096]{1,0:T(8,128)(2,1)S(1)}, u32[]{:S(2)}, u32[]{:S(2)}) collective-permute-start(bf16[64,4096]{1,0:T(8,128)(2,1)S(1)} %add_convert_fusion.4), channel_id=1, source_target_pairs={{248,0},{12,4},{0,8},{20,12},{8,16},{28,20},{16,24},{36,28},{24,32... | collective-permute-start | bytes 1572872 | tf_op jit(solution)/shard_map/ppermute | solution.py:20
  126.6 27.0 %collective-permute-start.24 = (bf16[64,4096]{1,0:T(8,128)(2,1)S(1)}, bf16[64,4096]{1,0:T(8,128)(2,1)S(1)}, u32[]{:S(2)}, u32[]{:S(2)}) collective-permute-start(bf16[64,4096]{1,0:T(8,128)(2,1)S(1)} %add_convert_fusion.1), channel_id=1, source_target_pairs={{0,4},{4,0},{8,12},{12,8},{16,20},{20,16},{24,28},{28,24},{32,36},... | collective-permute-start | bytes 1572872 | tf_op jit(solution)/shard_map/ppermute | solution.py:24
  126.7 26.9 %collective-permute-start.18 = (bf16[64,4096]{1,0:T(8,128)(2,1)S(1)}, bf16[64,4096]{1,0:T(8,128)(2,1)S(1)}, u32[]{:S(2)}, u32[]{:S(2)}) collective-permute-start(bf16[64,4096]{1,0:T(8,128)(2,1)S(1)} %add_convert_fusion.2), channel_id=1, source_target_pairs={{8,0},{252,4},{16,8},{4,12},{24,16},{12,20},{32,24},{20,28},{40,32... | collective-permute-start | bytes 1572872 | tf_op jit(solution)/shard_map/ppermute | solution.py:20
  127.2 26.5 %collective-permute-start.16 = (bf16[64,4096]{1,0:T(8,128)(2,1)S(1)}, bf16[64,4096]{1,0:T(8,128)(2,1)S(1)}, u32[]{:S(2)}, u32[]{:S(2)}) collective-permute-start(bf16[64,4096]{1,0:T(8,128)(2,1)S(1)} %add_convert_fusion.3), channel_id=1, source_target_pairs={{248,0},{12,4},{0,8},{20,12},{8,16},{28,20},{16,24},{36,28},{24,32... | collective-permute-start | bytes 1572872 | tf_op jit(solution)/shard_map/ppermute | solution.py:20
  132.6 13.7 %collective-permute-start.30 = (f32[64,256]{1,0:T(8,128)S(1)}, f32[64,256]{1,0:T(8,128)S(1)}, u32[]{:S(2)}, u32[]{:S(2)}) collective-permute-start(f32[64,256]{1,0:T(8,128)S(1)} %add_add_fusion.1), channel_id=1, source_target_pairs={{0,192},{4,196},{8,200},{12,204},{16,208},{20,212},{24,216},{28,22... | collective-permute-start | bytes 196616 | tf_op jit(solution)/shard_map/ppermute | solution.py:24
  132.7 18.0 %collective-permute-start.29 = (f32[64,256]{1,0:T(8,128)S(1)}, f32[64,256]{1,0:T(8,128)S(1)}, u32[]{:S(2)}, u32[]{:S(2)}) collective-permute-start(f32[64,256]{1,0:T(8,128)S(1)} %add_add_fusion.1), channel_id=1, source_target_pairs={{0,128},{4,132},{8,136},{12,140},{16,144},{20,148},{24,152},{28,15... | collective-permute-start | bytes 196616 | tf_op jit(solution)/shard_map/ppermute | solution.py:24
  146.3 6.7 %collective-permute-start.28 = (f32[64,256]{1,0:T(8,128)S(1)}, f32[64,256]{1,0:T(8,128)S(1)}, u32[]{:S(2)}, u32[]{:S(2)}) collective-permute-start(f32[64,256]{1,0:T(8,128)S(1)} %add_add_fusion.1), channel_id=1, source_target_pairs={{0,64},{4,68},{8,72},{12,76},{16,80},{20,84},{24,88},{28,92},{32,9... | collective-permute-start | bytes 196616 | tf_op jit(solution)/shard_map/ppermute | solution.py:24
  (7 other events, 91.4 us)

commit v3 on v2

--- a/solution.py
+++ b/solution.py
@@ -33,7 +33,7 @@
     return jnp.where(place // 2 == 1, halves, array)
 
 
-COST = pl.CostEstimate(flops=0, transcendentals=0, bytes_accessed=24_000_000)
+COST = pl.CostEstimate(flops=0, transcendentals=0, bytes_accessed=6_000_000)
 SMEM = pl.BlockSpec(memory_space=pltpu.SMEM)
 VMEM = pl.BlockSpec(memory_space=pltpu.VMEM)
 
@@ -204,7 +204,7 @@
     )(listed, near(vals), near(grad))
 
 
-def middle_body(*refs):
+def middle_body(factor, place_ref, *refs):
     ys, packed, (out_ref, grad_ref, wgrad_ref) = refs[0:4], refs[4:8], refs[8:]
     feats, nodes = ys[0].shape
     hidden = 4 * feats
@@ -234,33 +234,29 @@
         wgrad += lax.dot_general(
             ys[0][:, here], grad_pre, (((1,), (1,)), ((), ())), preferred_element_type=jnp.float32
         )
-    wgrad_ref[...] = wgrad
-
-
-def middle(ys, packed):
+    wgrad_ref[...] = exchanged_columns(wgrad, place_ref[0]) * factor
+
+
+def middle(place, ys, packed):
     feats, nodes = ys[0].shape
+    factor = 1.0 / math.sqrt(nodes * lax.axis_size("blk"))
     return pl.pallas_call(
-        middle_body,
+        functools.partial(middle_body, factor),
         out_shape=(
             jax.ShapeDtypeStruct((feats, nodes), jnp.bfloat16),
             pltpu.VMEM((feats, nodes), jnp.bfloat16),
             pltpu.VMEM((feats, 4 * feats), jnp.float32),
         ),
-        in_specs=[VMEM] * 8,
+        in_specs=[SMEM] + [VMEM] * 8,
         out_specs=(VMEM,) * 3,
         cost_estimate=COST,
         compiler_params=kept(10),
         name="middle",
-    )(*map(near, ys), *map(near, packed))
+    )(place.astype(jnp.int32).reshape(1), *map(near, ys), *map(near, packed))
 
 
 def fenced(*groups):
     return lax.optimization_barrier(groups)
-
-
-def summed(value, radix_bits):
-    low, high = radix_bits
-    return [flipped(value, "blk", low), flipped(value, "blk", high), flipped(value, "blk", low | high)]
 
 
 def per_device(x_t, weight, cotangent, tile_row, tile_col, tile_off, tile_vals, tile_count):
@@ -282,27 +278,35 @@
     packed = [own, flipped(own, "feat", 1), far, flipped(far, "feat", 1)]
     y = forward(2, listed, tile_vals, [xu, xv, mx], y, bf16)
     y_far = flipped(y, "feat", 2)
-    out_t, grad, wgrad = middle([y, flipped(y, "feat", 1), y_far, flipped(y_far, "feat", 1)], packed)
-
+    ys = [y, flipped(y, "feat", 1), y_far, flipped(y_far, "feat", 1)]
+    out_t, grad, wgrad = middle(place, ys, packed)
+
+    part = flipped(wgrad, "blk", 2)
     to_xu, to_xv, to_mx = backward(2, listed, tile_vals, grad, [bf16] * 3)
-    from_mx = flipped(to_mx, "blk", 1)
-    from_xu, from_xv = stepped(to_xu, False), stepped(to_xv, True)
+    to_xu, to_xv, to_mx, part, grad = fenced(to_xu, to_xv, to_mx, part, grad)
+    from_mx, from_xu, from_xv = flipped(to_mx, "blk", 1), stepped(to_xu, False), stepped(to_xv, True)
+    wgrad = wgrad + part
+    part = flipped(wgrad, "blk", 8)
     to_m, to_n = backward(1, listed, tile_vals, grad, [f32, bf16])
-    wgrad = exchanged_columns(wgrad, place) * (1.0 / math.sqrt(nodes * lax.axis_size("blk")))
-    parts = summed(wgrad, (1, 2))
-    from_mx, to_m, grad = fenced(from_mx, to_m, grad)
+    part, to_m, grad = fenced(part, to_m, grad)
+    wgrad = wgrad + part
+    part = flipped(wgrad, "blk", 16)
+    total, to_x, to_u, to_v = backward(0, listed, tile_vals, grad, [f32] * 4)
+    from_mx, from_xu, from_xv, to_m, to_n, total, to_x, to_u, to_v, part = fenced(
+        from_mx, from_xu, from_xv, to_m, to_n, total, to_x, to_u, to_v, part
+    )
     from_m = stepped((to_m + from_mx.astype(f32)).astype(bf16), False)
     from_n = stepped(to_n, True)
-    total, to_x, to_u, to_v = backward(0, listed, tile_vals, grad, [f32] * 4)
-    wgrad, parts, to_x = fenced(wgrad, parts, to_x)
-    wgrad = (wgrad + parts[0]) + (parts[1] + parts[2])
-    parts = summed(wgrad, (4, 8))
-    from_x = flipped((to_x + from_xu.astype(f32) + from_xv.astype(f32)).astype(bf16), "blk", 1)
+    to_x = (to_x + from_xu.astype(f32) + from_xv.astype(f32)).astype(bf16)
+    wgrad = wgrad + part
+    wgrad = wgrad + flipped(wgrad, "blk", 32)
+    wgrad = wgrad + flipped(wgrad, "blk", 1)
+    from_m, from_n, to_x, to_u, to_v, wgrad = fenced(from_m, from_n, to_x, to_u, to_v, wgrad)
+    part = flipped(wgrad, "blk", 4)
+    from_u = stepped((to_u + from_m.astype(f32)).astype(bf16), False)
     from_v = stepped((to_v + from_n.astype(f32)).astype(bf16), True)
-    from_u = stepped((to_u + from_m.astype(f32)).astype(bf16), False)
-    wgrad = (wgrad + parts[0]) + (parts[1] + parts[2])
-    parts = summed(wgrad, (16, 32))
-    wgrad = (wgrad + parts[0]) + (parts[1] + parts[2])
+    from_x = flipped(to_x, "blk", 1)
+    wgrad = wgrad + part
     total = total + from_u.astype(f32) + from_v.astype(f32) + from_x.astype(f32)
     return (out_t, total.astype(bf16), wgrad)
 

time: 156 us -> 142 us (0.910)
  the two profiles are of different devices: /device:TPU:6 before, /device:TPU:4 now
where the time goes in v3:
time: 142 us; the launch traced here: 144 us
  waiting for transfers between devices  55.2 us (39%)
  starting transfers between devices  44.6 us (31%)
  Pallas kernels  31.7 us (22%)
  local copies, waits for them, and re-layouts  6.62 us (5%)
  other arithmetic  4.14 us (3%)
  between operations  1.56 us (1%)
    ppermute x12, starting transfers between devices, stepped(): return lax.ppermute(block, 'blk', route)  31.7 us
    ppermute x16, waiting for transfers between devices, flipped(): lax.ppermute(block, axis, [(i, i ^ bit) for i in range(lax.axis_size(axis...  29.8 us
    ppermute x12, waiting for transfers between devices, stepped(): return lax.ppermute(block, 'blk', route)  25.4 us
    ppermute x16, starting transfers between devices, flipped(): lax.ppermute(block, axis, [(i, i ^ bit) for i in range(lax.axis_size(axis...  12.8 us
    pallas_call x3, Pallas kernels, backward(): pl.pallas_call(functools.partial(backward_body, wave), out_shape=tuple((p...  11.7 us
    pallas_call x3, Pallas kernels, forward(): pl.pallas_call(functools.partial(forward_body, wave, seed is not None), o...  11.5 us
    unnamed x16, local copies, waits for them, and re-layouts  5.74 us
    pallas_call x1, Pallas kernels, plan(): pl.pallas_call(functools.partial(plan_body, cap), out_shape=jax.ShapeDtyp...  5.11 us
  transfers between devices with their start and end apart: 28, of which 15 were waited for; matrix products, arithmetic and copies ran while one was open for 3% of the time, Pallas kernels for 17%

profile of v3, /device:TPU:4, one launch (start us, length us, event | category | flops | bytes accessed | tf_op | source)
XLA Modules:
  0.0 143.8 jit_solution(18312557461451906514)
XLA Ops:
  0.6 8.4 %collective-permute-start.1 = (bf16[64,4096]{1,0:T(8,128)(2,1)}, bf16[64,4096]{1,0:T(8,128)(2,1)S(1)}, u32[]{:S(2)}, u32[]{:S(2)}) collective-permute-start(bf16[64,4096]{1,0:T(8,128)(2,1)} %refs_2_.1), channel_id=1, source_target_pairs={{8,0},{252,4},{16,8},{4,12},{24,16},{12,20},{32,24},{20,28},{40,32... | collective-permute-start | bytes 1572872 | tf_op jit(solution)/shard_map/ppermute | solution.py:20
  13.5 5.1 %plan.1.refs_0_ = s32[904]{0:T(1024)S(1)} custom-call(s32[288]{0:T(512)S(1)} %copy-done.2, s32[288]{0:T(512)S(1)} %copy-done.3, s32[288]{0:T(512)S(1)} %copy-done.4, s32[1]{0:T(128)S(6)} %copy.11.count_ref, s32[1]{0:T(128)} %bitcast.1.sign_ref), custom_call_target="tpu_custom_call" | custom-call | bytes 6000000 | tf_op jit(solution)/shard_map/plan/pallas_call | solution.py:81
  18.6 1.1 pad_maximum_fusion.refs_4_
  20.5 2.1 %collective-permute-done.refs_3_ = bf16[64,4096]{1,0:T(8,128)(2,1)S(1)} collective-permute-done((bf16[64,4096]{1,0:T(8,128)(2,1)}, bf16[64,4096]{1,0:T(8,128)(2,1)S(1)}, u32[]{:S(2)}, u32[]{:S(2)}) %collective-permute-start) | collective-permute-done | bytes 524320 | tf_op jit(solution)/shard_map/ppermute | solution.py:24
  22.6 3.3 %collective-permute-done.2.refs_5_ = bf16[64,4096]{1,0:T(8,128)(2,1)S(1)} collective-permute-done((bf16[64,4096]{1,0:T(8,128)(2,1)}, bf16[64,4096]{1,0:T(8,128)(2,1)S(1)}, u32[]{:S(2)}, u32[]{:S(2)}) %collective-permute-start.2) | collective-permute-done | bytes 524320 | tf_op jit(solution)/shard_map/ppermute | solution.py:20
  26.2 1.7 %collective-permute-start.4 = (bf16[64,4096]{1,0:T(8,128)(2,1)S(1)}, bf16[64,4096]{1,0:T(8,128)(2,1)S(1)}, u32[]{:S(2)}, u32[]{:S(2)}) collective-permute-start(bf16[64,4096]{1,0:T(8,128)(2,1)S(1)} %collective-permute-done.2.refs_5_), channel_id=1, source_target_pairs={{248,0},{12,4},{0,8},{20,12},{8,16},{28,20},{16,24},{36,28},{24,32... | collective-permute-start | bytes 1572872 | tf_op jit(solution)/shard_map/ppermute | solution.py:20
  28.5 3.7 %copy-done = bf16[288,128,128]{2,1,0:T(8,128)(2,1)S(1)} copy-done((bf16[288,128,128]{2,1,0:T(8,128)(2,1)S(1)}, bf16[288,128,128]{2,1,0:T(8,128)(2,1)}, u32[]{:S(2)}) %copy-start) | copy-done | bytes 9437208
  32.2 4.7 %forward_0.1.refs_4_ = f32[64,4096]{1,0:T(8,128)S(1)} custom-call(s32[904]{0:T(1024)S(1)} %plan.1.refs_0_, bf16[288,128,128]{2,1,0:T(8,128)(2,1)S(1)} %copy-done, bf16[64,4096]{1,0:T(8,128)(2,1)S(1)} %copy-done.1, bf16[64,4096]{1,0:T(8,128)(2,1)S(1)} %collective-permute-done.refs_3_, bf16[64,4096]{1,0:T(8,128)(2,1)S(1)} %collective-permute-done.1.refs_4_, ...), custom_call_target="tpu_custom_call" | custom-call | bytes 6000000 | tf_op jit(solution)/shard_map/forward_0/pallas_call | solution.py:154
  36.9 1.5 %collective-permute-done.3.refs_2_ = bf16[64,4096]{1,0:T(8,128)(2,1)S(1)} collective-permute-done((bf16[64,4096]{1,0:T(8,128)(2,1)S(1)}, bf16[64,4096]{1,0:T(8,128)(2,1)S(1)}, u32[]{:S(2)}, u32[]{:S(2)}) %collective-permute-start.3) | collective-permute-done | bytes 524320 | tf_op jit(solution)/shard_map/ppermute | solution.py:20
  38.4 3.6 %collective-permute-done.4.refs_3_ = bf16[64,4096]{1,0:T(8,128)(2,1)S(1)} collective-permute-done((bf16[64,4096]{1,0:T(8,128)(2,1)S(1)}, bf16[64,4096]{1,0:T(8,128)(2,1)S(1)}, u32[]{:S(2)}, u32[]{:S(2)}) %collective-permute-start.4) | collective-permute-done | bytes 524320 | tf_op jit(solution)/shard_map/ppermute | solution.py:20
  42.1 5.3 %collective-permute-start.5 = (bf16[64,4096]{1,0:T(8,128)(2,1)S(1)}, bf16[64,4096]{1,0:T(8,128)(2,1)S(1)}, u32[]{:S(2)}, u32[]{:S(2)}) collective-permute-start(bf16[64,4096]{1,0:T(8,128)(2,1)S(1)} %collective-permute-done.refs_3_), channel_id=1, source_target_pairs={{8,0},{252,4},{16,8},{4,12},{24,16},{12,20},{32,24},{20,28},{40,32... | collective-permute-start | bytes 1572872 | tf_op jit(solution)/shard_map/ppermute | solution.py:20
  47.4 3.0 %forward_1.1.refs_5_ = f32[64,4096]{1,0:T(8,128)S(1)} custom-call(s32[904]{0:T(1024)S(1)} %plan.1.refs_0_, bf16[288,128,128]{2,1,0:T(8,128)(2,1)S(1)} %copy-done, bf16[64,4096]{1,0:T(8,128)(2,1)S(1)} %collective-permute-done.3.refs_2_, bf16[64,4096]{1,0:T(8,128)(2,1)S(1)} %collective-permute-done.4.refs_3_, f32[64,4096]{1,0:T(8,128)S(1)} %forward_0.1.refs_4_), custom_call_target="tpu_custom_call" | custom-call | bytes 6000000 | tf_op jit(solution)/shard_map/forward_1/pallas_call | solution.py:154
  50.4 6.6 %collective-permute-done.6.refs_3_ = bf16[64,4096]{1,0:T(8,128)(2,1)S(1)} collective-permute-done((bf16[64,4096]{1,0:T(8,128)(2,1)S(1)}, bf16[64,4096]{1,0:T(8,128)(2,1)S(1)}, u32[]{:S(2)}, u32[]{:S(2)}) %collective-permute-start.6) | collective-permute-done | bytes 524320 | tf_op jit(solution)/shard_map/ppermute | solution.py:20
  57.0 1.5 %collective-permute-done.7.refs_4_ = bf16[64,4096]{1,0:T(8,128)(2,1)S(1)} collective-permute-done((bf16[64,4096]{1,0:T(8,128)(2,1)S(1)}, bf16[64,4096]{1,0:T(8,128)(2,1)S(1)}, u32[]{:S(2)}, u32[]{:S(2)}) %collective-permute-start.7) | collective-permute-done | bytes 524320 | tf_op jit(solution)/shard_map/ppermute | solution.py:24
  58.4 3.8 %forward_2.1.refs_0_ = bf16[64,4096]{1,0:T(8,128)(2,1)S(1)} custom-call(s32[904]{0:T(1024)S(1)} %plan.1.refs_0_, bf16[288,128,128]{2,1,0:T(8,128)(2,1)S(1)} %copy-done, bf16[64,4096]{1,0:T(8,128)(2,1)S(1)} %collective-permute-done.5.refs_2_, bf16[64,4096]{1,0:T(8,128)(2,1)S(1)} %collective-permute-done.6.refs_3_, ...), custom_call_target="tpu_custom_call" | custom-call | bytes 6000000 | tf_op jit(solution)/shard_map/forward_2/pallas_call | solution.py:154
  63.4 10.6 %collective-permute-done.10.refs_2_ = bf16[64,4096]{1,0:T(8,128)(2,1)S(1)} collective-permute-done((bf16[64,4096]{1,0:T(8,128)(2,1)S(1)}, bf16[64,4096]{1,0:T(8,128)(2,1)S(1)}, u32[]{:S(2)}, u32[]{:S(2)}) %collective-permute-start.10) | collective-permute-done | bytes 524320 | tf_op jit(solution)/shard_map/ppermute | solution.py:24
  74.0 1.9 %collective-permute-done.11.refs_3_ = bf16[64,4096]{1,0:T(8,128)(2,1)S(1)} collective-permute-done((bf16[64,4096]{1,0:T(8,128)(2,1)S(1)}, bf16[64,4096]{1,0:T(8,128)(2,1)S(1)}, u32[]{:S(2)}, u32[]{:S(2)}) %collective-permute-start.11) | collective-permute-done | bytes 524320 | tf_op jit(solution)/shard_map/ppermute | solution.py:24
  75.9 3.4 %middle.1 = (bf16[64,4096]{1,0:T(8,128)(2,1)}, bf16[64,4096]{1,0:T(8,128)(2,1)S(1)}, f32[64,256]{1,0:T(8,128)S(1)}) custom-call(s32[1]{0:T(128)} %bitcast.place_ref, bf16[64,4096]{1,0:T(8,128)(2,1)S(1)} %forward_2.1.refs_0_, bf16[64,4096]{1,0:T(8,128)(2,1)S(1)} %collective-permute-done.9.refs_1_, bf16[64,4096]{1,0:T(8,128)(2,1)S(1)} %collective-permute-done.10.refs_2_, ...), custom_call_target="tpu_custom_call" | custom-call | bytes 6000000 | tf_op jit(solution)/shard_map/middle/pallas_call | solution.py:243
  79.3 3.8 %backward_2.1 = (bf16[64,4096]{1,0:T(8,128)(2,1)S(1)}, bf16[64,4096]{1,0:T(8,128)(2,1)S(1)}, bf16[64,4096]{1,0:T(8,128)(2,1)S(1)}) custom-call(s32[904]{0:T(1024)S(1)} %plan.1.refs_0_, bf16[288,128,128]{2,1,0:T(8,128)(2,1)S(1)} %bitcast.3, bf16[64,4096]{1,0:T(8,128)(2,1)S(1)} %get-tuple-element.83.refs_2_), custom_call_target="tpu_custom_call" | custom-call | bytes 6000000 | tf_op jit(solution)/shard_map/backward_2/pallas_call | solution.py:195
  83.6 5.2 %collective-permute-start.17 = (bf16[64,4096]{1,0:T(8,128)(2,1)S(1)}, bf16[64,4096]{1,0:T(8,128)(2,1)S(1)}, u32[]{:S(2)}, u32[]{:S(2)}) collective-permute-start(bf16[64,4096]{1,0:T(8,128)(2,1)S(1)} %get-tuple-element.77), channel_id=1, source_target_pairs={{8,0},{252,4},{16,8},{4,12},{24,16},{12,20},{32,24},{20,28},{40,32... | collective-permute-start | bytes 1572872 | tf_op jit(solution)/shard_map/ppermute | solution.py:20
  89.0 3.0 %backward_1.1 = (f32[64,4096]{1,0:T(8,128)S(1)}, bf16[64,4096]{1,0:T(8,128)(2,1)S(1)}) custom-call(s32[904]{0:T(1024)S(1)} %plan.1.refs_0_, bf16[288,128,128]{2,1,0:T(8,128)(2,1)S(1)} %bitcast.3, bf16[64,4096]{1,0:T(8,128)(2,1)S(1)} %get-tuple-element.83.refs_2_), custom_call_target="tpu_custom_call" | custom-call | bytes 6000000 | tf_op jit(solution)/shard_map/backward_1/pallas_call | solution.py:195
  91.9 1.3 collective-permute-done.18
  93.2 4.4 %collective-permute-start.19 = (f32[64,256]{1,0:T(8,128)S(1)}, f32[64,256]{1,0:T(8,128)S(1)}, u32[]{:S(2)}, u32[]{:S(2)}) collective-permute-start(f32[64,256]{1,0:T(8,128)S(1)} %add.53), channel_id=1, source_target_pairs={{0,64},{4,68},{8,72},{12,76},{16,80},{20,84},{24,88},{28,92},{32,9... | collective-permute-start | bytes 196616 | tf_op jit(solution)/shard_map/ppermute | solution.py:24
  97.6 4.9 %backward_0.1 = (f32[64,4096]{1,0:T(8,128)S(1)}, f32[64,4096]{1,0:T(8,128)S(1)}, f32[64,4096]{1,0:T(8,128)S(1)}, f32[64,4096]{1,0:T(8,128)S(1)}) custom-call(s32[904]{0:T(1024)S(1)} %plan.1.refs_0_, bf16[288,128,128]{2,1,0:T(8,128)(2,1)S(1)} %bitcast.3, bf16[64,4096]{1,0:T(8,128)(2,1)S(1)} %get-tuple-element.83.refs_2_), custom_call_target="tpu_custom_call" | custom-call | bytes 6000000 | tf_op jit(solution)/shard_map/backward_0/pallas_call | solution.py:195
  102.5 5.9 %collective-permute-start.22 = (f32[64,256]{1,0:T(8,128)S(1)}, f32[64,256]{1,0:T(8,128)S(1)}, u32[]{:S(2)}, u32[]{:S(2)}) collective-permute-start(f32[64,256]{1,0:T(8,128)S(1)} %add.57), channel_id=1, source_target_pairs={{0,128},{4,132},{8,136},{12,140},{16,144},{20,148},{24,152},{28,15... | collective-permute-start | bytes 196616 | tf_op jit(solution)/shard_map/ppermute | solution.py:24
  108.6 5.3 %collective-permute-start.21 = (bf16[64,4096]{1,0:T(8,128)(2,1)S(1)}, bf16[64,4096]{1,0:T(8,128)(2,1)S(1)}, u32[]{:S(2)}, u32[]{:S(2)}) collective-permute-start(bf16[64,4096]{1,0:T(8,128)(2,1)S(1)} %get-tuple-element.92), channel_id=1, source_target_pairs={{8,0},{252,4},{16,8},{4,12},{24,16},{12,20},{32,24},{20,28},{40,32... | collective-permute-start | bytes 1572872 | tf_op jit(solution)/shard_map/ppermute | solution.py:20
  114.2 4.1 %collective-permute-done.23 = f32[64,256]{1,0:T(8,128)S(1)} collective-permute-done((f32[64,256]{1,0:T(8,128)S(1)}, f32[64,256]{1,0:T(8,128)S(1)}, u32[]{:S(2)}, u32[]{:S(2)}) %collective-permute-start.23) | collective-permute-done | bytes 65568 | tf_op jit(solution)/shard_map/ppermute | solution.py:24
  118.3 4.7 %collective-permute-done.20 = bf16[64,4096]{1,0:T(8,128)(2,1)S(1)} collective-permute-done((bf16[64,4096]{1,0:T(8,128)(2,1)S(1)}, bf16[64,4096]{1,0:T(8,128)(2,1)S(1)}, u32[]{:S(2)}, u32[]{:S(2)}) %collective-permute-start.20) | collective-permute-done | bytes 524320 | tf_op jit(solution)/shard_map/ppermute | solution.py:20
  123.1 5.1 %collective-permute-start.25 = (bf16[64,4096]{1,0:T(8,128)(2,1)S(1)}, bf16[64,4096]{1,0:T(8,128)(2,1)S(1)}, u32[]{:S(2)}, u32[]{:S(2)}) collective-permute-start(bf16[64,4096]{1,0:T(8,128)(2,1)S(1)} %add_convert_fusion.1), channel_id=1, source_target_pairs={{8,0},{252,4},{16,8},{4,12},{24,16},{12,20},{32,24},{20,28},{40,32... | collective-permute-start | bytes 1572872 | tf_op jit(solution)/shard_map/ppermute | solution.py:20
  129.3 8.0 %collective-permute-done.27 = f32[64,256]{1,0:T(8,128)S(1)} collective-permute-done((f32[64,256]{1,0:T(8,128)S(1)}, f32[64,256]{1,0:T(8,128)S(1)}, u32[]{:S(2)}, u32[]{:S(2)}) %collective-permute-start.27) | collective-permute-done | bytes 65568 | tf_op jit(solution)/shard_map/ppermute | solution.py:24
  137.9 4.9 %collective-permute-done.24 = bf16[64,4096]{1,0:T(8,128)(2,1)S(1)} collective-permute-done((bf16[64,4096]{1,0:T(8,128)(2,1)S(1)}, bf16[64,4096]{1,0:T(8,128)(2,1)S(1)}, u32[]{:S(2)}, u32[]{:S(2)}) %collective-permute-start.24) | collective-permute-done | bytes 524320 | tf_op jit(solution)/shard_map/ppermute | solution.py:20
  142.8 1.0 add_convert_fusion
  (65 shorter events, 9.5 us)
Async XLA Ops:
  0.6 27.8 %copy-start.1 = (bf16[64,4096]{1,0:T(8,128)(2,1)S(1)}, bf16[64,4096]{1,0:T(8,128)(2,1)}, u32[]{:S(2)}) copy-start(bf16[64,4096]{1,0:T(8,128)(2,1)} %refs_2_.1) | copy-start | bytes 1572868
  0.6 19.9 %collective-permute-start.1 = (bf16[64,4096]{1,0:T(8,128)(2,1)}, bf16[64,4096]{1,0:T(8,128)(2,1)S(1)}, u32[]{:S(2)}, u32[]{:S(2)}) collective-permute-start(bf16[64,4096]{1,0:T(8,128)(2,1)} %refs_2_.1), channel_id=1, source_target_pairs={{8,0},{252,4},{16,8},{4,12},{24,16},{12,20},{32,24},{20,28},{40,32... | collective-permute-start | bytes 1572872 | tf_op jit(solution)/shard_map/ppermute | solution.py:20
  9.0 13.6 %collective-permute-start = (bf16[64,4096]{1,0:T(8,128)(2,1)}, bf16[64,4096]{1,0:T(8,128)(2,1)S(1)}, u32[]{:S(2)}, u32[]{:S(2)}) collective-permute-start(bf16[64,4096]{1,0:T(8,128)(2,1)} %refs_2_.1), channel_id=1, source_target_pairs={{0,4},{4,0},{8,12},{12,8},{16,20},{20,16},{24,28},{28,24},{32,36},... | collective-permute-start | bytes 1572872 | tf_op jit(solution)/shard_map/ppermute | solution.py:24
  9.0 16.9 %collective-permute-start.2 = (bf16[64,4096]{1,0:T(8,128)(2,1)}, bf16[64,4096]{1,0:T(8,128)(2,1)S(1)}, u32[]{:S(2)}, u32[]{:S(2)}) collective-permute-start(bf16[64,4096]{1,0:T(8,128)(2,1)} %refs_2_.1), channel_id=1, source_target_pairs={{248,0},{12,4},{0,8},{20,12},{8,16},{28,20},{16,24},{36,28},{24,32... | collective-permute-start | bytes 1572872 | tf_op jit(solution)/shard_map/ppermute | solution.py:20
  25.9 12.5 %collective-permute-start.3 = (bf16[64,4096]{1,0:T(8,128)(2,1)S(1)}, bf16[64,4096]{1,0:T(8,128)(2,1)S(1)}, u32[]{:S(2)}, u32[]{:S(2)}) collective-permute-start(bf16[64,4096]{1,0:T(8,128)(2,1)S(1)} %collective-permute-done.1.refs_4_), channel_id=1, source_target_pairs={{8,0},{252,4},{16,8},{4,12},{24,16},{12,20},{32,24},{20,28},{40,32... | collective-permute-start | bytes 1572872 | tf_op jit(solution)/shard_map/ppermute | solution.py:20
  26.2 15.8 %collective-permute-start.4 = (bf16[64,4096]{1,0:T(8,128)(2,1)S(1)}, bf16[64,4096]{1,0:T(8,128)(2,1)S(1)}, u32[]{:S(2)}, u32[]{:S(2)}) collective-permute-start(bf16[64,4096]{1,0:T(8,128)(2,1)S(1)} %collective-permute-done.2.refs_5_), channel_id=1, source_target_pairs={{248,0},{12,4},{0,8},{20,12},{8,16},{28,20},{16,24},{36,28},{24,32... | collective-permute-start | bytes 1572872 | tf_op jit(solution)/shard_map/ppermute | solution.py:20
  28.0 22.4 %collective-permute-start.8 = (bf16[64,4352]{1,0:T(8,128)(2,1)S(1)}, bf16[64,4352]{1,0:T(8,128)(2,1)S(1)}, u32[]{:S(2)}, u32[]{:S(2)}) collective-permute-start(bf16[64,4352]{1,0:T(8,128)(2,1)S(1)} %pad_maximum_fusion.refs_4_), channel_id=1, source_target_pairs={{0,2},{1,3},{2,0},{3,1},{4,6},{5,7},{6,4},{7,5},{8,10},{9,11},{10,... | collective-permute-start | bytes 1671176 | tf_op jit(solution)/shard_map/ppermute | solution.py:24
  42.1 14.9 %collective-permute-start.6 = (bf16[64,4096]{1,0:T(8,128)(2,1)S(1)}, bf16[64,4096]{1,0:T(8,128)(2,1)S(1)}, u32[]{:S(2)}, u32[]{:S(2)}) collective-permute-start(bf16[64,4096]{1,0:T(8,128)(2,1)S(1)} %collective-permute-done.refs_3_), channel_id=1, source_target_pairs={{248,0},{12,4},{0,8},{20,12},{8,16},{28,20},{16,24},{36,28},{24,32... | collective-permute-start | bytes 1572872 | tf_op jit(solution)/shard_map/ppermute | solution.py:20
  42.1 14.9 %collective-permute-start.5 = (bf16[64,4096]{1,0:T(8,128)(2,1)S(1)}, bf16[64,4096]{1,0:T(8,128)(2,1)S(1)}, u32[]{:S(2)}, u32[]{:S(2)}) collective-permute-start(bf16[64,4096]{1,0:T(8,128)(2,1)S(1)} %collective-permute-done.refs_3_), channel_id=1, source_target_pairs={{8,0},{252,4},{16,8},{4,12},{24,16},{12,20},{32,24},{20,28},{40,32... | collective-permute-start | bytes 1572872 | tf_op jit(solution)/shard_map/ppermute | solution.py:20
  47.4 11.0 %collective-permute-start.7 = (bf16[64,4096]{1,0:T(8,128)(2,1)S(1)}, bf16[64,4096]{1,0:T(8,128)(2,1)S(1)}, u32[]{:S(2)}, u32[]{:S(2)}) collective-permute-start(bf16[64,4096]{1,0:T(8,128)(2,1)S(1)} %collective-permute-done.3.refs_2_), channel_id=1, source_target_pairs={{0,4},{4,0},{8,12},{12,8},{16,20},{20,16},{24,28},{28,24},{32,36},... | collective-permute-start | bytes 1572872 | tf_op jit(solution)/shard_map/ppermute | solution.py:24
  47.4 31.8 %slice-start = ((s8[9437184]{0:T(1024)(128)(4,1)}), s8[4194304]{0:T(1024)(128)(4,1)S(1)}, s32[]{:S(2)}) async-start(s8[9437184]{0:T(1024)(128)(4,1)} %bitcast.2), calls=%async_computation | async-start | bytes 8388608
  47.4 31.8 %slice-start.1 = ((s8[9437184]{0:T(1024)(128)(4,1)}), s8[4194304]{0:T(1024)(128)(4,1)S(1)}, s32[]{:S(2)}) async-start(s8[9437184]{0:T(1024)(128)(4,1)} %bitcast.2), calls=%async_computation.1 | async-start | bytes 8388608
  50.4 28.8 %slice-start.2 = ((s8[9437184]{0:T(1024)(128)(4,1)}), s8[1048576]{0:T(1024)(128)(4,1)S(1)}, s32[]{:S(2)}) async-start(s8[9437184]{0:T(1024)(128)(4,1)} %bitcast.2), calls=%async_computation.2 | async-start | bytes 2097152
  62.2 11.7 %collective-permute-start.10 = (bf16[64,4096]{1,0:T(8,128)(2,1)S(1)}, bf16[64,4096]{1,0:T(8,128)(2,1)S(1)}, u32[]{:S(2)}, u32[]{:S(2)}) collective-permute-start(bf16[64,4096]{1,0:T(8,128)(2,1)S(1)} %forward_2.1.refs_0_), channel_id=1, source_target_pairs={{0,2},{1,3},{2,0},{3,1},{4,6},{5,7},{6,4},{7,5},{8,10},{9,11},{10,... | collective-permute-start | bytes 1572872 | tf_op jit(solution)/shard_map/ppermute | solution.py:24
  62.8 11.1 %collective-permute-start.12 = (bf16[64,4352]{1,0:T(8,128)(2,1)S(1)}, bf16[64,4352]{1,0:T(8,128)(2,1)S(1)}, u32[]{:S(2)}, u32[]{:S(2)}) collective-permute-start(bf16[64,4352]{1,0:T(8,128)(2,1)S(1)} %pad_maximum_fusion.refs_4_), channel_id=1, source_target_pairs={{0,1},{1,0},{2,3},{3,2},{4,5},{5,4},{6,7},{7,6},{8,9},{9,8},{10,11... | collective-permute-start | bytes 1671176 | tf_op jit(solution)/shard_map/ppermute | solution.py:24
  62.8 11.1 %collective-permute-start.13 = (bf16[64,4352]{1,0:T(8,128)(2,1)S(1)}, bf16[64,4352]{1,0:T(8,128)(2,1)S(1)}, u32[]{:S(2)}, u32[]{:S(2)}) collective-permute-start(bf16[64,4352]{1,0:T(8,128)(2,1)S(1)} %collective-permute-done.8.refs_6_), channel_id=1, source_target_pairs={{0,1},{1,0},{2,3},{3,2},{4,5},{5,4},{6,7},{7,6},{8,9},{9,8},{10,11... | collective-permute-start | bytes 1671176 | tf_op jit(solution)/shard_map/ppermute | solution.py:24
  63.3 10.6 %collective-permute-start.9 = (bf16[64,4096]{1,0:T(8,128)(2,1)S(1)}, bf16[64,4096]{1,0:T(8,128)(2,1)S(1)}, u32[]{:S(2)}, u32[]{:S(2)}) collective-permute-start(bf16[64,4096]{1,0:T(8,128)(2,1)S(1)} %forward_2.1.refs_0_), channel_id=1, source_target_pairs={{0,1},{1,0},{2,3},{3,2},{4,5},{5,4},{6,7},{7,6},{8,9},{9,8},{10,11... | collective-permute-start | bytes 1572872 | tf_op jit(solution)/shard_map/ppermute | solution.py:24
  73.9 1.9 %collective-permute-start.11 = (bf16[64,4096]{1,0:T(8,128)(2,1)S(1)}, bf16[64,4096]{1,0:T(8,128)(2,1)S(1)}, u32[]{:S(2)}, u32[]{:S(2)}) collective-permute-start(bf16[64,4096]{1,0:T(8,128)(2,1)S(1)} %collective-permute-done.10.refs_2_), channel_id=1, source_target_pairs={{0,1},{1,0},{2,3},{3,2},{4,5},{5,4},{6,7},{7,6},{8,9},{9,8},{10,11... | collective-permute-start | bytes 1572872 | tf_op jit(solution)/shard_map/ppermute | solution.py:24
  79.2 4.3 %collective-permute-start.14 = (f32[64,256]{1,0:T(8,128)S(1)}, f32[64,256]{1,0:T(8,128)S(1)}, u32[]{:S(2)}, u32[]{:S(2)}) collective-permute-start(f32[64,256]{1,0:T(8,128)S(1)} %get-tuple-element.74), channel_id=1, source_target_pairs={{0,8},{4,12},{8,0},{12,4},{16,24},{20,28},{24,16},{28,20},{32,40},... | collective-permute-start | bytes 196616 | tf_op jit(solution)/shard_map/ppermute | solution.py:24
  83.5 19.0 %collective-permute-start.15 = (bf16[64,4096]{1,0:T(8,128)(2,1)S(1)}, bf16[64,4096]{1,0:T(8,128)(2,1)S(1)}, u32[]{:S(2)}, u32[]{:S(2)}) collective-permute-start(bf16[64,4096]{1,0:T(8,128)(2,1)S(1)} %get-tuple-element.75), channel_id=1, source_target_pairs={{0,4},{4,0},{8,12},{12,8},{16,20},{20,16},{24,28},{28,24},{32,36},... | collective-permute-start | bytes 1572872 | tf_op jit(solution)/shard_map/ppermute | solution.py:24
  83.5 19.0 %collective-permute-start.16 = (bf16[64,4096]{1,0:T(8,128)(2,1)S(1)}, bf16[64,4096]{1,0:T(8,128)(2,1)S(1)}, u32[]{:S(2)}, u32[]{:S(2)}) collective-permute-start(bf16[64,4096]{1,0:T(8,128)(2,1)S(1)} %get-tuple-element.76), channel_id=1, source_target_pairs={{248,0},{12,4},{0,8},{20,12},{8,16},{28,20},{16,24},{36,28},{24,32... | collective-permute-start | bytes 1572872 | tf_op jit(solution)/shard_map/ppermute | solution.py:20
  83.6 18.9 %collective-permute-start.17 = (bf16[64,4096]{1,0:T(8,128)(2,1)S(1)}, bf16[64,4096]{1,0:T(8,128)(2,1)S(1)}, u32[]{:S(2)}, u32[]{:S(2)}) collective-permute-start(bf16[64,4096]{1,0:T(8,128)(2,1)S(1)} %get-tuple-element.77), channel_id=1, source_target_pairs={{8,0},{252,4},{16,8},{4,12},{24,16},{12,20},{32,24},{20,28},{40,32... | collective-permute-start | bytes 1572872 | tf_op jit(solution)/shard_map/ppermute | solution.py:20
  88.9 4.4 %collective-permute-start.18 = (f32[64,256]{1,0:T(8,128)S(1)}, f32[64,256]{1,0:T(8,128)S(1)}, u32[]{:S(2)}, u32[]{:S(2)}) collective-permute-start(f32[64,256]{1,0:T(8,128)S(1)} %add.52), channel_id=1, source_target_pairs={{0,32},{4,36},{8,40},{12,44},{16,48},{20,52},{24,56},{28,60},{32,0... | collective-permute-start | bytes 196616 | tf_op jit(solution)/shard_map/ppermute | solution.py:24
  93.2 9.3 %collective-permute-start.19 = (f32[64,256]{1,0:T(8,128)S(1)}, f32[64,256]{1,0:T(8,128)S(1)}, u32[]{:S(2)}, u32[]{:S(2)}) collective-permute-start(f32[64,256]{1,0:T(8,128)S(1)} %add.53), channel_id=1, source_target_pairs={{0,64},{4,68},{8,72},{12,76},{16,80},{20,84},{24,88},{28,92},{32,9... | collective-permute-start | bytes 196616 | tf_op jit(solution)/shard_map/ppermute | solution.py:24
  102.5 11.4 %collective-permute-start.22 = (f32[64,256]{1,0:T(8,128)S(1)}, f32[64,256]{1,0:T(8,128)S(1)}, u32[]{:S(2)}, u32[]{:S(2)}) collective-permute-start(f32[64,256]{1,0:T(8,128)S(1)} %add.57), channel_id=1, source_target_pairs={{0,128},{4,132},{8,136},{12,140},{16,144},{20,148},{24,152},{28,15... | collective-permute-start | bytes 196616 | tf_op jit(solution)/shard_map/ppermute | solution.py:24
  108.5 14.5 %collective-permute-start.20 = (bf16[64,4096]{1,0:T(8,128)(2,1)S(1)}, bf16[64,4096]{1,0:T(8,128)(2,1)S(1)}, u32[]{:S(2)}, u32[]{:S(2)}) collective-permute-start(bf16[64,4096]{1,0:T(8,128)(2,1)S(1)} %add_convert_fusion.4), channel_id=1, source_target_pairs={{248,0},{12,4},{0,8},{20,12},{8,16},{28,20},{16,24},{36,28},{24,32... | collective-permute-start | bytes 1572872 | tf_op jit(solution)/shard_map/ppermute | solution.py:20
  108.6 14.4 %collective-permute-start.21 = (bf16[64,4096]{1,0:T(8,128)(2,1)S(1)}, bf16[64,4096]{1,0:T(8,128)(2,1)S(1)}, u32[]{:S(2)}, u32[]{:S(2)}) collective-permute-start(bf16[64,4096]{1,0:T(8,128)(2,1)S(1)} %get-tuple-element.92), channel_id=1, source_target_pairs={{8,0},{252,4},{16,8},{4,12},{24,16},{12,20},{32,24},{20,28},{40,32... | collective-permute-start | bytes 1572872 | tf_op jit(solution)/shard_map/ppermute | solution.py:20
  113.9 4.4 %collective-permute-start.23 = (f32[64,256]{1,0:T(8,128)S(1)}, f32[64,256]{1,0:T(8,128)S(1)}, u32[]{:S(2)}, u32[]{:S(2)}) collective-permute-start(f32[64,256]{1,0:T(8,128)S(1)} %add.58), channel_id=1, source_target_pairs={{0,4},{4,0},{8,12},{12,8},{16,20},{20,16},{24,28},{28,24},{32,36},... | collective-permute-start | bytes 196616 | tf_op jit(solution)/shard_map/ppermute | solution.py:24
  123.1 14.8 %collective-permute-start.25 = (bf16[64,4096]{1,0:T(8,128)(2,1)S(1)}, bf16[64,4096]{1,0:T(8,128)(2,1)S(1)}, u32[]{:S(2)}, u32[]{:S(2)}) collective-permute-start(bf16[64,4096]{1,0:T(8,128)(2,1)S(1)} %add_convert_fusion.1), channel_id=1, source_target_pairs={{8,0},{252,4},{16,8},{4,12},{24,16},{12,20},{32,24},{20,28},{40,32... | collective-permute-start | bytes 1572872 | tf_op jit(solution)/shard_map/ppermute | solution.py:20
  128.3 14.4 %collective-permute-start.24 = (bf16[64,4096]{1,0:T(8,128)(2,1)S(1)}, bf16[64,4096]{1,0:T(8,128)(2,1)S(1)}, u32[]{:S(2)}, u32[]{:S(2)}) collective-permute-start(bf16[64,4096]{1,0:T(8,128)(2,1)S(1)} %add_convert_fusion.2), channel_id=1, source_target_pairs={{248,0},{12,4},{0,8},{20,12},{8,16},{28,20},{16,24},{36,28},{24,32... | collective-permute-start | bytes 1572872 | tf_op jit(solution)/shard_map/ppermute | solution.py:20
  128.4 14.3 %collective-permute-start.26 = (bf16[64,4096]{1,0:T(8,128)(2,1)S(1)}, bf16[64,4096]{1,0:T(8,128)(2,1)S(1)}, u32[]{:S(2)}, u32[]{:S(2)}) collective-permute-start(bf16[64,4096]{1,0:T(8,128)(2,1)S(1)} %add_convert_fusion.3), channel_id=1, source_target_pairs={{0,4},{4,0},{8,12},{12,8},{16,20},{20,16},{24,28},{28,24},{32,36},... | collective-permute-start | bytes 1572872 | tf_op jit(solution)/shard_map/ppermute | solution.py:24
  129.3 8.0 %collective-permute-start.27 = (f32[64,256]{1,0:T(8,128)S(1)}, f32[64,256]{1,0:T(8,128)S(1)}, u32[]{:S(2)}, u32[]{:S(2)}) collective-permute-start(f32[64,256]{1,0:T(8,128)S(1)} %add.59), channel_id=1, source_target_pairs={{0,16},{4,20},{8,24},{12,28},{16,0},{20,4},{24,8},{28,12},{32,48},... | collective-permute-start | bytes 196616 | tf_op jit(solution)/shard_map/ppermute | solution.py:24
  (4 other events, 5.7 us)

commit v4 on v3

--- a/solution.py
+++ b/solution.py
@@ -10,7 +10,7 @@
 
 REACH = 4
 GROUP = 8
-WAVES = [[0, 1, 2, -2], [4, -4], [3, -1, -3]]
+WAVES = [[0, 2, -2], [1, 4, -4], [3, -1], [-3]]
 MIB = 1 << 20
 
 
@@ -112,23 +112,29 @@
     )
 
 
-def forward_body(wave, seeded, *refs):
-    n = len(WAVES[wave])
+def forward_body(waves, parts, seeded, *refs):
+    n = len(parts)
     list_ref, vals_ref = refs[:2]
-    slabs, rest = refs[2 : 2 + n], refs[2 + n :]
+    slabs, rest = refs[2 : 2 + sum(parts)], refs[2 + sum(parts) :]
     if seeded:
         seed_ref, rest = rest[0], rest[1:]
     out_ref, held = rest[:2]
     acc = rest[2] if len(rest) > 2 else out_ref
     acc[...] = seed_ref[...] if seeded else jnp.zeros_like(acc)
-    for j, slab in enumerate(slabs):
-        held[j] = slab[...]
+    at = 0
+    for j, count in enumerate(parts):
+        row = 0
+        for slab in slabs[at : at + count]:
+            held[j, row : row + slab.shape[0]] = slab[...]
+            row += slab.shape[0]
+        at += count
     feats = acc.shape[0]
     held[n, :, 0:128] = jnp.zeros((feats, 128), held.dtype)
 
-    def multiply(entries, tiles):
+    def multiply(first, entries, tiles):
         pieces = [
-            held[(e >> 20) + ((e >> 14) & 1) * n, :, column((e >> 15) & 31)] for e in entries
+            held[jnp.where(((e >> 14) & 1) == 1, n, (e >> 20) + first), :, column((e >> 15) & 31)]
+            for e in entries
         ]
         products = [
             lax.dot_general(
@@ -143,25 +149,29 @@
             half = products[u // 2][u % 2 * feats : (u % 2 + 1) * feats]
             acc[:, column((e >> 9) & 31)] += half
 
-    tile_loop(wave, list_ref, vals_ref, multiply)
+    first = 0
+    for wave in waves:
+        tile_loop(wave, list_ref, vals_ref, functools.partial(multiply, first))
+        first += len(WAVES[wave])
     if acc is not out_ref:
         out_ref[...] = acc[...].astype(out_ref.dtype)
 
 
-def forward(wave, listed, vals, slabs, seed, dtype):
-    feats, nodes = slabs[0].shape
-    wide = dtype == jnp.float32
+def forward(waves, listed, vals, slabs, seed, dtype):
+    feats, nodes = slabs[0][0].shape[0] * len(slabs[0]), slabs[0][0].shape[1]
+    parts = [len(slab) for slab in slabs]
+    flat = [part for slab in slabs for part in slab]
     return pl.pallas_call(
-        functools.partial(forward_body, wave, seed is not None),
+        functools.partial(forward_body, waves, parts, seed is not None),
         out_shape=pltpu.VMEM((feats, nodes), dtype),
-        in_specs=[SMEM] + [VMEM] * (1 + len(slabs) + (seed is not None)),
+        in_specs=[SMEM] + [VMEM] * (1 + len(flat) + (seed is not None)),
         out_specs=VMEM,
-        scratch_shapes=[pltpu.VMEM((len(slabs) + 1, feats, nodes), slabs[0].dtype)]
-        + ([] if wide else [pltpu.VMEM((feats, nodes), jnp.float32)]),
+        scratch_shapes=[pltpu.VMEM((len(slabs) + 1, feats, nodes), flat[0].dtype)]
+        + ([] if dtype == jnp.float32 else [pltpu.VMEM((feats, nodes), jnp.float32)]),
         cost_estimate=COST,
         compiler_params=kept(8),
-        name=f"forward_{wave}",
-    )(listed, near(vals), *map(near, slabs), *(() if seed is None else (near(seed),)))
+        name=f"forward_{waves[0]}",
+    )(listed, near(vals), *map(near, flat), *(() if seed is None else (near(seed),)))
 
 
 def backward_body(wave, *refs):
@@ -205,18 +215,11 @@
 
 
 def middle_body(factor, place_ref, *refs):
-    ys, packed, (out_ref, grad_ref, wgrad_ref) = refs[0:4], refs[4:8], refs[8:]
+    ys, cots, weights, (out_ref, grad_ref, wgrad_ref) = refs[0:4], refs[4:8], refs[8:12], refs[12:]
     feats, nodes = ys[0].shape
     hidden = 4 * feats
     chunk = 512
-    rows = []
-    for k in range(4):
-        w = packed[k][:, nodes:]
-        rows.append(
-            jnp.concatenate(
-                [w[:, (j ^ k) * feats : ((j ^ k) + 1) * feats] for j in range(4)], axis=1
-            )
-        )
+    rows = [exchanged_columns(r[...], place_ref[0]) for r in weights]
     own_rows = rows[0]
     turned = jnp.concatenate(rows, axis=0).T
     wgrad = jnp.zeros((feats, hidden), jnp.float32)
@@ -226,7 +229,7 @@
         pre = jnp.dot(turned, y, preferred_element_type=jnp.float32)
         sig = jax.nn.sigmoid(pre)
         out_ref[:, here] = (pre[:feats] * sig[:feats]).astype(out_ref.dtype)
-        cot = jnp.concatenate([r[:, here] for r in packed], axis=0).astype(jnp.float32)
+        cot = jnp.concatenate([r[:, here] for r in cots], axis=0).astype(jnp.float32)
         grad_pre = (cot * (sig * (1.0 + pre * (1.0 - sig)))).astype(jnp.bfloat16)
         grad_ref[:, here] = jnp.dot(
             own_rows, grad_pre, preferred_element_type=jnp.float32
@@ -237,7 +240,7 @@
     wgrad_ref[...] = exchanged_columns(wgrad, place_ref[0]) * factor
 
 
-def middle(place, ys, packed):
+def middle(place, ys, cots, weights):
     feats, nodes = ys[0].shape
     factor = 1.0 / math.sqrt(nodes * lax.axis_size("blk"))
     return pl.pallas_call(
@@ -247,12 +250,12 @@
             pltpu.VMEM((feats, nodes), jnp.bfloat16),
             pltpu.VMEM((feats, 4 * feats), jnp.float32),
         ),
-        in_specs=[SMEM] + [VMEM] * 8,
+        in_specs=[SMEM] + [VMEM] * 12,
         out_specs=(VMEM,) * 3,
         cost_estimate=COST,
         compiler_params=kept(10),
         name="middle",
-    )(place.astype(jnp.int32).reshape(1), *map(near, ys), *map(near, packed))
+    )(place.astype(jnp.int32).reshape(1), *map(near, ys), *map(near, cots), *map(near, weights))
 
 
 def fenced(*groups):
@@ -264,34 +267,44 @@
     f32, bf16 = jnp.float32, jnp.bfloat16
     place = lax.axis_index("feat")
     sign = (1 - 2 * (lax.axis_index("blk") % 2)).astype(jnp.int32).reshape(1)
-    own = jnp.concatenate([cotangent, exchanged_columns(weight, place)], axis=1)
-
-    x, u, v = flipped(x_t, "blk", 1), stepped(x_t, True), stepped(x_t, False)
+    top, low = x_t[: x_t.shape[0] // 2], x_t[x_t.shape[0] // 2 :]
+    u = [stepped(top, True), stepped(low, True)]
+    x, v = flipped(x_t, "blk", 1), stepped(x_t, False)
+    cot_far = flipped(cotangent, "feat", 2)
     listed = plan(tile_row, tile_col, tile_off, tile_count, sign)
-    x, u, v, listed, own = fenced(x, u, v, listed, own)
-    m, n, far = stepped(u, True), stepped(v, False), flipped(own, "feat", 2)
-    y = forward(0, listed, tile_vals, [x_t, x, u, v], None, f32)
-    m, n, y, x = fenced(m, n, y, x)
-    mx, xu, xv = flipped(m, "blk", 1), stepped(x, True), stepped(x, False)
-    y = forward(1, listed, tile_vals, [m, n], y, f32)
-    xu, xv, mx, y, far, own = fenced(xu, xv, mx, y, far, own)
-    packed = [own, flipped(own, "feat", 1), far, flipped(far, "feat", 1)]
-    y = forward(2, listed, tile_vals, [xu, xv, mx], y, bf16)
+    u[0], listed = fenced(u[0], listed)
+    m = [stepped(half, True) for half in u]
+    n = stepped(v, False)
+    y = forward((0,), listed, tile_vals, [[x_t], u, [v]], None, f32)
+    m[0], x, y, cot_far, weight = fenced(m[0], x, y, cot_far, weight)
+    weight_far = flipped(weight, "feat", 2)
+    mx = [flipped(half, "blk", 1) for half in m]
+    xu, xv = stepped(x, True), stepped(x, False)
+    y = forward((1,), listed, tile_vals, [[x], m, [n]], y, f32)
+    weight, weight_far, y = fenced(weight, weight_far, y)
+    cots = [cotangent, flipped(cotangent, "feat", 1), cot_far, flipped(cot_far, "feat", 1)]
+    weights = [weight, flipped(weight, "feat", 1), weight_far, flipped(weight_far, "feat", 1)]
+    y = forward((3,), listed, tile_vals, [mx], y, f32)
+    y, cots, weights = fenced(y, cots, weights)
+    y = forward((2,), listed, tile_vals, [[xu], [xv]], y, bf16)
     y_far = flipped(y, "feat", 2)
     ys = [y, flipped(y, "feat", 1), y_far, flipped(y_far, "feat", 1)]
-    out_t, grad, wgrad = middle(place, ys, packed)
+    out_t, grad, wgrad = middle(place, ys, cots, weights)
 
     part = flipped(wgrad, "blk", 2)
-    to_xu, to_xv, to_mx = backward(2, listed, tile_vals, grad, [bf16] * 3)
-    to_xu, to_xv, to_mx, part, grad = fenced(to_xu, to_xv, to_mx, part, grad)
-    from_mx, from_xu, from_xv = flipped(to_mx, "blk", 1), stepped(to_xu, False), stepped(to_xv, True)
+    (to_mx,) = backward(3, listed, tile_vals, grad, [bf16])
+    to_mx, grad = fenced(to_mx, grad)
+    from_mx = flipped(to_mx, "blk", 1)
+    to_xu, to_xv = backward(2, listed, tile_vals, grad, [bf16] * 2)
+    to_xu, to_xv, grad, part = fenced(to_xu, to_xv, grad, part)
+    from_xu, from_xv = stepped(to_xu, False), stepped(to_xv, True)
+    wgrad = wgrad + part
+    part = flipped(wgrad, "blk", 4)
+    to_x, to_m, to_n = backward(1, listed, tile_vals, grad, [f32, f32, bf16])
+    part, to_m, grad = fenced(part, to_m, grad)
     wgrad = wgrad + part
     part = flipped(wgrad, "blk", 8)
-    to_m, to_n = backward(1, listed, tile_vals, grad, [f32, bf16])
-    part, to_m, grad = fenced(part, to_m, grad)
-    wgrad = wgrad + part
-    part = flipped(wgrad, "blk", 16)
-    total, to_x, to_u, to_v = backward(0, listed, tile_vals, grad, [f32] * 4)
+    total, to_u, to_v = backward(0, listed, tile_vals, grad, [f32] * 3)
     from_mx, from_xu, from_xv, to_m, to_n, total, to_x, to_u, to_v, part = fenced(
         from_mx, from_xu, from_xv, to_m, to_n, total, to_x, to_u, to_v, part
     )
@@ -299,10 +312,10 @@
     from_n = stepped(to_n, True)
     to_x = (to_x + from_xu.astype(f32) + from_xv.astype(f32)).astype(bf16)
     wgrad = wgrad + part
-    wgrad = wgrad + flipped(wgrad, "blk", 32)
     wgrad = wgrad + flipped(wgrad, "blk", 1)
+    wgrad = wgrad + flipped(wgrad, "blk", 16)
     from_m, from_n, to_x, to_u, to_v, wgrad = fenced(from_m, from_n, to_x, to_u, to_v, wgrad)
-    part = flipped(wgrad, "blk", 4)
+    part = flipped(wgrad, "blk", 32)
     from_u = stepped((to_u + from_m.astype(f32)).astype(bf16), False)
     from_v = stepped((to_v + from_n.astype(f32)).astype(bf16), True)
     from_x = flipped(to_x, "blk", 1)

time: 142 us -> 162 us (1.14)
  starting transfers between devices: 44.6 us -> 64.5 us
  Pallas kernels: 31.7 us -> 24.2 us
  local copies, waits for them, and re-layouts: 6.62 us -> 11.5 us
  waiting for transfers between devices: 55.2 us -> 58.8 us
  other arithmetic: 4.14 us -> 2.16 us
    ppermute x16 -> x20, waiting for transfers between devices: 29.8 us -> 48.6 us  [flipped(): lax.ppermute(block, axis, [(i, i ^ bit) for i in range(lax.axis_size(axis...]
    ppermute x12 -> x14, waiting for transfers between devices: 25.4 us -> 10.2 us  [stepped(): return lax.ppermute(block, 'blk', route)]
    ppermute x12 -> x14, starting transfers between devices: 31.7 us -> 41.8 us  [stepped(): return lax.ppermute(block, 'blk', route)]
    ppermute x16 -> x20, starting transfers between devices: 12.8 us -> 22.7 us  [flipped(): lax.ppermute(block, axis, [(i, i ^ bit) for i in range(lax.axis_size(axis...]
    unnamed x16 -> x22, local copies, waits for them, and re-layouts: 5.74 us -> 10.5 us
    pallas_call x3 -> x4, Pallas kernels: 11.7 us -> 8.1 us  [backward(): pl.pallas_call(functools.partial(backward_body, wave), out_shape=tuple((p...]
    pallas_call x3 -> x4, Pallas kernels: 11.5 us -> 8 us  [forward(): pl.pallas_call(functools.partial(forward_body, waves, parts, seed is not...]
    pallas_call x1, Pallas kernels: 5.11 us -> 3.24 us  [plan(): pl.pallas_call(functools.partial(plan_body, cap), out_shape=jax.ShapeDtyp...]
  transfers between devices with their start and end apart: 28 -> 34, of which waited for: 15 -> 12; matrix products, arithmetic and copies ran while one was open for 3% -> 1% of each run, Pallas kernels for 17% -> 11%
where the time goes in v4:
time: 162 us; the launch traced here: 163 us
  starting transfers between devices  64.5 us (40%)
  waiting for transfers between devices  58.8 us (36%)
  Pallas kernels  24.2 us (15%)
  local copies, waits for them, and re-layouts  11.5 us (7%)
  other arithmetic  2.16 us (1%)
  between operations  1.65 us (1%)
    ppermute x20, waiting for transfers between devices, flipped(): lax.ppermute(block, axis, [(i, i ^ bit) for i in range(lax.axis_size(axis...  48.6 us
    ppermute x14, starting transfers between devices, stepped(): return lax.ppermute(block, 'blk', route)  41.8 us
    ppermute x20, starting transfers between devices, flipped(): lax.ppermute(block, axis, [(i, i ^ bit) for i in range(lax.axis_size(axis...  22.7 us
    unnamed x22, local copies, waits for them, and re-layouts  10.5 us
    ppermute x14, waiting for transfers between devices, stepped(): return lax.ppermute(block, 'blk', route)  10.2 us
    pallas_call x4, Pallas kernels, backward(): pl.pallas_call(functools.partial(backward_body, wave), out_shape=tuple((p...  8.1 us
    pallas_call x4, Pallas kernels, forward(): pl.pallas_call(functools.partial(forward_body, waves, parts, seed is not...  8 us
    pallas_call x1, Pallas kernels, middle(): pl.pallas_call(functools.partial(middle_body, factor), out_shape=(jax.Sha...  4.83 us
  transfers between devices with their start and end apart: 34, of which 12 were waited for; matrix products, arithmetic and copies ran while one was open for 1% of the time, Pallas kernels for 11%

profile of v4, /device:TPU:4, one launch (start us, length us, event | category | flops | bytes accessed | tf_op | source)
XLA Modules:
  0.0 162.9 jit_solution(15732457644331515710)
XLA Ops:
  3.4 6.8 %collective-permute-start = (bf16[32,4096]{1,0:T(8,128)(2,1)S(1)}, bf16[32,4096]{1,0:T(8,128)(2,1)S(1)}, u32[]{:S(2)}, u32[]{:S(2)}) collective-permute-start(bf16[32,4096]{1,0:T(8,128)(2,1)S(1)} %get-tuple-element.114), channel_id=1, source_target_pairs={{8,0},{252,4},{16,8},{4,12},{24,16},{12,20},{32,24},{20,28},{40,32... | collective-permute-start | bytes 786440 | tf_op jit(solution)/shard_map/ppermute | solution.py:20
  10.2 2.0 %collective-permute-start.3 = (bf16[32,4096]{1,0:T(8,128)(2,1)S(1)}, bf16[32,4096]{1,0:T(8,128)(2,1)S(1)}, u32[]{:S(2)}, u32[]{:S(2)}) collective-permute-start(bf16[32,4096]{1,0:T(8,128)(2,1)S(1)} %get-tuple-element.113), channel_id=1, source_target_pairs={{8,0},{252,4},{16,8},{4,12},{24,16},{12,20},{32,24},{20,28},{40,32... | collective-permute-start | bytes 786440 | tf_op jit(solution)/shard_map/ppermute | solution.py:20
  15.4 3.2 %plan.1.refs_0_ = s32[1200]{0:T(1024)S(1)} custom-call(s32[288]{0:T(512)S(1)} %copy-done.5, s32[288]{0:T(512)S(1)} %copy-done.6, s32[288]{0:T(512)S(1)} %copy-done.7, s32[1]{0:T(128)S(6)} %copy.11.count_ref, s32[1]{0:T(128)} %bitcast.1.sign_ref), custom_call_target="tpu_custom_call" | custom-call | bytes 6000000 | tf_op jit(solution)/shard_map/plan/pallas_call | solution.py:81
  18.7 4.1 %collective-permute-start.1 = (bf16[32,4096]{1,0:T(8,128)(2,1)S(1)}, bf16[32,4096]{1,0:T(8,128)(2,1)S(1)}, u32[]{:S(2)}, u32[]{:S(2)}) collective-permute-start(bf16[32,4096]{1,0:T(8,128)(2,1)S(1)} %collective-permute-done.refs_3_), channel_id=1, source_target_pairs={{8,0},{252,4},{16,8},{4,12},{24,16},{12,20},{32,24},{20,28},{40,32... | collective-permute-start | bytes 786440 | tf_op jit(solution)/shard_map/ppermute | solution.py:20
  22.8 4.3 %collective-permute-done.1.refs_3_ = bf16[32,4096]{1,0:T(8,128)(2,1)S(1)} collective-permute-done((bf16[32,4096]{1,0:T(8,128)(2,1)S(1)}, bf16[32,4096]{1,0:T(8,128)(2,1)S(1)}, u32[]{:S(2)}, u32[]{:S(2)}) %collective-permute-start.1) | collective-permute-done | bytes 262176 | tf_op jit(solution)/shard_map/ppermute | solution.py:20
  27.2 5.8 %collective-permute-start.9 = (bf16[32,4096]{1,0:T(8,128)(2,1)S(1)}, bf16[32,4096]{1,0:T(8,128)(2,1)S(1)}, u32[]{:S(2)}, u32[]{:S(2)}) collective-permute-start(bf16[32,4096]{1,0:T(8,128)(2,1)S(1)} %collective-permute-done.3.refs_4_), channel_id=1, source_target_pairs={{8,0},{252,4},{16,8},{4,12},{24,16},{12,20},{32,24},{20,28},{40,32... | collective-permute-start | bytes 786440 | tf_op jit(solution)/shard_map/ppermute | solution.py:20
  33.0 3.7 %copy-done = bf16[288,128,128]{2,1,0:T(8,128)(2,1)S(1)} copy-done((bf16[288,128,128]{2,1,0:T(8,128)(2,1)S(1)}, bf16[288,128,128]{2,1,0:T(8,128)(2,1)}, u32[]{:S(2)}) %copy-start) | copy-done | bytes 9437208
  37.7 2.3 %forward_0.1.refs_6_ = f32[64,4096]{1,0:T(8,128)S(1)} custom-call(s32[1200]{0:T(1024)S(1)} %plan.1.refs_0_, bf16[288,128,128]{2,1,0:T(8,128)(2,1)S(1)} %copy-done, bf16[64,4096]{1,0:T(8,128)(2,1)S(1)} %copy-done.2, bf16[32,4096]{1,0:T(8,128)(2,1)S(1)} %collective-permute-done.refs_3_, bf16[32,4096]{1,0:T(8,128)(2,1)S(1)} %collective-permute-done.3.refs_4_, ...), custom_call_target="tpu_custom_call" | custom-call | bytes 6000000 | tf_op jit(solution)/shard_map/forward_0/pallas_call | solution.py:164
  40.2 5.3 %collective-permute-start.6 = (bf16[64,4096]{1,0:T(8,128)(2,1)S(1)}, bf16[64,4096]{1,0:T(8,128)(2,1)S(1)}, u32[]{:S(2)}, u32[]{:S(2)}) collective-permute-start(bf16[64,4096]{1,0:T(8,128)(2,1)S(1)} %collective-permute-done.2.refs_2_), channel_id=1, source_target_pairs={{8,0},{252,4},{16,8},{4,12},{24,16},{12,20},{32,24},{20,28},{40,32... | collective-permute-start | bytes 1572872 | tf_op jit(solution)/shard_map/ppermute | solution.py:20
  45.5 2.7 %collective-permute-start.11 = (bf16[64,256]{1,0:T(8,128)(2,1)S(1)}, bf16[64,256]{1,0:T(8,128)(2,1)S(1)}, u32[]{:S(2)}, u32[]{:S(2)}) collective-permute-start(bf16[64,256]{1,0:T(8,128)(2,1)S(1)} %copy-done.4), channel_id=1, source_target_pairs={{0,2},{1,3},{2,0},{3,1},{4,6},{5,7},{6,4},{7,5},{8,10},{9,11},{10,... | collective-permute-start | bytes 98312 | tf_op jit(solution)/shard_map/ppermute | solution.py:24
  48.3 2.7 %collective-permute-done.11.refs_10_ = bf16[64,256]{1,0:T(8,128)(2,1)S(1)} collective-permute-done((bf16[64,256]{1,0:T(8,128)(2,1)S(1)}, bf16[64,256]{1,0:T(8,128)(2,1)S(1)}, u32[]{:S(2)}, u32[]{:S(2)}) %collective-permute-start.11) | collective-permute-done | bytes 32800 | tf_op jit(solution)/shard_map/ppermute | solution.py:24
  53.0 2.3 %forward_1.1.refs_4_ = f32[64,4096]{1,0:T(8,128)S(1)} custom-call(s32[1200]{0:T(1024)S(1)} %plan.1.refs_0_, bf16[288,128,128]{2,1,0:T(8,128)(2,1)S(1)} %copy-done, bf16[64,4096]{1,0:T(8,128)(2,1)S(1)} %collective-permute-done.2.refs_2_, bf16[32,4096]{1,0:T(8,128)(2,1)S(1)} %collective-permute-done.1.refs_3_, ...), custom_call_target="tpu_custom_call" | custom-call | bytes 6000000 | tf_op jit(solution)/shard_map/forward_1/pallas_call | solution.py:164
  55.3 4.9 %collective-permute-done.10.refs_3_ = bf16[32,4096]{1,0:T(8,128)(2,1)S(1)} collective-permute-done((bf16[32,4096]{1,0:T(8,128)(2,1)S(1)}, bf16[32,4096]{1,0:T(8,128)(2,1)S(1)}, u32[]{:S(2)}, u32[]{:S(2)}) %collective-permute-start.10) | collective-permute-done | bytes 262176 | tf_op jit(solution)/shard_map/ppermute | solution.py:24
  60.2 3.6 %collective-permute-done.8.refs_2_ = bf16[32,4096]{1,0:T(8,128)(2,1)S(1)} collective-permute-done((bf16[32,4096]{1,0:T(8,128)(2,1)S(1)}, bf16[32,4096]{1,0:T(8,128)(2,1)S(1)}, u32[]{:S(2)}, u32[]{:S(2)}) %collective-permute-start.8) | collective-permute-done | bytes 262176 | tf_op jit(solution)/shard_map/ppermute | solution.py:24
  67.3 2.8 %collective-permute-start.18 = (bf16[64,4096]{1,0:T(8,128)(2,1)S(1)}, bf16[64,4096]{1,0:T(8,128)(2,1)S(1)}, u32[]{:S(2)}, u32[]{:S(2)}) collective-permute-start(bf16[64,4096]{1,0:T(8,128)(2,1)S(1)} %forward_2.1.refs_0_), channel_id=1, source_target_pairs={{0,2},{1,3},{2,0},{3,1},{4,6},{5,7},{6,4},{7,5},{8,10},{9,11},{10,... | collective-permute-start | bytes 1572872 | tf_op jit(solution)/shard_map/ppermute | solution.py:24
  70.4 12.9 %collective-permute-done.18.refs_2_ = bf16[64,4096]{1,0:T(8,128)(2,1)S(1)} collective-permute-done((bf16[64,4096]{1,0:T(8,128)(2,1)S(1)}, bf16[64,4096]{1,0:T(8,128)(2,1)S(1)}, u32[]{:S(2)}, u32[]{:S(2)}) %collective-permute-start.18) | collective-permute-done | bytes 524320 | tf_op jit(solution)/shard_map/ppermute | solution.py:24
  83.3 2.0 %collective-permute-done.19.refs_3_ = bf16[64,4096]{1,0:T(8,128)(2,1)} collective-permute-done((bf16[64,4096]{1,0:T(8,128)(2,1)S(1)}, bf16[64,4096]{1,0:T(8,128)(2,1)}, u32[]{:S(2)}, u32[]{:S(2)}) %collective-permute-start.19) | collective-permute-done | bytes 524320 | tf_op jit(solution)/shard_map/ppermute | solution.py:24
  85.3 4.8 %middle.1 = (bf16[64,4096]{1,0:T(8,128)(2,1)}, bf16[64,4096]{1,0:T(8,128)(2,1)S(1)}, f32[64,256]{1,0:T(8,128)S(1)}) custom-call(s32[1]{0:T(128)} %bitcast.place_ref, bf16[64,4096]{1,0:T(8,128)(2,1)S(1)} %forward_2.1.refs_0_, bf16[64,4096]{1,0:T(8,128)(2,1)} %collective-permute-done.17.refs_1_, bf16[64,4096]{1,0:T(8,128)(2,1)S(1)} %collective-permute-done.18.refs_2_, ...), custom_call_target="tpu_custom_call" | custom-call | bytes 6000000 | tf_op jit(solution)/shard_map/middle/pallas_call | solution.py:246
  90.1 3.7 %copy-done.1 = bf16[288,128,128]{2,1,0:T(8,128)(2,1)S(1)} copy-done((bf16[288,128,128]{2,1,0:T(8,128)(2,1)S(1)}, bf16[288,128,128]{2,1,0:T(8,128)(2,1)}, u32[]{:S(2)}) %copy-start.1) | copy-done | bytes 9437208
  97.2 2.8 %collective-permute-start.22 = (bf16[64,4096]{1,0:T(8,128)(2,1)S(1)}, bf16[64,4096]{1,0:T(8,128)(2,1)S(1)}, u32[]{:S(2)}, u32[]{:S(2)}) collective-permute-start(bf16[64,4096]{1,0:T(8,128)(2,1)S(1)} %get-tuple-element.84), channel_id=1, source_target_pairs={{248,0},{12,4},{0,8},{20,12},{8,16},{28,20},{16,24},{36,28},{24,32... | collective-permute-start | bytes 1572872 | tf_op jit(solution)/shard_map/ppermute | solution.py:20
  100.0 3.9 %collective-permute-start.23 = (bf16[64,4096]{1,0:T(8,128)(2,1)S(1)}, bf16[64,4096]{1,0:T(8,128)(2,1)S(1)}, u32[]{:S(2)}, u32[]{:S(2)}) collective-permute-start(bf16[64,4096]{1,0:T(8,128)(2,1)S(1)} %get-tuple-element.85), channel_id=1, source_target_pairs={{8,0},{252,4},{16,8},{4,12},{24,16},{12,20},{32,24},{20,28},{40,32... | collective-permute-start | bytes 1572872 | tf_op jit(solution)/shard_map/ppermute | solution.py:20
  104.1 2.4 %backward_1.1 = (f32[64,4096]{1,0:T(8,128)S(1)}, f32[64,4096]{1,0:T(8,128)S(1)}, bf16[64,4096]{1,0:T(8,128)(2,1)S(1)}) custom-call(s32[1200]{0:T(1024)S(1)} %plan.1.refs_0_, bf16[288,128,128]{2,1,0:T(8,128)(2,1)S(1)} %bitcast.3, bf16[64,4096]{1,0:T(8,128)(2,1)S(1)} %get-tuple-element.91.refs_2_), custom_call_target="tpu_custom_call" | custom-call | bytes 6000000 | tf_op jit(solution)/shard_map/backward_1/pallas_call | solution.py:205
  106.5 5.9 %collective-permute-done.24 = f32[64,256]{1,0:T(8,128)S(1)} collective-permute-done((f32[64,256]{1,0:T(8,128)S(1)}, f32[64,256]{1,0:T(8,128)S(1)}, u32[]{:S(2)}, u32[]{:S(2)}) %collective-permute-start.24) | collective-permute-done | bytes 65568 | tf_op jit(solution)/shard_map/ppermute | solution.py:24
  112.6 2.4 %backward_0.1 = (f32[64,4096]{1,0:T(8,128)S(1)}, f32[64,4096]{1,0:T(8,128)S(1)}, f32[64,4096]{1,0:T(8,128)S(1)}) custom-call(s32[1200]{0:T(1024)S(1)} %plan.1.refs_0_, bf16[288,128,128]{2,1,0:T(8,128)(2,1)S(1)} %bitcast.3, bf16[64,4096]{1,0:T(8,128)(2,1)S(1)} %get-tuple-element.91.refs_2_), custom_call_target="tpu_custom_call" | custom-call | bytes 6000000 | tf_op jit(solution)/shard_map/backward_0/pallas_call | solution.py:205
  117.2 6.1 %collective-permute-start.28 = (f32[64,256]{1,0:T(8,128)S(1)}, f32[64,256]{1,0:T(8,128)S(1)}, u32[]{:S(2)}, u32[]{:S(2)}) collective-permute-start(f32[64,256]{1,0:T(8,128)S(1)} %add.52), channel_id=1, source_target_pairs={{0,4},{4,0},{8,12},{12,8},{16,20},{20,16},{24,28},{28,24},{32,36},... | collective-permute-start | bytes 196616 | tf_op jit(solution)/shard_map/ppermute | solution.py:24
  123.5 5.3 %collective-permute-start.27 = (bf16[64,4096]{1,0:T(8,128)(2,1)S(1)}, bf16[64,4096]{1,0:T(8,128)(2,1)S(1)}, u32[]{:S(2)}, u32[]{:S(2)}) collective-permute-start(bf16[64,4096]{1,0:T(8,128)(2,1)S(1)} %get-tuple-element.100), channel_id=1, source_target_pairs={{8,0},{252,4},{16,8},{4,12},{24,16},{12,20},{32,24},{20,28},{40,32... | collective-permute-start | bytes 1572872 | tf_op jit(solution)/shard_map/ppermute | solution.py:20
  129.1 11.5 %collective-permute-done.29 = f32[64,256]{1,0:T(8,128)S(1)} collective-permute-done((f32[64,256]{1,0:T(8,128)S(1)}, f32[64,256]{1,0:T(8,128)S(1)}, u32[]{:S(2)}, u32[]{:S(2)}) %collective-permute-start.29) | collective-permute-done | bytes 65568 | tf_op jit(solution)/shard_map/ppermute | solution.py:24
  140.7 3.8 %collective-permute-start.31 = (bf16[64,4096]{1,0:T(8,128)(2,1)S(1)}, bf16[64,4096]{1,0:T(8,128)(2,1)S(1)}, u32[]{:S(2)}, u32[]{:S(2)}) collective-permute-start(bf16[64,4096]{1,0:T(8,128)(2,1)S(1)} %add_convert_fusion.1), channel_id=1, source_target_pairs={{8,0},{252,4},{16,8},{4,12},{24,16},{12,20},{32,24},{20,28},{40,32... | collective-permute-start | bytes 1572872 | tf_op jit(solution)/shard_map/ppermute | solution.py:20
  144.7 2.9 %collective-permute-start.32 = (bf16[64,4096]{1,0:T(8,128)(2,1)S(1)}, bf16[64,4096]{1,0:T(8,128)(2,1)S(1)}, u32[]{:S(2)}, u32[]{:S(2)}) collective-permute-start(bf16[64,4096]{1,0:T(8,128)(2,1)S(1)} %add_convert_fusion.3), channel_id=1, source_target_pairs={{0,4},{4,0},{8,12},{12,8},{16,20},{20,16},{24,28},{28,24},{32,36},... | collective-permute-start | bytes 1572872 | tf_op jit(solution)/shard_map/ppermute | solution.py:24
  147.6 4.8 %collective-permute-start.33 = (f32[64,256]{1,0:T(8,128)S(1)}, f32[64,256]{1,0:T(8,128)S(1)}, u32[]{:S(2)}, u32[]{:S(2)}) collective-permute-start(f32[64,256]{1,0:T(8,128)S(1)} %add.54), channel_id=1, source_target_pairs={{0,128},{4,132},{8,136},{12,140},{16,144},{20,148},{24,152},{28,15... | collective-permute-start | bytes 196616 | tf_op jit(solution)/shard_map/ppermute | solution.py:24
  152.4 3.3 %collective-permute-done.33 = f32[64,256]{1,0:T(8,128)S(1)} collective-permute-done((f32[64,256]{1,0:T(8,128)S(1)}, f32[64,256]{1,0:T(8,128)S(1)}, u32[]{:S(2)}, u32[]{:S(2)}) %collective-permute-start.33) | collective-permute-done | bytes 65568 | tf_op jit(solution)/shard_map/ppermute | solution.py:24
  156.4 5.4 %collective-permute-done.30 = bf16[64,4096]{1,0:T(8,128)(2,1)S(1)} collective-permute-done((bf16[64,4096]{1,0:T(8,128)(2,1)S(1)}, bf16[64,4096]{1,0:T(8,128)(2,1)S(1)}, u32[]{:S(2)}, u32[]{:S(2)}) %collective-permute-start.30) | collective-permute-done | bytes 524320 | tf_op jit(solution)/shard_map/ppermute | solution.py:20
  (81 shorter events, 20.6 us)
Async XLA Ops:
  0.6 22.1 %collective-permute-start.4 = (bf16[64,4096]{1,0:T(8,128)(2,1)}, bf16[64,4096]{1,0:T(8,128)(2,1)S(1)}, u32[]{:S(2)}, u32[]{:S(2)}) collective-permute-start(bf16[64,4096]{1,0:T(8,128)(2,1)} %refs_2_.1), channel_id=1, source_target_pairs={{248,0},{12,4},{0,8},{20,12},{8,16},{28,20},{16,24},{36,28},{24,32... | collective-permute-start | bytes 1572872 | tf_op jit(solution)/shard_map/ppermute | solution.py:20
  3.4 15.3 %collective-permute-start = (bf16[32,4096]{1,0:T(8,128)(2,1)S(1)}, bf16[32,4096]{1,0:T(8,128)(2,1)S(1)}, u32[]{:S(2)}, u32[]{:S(2)}) collective-permute-start(bf16[32,4096]{1,0:T(8,128)(2,1)S(1)} %get-tuple-element.114), channel_id=1, source_target_pairs={{8,0},{252,4},{16,8},{4,12},{24,16},{12,20},{32,24},{20,28},{40,32... | collective-permute-start | bytes 786440 | tf_op jit(solution)/shard_map/ppermute | solution.py:20
  10.2 12.6 %collective-permute-start.3 = (bf16[32,4096]{1,0:T(8,128)(2,1)S(1)}, bf16[32,4096]{1,0:T(8,128)(2,1)S(1)}, u32[]{:S(2)}, u32[]{:S(2)}) collective-permute-start(bf16[32,4096]{1,0:T(8,128)(2,1)S(1)} %get-tuple-element.113), channel_id=1, source_target_pairs={{8,0},{252,4},{16,8},{4,12},{24,16},{12,20},{32,24},{20,28},{40,32... | collective-permute-start | bytes 786440 | tf_op jit(solution)/shard_map/ppermute | solution.py:20
  12.2 27.8 %collective-permute-start.2 = (bf16[64,4096]{1,0:T(8,128)(2,1)}, bf16[64,4096]{1,0:T(8,128)(2,1)S(1)}, u32[]{:S(2)}, u32[]{:S(2)}) collective-permute-start(bf16[64,4096]{1,0:T(8,128)(2,1)} %refs_2_.1), channel_id=1, source_target_pairs={{0,4},{4,0},{8,12},{12,8},{16,20},{20,16},{24,28},{28,24},{32,36},... | collective-permute-start | bytes 1572872 | tf_op jit(solution)/shard_map/ppermute | solution.py:24
  12.2 27.8 %collective-permute-start.5 = (bf16[64,4096]{1,0:T(8,128)(2,1)}, bf16[64,4096]{1,0:T(8,128)(2,1)S(1)}, u32[]{:S(2)}, u32[]{:S(2)}) collective-permute-start(bf16[64,4096]{1,0:T(8,128)(2,1)} %refs_4_), channel_id=1, source_target_pairs={{0,2},{1,3},{2,0},{3,1},{4,6},{5,7},{6,4},{7,5},{8,10},{9,11},{10,... | collective-permute-start | bytes 1572872 | tf_op jit(solution)/shard_map/ppermute | solution.py:24
  18.7 8.5 %collective-permute-start.1 = (bf16[32,4096]{1,0:T(8,128)(2,1)S(1)}, bf16[32,4096]{1,0:T(8,128)(2,1)S(1)}, u32[]{:S(2)}, u32[]{:S(2)}) collective-permute-start(bf16[32,4096]{1,0:T(8,128)(2,1)S(1)} %collective-permute-done.refs_3_), channel_id=1, source_target_pairs={{8,0},{252,4},{16,8},{4,12},{24,16},{12,20},{32,24},{20,28},{40,32... | collective-permute-start | bytes 786440 | tf_op jit(solution)/shard_map/ppermute | solution.py:20
  22.7 22.8 %collective-permute-start.13 = (bf16[64,4096]{1,0:T(8,128)(2,1)}, bf16[64,4096]{1,0:T(8,128)(2,1)S(1)}, u32[]{:S(2)}, u32[]{:S(2)}) collective-permute-start(bf16[64,4096]{1,0:T(8,128)(2,1)} %refs_4_), channel_id=1, source_target_pairs={{0,1},{1,0},{2,3},{3,2},{4,5},{5,4},{6,7},{7,6},{8,9},{9,8},{10,11... | collective-permute-start | bytes 1572872 | tf_op jit(solution)/shard_map/ppermute | solution.py:24
  22.7 29.0 %collective-permute-start.12 = (bf16[64,4096]{1,0:T(8,128)(2,1)S(1)}, bf16[64,4096]{1,0:T(8,128)(2,1)S(1)}, u32[]{:S(2)}, u32[]{:S(2)}) collective-permute-start(bf16[64,4096]{1,0:T(8,128)(2,1)S(1)} %collective-permute-done.4.refs_5_), channel_id=1, source_target_pairs={{248,0},{12,4},{0,8},{20,12},{8,16},{28,20},{16,24},{36,28},{24,32... | collective-permute-start | bytes 1572872 | tf_op jit(solution)/shard_map/ppermute | solution.py:20
  27.2 13.0 %collective-permute-start.9 = (bf16[32,4096]{1,0:T(8,128)(2,1)S(1)}, bf16[32,4096]{1,0:T(8,128)(2,1)S(1)}, u32[]{:S(2)}, u32[]{:S(2)}) collective-permute-start(bf16[32,4096]{1,0:T(8,128)(2,1)S(1)} %collective-permute-done.3.refs_4_), channel_id=1, source_target_pairs={{8,0},{252,4},{16,8},{4,12},{24,16},{12,20},{32,24},{20,28},{40,32... | collective-permute-start | bytes 786440 | tf_op jit(solution)/shard_map/ppermute | solution.py:20
  40.0 25.5 %collective-permute-start.14 = (bf16[64,4096]{1,0:T(8,128)(2,1)S(1)}, bf16[64,4096]{1,0:T(8,128)(2,1)S(1)}, u32[]{:S(2)}, u32[]{:S(2)}) collective-permute-start(bf16[64,4096]{1,0:T(8,128)(2,1)S(1)} %collective-permute-done.5.refs_6_), channel_id=1, source_target_pairs={{0,1},{1,0},{2,3},{3,2},{4,5},{5,4},{6,7},{7,6},{8,9},{9,8},{10,11... | collective-permute-start | bytes 1572872 | tf_op jit(solution)/shard_map/ppermute | solution.py:24
  40.1 25.4 %collective-permute-start.7 = (bf16[64,4096]{1,0:T(8,128)(2,1)S(1)}, bf16[64,4096]{1,0:T(8,128)(2,1)S(1)}, u32[]{:S(2)}, u32[]{:S(2)}) collective-permute-start(bf16[64,4096]{1,0:T(8,128)(2,1)S(1)} %collective-permute-done.2.refs_2_), channel_id=1, source_target_pairs={{248,0},{12,4},{0,8},{20,12},{8,16},{28,20},{16,24},{36,28},{24,32... | collective-permute-start | bytes 1572872 | tf_op jit(solution)/shard_map/ppermute | solution.py:20
  40.2 25.3 %collective-permute-start.6 = (bf16[64,4096]{1,0:T(8,128)(2,1)S(1)}, bf16[64,4096]{1,0:T(8,128)(2,1)S(1)}, u32[]{:S(2)}, u32[]{:S(2)}) collective-permute-start(bf16[64,4096]{1,0:T(8,128)(2,1)S(1)} %collective-permute-done.2.refs_2_), channel_id=1, source_target_pairs={{8,0},{252,4},{16,8},{4,12},{24,16},{12,20},{32,24},{20,28},{40,32... | collective-permute-start | bytes 1572872 | tf_op jit(solution)/shard_map/ppermute | solution.py:20
  45.5 5.4 %collective-permute-start.11 = (bf16[64,256]{1,0:T(8,128)(2,1)S(1)}, bf16[64,256]{1,0:T(8,128)(2,1)S(1)}, u32[]{:S(2)}, u32[]{:S(2)}) collective-permute-start(bf16[64,256]{1,0:T(8,128)(2,1)S(1)} %copy-done.4), channel_id=1, source_target_pairs={{0,2},{1,3},{2,0},{3,1},{4,6},{5,7},{6,4},{7,5},{8,10},{9,11},{10,... | collective-permute-start | bytes 98312 | tf_op jit(solution)/shard_map/ppermute | solution.py:24
  51.0 9.2 %collective-permute-start.10 = (bf16[32,4096]{1,0:T(8,128)(2,1)S(1)}, bf16[32,4096]{1,0:T(8,128)(2,1)S(1)}, u32[]{:S(2)}, u32[]{:S(2)}) collective-permute-start(bf16[32,4096]{1,0:T(8,128)(2,1)S(1)} %collective-permute-done.9.refs_4_), channel_id=1, source_target_pairs={{0,4},{4,0},{8,12},{12,8},{16,20},{20,16},{24,28},{28,24},{32,36},... | collective-permute-start | bytes 786440 | tf_op jit(solution)/shard_map/ppermute | solution.py:24
  51.8 12.1 %collective-permute-start.8 = (bf16[32,4096]{1,0:T(8,128)(2,1)S(1)}, bf16[32,4096]{1,0:T(8,128)(2,1)S(1)}, u32[]{:S(2)}, u32[]{:S(2)}) collective-permute-start(bf16[32,4096]{1,0:T(8,128)(2,1)S(1)} %collective-permute-done.1.refs_3_), channel_id=1, source_target_pairs={{0,4},{4,0},{8,12},{12,8},{16,20},{20,16},{24,28},{28,24},{32,36},... | collective-permute-start | bytes 786440 | tf_op jit(solution)/shard_map/ppermute | solution.py:24
  60.2 5.3 %collective-permute-start.15 = (bf16[64,256]{1,0:T(8,128)(2,1)S(1)}, bf16[64,256]{1,0:T(8,128)(2,1)S(1)}, u32[]{:S(2)}, u32[]{:S(2)}) collective-permute-start(bf16[64,256]{1,0:T(8,128)(2,1)S(1)} %copy-done.4), channel_id=1, source_target_pairs={{0,1},{1,0},{2,3},{3,2},{4,5},{5,4},{6,7},{7,6},{8,9},{9,8},{10,11... | collective-permute-start | bytes 98312 | tf_op jit(solution)/shard_map/ppermute | solution.py:24
  67.3 15.9 %collective-permute-start.18 = (bf16[64,4096]{1,0:T(8,128)(2,1)S(1)}, bf16[64,4096]{1,0:T(8,128)(2,1)S(1)}, u32[]{:S(2)}, u32[]{:S(2)}) collective-permute-start(bf16[64,4096]{1,0:T(8,128)(2,1)S(1)} %forward_2.1.refs_0_), channel_id=1, source_target_pairs={{0,2},{1,3},{2,0},{3,1},{4,6},{5,7},{6,4},{7,5},{8,10},{9,11},{10,... | collective-permute-start | bytes 1572872 | tf_op jit(solution)/shard_map/ppermute | solution.py:24
  70.2 13.1 %collective-permute-start.17 = (bf16[64,4096]{1,0:T(8,128)(2,1)S(1)}, bf16[64,4096]{1,0:T(8,128)(2,1)}, u32[]{:S(2)}, u32[]{:S(2)}) collective-permute-start(bf16[64,4096]{1,0:T(8,128)(2,1)S(1)} %forward_2.1.refs_0_), channel_id=1, source_target_pairs={{0,1},{1,0},{2,3},{3,2},{4,5},{5,4},{6,7},{7,6},{8,9},{9,8},{10,11... | collective-permute-start | bytes 1572872 | tf_op jit(solution)/shard_map/ppermute | solution.py:24
  90.1 7.1 %collective-permute-start.21 = (f32[64,256]{1,0:T(8,128)S(1)}, f32[64,256]{1,0:T(8,128)S(1)}, u32[]{:S(2)}, u32[]{:S(2)}) collective-permute-start(f32[64,256]{1,0:T(8,128)S(1)} %get-tuple-element.83), channel_id=1, source_target_pairs={{0,8},{4,12},{8,0},{12,4},{16,24},{20,28},{24,16},{28,20},{32,40},... | collective-permute-start | bytes 196616 | tf_op jit(solution)/shard_map/ppermute | solution.py:24
  95.3 21.4 %collective-permute-start.20 = (bf16[64,4096]{1,0:T(8,128)(2,1)S(1)}, bf16[64,4096]{1,0:T(8,128)(2,1)S(1)}, u32[]{:S(2)}, u32[]{:S(2)}) collective-permute-start(bf16[64,4096]{1,0:T(8,128)(2,1)S(1)} %backward_3.1), channel_id=1, source_target_pairs={{0,4},{4,0},{8,12},{12,8},{16,20},{20,16},{24,28},{28,24},{32,36},... | collective-permute-start | bytes 1572872 | tf_op jit(solution)/shard_map/ppermute | solution.py:24
  97.2 20.0 %collective-permute-start.22 = (bf16[64,4096]{1,0:T(8,128)(2,1)S(1)}, bf16[64,4096]{1,0:T(8,128)(2,1)S(1)}, u32[]{:S(2)}, u32[]{:S(2)}) collective-permute-start(bf16[64,4096]{1,0:T(8,128)(2,1)S(1)} %get-tuple-element.84), channel_id=1, source_target_pairs={{248,0},{12,4},{0,8},{20,12},{8,16},{28,20},{16,24},{36,28},{24,32... | collective-permute-start | bytes 1572872 | tf_op jit(solution)/shard_map/ppermute | solution.py:20
  100.0 17.1 %collective-permute-start.23 = (bf16[64,4096]{1,0:T(8,128)(2,1)S(1)}, bf16[64,4096]{1,0:T(8,128)(2,1)S(1)}, u32[]{:S(2)}, u32[]{:S(2)}) collective-permute-start(bf16[64,4096]{1,0:T(8,128)(2,1)S(1)} %get-tuple-element.85), channel_id=1, source_target_pairs={{8,0},{252,4},{16,8},{4,12},{24,16},{12,20},{32,24},{20,28},{40,32... | collective-permute-start | bytes 1572872 | tf_op jit(solution)/shard_map/ppermute | solution.py:20
  103.9 8.4 %collective-permute-start.24 = (f32[64,256]{1,0:T(8,128)S(1)}, f32[64,256]{1,0:T(8,128)S(1)}, u32[]{:S(2)}, u32[]{:S(2)}) collective-permute-start(f32[64,256]{1,0:T(8,128)S(1)} %add.47), channel_id=1, source_target_pairs={{0,16},{4,20},{8,24},{12,28},{16,0},{20,4},{24,8},{28,12},{32,48},... | collective-permute-start | bytes 196616 | tf_op jit(solution)/shard_map/ppermute | solution.py:24
  112.4 4.4 %collective-permute-start.25 = (f32[64,256]{1,0:T(8,128)S(1)}, f32[64,256]{1,0:T(8,128)S(1)}, u32[]{:S(2)}, u32[]{:S(2)}) collective-permute-start(f32[64,256]{1,0:T(8,128)S(1)} %add.48), channel_id=1, source_target_pairs={{0,32},{4,36},{8,40},{12,44},{16,48},{20,52},{24,56},{28,60},{32,0... | collective-permute-start | bytes 196616 | tf_op jit(solution)/shard_map/ppermute | solution.py:24
  117.2 11.6 %collective-permute-start.28 = (f32[64,256]{1,0:T(8,128)S(1)}, f32[64,256]{1,0:T(8,128)S(1)}, u32[]{:S(2)}, u32[]{:S(2)}) collective-permute-start(f32[64,256]{1,0:T(8,128)S(1)} %add.52), channel_id=1, source_target_pairs={{0,4},{4,0},{8,12},{12,8},{16,20},{20,16},{24,28},{28,24},{32,36},... | collective-permute-start | bytes 196616 | tf_op jit(solution)/shard_map/ppermute | solution.py:24
  123.4 17.2 %collective-permute-start.26 = (bf16[64,4096]{1,0:T(8,128)(2,1)S(1)}, bf16[64,4096]{1,0:T(8,128)(2,1)S(1)}, u32[]{:S(2)}, u32[]{:S(2)}) collective-permute-start(bf16[64,4096]{1,0:T(8,128)(2,1)S(1)} %add_convert_fusion.4), channel_id=1, source_target_pairs={{248,0},{12,4},{0,8},{20,12},{8,16},{28,20},{16,24},{36,28},{24,32... | collective-permute-start | bytes 1572872 | tf_op jit(solution)/shard_map/ppermute | solution.py:20
  123.5 17.2 %collective-permute-start.27 = (bf16[64,4096]{1,0:T(8,128)(2,1)S(1)}, bf16[64,4096]{1,0:T(8,128)(2,1)S(1)}, u32[]{:S(2)}, u32[]{:S(2)}) collective-permute-start(bf16[64,4096]{1,0:T(8,128)(2,1)S(1)} %get-tuple-element.100), channel_id=1, source_target_pairs={{8,0},{252,4},{16,8},{4,12},{24,16},{12,20},{32,24},{20,28},{40,32... | collective-permute-start | bytes 1572872 | tf_op jit(solution)/shard_map/ppermute | solution.py:20
  128.8 11.8 %collective-permute-start.29 = (f32[64,256]{1,0:T(8,128)S(1)}, f32[64,256]{1,0:T(8,128)S(1)}, u32[]{:S(2)}, u32[]{:S(2)}) collective-permute-start(f32[64,256]{1,0:T(8,128)S(1)} %add.53), channel_id=1, source_target_pairs={{0,64},{4,68},{8,72},{12,76},{16,80},{20,84},{24,88},{28,92},{32,9... | collective-permute-start | bytes 196616 | tf_op jit(solution)/shard_map/ppermute | solution.py:24
  140.7 15.7 %collective-permute-start.31 = (bf16[64,4096]{1,0:T(8,128)(2,1)S(1)}, bf16[64,4096]{1,0:T(8,128)(2,1)S(1)}, u32[]{:S(2)}, u32[]{:S(2)}) collective-permute-start(bf16[64,4096]{1,0:T(8,128)(2,1)S(1)} %add_convert_fusion.1), channel_id=1, source_target_pairs={{8,0},{252,4},{16,8},{4,12},{24,16},{12,20},{32,24},{20,28},{40,32... | collective-permute-start | bytes 1572872 | tf_op jit(solution)/shard_map/ppermute | solution.py:20
  144.6 17.2 %collective-permute-start.30 = (bf16[64,4096]{1,0:T(8,128)(2,1)S(1)}, bf16[64,4096]{1,0:T(8,128)(2,1)S(1)}, u32[]{:S(2)}, u32[]{:S(2)}) collective-permute-start(bf16[64,4096]{1,0:T(8,128)(2,1)S(1)} %add_convert_fusion.2), channel_id=1, source_target_pairs={{248,0},{12,4},{0,8},{20,12},{8,16},{28,20},{16,24},{36,28},{24,32... | collective-permute-start | bytes 1572872 | tf_op jit(solution)/shard_map/ppermute | solution.py:20
  144.7 17.1 %collective-permute-start.32 = (bf16[64,4096]{1,0:T(8,128)(2,1)S(1)}, bf16[64,4096]{1,0:T(8,128)(2,1)S(1)}, u32[]{:S(2)}, u32[]{:S(2)}) collective-permute-start(bf16[64,4096]{1,0:T(8,128)(2,1)S(1)} %add_convert_fusion.3), channel_id=1, source_target_pairs={{0,4},{4,0},{8,12},{12,8},{16,20},{20,16},{24,28},{28,24},{32,36},... | collective-permute-start | bytes 1572872 | tf_op jit(solution)/shard_map/ppermute | solution.py:24
  147.6 8.2 %collective-permute-start.33 = (f32[64,256]{1,0:T(8,128)S(1)}, f32[64,256]{1,0:T(8,128)S(1)}, u32[]{:S(2)}, u32[]{:S(2)}) collective-permute-start(f32[64,256]{1,0:T(8,128)S(1)} %add.54), channel_id=1, source_target_pairs={{0,128},{4,132},{8,136},{12,140},{16,144},{20,148},{24,152},{28,15... | collective-permute-start | bytes 196616 | tf_op jit(solution)/shard_map/ppermute | solution.py:24
  (13 other events, 118.3 us)

commit v5 on v3

--- a/solution.py
+++ b/solution.py
@@ -271,11 +271,11 @@
     x, u, v, listed, own = fenced(x, u, v, listed, own)
     m, n, far = stepped(u, True), stepped(v, False), flipped(own, "feat", 2)
     y = forward(0, listed, tile_vals, [x_t, x, u, v], None, f32)
-    m, n, y, x = fenced(m, n, y, x)
+    m, n, y, x, far, own = fenced(m, n, y, x, far, own)
     mx, xu, xv = flipped(m, "blk", 1), stepped(x, True), stepped(x, False)
     y = forward(1, listed, tile_vals, [m, n], y, f32)
-    xu, xv, mx, y, far, own = fenced(xu, xv, mx, y, far, own)
     packed = [own, flipped(own, "feat", 1), far, flipped(far, "feat", 1)]
+    xu, xv, mx, y, packed = fenced(xu, xv, mx, y, packed)
     y = forward(2, listed, tile_vals, [xu, xv, mx], y, bf16)
     y_far = flipped(y, "feat", 2)
     ys = [y, flipped(y, "feat", 1), y_far, flipped(y_far, "feat", 1)]
@@ -299,10 +299,10 @@
     from_n = stepped(to_n, True)
     to_x = (to_x + from_xu.astype(f32) + from_xv.astype(f32)).astype(bf16)
     wgrad = wgrad + part
-    wgrad = wgrad + flipped(wgrad, "blk", 32)
     wgrad = wgrad + flipped(wgrad, "blk", 1)
+    wgrad = wgrad + flipped(wgrad, "blk", 4)
     from_m, from_n, to_x, to_u, to_v, wgrad = fenced(from_m, from_n, to_x, to_u, to_v, wgrad)
-    part = flipped(wgrad, "blk", 4)
+    part = flipped(wgrad, "blk", 32)
     from_u = stepped((to_u + from_m.astype(f32)).astype(bf16), False)
     from_v = stepped((to_v + from_n.astype(f32)).astype(bf16), True)
     from_x = flipped(to_x, "blk", 1)

time: 142 us -> 149 us (1.049); the launches traced: 144 us -> 149 us
  waiting for transfers between devices: 55.2 us -> 58.6 us
    ppermute x16, waiting for transfers between devices: 29.8 us -> 32.8 us  [flipped(): lax.ppermute(block, axis, [(i, i ^ bit) for i in range(lax.axis_size(axis...]
  transfers between devices with their start and end apart: 28 -> 28, of which waited for: 15 -> 16; matrix products, arithmetic and copies ran while one was open for 3% -> 3% of each run, Pallas kernels for 17% -> 16%
where the time goes in v5:
time: 149 us
  waiting for transfers between devices  58.6 us (39%)
  starting transfers between devices  46 us (31%)
  Pallas kernels  31.7 us (21%)
  local copies, waits for them, and re-layouts  6.62 us (4%)
  other arithmetic  4.14 us (3%)
  between operations  1.52 us (1%)
    ppermute x16, waiting for transfers between devices, flipped(): lax.ppermute(block, axis, [(i, i ^ bit) for i in range(lax.axis_size(axis...  32.8 us
    ppermute x12, starting transfers between devices, stepped(): return lax.ppermute(block, 'blk', route)  31.7 us
    ppermute x12, waiting for transfers between devices, stepped(): return lax.ppermute(block, 'blk', route)  25.8 us
    ppermute x16, starting transfers between devices, flipped(): lax.ppermute(block, axis, [(i, i ^ bit) for i in range(lax.axis_size(axis...  14.2 us
    pallas_call x3, Pallas kernels, backward(): pl.pallas_call(functools.partial(backward_body, wave), out_shape=tuple((p...  11.7 us
    pallas_call x3, Pallas kernels, forward(): pl.pallas_call(functools.partial(forward_body, wave, seed is not None), o...  11.5 us
    unnamed x16, local copies, waits for them, and re-layouts  5.74 us
    pallas_call x1, Pallas kernels, plan(): pl.pallas_call(functools.partial(plan_body, cap), out_shape=jax.ShapeDtyp...  5.11 us
  transfers between devices with their start and end apart: 28, of which 16 were waited for; matrix products, arithmetic and copies ran while one was open for 3% of the time, Pallas kernels for 16%

profile of v5, /device:TPU:4, one launch (start us, length us, event | category | flops | bytes accessed | tf_op | source)
XLA Modules:
  0.0 148.6 jit_solution(13045606936319994061)
XLA Ops:
  0.6 8.4 %collective-permute-start.1 = (bf16[64,4096]{1,0:T(8,128)(2,1)}, bf16[64,4096]{1,0:T(8,128)(2,1)S(1)}, u32[]{:S(2)}, u32[]{:S(2)}) collective-permute-start(bf16[64,4096]{1,0:T(8,128)(2,1)} %refs_2_.1), channel_id=1, source_target_pairs={{8,0},{252,4},{16,8},{4,12},{24,16},{12,20},{32,24},{20,28},{40,32... | collective-permute-start | bytes 1572872 | tf_op jit(solution)/shard_map/ppermute | solution.py:20
  13.5 5.1 %plan.1.refs_0_ = s32[904]{0:T(1024)S(1)} custom-call(s32[288]{0:T(512)S(1)} %copy-done.2, s32[288]{0:T(512)S(1)} %copy-done.3, s32[288]{0:T(512)S(1)} %copy-done.4, s32[1]{0:T(128)S(6)} %copy.11.count_ref, s32[1]{0:T(128)} %bitcast.1.sign_ref), custom_call_target="tpu_custom_call" | custom-call | bytes 6000000 | tf_op jit(solution)/shard_map/plan/pallas_call | solution.py:81
  20.5 2.1 %collective-permute-done.refs_3_ = bf16[64,4096]{1,0:T(8,128)(2,1)S(1)} collective-permute-done((bf16[64,4096]{1,0:T(8,128)(2,1)}, bf16[64,4096]{1,0:T(8,128)(2,1)S(1)}, u32[]{:S(2)}, u32[]{:S(2)}) %collective-permute-start) | collective-permute-done | bytes 524320 | tf_op jit(solution)/shard_map/ppermute | solution.py:24
  22.6 3.3 %collective-permute-done.2.refs_5_ = bf16[64,4096]{1,0:T(8,128)(2,1)S(1)} collective-permute-done((bf16[64,4096]{1,0:T(8,128)(2,1)}, bf16[64,4096]{1,0:T(8,128)(2,1)S(1)}, u32[]{:S(2)}, u32[]{:S(2)}) %collective-permute-start.2) | collective-permute-done | bytes 524320 | tf_op jit(solution)/shard_map/ppermute | solution.py:20
  26.7 1.7 %collective-permute-start.4 = (bf16[64,4096]{1,0:T(8,128)(2,1)S(1)}, bf16[64,4096]{1,0:T(8,128)(2,1)S(1)}, u32[]{:S(2)}, u32[]{:S(2)}) collective-permute-start(bf16[64,4096]{1,0:T(8,128)(2,1)S(1)} %collective-permute-done.2.refs_5_), channel_id=1, source_target_pairs={{248,0},{12,4},{0,8},{20,12},{8,16},{28,20},{16,24},{36,28},{24,32... | collective-permute-start | bytes 1572872 | tf_op jit(solution)/shard_map/ppermute | solution.py:20
  28.5 3.7 %copy-done = bf16[288,128,128]{2,1,0:T(8,128)(2,1)S(1)} copy-done((bf16[288,128,128]{2,1,0:T(8,128)(2,1)S(1)}, bf16[288,128,128]{2,1,0:T(8,128)(2,1)}, u32[]{:S(2)}) %copy-start) | copy-done | bytes 9437208
  32.2 4.7 %forward_0.1.refs_4_ = f32[64,4096]{1,0:T(8,128)S(1)} custom-call(s32[904]{0:T(1024)S(1)} %plan.1.refs_0_, bf16[288,128,128]{2,1,0:T(8,128)(2,1)S(1)} %copy-done, bf16[64,4096]{1,0:T(8,128)(2,1)S(1)} %copy-done.1, bf16[64,4096]{1,0:T(8,128)(2,1)S(1)} %collective-permute-done.refs_3_, bf16[64,4096]{1,0:T(8,128)(2,1)S(1)} %collective-permute-done.1.refs_4_, ...), custom_call_target="tpu_custom_call" | custom-call | bytes 6000000 | tf_op jit(solution)/shard_map/forward_0/pallas_call | solution.py:154
  36.9 1.7 %collective-permute-done.3.refs_2_ = bf16[64,4096]{1,0:T(8,128)(2,1)S(1)} collective-permute-done((bf16[64,4096]{1,0:T(8,128)(2,1)S(1)}, bf16[64,4096]{1,0:T(8,128)(2,1)S(1)}, u32[]{:S(2)}, u32[]{:S(2)}) %collective-permute-start.3) | collective-permute-done | bytes 524320 | tf_op jit(solution)/shard_map/ppermute | solution.py:20
  38.6 3.6 %collective-permute-done.4.refs_3_ = bf16[64,4096]{1,0:T(8,128)(2,1)S(1)} collective-permute-done((bf16[64,4096]{1,0:T(8,128)(2,1)S(1)}, bf16[64,4096]{1,0:T(8,128)(2,1)S(1)}, u32[]{:S(2)}, u32[]{:S(2)}) %collective-permute-start.4) | collective-permute-done | bytes 524320 | tf_op jit(solution)/shard_map/ppermute | solution.py:20
  42.8 5.3 %collective-permute-start.6 = (bf16[64,4096]{1,0:T(8,128)(2,1)S(1)}, bf16[64,4096]{1,0:T(8,128)(2,1)S(1)}, u32[]{:S(2)}, u32[]{:S(2)}) collective-permute-start(bf16[64,4096]{1,0:T(8,128)(2,1)S(1)} %collective-permute-done.refs_3_), channel_id=1, source_target_pairs={{8,0},{252,4},{16,8},{4,12},{24,16},{12,20},{32,24},{20,28},{40,32... | collective-permute-start | bytes 1572872 | tf_op jit(solution)/shard_map/ppermute | solution.py:20
  48.2 3.0 %forward_1.1.refs_5_ = f32[64,4096]{1,0:T(8,128)S(1)} custom-call(s32[904]{0:T(1024)S(1)} %plan.1.refs_0_, bf16[288,128,128]{2,1,0:T(8,128)(2,1)S(1)} %copy-done, bf16[64,4096]{1,0:T(8,128)(2,1)S(1)} %collective-permute-done.3.refs_2_, bf16[64,4096]{1,0:T(8,128)(2,1)S(1)} %collective-permute-done.4.refs_3_, f32[64,4096]{1,0:T(8,128)S(1)} %forward_0.1.refs_4_), custom_call_target="tpu_custom_call" | custom-call | bytes 6000000 | tf_op jit(solution)/shard_map/forward_1/pallas_call | solution.py:154
  51.2 8.8 %collective-permute-done.7.refs_3_ = bf16[64,4096]{1,0:T(8,128)(2,1)S(1)} collective-permute-done((bf16[64,4096]{1,0:T(8,128)(2,1)S(1)}, bf16[64,4096]{1,0:T(8,128)(2,1)S(1)}, u32[]{:S(2)}, u32[]{:S(2)}) %collective-permute-start.7) | collective-permute-done | bytes 524320 | tf_op jit(solution)/shard_map/ppermute | solution.py:20
  60.0 1.5 collective-permute-done.8.refs_4_
  61.4 3.8 %forward_2.1.refs_0_ = bf16[64,4096]{1,0:T(8,128)(2,1)S(1)} custom-call(s32[904]{0:T(1024)S(1)} %plan.1.refs_0_, bf16[288,128,128]{2,1,0:T(8,128)(2,1)S(1)} %copy-done, bf16[64,4096]{1,0:T(8,128)(2,1)S(1)} %collective-permute-done.6.refs_2_, bf16[64,4096]{1,0:T(8,128)(2,1)S(1)} %collective-permute-done.7.refs_3_, ...), custom_call_target="tpu_custom_call" | custom-call | bytes 6000000 | tf_op jit(solution)/shard_map/forward_2/pallas_call | solution.py:154
  65.2 3.1 %collective-permute-start.12 = (bf16[64,4096]{1,0:T(8,128)(2,1)S(1)}, bf16[64,4096]{1,0:T(8,128)(2,1)S(1)}, u32[]{:S(2)}, u32[]{:S(2)}) collective-permute-start(bf16[64,4096]{1,0:T(8,128)(2,1)S(1)} %forward_2.1.refs_0_), channel_id=1, source_target_pairs={{0,2},{1,3},{2,0},{3,1},{4,6},{5,7},{6,4},{7,5},{8,10},{9,11},{10,... | collective-permute-start | bytes 1572872 | tf_op jit(solution)/shard_map/ppermute | solution.py:24
  68.3 10.8 %collective-permute-done.12.refs_2_ = bf16[64,4096]{1,0:T(8,128)(2,1)S(1)} collective-permute-done((bf16[64,4096]{1,0:T(8,128)(2,1)S(1)}, bf16[64,4096]{1,0:T(8,128)(2,1)S(1)}, u32[]{:S(2)}, u32[]{:S(2)}) %collective-permute-start.12) | collective-permute-done | bytes 524320 | tf_op jit(solution)/shard_map/ppermute | solution.py:24
  79.2 1.9 %collective-permute-done.13.refs_3_ = bf16[64,4096]{1,0:T(8,128)(2,1)S(1)} collective-permute-done((bf16[64,4096]{1,0:T(8,128)(2,1)S(1)}, bf16[64,4096]{1,0:T(8,128)(2,1)S(1)}, u32[]{:S(2)}, u32[]{:S(2)}) %collective-permute-start.13) | collective-permute-done | bytes 524320 | tf_op jit(solution)/shard_map/ppermute | solution.py:24
  81.1 3.4 %middle.1 = (bf16[64,4096]{1,0:T(8,128)(2,1)}, bf16[64,4096]{1,0:T(8,128)(2,1)S(1)}, f32[64,256]{1,0:T(8,128)S(1)}) custom-call(s32[1]{0:T(128)} %bitcast.place_ref, bf16[64,4096]{1,0:T(8,128)(2,1)S(1)} %forward_2.1.refs_0_, bf16[64,4096]{1,0:T(8,128)(2,1)S(1)} %collective-permute-done.11.refs_1_, bf16[64,4096]{1,0:T(8,128)(2,1)S(1)} %collective-permute-done.12.refs_2_, ...), custom_call_target="tpu_custom_call" | custom-call | bytes 6000000 | tf_op jit(solution)/shard_map/middle/pallas_call | solution.py:243
  84.5 3.8 %backward_2.1 = (bf16[64,4096]{1,0:T(8,128)(2,1)S(1)}, bf16[64,4096]{1,0:T(8,128)(2,1)S(1)}, bf16[64,4096]{1,0:T(8,128)(2,1)S(1)}) custom-call(s32[904]{0:T(1024)S(1)} %plan.1.refs_0_, bf16[288,128,128]{2,1,0:T(8,128)(2,1)S(1)} %bitcast.3, bf16[64,4096]{1,0:T(8,128)(2,1)S(1)} %get-tuple-element.91.refs_2_), custom_call_target="tpu_custom_call" | custom-call | bytes 6000000 | tf_op jit(solution)/shard_map/backward_2/pallas_call | solution.py:195
  88.7 2.3 %collective-permute-start.15 = (bf16[64,4096]{1,0:T(8,128)(2,1)S(1)}, bf16[64,4096]{1,0:T(8,128)(2,1)S(1)}, u32[]{:S(2)}, u32[]{:S(2)}) collective-permute-start(bf16[64,4096]{1,0:T(8,128)(2,1)S(1)} %get-tuple-element.83), channel_id=1, source_target_pairs={{0,4},{4,0},{8,12},{12,8},{16,20},{20,16},{24,28},{28,24},{32,36},... | collective-permute-start | bytes 1572872 | tf_op jit(solution)/shard_map/ppermute | solution.py:24
  91.0 1.4 collective-permute-start.16
  92.5 3.9 %collective-permute-start.17 = (bf16[64,4096]{1,0:T(8,128)(2,1)S(1)}, bf16[64,4096]{1,0:T(8,128)(2,1)S(1)}, u32[]{:S(2)}, u32[]{:S(2)}) collective-permute-start(bf16[64,4096]{1,0:T(8,128)(2,1)S(1)} %get-tuple-element.85), channel_id=1, source_target_pairs={{8,0},{252,4},{16,8},{4,12},{24,16},{12,20},{32,24},{20,28},{40,32... | collective-permute-start | bytes 1572872 | tf_op jit(solution)/shard_map/ppermute | solution.py:20
  96.5 3.0 %backward_1.1 = (f32[64,4096]{1,0:T(8,128)S(1)}, bf16[64,4096]{1,0:T(8,128)(2,1)S(1)}) custom-call(s32[904]{0:T(1024)S(1)} %plan.1.refs_0_, bf16[288,128,128]{2,1,0:T(8,128)(2,1)S(1)} %bitcast.3, bf16[64,4096]{1,0:T(8,128)(2,1)S(1)} %get-tuple-element.91.refs_2_), custom_call_target="tpu_custom_call" | custom-call | bytes 6000000 | tf_op jit(solution)/shard_map/backward_1/pallas_call | solution.py:195
  101.5 4.9 %backward_0.1 = (f32[64,4096]{1,0:T(8,128)S(1)}, f32[64,4096]{1,0:T(8,128)S(1)}, f32[64,4096]{1,0:T(8,128)S(1)}, f32[64,4096]{1,0:T(8,128)S(1)}) custom-call(s32[904]{0:T(1024)S(1)} %plan.1.refs_0_, bf16[288,128,128]{2,1,0:T(8,128)(2,1)S(1)} %bitcast.3, bf16[64,4096]{1,0:T(8,128)(2,1)S(1)} %get-tuple-element.91.refs_2_), custom_call_target="tpu_custom_call" | custom-call | bytes 6000000 | tf_op jit(solution)/shard_map/backward_0/pallas_call | solution.py:195
  106.4 1.5 %collective-permute-done.16 = bf16[64,4096]{1,0:T(8,128)(2,1)S(1)} collective-permute-done((bf16[64,4096]{1,0:T(8,128)(2,1)S(1)}, bf16[64,4096]{1,0:T(8,128)(2,1)S(1)}, u32[]{:S(2)}, u32[]{:S(2)}) %collective-permute-start.16) | collective-permute-done | bytes 524320 | tf_op jit(solution)/shard_map/ppermute | solution.py:20
  109.0 5.3 %collective-permute-start.21 = (bf16[64,4096]{1,0:T(8,128)(2,1)S(1)}, bf16[64,4096]{1,0:T(8,128)(2,1)S(1)}, u32[]{:S(2)}, u32[]{:S(2)}) collective-permute-start(bf16[64,4096]{1,0:T(8,128)(2,1)S(1)} %get-tuple-element.100), channel_id=1, source_target_pairs={{8,0},{252,4},{16,8},{4,12},{24,16},{12,20},{32,24},{20,28},{40,32... | collective-permute-start | bytes 1572872 | tf_op jit(solution)/shard_map/ppermute | solution.py:20
  114.7 6.7 %collective-permute-done.23 = f32[64,256]{1,0:T(8,128)S(1)} collective-permute-done((f32[64,256]{1,0:T(8,128)S(1)}, f32[64,256]{1,0:T(8,128)S(1)}, u32[]{:S(2)}, u32[]{:S(2)}) %collective-permute-start.23) | collective-permute-done | bytes 65568 | tf_op jit(solution)/shard_map/ppermute | solution.py:24
  121.4 4.3 %collective-permute-done.20 = bf16[64,4096]{1,0:T(8,128)(2,1)S(1)} collective-permute-done((bf16[64,4096]{1,0:T(8,128)(2,1)S(1)}, bf16[64,4096]{1,0:T(8,128)(2,1)S(1)}, u32[]{:S(2)}, u32[]{:S(2)}) %collective-permute-start.20) | collective-permute-done | bytes 524320 | tf_op jit(solution)/shard_map/ppermute | solution.py:20
  125.7 5.1 %collective-permute-start.25 = (bf16[64,4096]{1,0:T(8,128)(2,1)S(1)}, bf16[64,4096]{1,0:T(8,128)(2,1)S(1)}, u32[]{:S(2)}, u32[]{:S(2)}) collective-permute-start(bf16[64,4096]{1,0:T(8,128)(2,1)S(1)} %add_convert_fusion.1), channel_id=1, source_target_pairs={{8,0},{252,4},{16,8},{4,12},{24,16},{12,20},{32,24},{20,28},{40,32... | collective-permute-start | bytes 1572872 | tf_op jit(solution)/shard_map/ppermute | solution.py:20
  131.1 5.9 %collective-permute-start.26 = (bf16[64,4096]{1,0:T(8,128)(2,1)S(1)}, bf16[64,4096]{1,0:T(8,128)(2,1)S(1)}, u32[]{:S(2)}, u32[]{:S(2)}) collective-permute-start(bf16[64,4096]{1,0:T(8,128)(2,1)S(1)} %add_convert_fusion.3), channel_id=1, source_target_pairs={{0,4},{4,0},{8,12},{12,8},{16,20},{20,16},{24,28},{28,24},{32,36},... | collective-permute-start | bytes 1572872 | tf_op jit(solution)/shard_map/ppermute | solution.py:24
  137.0 8.2 %collective-permute-done.27 = f32[64,256]{1,0:T(8,128)S(1)} collective-permute-done((f32[64,256]{1,0:T(8,128)S(1)}, f32[64,256]{1,0:T(8,128)S(1)}, u32[]{:S(2)}, u32[]{:S(2)}) %collective-permute-start.27) | collective-permute-done | bytes 65568 | tf_op jit(solution)/shard_map/ppermute | solution.py:24
  145.8 1.7 %collective-permute-done.24 = bf16[64,4096]{1,0:T(8,128)(2,1)S(1)} collective-permute-done((bf16[64,4096]{1,0:T(8,128)(2,1)S(1)}, bf16[64,4096]{1,0:T(8,128)(2,1)S(1)}, u32[]{:S(2)}, u32[]{:S(2)}) %collective-permute-start.24) | collective-permute-done | bytes 524320 | tf_op jit(solution)/shard_map/ppermute | solution.py:20
  (65 shorter events, 13.0 us)
Async XLA Ops:
  0.6 27.8 %copy-start.1 = (bf16[64,4096]{1,0:T(8,128)(2,1)S(1)}, bf16[64,4096]{1,0:T(8,128)(2,1)}, u32[]{:S(2)}) copy-start(bf16[64,4096]{1,0:T(8,128)(2,1)} %refs_2_.1) | copy-start | bytes 1572868
  0.6 19.9 %collective-permute-start.1 = (bf16[64,4096]{1,0:T(8,128)(2,1)}, bf16[64,4096]{1,0:T(8,128)(2,1)S(1)}, u32[]{:S(2)}, u32[]{:S(2)}) collective-permute-start(bf16[64,4096]{1,0:T(8,128)(2,1)} %refs_2_.1), channel_id=1, source_target_pairs={{8,0},{252,4},{16,8},{4,12},{24,16},{12,20},{32,24},{20,28},{40,32... | collective-permute-start | bytes 1572872 | tf_op jit(solution)/shard_map/ppermute | solution.py:20
  9.0 13.6 %collective-permute-start = (bf16[64,4096]{1,0:T(8,128)(2,1)}, bf16[64,4096]{1,0:T(8,128)(2,1)S(1)}, u32[]{:S(2)}, u32[]{:S(2)}) collective-permute-start(bf16[64,4096]{1,0:T(8,128)(2,1)} %refs_2_.1), channel_id=1, source_target_pairs={{0,4},{4,0},{8,12},{12,8},{16,20},{20,16},{24,28},{28,24},{32,36},... | collective-permute-start | bytes 1572872 | tf_op jit(solution)/shard_map/ppermute | solution.py:24
  9.0 16.9 %collective-permute-start.2 = (bf16[64,4096]{1,0:T(8,128)(2,1)}, bf16[64,4096]{1,0:T(8,128)(2,1)S(1)}, u32[]{:S(2)}, u32[]{:S(2)}) collective-permute-start(bf16[64,4096]{1,0:T(8,128)(2,1)} %refs_2_.1), channel_id=1, source_target_pairs={{248,0},{12,4},{0,8},{20,12},{8,16},{28,20},{16,24},{36,28},{24,32... | collective-permute-start | bytes 1572872 | tf_op jit(solution)/shard_map/ppermute | solution.py:20
  25.9 16.3 %collective-permute-start.5 = (bf16[64,4352]{1,0:T(8,128)(2,1)S(1)}, bf16[64,4352]{1,0:T(8,128)(2,1)S(1)}, u32[]{:S(2)}, u32[]{:S(2)}) collective-permute-start(bf16[64,4352]{1,0:T(8,128)(2,1)S(1)} %pad_maximum_fusion.refs_4_), channel_id=1, source_target_pairs={{0,2},{1,3},{2,0},{3,1},{4,6},{5,7},{6,4},{7,5},{8,10},{9,11},{10,... | collective-permute-start | bytes 1671176 | tf_op jit(solution)/shard_map/ppermute | solution.py:24
  26.4 12.2 %collective-permute-start.3 = (bf16[64,4096]{1,0:T(8,128)(2,1)S(1)}, bf16[64,4096]{1,0:T(8,128)(2,1)S(1)}, u32[]{:S(2)}, u32[]{:S(2)}) collective-permute-start(bf16[64,4096]{1,0:T(8,128)(2,1)S(1)} %collective-permute-done.1.refs_4_), channel_id=1, source_target_pairs={{8,0},{252,4},{16,8},{4,12},{24,16},{12,20},{32,24},{20,28},{40,32... | collective-permute-start | bytes 1572872 | tf_op jit(solution)/shard_map/ppermute | solution.py:20
  26.7 15.6 %collective-permute-start.4 = (bf16[64,4096]{1,0:T(8,128)(2,1)S(1)}, bf16[64,4096]{1,0:T(8,128)(2,1)S(1)}, u32[]{:S(2)}, u32[]{:S(2)}) collective-permute-start(bf16[64,4096]{1,0:T(8,128)(2,1)S(1)} %collective-permute-done.2.refs_5_), channel_id=1, source_target_pairs={{248,0},{12,4},{0,8},{20,12},{8,16},{28,20},{16,24},{36,28},{24,32... | collective-permute-start | bytes 1572872 | tf_op jit(solution)/shard_map/ppermute | solution.py:20
  42.3 19.1 %collective-permute-start.9 = (bf16[64,4352]{1,0:T(8,128)(2,1)S(1)}, bf16[64,4352]{1,0:T(8,128)(2,1)S(1)}, u32[]{:S(2)}, u32[]{:S(2)}) collective-permute-start(bf16[64,4352]{1,0:T(8,128)(2,1)S(1)} %pad_maximum_fusion.refs_4_), channel_id=1, source_target_pairs={{0,1},{1,0},{2,3},{3,2},{4,5},{5,4},{6,7},{7,6},{8,9},{9,8},{10,11... | collective-permute-start | bytes 1671176 | tf_op jit(solution)/shard_map/ppermute | solution.py:24
  42.3 19.1 %collective-permute-start.10 = (bf16[64,4352]{1,0:T(8,128)(2,1)S(1)}, bf16[64,4352]{1,0:T(8,128)(2,1)S(1)}, u32[]{:S(2)}, u32[]{:S(2)}) collective-permute-start(bf16[64,4352]{1,0:T(8,128)(2,1)S(1)} %collective-permute-done.5.refs_6_), channel_id=1, source_target_pairs={{0,1},{1,0},{2,3},{3,2},{4,5},{5,4},{6,7},{7,6},{8,9},{9,8},{10,11... | collective-permute-start | bytes 1671176 | tf_op jit(solution)/shard_map/ppermute | solution.py:24
  42.8 17.2 %collective-permute-start.7 = (bf16[64,4096]{1,0:T(8,128)(2,1)S(1)}, bf16[64,4096]{1,0:T(8,128)(2,1)S(1)}, u32[]{:S(2)}, u32[]{:S(2)}) collective-permute-start(bf16[64,4096]{1,0:T(8,128)(2,1)S(1)} %collective-permute-done.refs_3_), channel_id=1, source_target_pairs={{248,0},{12,4},{0,8},{20,12},{8,16},{28,20},{16,24},{36,28},{24,32... | collective-permute-start | bytes 1572872 | tf_op jit(solution)/shard_map/ppermute | solution.py:20
  42.8 17.2 %collective-permute-start.6 = (bf16[64,4096]{1,0:T(8,128)(2,1)S(1)}, bf16[64,4096]{1,0:T(8,128)(2,1)S(1)}, u32[]{:S(2)}, u32[]{:S(2)}) collective-permute-start(bf16[64,4096]{1,0:T(8,128)(2,1)S(1)} %collective-permute-done.refs_3_), channel_id=1, source_target_pairs={{8,0},{252,4},{16,8},{4,12},{24,16},{12,20},{32,24},{20,28},{40,32... | collective-permute-start | bytes 1572872 | tf_op jit(solution)/shard_map/ppermute | solution.py:20
  48.1 13.3 %collective-permute-start.8 = (bf16[64,4096]{1,0:T(8,128)(2,1)S(1)}, bf16[64,4096]{1,0:T(8,128)(2,1)S(1)}, u32[]{:S(2)}, u32[]{:S(2)}) collective-permute-start(bf16[64,4096]{1,0:T(8,128)(2,1)S(1)} %collective-permute-done.3.refs_2_), channel_id=1, source_target_pairs={{0,4},{4,0},{8,12},{12,8},{16,20},{20,16},{24,28},{28,24},{32,36},... | collective-permute-start | bytes 1572872 | tf_op jit(solution)/shard_map/ppermute | solution.py:24
  48.2 36.3 %slice-start = ((s8[9437184]{0:T(1024)(128)(4,1)}), s8[4194304]{0:T(1024)(128)(4,1)S(1)}, s32[]{:S(2)}) async-start(s8[9437184]{0:T(1024)(128)(4,1)} %bitcast.2), calls=%async_computation | async-start | bytes 8388608
  48.2 36.3 %slice-start.1 = ((s8[9437184]{0:T(1024)(128)(4,1)}), s8[4194304]{0:T(1024)(128)(4,1)S(1)}, s32[]{:S(2)}) async-start(s8[9437184]{0:T(1024)(128)(4,1)} %bitcast.2), calls=%async_computation.1 | async-start | bytes 8388608
  51.1 33.3 %slice-start.2 = ((s8[9437184]{0:T(1024)(128)(4,1)}), s8[1048576]{0:T(1024)(128)(4,1)S(1)}, s32[]{:S(2)}) async-start(s8[9437184]{0:T(1024)(128)(4,1)} %bitcast.2), calls=%async_computation.2 | async-start | bytes 2097152
  65.2 13.9 %collective-permute-start.12 = (bf16[64,4096]{1,0:T(8,128)(2,1)S(1)}, bf16[64,4096]{1,0:T(8,128)(2,1)S(1)}, u32[]{:S(2)}, u32[]{:S(2)}) collective-permute-start(bf16[64,4096]{1,0:T(8,128)(2,1)S(1)} %forward_2.1.refs_0_), channel_id=1, source_target_pairs={{0,2},{1,3},{2,0},{3,1},{4,6},{5,7},{6,4},{7,5},{8,10},{9,11},{10,... | collective-permute-start | bytes 1572872 | tf_op jit(solution)/shard_map/ppermute | solution.py:24
  68.3 10.8 %collective-permute-start.11 = (bf16[64,4096]{1,0:T(8,128)(2,1)S(1)}, bf16[64,4096]{1,0:T(8,128)(2,1)S(1)}, u32[]{:S(2)}, u32[]{:S(2)}) collective-permute-start(bf16[64,4096]{1,0:T(8,128)(2,1)S(1)} %forward_2.1.refs_0_), channel_id=1, source_target_pairs={{0,1},{1,0},{2,3},{3,2},{4,5},{5,4},{6,7},{7,6},{8,9},{9,8},{10,11... | collective-permute-start | bytes 1572872 | tf_op jit(solution)/shard_map/ppermute | solution.py:24
  79.2 1.9 %collective-permute-start.13 = (bf16[64,4096]{1,0:T(8,128)(2,1)S(1)}, bf16[64,4096]{1,0:T(8,128)(2,1)S(1)}, u32[]{:S(2)}, u32[]{:S(2)}) collective-permute-start(bf16[64,4096]{1,0:T(8,128)(2,1)S(1)} %collective-permute-done.12.refs_2_), channel_id=1, source_target_pairs={{0,1},{1,0},{2,3},{3,2},{4,5},{5,4},{6,7},{7,6},{8,9},{9,8},{10,11... | collective-permute-start | bytes 1572872 | tf_op jit(solution)/shard_map/ppermute | solution.py:24
  84.5 4.3 %collective-permute-start.14 = (f32[64,256]{1,0:T(8,128)S(1)}, f32[64,256]{1,0:T(8,128)S(1)}, u32[]{:S(2)}, u32[]{:S(2)}) collective-permute-start(f32[64,256]{1,0:T(8,128)S(1)} %get-tuple-element.82), channel_id=1, source_target_pairs={{0,8},{4,12},{8,0},{12,4},{16,24},{20,28},{24,16},{28,20},{32,40},... | collective-permute-start | bytes 196616 | tf_op jit(solution)/shard_map/ppermute | solution.py:24
  88.7 17.7 %collective-permute-start.15 = (bf16[64,4096]{1,0:T(8,128)(2,1)S(1)}, bf16[64,4096]{1,0:T(8,128)(2,1)S(1)}, u32[]{:S(2)}, u32[]{:S(2)}) collective-permute-start(bf16[64,4096]{1,0:T(8,128)(2,1)S(1)} %get-tuple-element.83), channel_id=1, source_target_pairs={{0,4},{4,0},{8,12},{12,8},{16,20},{20,16},{24,28},{28,24},{32,36},... | collective-permute-start | bytes 1572872 | tf_op jit(solution)/shard_map/ppermute | solution.py:24
  91.0 16.9 %collective-permute-start.16 = (bf16[64,4096]{1,0:T(8,128)(2,1)S(1)}, bf16[64,4096]{1,0:T(8,128)(2,1)S(1)}, u32[]{:S(2)}, u32[]{:S(2)}) collective-permute-start(bf16[64,4096]{1,0:T(8,128)(2,1)S(1)} %get-tuple-element.84), channel_id=1, source_target_pairs={{248,0},{12,4},{0,8},{20,12},{8,16},{28,20},{16,24},{36,28},{24,32... | collective-permute-start | bytes 1572872 | tf_op jit(solution)/shard_map/ppermute | solution.py:20
  92.5 15.5 %collective-permute-start.17 = (bf16[64,4096]{1,0:T(8,128)(2,1)S(1)}, bf16[64,4096]{1,0:T(8,128)(2,1)S(1)}, u32[]{:S(2)}, u32[]{:S(2)}) collective-permute-start(bf16[64,4096]{1,0:T(8,128)(2,1)S(1)} %get-tuple-element.85), channel_id=1, source_target_pairs={{8,0},{252,4},{16,8},{4,12},{24,16},{12,20},{32,24},{20,28},{40,32... | collective-permute-start | bytes 1572872 | tf_op jit(solution)/shard_map/ppermute | solution.py:20
  96.4 4.4 %collective-permute-start.18 = (f32[64,256]{1,0:T(8,128)S(1)}, f32[64,256]{1,0:T(8,128)S(1)}, u32[]{:S(2)}, u32[]{:S(2)}) collective-permute-start(f32[64,256]{1,0:T(8,128)S(1)} %add.52), channel_id=1, source_target_pairs={{0,32},{4,36},{8,40},{12,44},{16,48},{20,52},{24,56},{28,60},{32,0... | collective-permute-start | bytes 196616 | tf_op jit(solution)/shard_map/ppermute | solution.py:24
  100.8 5.7 %collective-permute-start.19 = (f32[64,256]{1,0:T(8,128)S(1)}, f32[64,256]{1,0:T(8,128)S(1)}, u32[]{:S(2)}, u32[]{:S(2)}) collective-permute-start(f32[64,256]{1,0:T(8,128)S(1)} %add.53), channel_id=1, source_target_pairs={{0,64},{4,68},{8,72},{12,76},{16,80},{20,84},{24,88},{28,92},{32,9... | collective-permute-start | bytes 196616 | tf_op jit(solution)/shard_map/ppermute | solution.py:24
  107.9 6.4 %collective-permute-start.22 = (f32[64,256]{1,0:T(8,128)S(1)}, f32[64,256]{1,0:T(8,128)S(1)}, u32[]{:S(2)}, u32[]{:S(2)}) collective-permute-start(f32[64,256]{1,0:T(8,128)S(1)} %add.57), channel_id=1, source_target_pairs={{0,4},{4,0},{8,12},{12,8},{16,20},{20,16},{24,28},{28,24},{32,36},... | collective-permute-start | bytes 196616 | tf_op jit(solution)/shard_map/ppermute | solution.py:24
  109.0 16.7 %collective-permute-start.20 = (bf16[64,4096]{1,0:T(8,128)(2,1)S(1)}, bf16[64,4096]{1,0:T(8,128)(2,1)S(1)}, u32[]{:S(2)}, u32[]{:S(2)}) collective-permute-start(bf16[64,4096]{1,0:T(8,128)(2,1)S(1)} %add_convert_fusion.4), channel_id=1, source_target_pairs={{248,0},{12,4},{0,8},{20,12},{8,16},{28,20},{16,24},{36,28},{24,32... | collective-permute-start | bytes 1572872 | tf_op jit(solution)/shard_map/ppermute | solution.py:20
  109.0 16.6 %collective-permute-start.21 = (bf16[64,4096]{1,0:T(8,128)(2,1)S(1)}, bf16[64,4096]{1,0:T(8,128)(2,1)S(1)}, u32[]{:S(2)}, u32[]{:S(2)}) collective-permute-start(bf16[64,4096]{1,0:T(8,128)(2,1)S(1)} %get-tuple-element.100), channel_id=1, source_target_pairs={{8,0},{252,4},{16,8},{4,12},{24,16},{12,20},{32,24},{20,28},{40,32... | collective-permute-start | bytes 1572872 | tf_op jit(solution)/shard_map/ppermute | solution.py:20
  114.4 6.9 %collective-permute-start.23 = (f32[64,256]{1,0:T(8,128)S(1)}, f32[64,256]{1,0:T(8,128)S(1)}, u32[]{:S(2)}, u32[]{:S(2)}) collective-permute-start(f32[64,256]{1,0:T(8,128)S(1)} %add.58), channel_id=1, source_target_pairs={{0,16},{4,20},{8,24},{12,28},{16,0},{20,4},{24,8},{28,12},{32,48},... | collective-permute-start | bytes 196616 | tf_op jit(solution)/shard_map/ppermute | solution.py:24
  125.7 20.1 %collective-permute-start.25 = (bf16[64,4096]{1,0:T(8,128)(2,1)S(1)}, bf16[64,4096]{1,0:T(8,128)(2,1)S(1)}, u32[]{:S(2)}, u32[]{:S(2)}) collective-permute-start(bf16[64,4096]{1,0:T(8,128)(2,1)S(1)} %add_convert_fusion.1), channel_id=1, source_target_pairs={{8,0},{252,4},{16,8},{4,12},{24,16},{12,20},{32,24},{20,28},{40,32... | collective-permute-start | bytes 1572872 | tf_op jit(solution)/shard_map/ppermute | solution.py:20
  131.0 16.5 %collective-permute-start.24 = (bf16[64,4096]{1,0:T(8,128)(2,1)S(1)}, bf16[64,4096]{1,0:T(8,128)(2,1)S(1)}, u32[]{:S(2)}, u32[]{:S(2)}) collective-permute-start(bf16[64,4096]{1,0:T(8,128)(2,1)S(1)} %add_convert_fusion.2), channel_id=1, source_target_pairs={{248,0},{12,4},{0,8},{20,12},{8,16},{28,20},{16,24},{36,28},{24,32... | collective-permute-start | bytes 1572872 | tf_op jit(solution)/shard_map/ppermute | solution.py:20
  131.1 16.5 %collective-permute-start.26 = (bf16[64,4096]{1,0:T(8,128)(2,1)S(1)}, bf16[64,4096]{1,0:T(8,128)(2,1)S(1)}, u32[]{:S(2)}, u32[]{:S(2)}) collective-permute-start(bf16[64,4096]{1,0:T(8,128)(2,1)S(1)} %add_convert_fusion.3), channel_id=1, source_target_pairs={{0,4},{4,0},{8,12},{12,8},{16,20},{20,16},{24,28},{28,24},{32,36},... | collective-permute-start | bytes 1572872 | tf_op jit(solution)/shard_map/ppermute | solution.py:24
  137.0 8.2 %collective-permute-start.27 = (f32[64,256]{1,0:T(8,128)S(1)}, f32[64,256]{1,0:T(8,128)S(1)}, u32[]{:S(2)}, u32[]{:S(2)}) collective-permute-start(f32[64,256]{1,0:T(8,128)S(1)} %add.59), channel_id=1, source_target_pairs={{0,128},{4,132},{8,136},{12,140},{16,144},{20,148},{24,152},{28,15... | collective-permute-start | bytes 196616 | tf_op jit(solution)/shard_map/ppermute | solution.py:24
  (4 other events, 5.7 us)

commit v6 on v5

--- a/solution.py
+++ b/solution.py
@@ -10,7 +10,7 @@
 
 REACH = 4
 GROUP = 8
-WAVES = [[0, 1, 2, -2], [4, -4], [3, -1, -3]]
+WAVES = [[0, 2, -2], [1, 4, -4], [3, -1, -3]]
 MIB = 1 << 20
 
 
@@ -267,13 +267,14 @@
     own = jnp.concatenate([cotangent, exchanged_columns(weight, place)], axis=1)
 
     x, u, v = flipped(x_t, "blk", 1), stepped(x_t, True), stepped(x_t, False)
+    far = flipped(own, "feat", 2)
     listed = plan(tile_row, tile_col, tile_off, tile_count, sign)
-    x, u, v, listed, own = fenced(x, u, v, listed, own)
-    m, n, far = stepped(u, True), stepped(v, False), flipped(own, "feat", 2)
-    y = forward(0, listed, tile_vals, [x_t, x, u, v], None, f32)
+    u, v, listed = fenced(u, v, listed)
+    m, n = stepped(u, True), stepped(v, False)
+    y = forward(0, listed, tile_vals, [x_t, u, v], None, f32)
     m, n, y, x, far, own = fenced(m, n, y, x, far, own)
     mx, xu, xv = flipped(m, "blk", 1), stepped(x, True), stepped(x, False)
-    y = forward(1, listed, tile_vals, [m, n], y, f32)
+    y = forward(1, listed, tile_vals, [x, m, n], y, f32)
     packed = [own, flipped(own, "feat", 1), far, flipped(far, "feat", 1)]
     xu, xv, mx, y, packed = fenced(xu, xv, mx, y, packed)
     y = forward(2, listed, tile_vals, [xu, xv, mx], y, bf16)
@@ -281,31 +282,30 @@
     ys = [y, flipped(y, "feat", 1), y_far, flipped(y_far, "feat", 1)]
     out_t, grad, wgrad = middle(place, ys, packed)
 
-    part = flipped(wgrad, "blk", 2)
+    parts = [flipped(wgrad, "blk", bit) for bit in (2, 4, 6)]
     to_xu, to_xv, to_mx = backward(2, listed, tile_vals, grad, [bf16] * 3)
-    to_xu, to_xv, to_mx, part, grad = fenced(to_xu, to_xv, to_mx, part, grad)
+    to_xu, to_xv, to_mx, parts, grad = fenced(to_xu, to_xv, to_mx, parts, grad)
     from_mx, from_xu, from_xv = flipped(to_mx, "blk", 1), stepped(to_xu, False), stepped(to_xv, True)
-    wgrad = wgrad + part
+    wgrad = (wgrad + parts[0]) + (parts[1] + parts[2])
     part = flipped(wgrad, "blk", 8)
-    to_m, to_n = backward(1, listed, tile_vals, grad, [f32, bf16])
-    part, to_m, grad = fenced(part, to_m, grad)
-    wgrad = wgrad + part
-    part = flipped(wgrad, "blk", 16)
-    total, to_x, to_u, to_v = backward(0, listed, tile_vals, grad, [f32] * 4)
-    from_mx, from_xu, from_xv, to_m, to_n, total, to_x, to_u, to_v, part = fenced(
-        from_mx, from_xu, from_xv, to_m, to_n, total, to_x, to_u, to_v, part
+    to_x, to_m, to_n = backward(1, listed, tile_vals, grad, [f32, f32, bf16])
+    from_mx, from_xu, from_xv, to_m, to_n, to_x, grad, part = fenced(
+        from_mx, from_xu, from_xv, to_m, to_n, to_x, grad, part
     )
     from_m = stepped((to_m + from_mx.astype(f32)).astype(bf16), False)
     from_n = stepped(to_n, True)
-    to_x = (to_x + from_xu.astype(f32) + from_xv.astype(f32)).astype(bf16)
+    total, to_u, to_v = backward(0, listed, tile_vals, grad, [f32] * 3)
+    from_x = flipped((to_x + from_xu.astype(f32) + from_xv.astype(f32)).astype(bf16), "blk", 1)
     wgrad = wgrad + part
-    wgrad = wgrad + flipped(wgrad, "blk", 1)
-    wgrad = wgrad + flipped(wgrad, "blk", 4)
-    from_m, from_n, to_x, to_u, to_v, wgrad = fenced(from_m, from_n, to_x, to_u, to_v, wgrad)
+    part = flipped(wgrad, "blk", 16)
+    total, to_u, to_v, part = fenced(total, to_u, to_v, part)
+    wgrad = wgrad + part
     part = flipped(wgrad, "blk", 32)
+    from_m, from_n, to_u, to_v, part = fenced(from_m, from_n, to_u, to_v, part)
+    wgrad = wgrad + part
+    part = flipped(wgrad, "blk", 1)
     from_u = stepped((to_u + from_m.astype(f32)).astype(bf16), False)
     from_v = stepped((to_v + from_n.astype(f32)).astype(bf16), True)
-    from_x = flipped(to_x, "blk", 1)
     wgrad = wgrad + part
     total = total + from_u.astype(f32) + from_v.astype(f32) + from_x.astype(f32)
     return (out_t, total.astype(bf16), wgrad)

time: 149 us -> 149 us (level)
  starting transfers between devices: 46 us -> 54.7 us
  waiting for transfers between devices: 58.6 us -> 53.1 us
  local copies, waits for them, and re-layouts: 6.62 us -> 4.59 us
    ppermute x12, waiting for transfers between devices: 25.8 us -> 18.1 us  [stepped(): return lax.ppermute(block, 'blk', route)]
    ppermute x16 -> x17, starting transfers between devices: 14.2 us -> 20.2 us  [flipped(): lax.ppermute(block, axis, [(i, i ^ bit) for i in range(lax.axis_size(axis...]
    ppermute x12, starting transfers between devices: 31.7 us -> 34.5 us  [stepped(): return lax.ppermute(block, 'blk', route)]
    ppermute x16 -> x17, waiting for transfers between devices: 32.8 us -> 34.9 us  [flipped(): lax.ppermute(block, axis, [(i, i ^ bit) for i in range(lax.axis_size(axis...]
    unnamed x16, local copies, waits for them, and re-layouts: 5.74 us -> 3.71 us
  transfers between devices with their start and end apart: 28 -> 29, of which waited for: 16 -> 13; matrix products, arithmetic and copies ran while one was open for 3% -> 3% of each run, Pallas kernels for 16% -> 16%
where the time goes in v6:
time: 149 us; the launch traced here: 150 us
  starting transfers between devices  54.7 us (37%)
  waiting for transfers between devices  53.1 us (36%)
  Pallas kernels  31.6 us (21%)
  local copies, waits for them, and re-layouts  4.59 us (3%)
  other arithmetic  4.2 us (3%)
  between operations  1.56 us (1%)
    ppermute x17, waiting for transfers between devices, flipped(): lax.ppermute(block, axis, [(i, i ^ bit) for i in range(lax.axis_size(axis...  34.9 us
    ppermute x12, starting transfers between devices, stepped(): return lax.ppermute(block, 'blk', route)  34.5 us
    ppermute x17, starting transfers between devices, flipped(): lax.ppermute(block, axis, [(i, i ^ bit) for i in range(lax.axis_size(axis...  20.2 us
    ppermute x12, waiting for transfers between devices, stepped(): return lax.ppermute(block, 'blk', route)  18.1 us
    pallas_call x3, Pallas kernels, backward(): pl.pallas_call(functools.partial(backward_body, wave), out_shape=tuple((p...  11.6 us
    pallas_call x3, Pallas kernels, forward(): pl.pallas_call(functools.partial(forward_body, wave, seed is not None), o...  11.5 us
    pallas_call x1, Pallas kernels, plan(): pl.pallas_call(functools.partial(plan_body, cap), out_shape=jax.ShapeDtyp...  5.11 us
    unnamed x16, local copies, waits for them, and re-layouts  3.71 us
  transfers between devices with their start and end apart: 29, of which 13 were waited for; matrix products, arithmetic and copies ran while one was open for 3% of the time, Pallas kernels for 16%

profile of v6, /device:TPU:4, one launch (start us, length us, event | category | flops | bytes accessed | tf_op | source)
XLA Modules:
  0.0 149.8 jit_solution(16576465271471585493)
XLA Ops:
  0.7 1.7 %collective-permute-start.1 = (bf16[64,4096]{1,0:T(8,128)(2,1)}, bf16[64,4096]{1,0:T(8,128)(2,1)S(1)}, u32[]{:S(2)}, u32[]{:S(2)}) collective-permute-start(bf16[64,4096]{1,0:T(8,128)(2,1)} %refs_2_.1), channel_id=1, source_target_pairs={{248,0},{12,4},{0,8},{20,12},{8,16},{28,20},{16,24},{36,28},{24,32... | collective-permute-start | bytes 1572872 | tf_op jit(solution)/shard_map/ppermute | solution.py:20
  2.3 6.8 %collective-permute-start = (bf16[64,4096]{1,0:T(8,128)(2,1)}, bf16[64,4096]{1,0:T(8,128)(2,1)S(1)}, u32[]{:S(2)}, u32[]{:S(2)}) collective-permute-start(bf16[64,4096]{1,0:T(8,128)(2,1)} %refs_2_.1), channel_id=1, source_target_pairs={{8,0},{252,4},{16,8},{4,12},{24,16},{12,20},{32,24},{20,28},{40,32... | collective-permute-start | bytes 1572872 | tf_op jit(solution)/shard_map/ppermute | solution.py:20
  12.6 2.0 %collective-permute-start.4 = (bf16[64,4096]{1,0:T(8,128)(2,1)S(1)}, bf16[64,4096]{1,0:T(8,128)(2,1)S(1)}, u32[]{:S(2)}, u32[]{:S(2)}) collective-permute-start(bf16[64,4096]{1,0:T(8,128)(2,1)S(1)} %copy-done.1), channel_id=1, source_target_pairs={{0,4},{4,0},{8,12},{12,8},{16,20},{20,16},{24,28},{28,24},{32,36},... | collective-permute-start | bytes 1572872 | tf_op jit(solution)/shard_map/ppermute | solution.py:24
  15.3 5.1 %plan.1.refs_0_ = s32[904]{0:T(1024)S(1)} custom-call(s32[288]{0:T(512)S(1)} %copy-done.2, s32[288]{0:T(512)S(1)} %copy-done.3, s32[288]{0:T(512)S(1)} %copy-done.4, s32[1]{0:T(128)S(6)} %copy.11.count_ref, s32[1]{0:T(128)} %bitcast.1.sign_ref), custom_call_target="tpu_custom_call" | custom-call | bytes 6000000 | tf_op jit(solution)/shard_map/plan/pallas_call | solution.py:81
  21.2 5.1 %collective-permute-start.2 = (bf16[64,4096]{1,0:T(8,128)(2,1)S(1)}, bf16[64,4096]{1,0:T(8,128)(2,1)S(1)}, u32[]{:S(2)}, u32[]{:S(2)}) collective-permute-start(bf16[64,4096]{1,0:T(8,128)(2,1)S(1)} %collective-permute-done.refs_3_), channel_id=1, source_target_pairs={{8,0},{252,4},{16,8},{4,12},{24,16},{12,20},{32,24},{20,28},{40,32... | collective-permute-start | bytes 1572872 | tf_op jit(solution)/shard_map/ppermute | solution.py:20
  26.3 3.7 %copy-done = bf16[288,128,128]{2,1,0:T(8,128)(2,1)S(1)} copy-done((bf16[288,128,128]{2,1,0:T(8,128)(2,1)S(1)}, bf16[288,128,128]{2,1,0:T(8,128)(2,1)}, u32[]{:S(2)}) %copy-start) | copy-done | bytes 9437208
  30.0 3.7 %forward_0.1.refs_5_ = f32[64,4096]{1,0:T(8,128)S(1)} custom-call(s32[904]{0:T(1024)S(1)} %plan.1.refs_0_, bf16[288,128,128]{2,1,0:T(8,128)(2,1)S(1)} %copy-done, bf16[64,4096]{1,0:T(8,128)(2,1)S(1)} %copy-done.1, bf16[64,4096]{1,0:T(8,128)(2,1)S(1)} %collective-permute-done.refs_3_, bf16[64,4096]{1,0:T(8,128)(2,1)S(1)} %collective-permute-done.1.refs_4_), custom_call_target="tpu_custom_call" | custom-call | bytes 6000000 | tf_op jit(solution)/shard_map/forward_0/pallas_call | solution.py:154
  33.8 3.4 %collective-permute-done.4.refs_2_ = bf16[64,4096]{1,0:T(8,128)(2,1)S(1)} collective-permute-done((bf16[64,4096]{1,0:T(8,128)(2,1)S(1)}, bf16[64,4096]{1,0:T(8,128)(2,1)S(1)}, u32[]{:S(2)}, u32[]{:S(2)}) %collective-permute-start.4) | collective-permute-done | bytes 524320 | tf_op jit(solution)/shard_map/ppermute | solution.py:24
  37.2 5.0 %collective-permute-done.3.refs_4_ = bf16[64,4096]{1,0:T(8,128)(2,1)S(1)} collective-permute-done((bf16[64,4096]{1,0:T(8,128)(2,1)S(1)}, bf16[64,4096]{1,0:T(8,128)(2,1)S(1)}, u32[]{:S(2)}, u32[]{:S(2)}) %collective-permute-start.3) | collective-permute-done | bytes 524320 | tf_op jit(solution)/shard_map/ppermute | solution.py:20
  43.5 5.3 %collective-permute-start.6 = (bf16[64,4096]{1,0:T(8,128)(2,1)S(1)}, bf16[64,4096]{1,0:T(8,128)(2,1)S(1)}, u32[]{:S(2)}, u32[]{:S(2)}) collective-permute-start(bf16[64,4096]{1,0:T(8,128)(2,1)S(1)} %collective-permute-done.4.refs_2_), channel_id=1, source_target_pairs={{8,0},{252,4},{16,8},{4,12},{24,16},{12,20},{32,24},{20,28},{40,32... | collective-permute-start | bytes 1572872 | tf_op jit(solution)/shard_map/ppermute | solution.py:20
  48.8 4.0 %forward_1.1.refs_5_ = f32[64,4096]{1,0:T(8,128)S(1)} custom-call(s32[904]{0:T(1024)S(1)} %plan.1.refs_0_, bf16[288,128,128]{2,1,0:T(8,128)(2,1)S(1)} %copy-done, bf16[64,4096]{1,0:T(8,128)(2,1)S(1)} %collective-permute-done.4.refs_2_, bf16[64,4096]{1,0:T(8,128)(2,1)S(1)} %collective-permute-done.2.refs_3_, ...), custom_call_target="tpu_custom_call" | custom-call | bytes 6000000 | tf_op jit(solution)/shard_map/forward_1/pallas_call | solution.py:154
  52.8 3.7 %collective-permute-done.8.refs_4_ = bf16[64,4096]{1,0:T(8,128)(2,1)S(1)} collective-permute-done((bf16[64,4096]{1,0:T(8,128)(2,1)S(1)}, bf16[64,4096]{1,0:T(8,128)(2,1)S(1)}, u32[]{:S(2)}, u32[]{:S(2)}) %collective-permute-start.8) | collective-permute-done | bytes 524320 | tf_op jit(solution)/shard_map/ppermute | solution.py:24
  56.5 3.8 %collective-permute-done.7.refs_3_ = bf16[64,4096]{1,0:T(8,128)(2,1)S(1)} collective-permute-done((bf16[64,4096]{1,0:T(8,128)(2,1)S(1)}, bf16[64,4096]{1,0:T(8,128)(2,1)S(1)}, u32[]{:S(2)}, u32[]{:S(2)}) %collective-permute-start.7) | collective-permute-done | bytes 524320 | tf_op jit(solution)/shard_map/ppermute | solution.py:20
  60.4 3.8 %forward_2.1.refs_0_ = bf16[64,4096]{1,0:T(8,128)(2,1)S(1)} custom-call(s32[904]{0:T(1024)S(1)} %plan.1.refs_0_, bf16[288,128,128]{2,1,0:T(8,128)(2,1)S(1)} %copy-done, bf16[64,4096]{1,0:T(8,128)(2,1)S(1)} %collective-permute-done.6.refs_2_, bf16[64,4096]{1,0:T(8,128)(2,1)S(1)} %collective-permute-done.7.refs_3_, ...), custom_call_target="tpu_custom_call" | custom-call | bytes 6000000 | tf_op jit(solution)/shard_map/forward_2/pallas_call | solution.py:154
  65.1 13.4 %collective-permute-done.12.refs_2_ = bf16[64,4096]{1,0:T(8,128)(2,1)S(1)} collective-permute-done((bf16[64,4096]{1,0:T(8,128)(2,1)S(1)}, bf16[64,4096]{1,0:T(8,128)(2,1)S(1)}, u32[]{:S(2)}, u32[]{:S(2)}) %collective-permute-start.12) | collective-permute-done | bytes 524320 | tf_op jit(solution)/shard_map/ppermute | solution.py:24
  78.4 1.9 %collective-permute-done.13.refs_3_ = bf16[64,4096]{1,0:T(8,128)(2,1)S(1)} collective-permute-done((bf16[64,4096]{1,0:T(8,128)(2,1)S(1)}, bf16[64,4096]{1,0:T(8,128)(2,1)S(1)}, u32[]{:S(2)}, u32[]{:S(2)}) %collective-permute-start.13) | collective-permute-done | bytes 524320 | tf_op jit(solution)/shard_map/ppermute | solution.py:24
  80.3 3.4 %middle.1 = (bf16[64,4096]{1,0:T(8,128)(2,1)}, bf16[64,4096]{1,0:T(8,128)(2,1)S(1)}, f32[64,256]{1,0:T(8,128)S(1)}) custom-call(s32[1]{0:T(128)} %bitcast.place_ref, bf16[64,4096]{1,0:T(8,128)(2,1)S(1)} %forward_2.1.refs_0_, bf16[64,4096]{1,0:T(8,128)(2,1)S(1)} %collective-permute-done.11.refs_1_, bf16[64,4096]{1,0:T(8,128)(2,1)S(1)} %collective-permute-done.12.refs_2_, ...), custom_call_target="tpu_custom_call" | custom-call | bytes 6000000 | tf_op jit(solution)/shard_map/middle/pallas_call | solution.py:243
  83.7 4.1 %collective-permute-start.14 = (f32[64,256]{1,0:T(8,128)S(1)}, f32[64,256]{1,0:T(8,128)S(1)}, u32[]{:S(2)}, u32[]{:S(2)}) collective-permute-start(f32[64,256]{1,0:T(8,128)S(1)} %get-tuple-element.78), channel_id=1, source_target_pairs={{0,8},{4,12},{8,0},{12,4},{16,24},{20,28},{24,16},{28,20},{32,40},... | collective-permute-start | bytes 196616 | tf_op jit(solution)/shard_map/ppermute | solution.py:24
  87.8 3.8 %backward_2.1 = (bf16[64,4096]{1,0:T(8,128)(2,1)S(1)}, bf16[64,4096]{1,0:T(8,128)(2,1)S(1)}, bf16[64,4096]{1,0:T(8,128)(2,1)S(1)}) custom-call(s32[904]{0:T(1024)S(1)} %plan.1.refs_0_, bf16[288,128,128]{2,1,0:T(8,128)(2,1)S(1)} %bitcast.3, bf16[64,4096]{1,0:T(8,128)(2,1)S(1)} %get-tuple-element.89.refs_2_), custom_call_target="tpu_custom_call" | custom-call | bytes 6000000 | tf_op jit(solution)/shard_map/backward_2/pallas_call | solution.py:195
  91.6 4.6 %collective-permute-start.17 = (bf16[64,4096]{1,0:T(8,128)(2,1)S(1)}, bf16[64,4096]{1,0:T(8,128)(2,1)S(1)}, u32[]{:S(2)}, u32[]{:S(2)}) collective-permute-start(bf16[64,4096]{1,0:T(8,128)(2,1)S(1)} %get-tuple-element.79), channel_id=1, source_target_pairs={{0,4},{4,0},{8,12},{12,8},{16,20},{20,16},{24,28},{28,24},{32,36},... | collective-permute-start | bytes 1572872 | tf_op jit(solution)/shard_map/ppermute | solution.py:24
  96.9 4.8 %collective-permute-start.19 = (bf16[64,4096]{1,0:T(8,128)(2,1)S(1)}, bf16[64,4096]{1,0:T(8,128)(2,1)S(1)}, u32[]{:S(2)}, u32[]{:S(2)}) collective-permute-start(bf16[64,4096]{1,0:T(8,128)(2,1)S(1)} %get-tuple-element.81), channel_id=1, source_target_pairs={{8,0},{252,4},{16,8},{4,12},{24,16},{12,20},{32,24},{20,28},{40,32... | collective-permute-start | bytes 1572872 | tf_op jit(solution)/shard_map/ppermute | solution.py:20
  101.8 4.0 %backward_1.1 = (f32[64,4096]{1,0:T(8,128)S(1)}, f32[64,4096]{1,0:T(8,128)S(1)}, bf16[64,4096]{1,0:T(8,128)(2,1)S(1)}) custom-call(s32[904]{0:T(1024)S(1)} %plan.1.refs_0_, bf16[288,128,128]{2,1,0:T(8,128)(2,1)S(1)} %bitcast.3, bf16[64,4096]{1,0:T(8,128)(2,1)S(1)} %get-tuple-element.89.refs_2_), custom_call_target="tpu_custom_call" | custom-call | bytes 6000000 | tf_op jit(solution)/shard_map/backward_1/pallas_call | solution.py:195
  105.8 4.9 %collective-permute-done.20 = f32[64,256]{1,0:T(8,128)S(1)} collective-permute-done((f32[64,256]{1,0:T(8,128)S(1)}, f32[64,256]{1,0:T(8,128)S(1)}, u32[]{:S(2)}, u32[]{:S(2)}) %collective-permute-start.20) | collective-permute-done | bytes 65568 | tf_op jit(solution)/shard_map/ppermute | solution.py:24
  110.7 1.7 %collective-permute-done.18 = bf16[64,4096]{1,0:T(8,128)(2,1)S(1)} collective-permute-done((bf16[64,4096]{1,0:T(8,128)(2,1)S(1)}, bf16[64,4096]{1,0:T(8,128)(2,1)S(1)}, u32[]{:S(2)}, u32[]{:S(2)}) %collective-permute-start.18) | collective-permute-done | bytes 524320 | tf_op jit(solution)/shard_map/ppermute | solution.py:20
  113.3 5.3 %collective-permute-start.23 = (bf16[64,4096]{1,0:T(8,128)(2,1)S(1)}, bf16[64,4096]{1,0:T(8,128)(2,1)S(1)}, u32[]{:S(2)}, u32[]{:S(2)}) collective-permute-start(bf16[64,4096]{1,0:T(8,128)(2,1)S(1)} %get-tuple-element.97), channel_id=1, source_target_pairs={{8,0},{252,4},{16,8},{4,12},{24,16},{12,20},{32,24},{20,28},{40,32... | collective-permute-start | bytes 1572872 | tf_op jit(solution)/shard_map/ppermute | solution.py:20
  118.7 3.8 %backward_0.1 = (f32[64,4096]{1,0:T(8,128)S(1)}, f32[64,4096]{1,0:T(8,128)S(1)}, f32[64,4096]{1,0:T(8,128)S(1)}) custom-call(s32[904]{0:T(1024)S(1)} %plan.1.refs_0_, bf16[288,128,128]{2,1,0:T(8,128)(2,1)S(1)} %bitcast.3, bf16[64,4096]{1,0:T(8,128)(2,1)S(1)} %get-tuple-element.89.refs_2_), custom_call_target="tpu_custom_call" | custom-call | bytes 6000000 | tf_op jit(solution)/shard_map/backward_0/pallas_call | solution.py:195
  124.1 1.7 %collective-permute-start.27 = (bf16[64,4096]{1,0:T(8,128)(2,1)S(1)}, bf16[64,4096]{1,0:T(8,128)(2,1)S(1)}, u32[]{:S(2)}, u32[]{:S(2)}) collective-permute-start(bf16[64,4096]{1,0:T(8,128)(2,1)S(1)} %add_convert_fusion.1), channel_id=1, source_target_pairs={{0,4},{4,0},{8,12},{12,8},{16,20},{20,16},{24,28},{28,24},{32,36},... | collective-permute-start | bytes 1572872 | tf_op jit(solution)/shard_map/ppermute | solution.py:24
  125.8 5.4 %collective-permute-done.24 = f32[64,256]{1,0:T(8,128)S(1)} collective-permute-done((f32[64,256]{1,0:T(8,128)S(1)}, f32[64,256]{1,0:T(8,128)S(1)}, u32[]{:S(2)}, u32[]{:S(2)}) %collective-permute-start.24) | collective-permute-done | bytes 65568 | tf_op jit(solution)/shard_map/ppermute | solution.py:24
  131.3 4.7 %collective-permute-start.26 = (bf16[64,4096]{1,0:T(8,128)(2,1)S(1)}, bf16[64,4096]{1,0:T(8,128)(2,1)S(1)}, u32[]{:S(2)}, u32[]{:S(2)}) collective-permute-start(bf16[64,4096]{1,0:T(8,128)(2,1)S(1)} %add_convert_fusion.2), channel_id=1, source_target_pairs={{8,0},{252,4},{16,8},{4,12},{24,16},{12,20},{32,24},{20,28},{40,32... | collective-permute-start | bytes 1572872 | tf_op jit(solution)/shard_map/ppermute | solution.py:20
  136.3 2.8 %collective-permute-start.28 = (f32[64,256]{1,0:T(8,128)S(1)}, f32[64,256]{1,0:T(8,128)S(1)}, u32[]{:S(2)}, u32[]{:S(2)}) collective-permute-start(f32[64,256]{1,0:T(8,128)S(1)} %add.68), channel_id=1, source_target_pairs={{0,4},{4,0},{8,12},{12,8},{16,20},{20,16},{24,28},{28,24},{32,36},... | collective-permute-start | bytes 196616 | tf_op jit(solution)/shard_map/ppermute | solution.py:24
  139.1 2.2 %collective-permute-done.28 = f32[64,256]{1,0:T(8,128)S(1)} collective-permute-done((f32[64,256]{1,0:T(8,128)S(1)}, f32[64,256]{1,0:T(8,128)S(1)}, u32[]{:S(2)}, u32[]{:S(2)}) %collective-permute-start.28) | collective-permute-done | bytes 65568 | tf_op jit(solution)/shard_map/ppermute | solution.py:24
  142.8 6.0 %collective-permute-done.25 = bf16[64,4096]{1,0:T(8,128)(2,1)S(1)} collective-permute-done((bf16[64,4096]{1,0:T(8,128)(2,1)S(1)}, bf16[64,4096]{1,0:T(8,128)(2,1)S(1)}, u32[]{:S(2)}, u32[]{:S(2)}) %collective-permute-start.25) | collective-permute-done | bytes 524320 | tf_op jit(solution)/shard_map/ppermute | solution.py:20
  (66 shorter events, 12.5 us)
Async XLA Ops:
  0.7 20.5 %collective-permute-start.1 = (bf16[64,4096]{1,0:T(8,128)(2,1)}, bf16[64,4096]{1,0:T(8,128)(2,1)S(1)}, u32[]{:S(2)}, u32[]{:S(2)}) collective-permute-start(bf16[64,4096]{1,0:T(8,128)(2,1)} %refs_2_.1), channel_id=1, source_target_pairs={{248,0},{12,4},{0,8},{20,12},{8,16},{28,20},{16,24},{36,28},{24,32... | collective-permute-start | bytes 1572872 | tf_op jit(solution)/shard_map/ppermute | solution.py:20
  2.3 18.9 %collective-permute-start = (bf16[64,4096]{1,0:T(8,128)(2,1)}, bf16[64,4096]{1,0:T(8,128)(2,1)S(1)}, u32[]{:S(2)}, u32[]{:S(2)}) collective-permute-start(bf16[64,4096]{1,0:T(8,128)(2,1)} %refs_2_.1), channel_id=1, source_target_pairs={{8,0},{252,4},{16,8},{4,12},{24,16},{12,20},{32,24},{20,28},{40,32... | collective-permute-start | bytes 1572872 | tf_op jit(solution)/shard_map/ppermute | solution.py:20
  12.0 25.1 %collective-permute-start.5 = (bf16[64,4352]{1,0:T(8,128)(2,1)S(1)}, bf16[64,4352]{1,0:T(8,128)(2,1)S(1)}, u32[]{:S(2)}, u32[]{:S(2)}) collective-permute-start(bf16[64,4352]{1,0:T(8,128)(2,1)S(1)} %pad_maximum_fusion.refs_4_), channel_id=1, source_target_pairs={{0,2},{1,3},{2,0},{3,1},{4,6},{5,7},{6,4},{7,5},{8,10},{9,11},{10,... | collective-permute-start | bytes 1671176 | tf_op jit(solution)/shard_map/ppermute | solution.py:24
  12.6 24.5 %collective-permute-start.4 = (bf16[64,4096]{1,0:T(8,128)(2,1)S(1)}, bf16[64,4096]{1,0:T(8,128)(2,1)S(1)}, u32[]{:S(2)}, u32[]{:S(2)}) collective-permute-start(bf16[64,4096]{1,0:T(8,128)(2,1)S(1)} %copy-done.1), channel_id=1, source_target_pairs={{0,4},{4,0},{8,12},{12,8},{16,20},{20,16},{24,28},{28,24},{32,36},... | collective-permute-start | bytes 1572872 | tf_op jit(solution)/shard_map/ppermute | solution.py:24
  21.2 16.0 %collective-permute-start.2 = (bf16[64,4096]{1,0:T(8,128)(2,1)S(1)}, bf16[64,4096]{1,0:T(8,128)(2,1)S(1)}, u32[]{:S(2)}, u32[]{:S(2)}) collective-permute-start(bf16[64,4096]{1,0:T(8,128)(2,1)S(1)} %collective-permute-done.refs_3_), channel_id=1, source_target_pairs={{8,0},{252,4},{16,8},{4,12},{24,16},{12,20},{32,24},{20,28},{40,32... | collective-permute-start | bytes 1572872 | tf_op jit(solution)/shard_map/ppermute | solution.py:20
  26.3 15.8 %collective-permute-start.3 = (bf16[64,4096]{1,0:T(8,128)(2,1)S(1)}, bf16[64,4096]{1,0:T(8,128)(2,1)S(1)}, u32[]{:S(2)}, u32[]{:S(2)}) collective-permute-start(bf16[64,4096]{1,0:T(8,128)(2,1)S(1)} %collective-permute-done.1.refs_4_), channel_id=1, source_target_pairs={{248,0},{12,4},{0,8},{20,12},{8,16},{28,20},{16,24},{36,28},{24,32... | collective-permute-start | bytes 1572872 | tf_op jit(solution)/shard_map/ppermute | solution.py:20
  42.2 18.2 %collective-permute-start.9 = (bf16[64,4352]{1,0:T(8,128)(2,1)S(1)}, bf16[64,4352]{1,0:T(8,128)(2,1)S(1)}, u32[]{:S(2)}, u32[]{:S(2)}) collective-permute-start(bf16[64,4352]{1,0:T(8,128)(2,1)S(1)} %pad_maximum_fusion.refs_4_), channel_id=1, source_target_pairs={{0,1},{1,0},{2,3},{3,2},{4,5},{5,4},{6,7},{7,6},{8,9},{9,8},{10,11... | collective-permute-start | bytes 1671176 | tf_op jit(solution)/shard_map/ppermute | solution.py:24
  42.2 18.2 %collective-permute-start.10 = (bf16[64,4352]{1,0:T(8,128)(2,1)S(1)}, bf16[64,4352]{1,0:T(8,128)(2,1)S(1)}, u32[]{:S(2)}, u32[]{:S(2)}) collective-permute-start(bf16[64,4352]{1,0:T(8,128)(2,1)S(1)} %collective-permute-done.5.refs_6_), channel_id=1, source_target_pairs={{0,1},{1,0},{2,3},{3,2},{4,5},{5,4},{6,7},{7,6},{8,9},{9,8},{10,11... | collective-permute-start | bytes 1671176 | tf_op jit(solution)/shard_map/ppermute | solution.py:24
  42.7 13.8 %collective-permute-start.8 = (bf16[64,4096]{1,0:T(8,128)(2,1)S(1)}, bf16[64,4096]{1,0:T(8,128)(2,1)S(1)}, u32[]{:S(2)}, u32[]{:S(2)}) collective-permute-start(bf16[64,4096]{1,0:T(8,128)(2,1)S(1)} %collective-permute-done.2.refs_3_), channel_id=1, source_target_pairs={{0,4},{4,0},{8,12},{12,8},{16,20},{20,16},{24,28},{28,24},{32,36},... | collective-permute-start | bytes 1572872 | tf_op jit(solution)/shard_map/ppermute | solution.py:24
  43.5 16.9 %collective-permute-start.7 = (bf16[64,4096]{1,0:T(8,128)(2,1)S(1)}, bf16[64,4096]{1,0:T(8,128)(2,1)S(1)}, u32[]{:S(2)}, u32[]{:S(2)}) collective-permute-start(bf16[64,4096]{1,0:T(8,128)(2,1)S(1)} %collective-permute-done.4.refs_2_), channel_id=1, source_target_pairs={{248,0},{12,4},{0,8},{20,12},{8,16},{28,20},{16,24},{36,28},{24,32... | collective-permute-start | bytes 1572872 | tf_op jit(solution)/shard_map/ppermute | solution.py:20
  43.5 16.9 %collective-permute-start.6 = (bf16[64,4096]{1,0:T(8,128)(2,1)S(1)}, bf16[64,4096]{1,0:T(8,128)(2,1)S(1)}, u32[]{:S(2)}, u32[]{:S(2)}) collective-permute-start(bf16[64,4096]{1,0:T(8,128)(2,1)S(1)} %collective-permute-done.4.refs_2_), channel_id=1, source_target_pairs={{8,0},{252,4},{16,8},{4,12},{24,16},{12,20},{32,24},{20,28},{40,32... | collective-permute-start | bytes 1572872 | tf_op jit(solution)/shard_map/ppermute | solution.py:20
  48.8 39.0 %slice-start = ((s8[9437184]{0:T(1024)(128)(4,1)}), s8[4194304]{0:T(1024)(128)(4,1)S(1)}, s32[]{:S(2)}) async-start(s8[9437184]{0:T(1024)(128)(4,1)} %bitcast.2), calls=%async_computation | async-start | bytes 8388608
  48.8 39.0 %slice-start.1 = ((s8[9437184]{0:T(1024)(128)(4,1)}), s8[4194304]{0:T(1024)(128)(4,1)S(1)}, s32[]{:S(2)}) async-start(s8[9437184]{0:T(1024)(128)(4,1)} %bitcast.2), calls=%async_computation.1 | async-start | bytes 8388608
  52.8 35.0 %slice-start.2 = ((s8[9437184]{0:T(1024)(128)(4,1)}), s8[1048576]{0:T(1024)(128)(4,1)S(1)}, s32[]{:S(2)}) async-start(s8[9437184]{0:T(1024)(128)(4,1)} %bitcast.2), calls=%async_computation.2 | async-start | bytes 2097152
  64.2 14.3 %collective-permute-start.12 = (bf16[64,4096]{1,0:T(8,128)(2,1)S(1)}, bf16[64,4096]{1,0:T(8,128)(2,1)S(1)}, u32[]{:S(2)}, u32[]{:S(2)}) collective-permute-start(bf16[64,4096]{1,0:T(8,128)(2,1)S(1)} %forward_2.1.refs_0_), channel_id=1, source_target_pairs={{0,2},{1,3},{2,0},{3,1},{4,6},{5,7},{6,4},{7,5},{8,10},{9,11},{10,... | collective-permute-start | bytes 1572872 | tf_op jit(solution)/shard_map/ppermute | solution.py:24
  65.1 13.4 %collective-permute-start.11 = (bf16[64,4096]{1,0:T(8,128)(2,1)S(1)}, bf16[64,4096]{1,0:T(8,128)(2,1)S(1)}, u32[]{:S(2)}, u32[]{:S(2)}) collective-permute-start(bf16[64,4096]{1,0:T(8,128)(2,1)S(1)} %forward_2.1.refs_0_), channel_id=1, source_target_pairs={{0,1},{1,0},{2,3},{3,2},{4,5},{5,4},{6,7},{7,6},{8,9},{9,8},{10,11... | collective-permute-start | bytes 1572872 | tf_op jit(solution)/shard_map/ppermute | solution.py:24
  78.4 1.9 %collective-permute-start.13 = (bf16[64,4096]{1,0:T(8,128)(2,1)S(1)}, bf16[64,4096]{1,0:T(8,128)(2,1)S(1)}, u32[]{:S(2)}, u32[]{:S(2)}) collective-permute-start(bf16[64,4096]{1,0:T(8,128)(2,1)S(1)} %collective-permute-done.12.refs_2_), channel_id=1, source_target_pairs={{0,1},{1,0},{2,3},{3,2},{4,5},{5,4},{6,7},{7,6},{8,9},{9,8},{10,11... | collective-permute-start | bytes 1572872 | tf_op jit(solution)/shard_map/ppermute | solution.py:24
  83.7 7.9 %collective-permute-start.16 = (f32[64,256]{1,0:T(8,128)S(1)}, f32[64,256]{1,0:T(8,128)S(1)}, u32[]{:S(2)}, u32[]{:S(2)}) collective-permute-start(f32[64,256]{1,0:T(8,128)S(1)} %get-tuple-element.78), channel_id=1, source_target_pairs={{0,24},{4,28},{8,16},{12,20},{16,8},{20,12},{24,0},{28,4},{32,56},... | collective-permute-start | bytes 196616 | tf_op jit(solution)/shard_map/ppermute | solution.py:24
  83.7 7.9 %collective-permute-start.15 = (f32[64,256]{1,0:T(8,128)S(1)}, f32[64,256]{1,0:T(8,128)S(1)}, u32[]{:S(2)}, u32[]{:S(2)}) collective-permute-start(f32[64,256]{1,0:T(8,128)S(1)} %get-tuple-element.78), channel_id=1, source_target_pairs={{0,16},{4,20},{8,24},{12,28},{16,0},{20,4},{24,8},{28,12},{32,48},... | collective-permute-start | bytes 196616 | tf_op jit(solution)/shard_map/ppermute | solution.py:24
  83.7 7.9 %collective-permute-start.14 = (f32[64,256]{1,0:T(8,128)S(1)}, f32[64,256]{1,0:T(8,128)S(1)}, u32[]{:S(2)}, u32[]{:S(2)}) collective-permute-start(f32[64,256]{1,0:T(8,128)S(1)} %get-tuple-element.78), channel_id=1, source_target_pairs={{0,8},{4,12},{8,0},{12,4},{16,24},{20,28},{24,16},{28,20},{32,40},... | collective-permute-start | bytes 196616 | tf_op jit(solution)/shard_map/ppermute | solution.py:24
  91.6 19.1 %collective-permute-start.17 = (bf16[64,4096]{1,0:T(8,128)(2,1)S(1)}, bf16[64,4096]{1,0:T(8,128)(2,1)S(1)}, u32[]{:S(2)}, u32[]{:S(2)}) collective-permute-start(bf16[64,4096]{1,0:T(8,128)(2,1)S(1)} %get-tuple-element.79), channel_id=1, source_target_pairs={{0,4},{4,0},{8,12},{12,8},{16,20},{20,16},{24,28},{28,24},{32,36},... | collective-permute-start | bytes 1572872 | tf_op jit(solution)/shard_map/ppermute | solution.py:24
  96.3 16.2 %collective-permute-start.18 = (bf16[64,4096]{1,0:T(8,128)(2,1)S(1)}, bf16[64,4096]{1,0:T(8,128)(2,1)S(1)}, u32[]{:S(2)}, u32[]{:S(2)}) collective-permute-start(bf16[64,4096]{1,0:T(8,128)(2,1)S(1)} %get-tuple-element.80), channel_id=1, source_target_pairs={{248,0},{12,4},{0,8},{20,12},{8,16},{28,20},{16,24},{36,28},{24,32... | collective-permute-start | bytes 1572872 | tf_op jit(solution)/shard_map/ppermute | solution.py:20
  96.9 15.6 %collective-permute-start.19 = (bf16[64,4096]{1,0:T(8,128)(2,1)S(1)}, bf16[64,4096]{1,0:T(8,128)(2,1)S(1)}, u32[]{:S(2)}, u32[]{:S(2)}) collective-permute-start(bf16[64,4096]{1,0:T(8,128)(2,1)S(1)} %get-tuple-element.81), channel_id=1, source_target_pairs={{8,0},{252,4},{16,8},{4,12},{24,16},{12,20},{32,24},{20,28},{40,32... | collective-permute-start | bytes 1572872 | tf_op jit(solution)/shard_map/ppermute | solution.py:20
  101.7 9.1 %collective-permute-start.20 = (f32[64,256]{1,0:T(8,128)S(1)}, f32[64,256]{1,0:T(8,128)S(1)}, u32[]{:S(2)}, u32[]{:S(2)}) collective-permute-start(f32[64,256]{1,0:T(8,128)S(1)} %add_add_fusion), channel_id=1, source_target_pairs={{0,32},{4,36},{8,40},{12,44},{16,48},{20,52},{24,56},{28,60},{32,0... | collective-permute-start | bytes 196616 | tf_op jit(solution)/shard_map/ppermute | solution.py:24
  112.5 10.0 %collective-permute-start.21 = (f32[64,256]{1,0:T(8,128)S(1)}, f32[64,256]{1,0:T(8,128)S(1)}, u32[]{:S(2)}, u32[]{:S(2)}) collective-permute-start(f32[64,256]{1,0:T(8,128)S(1)} %add.58), channel_id=1, source_target_pairs={{0,64},{4,68},{8,72},{12,76},{16,80},{20,84},{24,88},{28,92},{32,9... | collective-permute-start | bytes 196616 | tf_op jit(solution)/shard_map/ppermute | solution.py:24
  113.2 18.0 %collective-permute-start.22 = (bf16[64,4096]{1,0:T(8,128)(2,1)S(1)}, bf16[64,4096]{1,0:T(8,128)(2,1)S(1)}, u32[]{:S(2)}, u32[]{:S(2)}) collective-permute-start(bf16[64,4096]{1,0:T(8,128)(2,1)S(1)} %add_convert_fusion.4), channel_id=1, source_target_pairs={{248,0},{12,4},{0,8},{20,12},{8,16},{28,20},{16,24},{36,28},{24,32... | collective-permute-start | bytes 1572872 | tf_op jit(solution)/shard_map/ppermute | solution.py:20
  113.3 17.9 %collective-permute-start.23 = (bf16[64,4096]{1,0:T(8,128)(2,1)S(1)}, bf16[64,4096]{1,0:T(8,128)(2,1)S(1)}, u32[]{:S(2)}, u32[]{:S(2)}) collective-permute-start(bf16[64,4096]{1,0:T(8,128)(2,1)S(1)} %get-tuple-element.97), channel_id=1, source_target_pairs={{8,0},{252,4},{16,8},{4,12},{24,16},{12,20},{32,24},{20,28},{40,32... | collective-permute-start | bytes 1572872 | tf_op jit(solution)/shard_map/ppermute | solution.py:20
  122.5 8.7 %collective-permute-start.24 = (f32[64,256]{1,0:T(8,128)S(1)}, f32[64,256]{1,0:T(8,128)S(1)}, u32[]{:S(2)}, u32[]{:S(2)}) collective-permute-start(f32[64,256]{1,0:T(8,128)S(1)} %add.60), channel_id=1, source_target_pairs={{0,128},{4,132},{8,136},{12,140},{16,144},{20,148},{24,152},{28,15... | collective-permute-start | bytes 196616 | tf_op jit(solution)/shard_map/ppermute | solution.py:24
  124.1 17.8 %collective-permute-start.27 = (bf16[64,4096]{1,0:T(8,128)(2,1)S(1)}, bf16[64,4096]{1,0:T(8,128)(2,1)S(1)}, u32[]{:S(2)}, u32[]{:S(2)}) collective-permute-start(bf16[64,4096]{1,0:T(8,128)(2,1)S(1)} %add_convert_fusion.1), channel_id=1, source_target_pairs={{0,4},{4,0},{8,12},{12,8},{16,20},{20,16},{24,28},{28,24},{32,36},... | collective-permute-start | bytes 1572872 | tf_op jit(solution)/shard_map/ppermute | solution.py:24
  131.3 11.4 %collective-permute-start.26 = (bf16[64,4096]{1,0:T(8,128)(2,1)S(1)}, bf16[64,4096]{1,0:T(8,128)(2,1)S(1)}, u32[]{:S(2)}, u32[]{:S(2)}) collective-permute-start(bf16[64,4096]{1,0:T(8,128)(2,1)S(1)} %add_convert_fusion.2), channel_id=1, source_target_pairs={{8,0},{252,4},{16,8},{4,12},{24,16},{12,20},{32,24},{20,28},{40,32... | collective-permute-start | bytes 1572872 | tf_op jit(solution)/shard_map/ppermute | solution.py:20
  136.2 12.6 %collective-permute-start.25 = (bf16[64,4096]{1,0:T(8,128)(2,1)S(1)}, bf16[64,4096]{1,0:T(8,128)(2,1)S(1)}, u32[]{:S(2)}, u32[]{:S(2)}) collective-permute-start(bf16[64,4096]{1,0:T(8,128)(2,1)S(1)} %add_convert_fusion.3), channel_id=1, source_target_pairs={{248,0},{12,4},{0,8},{20,12},{8,16},{28,20},{16,24},{36,28},{24,32... | collective-permute-start | bytes 1572872 | tf_op jit(solution)/shard_map/ppermute | solution.py:20
  136.3 5.0 %collective-permute-start.28 = (f32[64,256]{1,0:T(8,128)S(1)}, f32[64,256]{1,0:T(8,128)S(1)}, u32[]{:S(2)}, u32[]{:S(2)}) collective-permute-start(f32[64,256]{1,0:T(8,128)S(1)} %add.68), channel_id=1, source_target_pairs={{0,4},{4,0},{8,12},{12,8},{16,20},{20,16},{24,28},{28,24},{32,36},... | collective-permute-start | bytes 196616 | tf_op jit(solution)/shard_map/ppermute | solution.py:24
  (5 other events, 59.5 us)

commit v7 on v6

--- a/solution.py
+++ b/solution.py
@@ -267,16 +267,15 @@
     own = jnp.concatenate([cotangent, exchanged_columns(weight, place)], axis=1)
 
     x, u, v = flipped(x_t, "blk", 1), stepped(x_t, True), stepped(x_t, False)
-    far = flipped(own, "feat", 2)
     listed = plan(tile_row, tile_col, tile_off, tile_count, sign)
-    u, v, listed = fenced(u, v, listed)
-    m, n = stepped(u, True), stepped(v, False)
+    x, u, v, listed, own = fenced(x, u, v, listed, own)
+    m, n, far = stepped(u, True), stepped(v, False), flipped(own, "feat", 2)
     y = forward(0, listed, tile_vals, [x_t, u, v], None, f32)
-    m, n, y, x, far, own = fenced(m, n, y, x, far, own)
+    m, n, y, x = fenced(m, n, y, x)
     mx, xu, xv = flipped(m, "blk", 1), stepped(x, True), stepped(x, False)
     y = forward(1, listed, tile_vals, [x, m, n], y, f32)
+    xu, xv, mx, y, far, own = fenced(xu, xv, mx, y, far, own)
     packed = [own, flipped(own, "feat", 1), far, flipped(far, "feat", 1)]
-    xu, xv, mx, y, packed = fenced(xu, xv, mx, y, packed)
     y = forward(2, listed, tile_vals, [xu, xv, mx], y, bf16)
     y_far = flipped(y, "feat", 2)
     ys = [y, flipped(y, "feat", 1), y_far, flipped(y_far, "feat", 1)]

time: 149 us -> 142 us (0.953)
  Pallas kernels: 31.6 us -> 16.3 us
  waiting for transfers between devices: 53.1 us -> 58.2 us
  local copies, waits for them, and re-layouts: 4.59 us -> 6.62 us
    ppermute x12, waiting for transfers between devices: 18.1 us -> 26.6 us  [stepped(): return lax.ppermute(block, 'blk', route)]
    pallas_call x3, Pallas kernels: 11.5 us -> 5.09 us  [forward(): pl.pallas_call(functools.partial(forward_body, wave, seed is not None), o...]
    pallas_call x3, Pallas kernels: 11.6 us -> 5.56 us  [backward(): pl.pallas_call(functools.partial(backward_body, wave), out_shape=tuple((p...]
    ppermute x17, waiting for transfers between devices: 34.9 us -> 31.6 us  [flipped(): lax.ppermute(block, axis, [(i, i ^ bit) for i in range(lax.axis_size(axis...]
    ppermute x17, starting transfers between devices: 20.2 us -> 23.2 us  [flipped(): lax.ppermute(block, axis, [(i, i ^ bit) for i in range(lax.axis_size(axis...]
    pallas_call x1, Pallas kernels: 5.11 us -> 2.31 us  [plan(): pl.pallas_call(functools.partial(plan_body, cap), out_shape=jax.ShapeDtyp...]
    unnamed x16, local copies, waits for them, and re-layouts: 3.71 us -> 5.74 us
    ppermute x12, starting transfers between devices: 34.5 us -> 32.8 us  [stepped(): return lax.ppermute(block, 'blk', route)]
  transfers between devices with their start and end apart: 29 -> 29, of which waited for: 13 -> 16; matrix products, arithmetic and copies ran while one was open for 3% -> 3% of each run, Pallas kernels for 16% -> 8%
where the time goes in v7:
time: 142 us; the launch traced here: 143 us
  waiting for transfers between devices  58.2 us (41%)
  starting transfers between devices  56 us (39%)
  Pallas kernels  16.3 us (11%)
  local copies, waits for them, and re-layouts  6.62 us (5%)
  other arithmetic  4.2 us (3%)
  between operations  1.53 us (1%)
    ppermute x12, starting transfers between devices, stepped(): return lax.ppermute(block, 'blk', route)  32.8 us
    ppermute x17, waiting for transfers between devices, flipped(): lax.ppermute(block, axis, [(i, i ^ bit) for i in range(lax.axis_size(axis...  31.6 us
    ppermute x12, waiting for transfers between devices, stepped(): return lax.ppermute(block, 'blk', route)  26.6 us
    ppermute x17, starting transfers between devices, flipped(): lax.ppermute(block, axis, [(i, i ^ bit) for i in range(lax.axis_size(axis...  23.2 us
    unnamed x16, local copies, waits for them, and re-layouts  5.74 us
    pallas_call x3, Pallas kernels, backward(): pl.pallas_call(functools.partial(backward_body, wave), out_shape=tuple((p...  5.56 us
    pallas_call x3, Pallas kernels, forward(): pl.pallas_call(functools.partial(forward_body, wave, seed is not None), o...  5.09 us
    pallas_call x1, Pallas kernels, middle(): pl.pallas_call(functools.partial(middle_body, factor), out_shape=(jax.Sha...  3.37 us
  transfers between devices with their start and end apart: 29, of which 16 were waited for; matrix products, arithmetic and copies ran while one was open for 3% of the time, Pallas kernels for 8%

profile of v7, /device:TPU:4, one launch (start us, length us, event | category | flops | bytes accessed | tf_op | source)
XLA Modules:
  0.0 142.9 jit_solution(1354636063332103501)
XLA Ops:
  0.6 8.4 %collective-permute-start.1 = (bf16[64,4096]{1,0:T(8,128)(2,1)}, bf16[64,4096]{1,0:T(8,128)(2,1)S(1)}, u32[]{:S(2)}, u32[]{:S(2)}) collective-permute-start(bf16[64,4096]{1,0:T(8,128)(2,1)} %refs_2_.1), channel_id=1, source_target_pairs={{8,0},{252,4},{16,8},{4,12},{24,16},{12,20},{32,24},{20,28},{40,32... | collective-permute-start | bytes 1572872 | tf_op jit(solution)/shard_map/ppermute | solution.py:20
  13.5 2.3 %plan.1.refs_0_ = s32[904]{0:T(1024)S(1)} custom-call(s32[288]{0:T(512)S(1)} %copy-done.2, s32[288]{0:T(512)S(1)} %copy-done.3, s32[288]{0:T(512)S(1)} %copy-done.4, s32[1]{0:T(128)S(6)} %copy.11.count_ref, s32[1]{0:T(128)} %bitcast.1.sign_ref), custom_call_target="tpu_custom_call" | custom-call | bytes 6000000 | tf_op jit(solution)/shard_map/plan/pallas_call | solution.py:81
  16.9 3.6 %collective-permute-done.1.refs_3_ = bf16[64,4096]{1,0:T(8,128)(2,1)S(1)} collective-permute-done((bf16[64,4096]{1,0:T(8,128)(2,1)}, bf16[64,4096]{1,0:T(8,128)(2,1)S(1)}, u32[]{:S(2)}, u32[]{:S(2)}) %collective-permute-start.1) | collective-permute-done | bytes 524320 | tf_op jit(solution)/shard_map/ppermute | solution.py:20
  20.5 2.1 %collective-permute-done.refs_2_ = bf16[64,4096]{1,0:T(8,128)(2,1)S(1)} collective-permute-done((bf16[64,4096]{1,0:T(8,128)(2,1)}, bf16[64,4096]{1,0:T(8,128)(2,1)S(1)}, u32[]{:S(2)}, u32[]{:S(2)}) %collective-permute-start) | collective-permute-done | bytes 524320 | tf_op jit(solution)/shard_map/ppermute | solution.py:24
  22.6 3.3 %collective-permute-done.2.refs_4_ = bf16[64,4096]{1,0:T(8,128)(2,1)S(1)} collective-permute-done((bf16[64,4096]{1,0:T(8,128)(2,1)}, bf16[64,4096]{1,0:T(8,128)(2,1)S(1)}, u32[]{:S(2)}, u32[]{:S(2)}) %collective-permute-start.2) | collective-permute-done | bytes 524320 | tf_op jit(solution)/shard_map/ppermute | solution.py:20
  26.2 1.7 %collective-permute-start.4 = (bf16[64,4096]{1,0:T(8,128)(2,1)S(1)}, bf16[64,4096]{1,0:T(8,128)(2,1)S(1)}, u32[]{:S(2)}, u32[]{:S(2)}) collective-permute-start(bf16[64,4096]{1,0:T(8,128)(2,1)S(1)} %collective-permute-done.2.refs_4_), channel_id=1, source_target_pairs={{248,0},{12,4},{0,8},{20,12},{8,16},{28,20},{16,24},{36,28},{24,32... | collective-permute-start | bytes 1572872 | tf_op jit(solution)/shard_map/ppermute | solution.py:20
  28.5 3.7 %copy-done = bf16[288,128,128]{2,1,0:T(8,128)(2,1)S(1)} copy-done((bf16[288,128,128]{2,1,0:T(8,128)(2,1)S(1)}, bf16[288,128,128]{2,1,0:T(8,128)(2,1)}, u32[]{:S(2)}) %copy-start) | copy-done | bytes 9437208
  33.7 4.7 %collective-permute-done.3.refs_3_ = bf16[64,4096]{1,0:T(8,128)(2,1)S(1)} collective-permute-done((bf16[64,4096]{1,0:T(8,128)(2,1)S(1)}, bf16[64,4096]{1,0:T(8,128)(2,1)S(1)}, u32[]{:S(2)}, u32[]{:S(2)}) %collective-permute-start.3) | collective-permute-done | bytes 524320 | tf_op jit(solution)/shard_map/ppermute | solution.py:20
  38.4 3.6 %collective-permute-done.4.refs_4_ = bf16[64,4096]{1,0:T(8,128)(2,1)S(1)} collective-permute-done((bf16[64,4096]{1,0:T(8,128)(2,1)S(1)}, bf16[64,4096]{1,0:T(8,128)(2,1)S(1)}, u32[]{:S(2)}, u32[]{:S(2)}) %collective-permute-start.4) | collective-permute-done | bytes 524320 | tf_op jit(solution)/shard_map/ppermute | solution.py:20
  42.1 5.3 %collective-permute-start.5 = (bf16[64,4096]{1,0:T(8,128)(2,1)S(1)}, bf16[64,4096]{1,0:T(8,128)(2,1)S(1)}, u32[]{:S(2)}, u32[]{:S(2)}) collective-permute-start(bf16[64,4096]{1,0:T(8,128)(2,1)S(1)} %collective-permute-done.refs_2_), channel_id=1, source_target_pairs={{8,0},{252,4},{16,8},{4,12},{24,16},{12,20},{32,24},{20,28},{40,32... | collective-permute-start | bytes 1572872 | tf_op jit(solution)/shard_map/ppermute | solution.py:20
  47.4 1.8 %forward_1.1.refs_5_ = f32[64,4096]{1,0:T(8,128)S(1)} custom-call(s32[904]{0:T(1024)S(1)} %plan.1.refs_0_, bf16[288,128,128]{2,1,0:T(8,128)(2,1)S(1)} %copy-done, bf16[64,4096]{1,0:T(8,128)(2,1)S(1)} %collective-permute-done.refs_2_, bf16[64,4096]{1,0:T(8,128)(2,1)S(1)} %collective-permute-done.3.refs_3_, ...), custom_call_target="tpu_custom_call" | custom-call | bytes 6000000 | tf_op jit(solution)/shard_map/forward_1/pallas_call | solution.py:154
  49.2 4.4 %collective-permute-done.7.refs_4_ = bf16[64,4096]{1,0:T(8,128)(2,1)S(1)} collective-permute-done((bf16[64,4096]{1,0:T(8,128)(2,1)S(1)}, bf16[64,4096]{1,0:T(8,128)(2,1)S(1)}, u32[]{:S(2)}, u32[]{:S(2)}) %collective-permute-start.7) | collective-permute-done | bytes 524320 | tf_op jit(solution)/shard_map/ppermute | solution.py:24
  53.6 3.3 %collective-permute-done.6.refs_3_ = bf16[64,4096]{1,0:T(8,128)(2,1)S(1)} collective-permute-done((bf16[64,4096]{1,0:T(8,128)(2,1)S(1)}, bf16[64,4096]{1,0:T(8,128)(2,1)S(1)}, u32[]{:S(2)}, u32[]{:S(2)}) %collective-permute-start.6) | collective-permute-done | bytes 524320 | tf_op jit(solution)/shard_map/ppermute | solution.py:20
  57.0 1.8 %forward_2.1.refs_0_ = bf16[64,4096]{1,0:T(8,128)(2,1)S(1)} custom-call(s32[904]{0:T(1024)S(1)} %plan.1.refs_0_, bf16[288,128,128]{2,1,0:T(8,128)(2,1)S(1)} %copy-done, bf16[64,4096]{1,0:T(8,128)(2,1)S(1)} %collective-permute-done.5.refs_2_, bf16[64,4096]{1,0:T(8,128)(2,1)S(1)} %collective-permute-done.6.refs_3_, ...), custom_call_target="tpu_custom_call" | custom-call | bytes 6000000 | tf_op jit(solution)/shard_map/forward_2/pallas_call | solution.py:154
  59.9 11.2 %collective-permute-done.10.refs_2_ = bf16[64,4096]{1,0:T(8,128)(2,1)S(1)} collective-permute-done((bf16[64,4096]{1,0:T(8,128)(2,1)S(1)}, bf16[64,4096]{1,0:T(8,128)(2,1)S(1)}, u32[]{:S(2)}, u32[]{:S(2)}) %collective-permute-start.10) | collective-permute-done | bytes 524320 | tf_op jit(solution)/shard_map/ppermute | solution.py:24
  71.1 1.9 %collective-permute-done.11.refs_3_ = bf16[64,4096]{1,0:T(8,128)(2,1)S(1)} collective-permute-done((bf16[64,4096]{1,0:T(8,128)(2,1)S(1)}, bf16[64,4096]{1,0:T(8,128)(2,1)S(1)}, u32[]{:S(2)}, u32[]{:S(2)}) %collective-permute-start.11) | collective-permute-done | bytes 524320 | tf_op jit(solution)/shard_map/ppermute | solution.py:24
  73.0 3.4 %middle.1 = (bf16[64,4096]{1,0:T(8,128)(2,1)}, bf16[64,4096]{1,0:T(8,128)(2,1)S(1)}, f32[64,256]{1,0:T(8,128)S(1)}) custom-call(s32[1]{0:T(128)} %bitcast.place_ref, bf16[64,4096]{1,0:T(8,128)(2,1)S(1)} %forward_2.1.refs_0_, bf16[64,4096]{1,0:T(8,128)(2,1)S(1)} %collective-permute-done.9.refs_1_, bf16[64,4096]{1,0:T(8,128)(2,1)S(1)} %collective-permute-done.10.refs_2_, ...), custom_call_target="tpu_custom_call" | custom-call | bytes 6000000 | tf_op jit(solution)/shard_map/middle/pallas_call | solution.py:243
  77.6 2.8 %collective-permute-start.14 = (f32[64,256]{1,0:T(8,128)S(1)}, f32[64,256]{1,0:T(8,128)S(1)}, u32[]{:S(2)}, u32[]{:S(2)}) collective-permute-start(f32[64,256]{1,0:T(8,128)S(1)} %get-tuple-element.74), channel_id=1, source_target_pairs={{0,8},{4,12},{8,0},{12,4},{16,24},{20,28},{24,16},{28,20},{32,40},... | collective-permute-start | bytes 196616 | tf_op jit(solution)/shard_map/ppermute | solution.py:24
  80.5 1.9 %backward_2.1 = (bf16[64,4096]{1,0:T(8,128)(2,1)S(1)}, bf16[64,4096]{1,0:T(8,128)(2,1)S(1)}, bf16[64,4096]{1,0:T(8,128)(2,1)S(1)}) custom-call(s32[904]{0:T(1024)S(1)} %plan.1.refs_0_, bf16[288,128,128]{2,1,0:T(8,128)(2,1)S(1)} %bitcast.3, bf16[64,4096]{1,0:T(8,128)(2,1)S(1)} %get-tuple-element.85.refs_2_), custom_call_target="tpu_custom_call" | custom-call | bytes 6000000 | tf_op jit(solution)/shard_map/backward_2/pallas_call | solution.py:195
  83.7 1.9 %collective-permute-start.17 = (bf16[64,4096]{1,0:T(8,128)(2,1)S(1)}, bf16[64,4096]{1,0:T(8,128)(2,1)S(1)}, u32[]{:S(2)}, u32[]{:S(2)}) collective-permute-start(bf16[64,4096]{1,0:T(8,128)(2,1)S(1)} %get-tuple-element.75), channel_id=1, source_target_pairs={{0,4},{4,0},{8,12},{12,8},{16,20},{20,16},{24,28},{28,24},{32,36},... | collective-permute-start | bytes 1572872 | tf_op jit(solution)/shard_map/ppermute | solution.py:24
  86.6 5.2 %collective-permute-start.19 = (bf16[64,4096]{1,0:T(8,128)(2,1)S(1)}, bf16[64,4096]{1,0:T(8,128)(2,1)S(1)}, u32[]{:S(2)}, u32[]{:S(2)}) collective-permute-start(bf16[64,4096]{1,0:T(8,128)(2,1)S(1)} %get-tuple-element.77), channel_id=1, source_target_pairs={{8,0},{252,4},{16,8},{4,12},{24,16},{12,20},{32,24},{20,28},{40,32... | collective-permute-start | bytes 1572872 | tf_op jit(solution)/shard_map/ppermute | solution.py:20
  91.9 1.9 %backward_1.1 = (f32[64,4096]{1,0:T(8,128)S(1)}, f32[64,4096]{1,0:T(8,128)S(1)}, bf16[64,4096]{1,0:T(8,128)(2,1)S(1)}) custom-call(s32[904]{0:T(1024)S(1)} %plan.1.refs_0_, bf16[288,128,128]{2,1,0:T(8,128)(2,1)S(1)} %bitcast.3, bf16[64,4096]{1,0:T(8,128)(2,1)S(1)} %get-tuple-element.85.refs_2_), custom_call_target="tpu_custom_call" | custom-call | bytes 6000000 | tf_op jit(solution)/shard_map/backward_1/pallas_call | solution.py:195
  93.9 6.5 %collective-permute-done.20 = f32[64,256]{1,0:T(8,128)S(1)} collective-permute-done((f32[64,256]{1,0:T(8,128)S(1)}, f32[64,256]{1,0:T(8,128)S(1)}, u32[]{:S(2)}, u32[]{:S(2)}) %collective-permute-start.20) | collective-permute-done | bytes 65568 | tf_op jit(solution)/shard_map/ppermute | solution.py:24
  100.4 2.7 %collective-permute-done.18 = bf16[64,4096]{1,0:T(8,128)(2,1)S(1)} collective-permute-done((bf16[64,4096]{1,0:T(8,128)(2,1)S(1)}, bf16[64,4096]{1,0:T(8,128)(2,1)S(1)}, u32[]{:S(2)}, u32[]{:S(2)}) %collective-permute-start.18) | collective-permute-done | bytes 524320 | tf_op jit(solution)/shard_map/ppermute | solution.py:20
  103.4 5.3 %collective-permute-start.23 = (bf16[64,4096]{1,0:T(8,128)(2,1)S(1)}, bf16[64,4096]{1,0:T(8,128)(2,1)S(1)}, u32[]{:S(2)}, u32[]{:S(2)}) collective-permute-start(bf16[64,4096]{1,0:T(8,128)(2,1)S(1)} %get-tuple-element.93), channel_id=1, source_target_pairs={{8,0},{252,4},{16,8},{4,12},{24,16},{12,20},{32,24},{20,28},{40,32... | collective-permute-start | bytes 1572872 | tf_op jit(solution)/shard_map/ppermute | solution.py:20
  108.8 1.7 %backward_0.1 = (f32[64,4096]{1,0:T(8,128)S(1)}, f32[64,4096]{1,0:T(8,128)S(1)}, f32[64,4096]{1,0:T(8,128)S(1)}) custom-call(s32[904]{0:T(1024)S(1)} %plan.1.refs_0_, bf16[288,128,128]{2,1,0:T(8,128)(2,1)S(1)} %bitcast.3, bf16[64,4096]{1,0:T(8,128)(2,1)S(1)} %get-tuple-element.85.refs_2_), custom_call_target="tpu_custom_call" | custom-call | bytes 6000000 | tf_op jit(solution)/shard_map/backward_0/pallas_call | solution.py:195
  110.5 9.1 %collective-permute-start.24 = (f32[64,256]{1,0:T(8,128)S(1)}, f32[64,256]{1,0:T(8,128)S(1)}, u32[]{:S(2)}, u32[]{:S(2)}) collective-permute-start(f32[64,256]{1,0:T(8,128)S(1)} %add.60), channel_id=1, source_target_pairs={{0,128},{4,132},{8,136},{12,140},{16,144},{20,148},{24,152},{28,15... | collective-permute-start | bytes 196616 | tf_op jit(solution)/shard_map/ppermute | solution.py:24
  119.9 2.0 %collective-permute-done.24 = f32[64,256]{1,0:T(8,128)S(1)} collective-permute-done((f32[64,256]{1,0:T(8,128)S(1)}, f32[64,256]{1,0:T(8,128)S(1)}, u32[]{:S(2)}, u32[]{:S(2)}) %collective-permute-start.24) | collective-permute-done | bytes 65568 | tf_op jit(solution)/shard_map/ppermute | solution.py:24
  122.0 5.3 %collective-permute-start.26 = (bf16[64,4096]{1,0:T(8,128)(2,1)S(1)}, bf16[64,4096]{1,0:T(8,128)(2,1)S(1)}, u32[]{:S(2)}, u32[]{:S(2)}) collective-permute-start(bf16[64,4096]{1,0:T(8,128)(2,1)S(1)} %add_convert_fusion.2), channel_id=1, source_target_pairs={{8,0},{252,4},{16,8},{4,12},{24,16},{12,20},{32,24},{20,28},{40,32... | collective-permute-start | bytes 1572872 | tf_op jit(solution)/shard_map/ppermute | solution.py:20
  127.5 6.2 %collective-permute-start.28 = (f32[64,256]{1,0:T(8,128)S(1)}, f32[64,256]{1,0:T(8,128)S(1)}, u32[]{:S(2)}, u32[]{:S(2)}) collective-permute-start(f32[64,256]{1,0:T(8,128)S(1)} %add.68), channel_id=1, source_target_pairs={{0,4},{4,0},{8,12},{12,8},{16,20},{20,16},{24,28},{28,24},{32,36},... | collective-permute-start | bytes 196616 | tf_op jit(solution)/shard_map/ppermute | solution.py:24
  133.8 2.2 %collective-permute-done.28 = f32[64,256]{1,0:T(8,128)S(1)} collective-permute-done((f32[64,256]{1,0:T(8,128)S(1)}, f32[64,256]{1,0:T(8,128)S(1)}, u32[]{:S(2)}, u32[]{:S(2)}) %collective-permute-start.28) | collective-permute-done | bytes 65568 | tf_op jit(solution)/shard_map/ppermute | solution.py:24
  136.6 5.2 %collective-permute-done.25 = bf16[64,4096]{1,0:T(8,128)(2,1)S(1)} collective-permute-done((bf16[64,4096]{1,0:T(8,128)(2,1)S(1)}, bf16[64,4096]{1,0:T(8,128)(2,1)S(1)}, u32[]{:S(2)}, u32[]{:S(2)}) %collective-permute-start.25) | collective-permute-done | bytes 524320 | tf_op jit(solution)/shard_map/ppermute | solution.py:20
  (66 shorter events, 14.7 us)
Async XLA Ops:
  0.6 19.9 %collective-permute-start.1 = (bf16[64,4096]{1,0:T(8,128)(2,1)}, bf16[64,4096]{1,0:T(8,128)(2,1)S(1)}, u32[]{:S(2)}, u32[]{:S(2)}) collective-permute-start(bf16[64,4096]{1,0:T(8,128)(2,1)} %refs_2_.1), channel_id=1, source_target_pairs={{8,0},{252,4},{16,8},{4,12},{24,16},{12,20},{32,24},{20,28},{40,32... | collective-permute-start | bytes 1572872 | tf_op jit(solution)/shard_map/ppermute | solution.py:20
  9.0 13.6 %collective-permute-start = (bf16[64,4096]{1,0:T(8,128)(2,1)}, bf16[64,4096]{1,0:T(8,128)(2,1)S(1)}, u32[]{:S(2)}, u32[]{:S(2)}) collective-permute-start(bf16[64,4096]{1,0:T(8,128)(2,1)} %refs_2_.1), channel_id=1, source_target_pairs={{0,4},{4,0},{8,12},{12,8},{16,20},{20,16},{24,28},{28,24},{32,36},... | collective-permute-start | bytes 1572872 | tf_op jit(solution)/shard_map/ppermute | solution.py:24
  9.0 16.9 %collective-permute-start.2 = (bf16[64,4096]{1,0:T(8,128)(2,1)}, bf16[64,4096]{1,0:T(8,128)(2,1)S(1)}, u32[]{:S(2)}, u32[]{:S(2)}) collective-permute-start(bf16[64,4096]{1,0:T(8,128)(2,1)} %refs_2_.1), channel_id=1, source_target_pairs={{248,0},{12,4},{0,8},{20,12},{8,16},{28,20},{16,24},{36,28},{24,32... | collective-permute-start | bytes 1572872 | tf_op jit(solution)/shard_map/ppermute | solution.py:20
  25.9 12.5 %collective-permute-start.3 = (bf16[64,4096]{1,0:T(8,128)(2,1)S(1)}, bf16[64,4096]{1,0:T(8,128)(2,1)S(1)}, u32[]{:S(2)}, u32[]{:S(2)}) collective-permute-start(bf16[64,4096]{1,0:T(8,128)(2,1)S(1)} %collective-permute-done.1.refs_3_), channel_id=1, source_target_pairs={{8,0},{252,4},{16,8},{4,12},{24,16},{12,20},{32,24},{20,28},{40,32... | collective-permute-start | bytes 1572872 | tf_op jit(solution)/shard_map/ppermute | solution.py:20
  26.2 15.8 %collective-permute-start.4 = (bf16[64,4096]{1,0:T(8,128)(2,1)S(1)}, bf16[64,4096]{1,0:T(8,128)(2,1)S(1)}, u32[]{:S(2)}, u32[]{:S(2)}) collective-permute-start(bf16[64,4096]{1,0:T(8,128)(2,1)S(1)} %collective-permute-done.2.refs_4_), channel_id=1, source_target_pairs={{248,0},{12,4},{0,8},{20,12},{8,16},{28,20},{16,24},{36,28},{24,32... | collective-permute-start | bytes 1572872 | tf_op jit(solution)/shard_map/ppermute | solution.py:20
  28.0 21.2 %collective-permute-start.8 = (bf16[64,4352]{1,0:T(8,128)(2,1)S(1)}, bf16[64,4352]{1,0:T(8,128)(2,1)S(1)}, u32[]{:S(2)}, u32[]{:S(2)}) collective-permute-start(bf16[64,4352]{1,0:T(8,128)(2,1)S(1)} %pad_maximum_fusion.refs_4_), channel_id=1, source_target_pairs={{0,2},{1,3},{2,0},{3,1},{4,6},{5,7},{6,4},{7,5},{8,10},{9,11},{10,... | collective-permute-start | bytes 1671176 | tf_op jit(solution)/shard_map/ppermute | solution.py:24
  42.1 11.6 %collective-permute-start.7 = (bf16[64,4096]{1,0:T(8,128)(2,1)S(1)}, bf16[64,4096]{1,0:T(8,128)(2,1)S(1)}, u32[]{:S(2)}, u32[]{:S(2)}) collective-permute-start(bf16[64,4096]{1,0:T(8,128)(2,1)S(1)} %collective-permute-done.3.refs_3_), channel_id=1, source_target_pairs={{0,4},{4,0},{8,12},{12,8},{16,20},{20,16},{24,28},{28,24},{32,36},... | collective-permute-start | bytes 1572872 | tf_op jit(solution)/shard_map/ppermute | solution.py:24
  42.1 14.9 %collective-permute-start.6 = (bf16[64,4096]{1,0:T(8,128)(2,1)S(1)}, bf16[64,4096]{1,0:T(8,128)(2,1)S(1)}, u32[]{:S(2)}, u32[]{:S(2)}) collective-permute-start(bf16[64,4096]{1,0:T(8,128)(2,1)S(1)} %collective-permute-done.refs_2_), channel_id=1, source_target_pairs={{248,0},{12,4},{0,8},{20,12},{8,16},{28,20},{16,24},{36,28},{24,32... | collective-permute-start | bytes 1572872 | tf_op jit(solution)/shard_map/ppermute | solution.py:20
  42.1 14.9 %collective-permute-start.5 = (bf16[64,4096]{1,0:T(8,128)(2,1)S(1)}, bf16[64,4096]{1,0:T(8,128)(2,1)S(1)}, u32[]{:S(2)}, u32[]{:S(2)}) collective-permute-start(bf16[64,4096]{1,0:T(8,128)(2,1)S(1)} %collective-permute-done.refs_2_), channel_id=1, source_target_pairs={{8,0},{252,4},{16,8},{4,12},{24,16},{12,20},{32,24},{20,28},{40,32... | collective-permute-start | bytes 1572872 | tf_op jit(solution)/shard_map/ppermute | solution.py:20
  47.4 33.0 %slice-start = ((s8[9437184]{0:T(1024)(128)(4,1)}), s8[4194304]{0:T(1024)(128)(4,1)S(1)}, s32[]{:S(2)}) async-start(s8[9437184]{0:T(1024)(128)(4,1)} %bitcast.2), calls=%async_computation | async-start | bytes 8388608
  47.4 33.0 %slice-start.1 = ((s8[9437184]{0:T(1024)(128)(4,1)}), s8[4194304]{0:T(1024)(128)(4,1)S(1)}, s32[]{:S(2)}) async-start(s8[9437184]{0:T(1024)(128)(4,1)} %bitcast.2), calls=%async_computation.1 | async-start | bytes 8388608
  49.2 31.3 %slice-start.2 = ((s8[9437184]{0:T(1024)(128)(4,1)}), s8[1048576]{0:T(1024)(128)(4,1)S(1)}, s32[]{:S(2)}) async-start(s8[9437184]{0:T(1024)(128)(4,1)} %bitcast.2), calls=%async_computation.2 | async-start | bytes 2097152
  58.8 12.3 %collective-permute-start.10 = (bf16[64,4096]{1,0:T(8,128)(2,1)S(1)}, bf16[64,4096]{1,0:T(8,128)(2,1)S(1)}, u32[]{:S(2)}, u32[]{:S(2)}) collective-permute-start(bf16[64,4096]{1,0:T(8,128)(2,1)S(1)} %forward_2.1.refs_0_), channel_id=1, source_target_pairs={{0,2},{1,3},{2,0},{3,1},{4,6},{5,7},{6,4},{7,5},{8,10},{9,11},{10,... | collective-permute-start | bytes 1572872 | tf_op jit(solution)/shard_map/ppermute | solution.py:24
  59.4 11.7 %collective-permute-start.12 = (bf16[64,4352]{1,0:T(8,128)(2,1)S(1)}, bf16[64,4352]{1,0:T(8,128)(2,1)S(1)}, u32[]{:S(2)}, u32[]{:S(2)}) collective-permute-start(bf16[64,4352]{1,0:T(8,128)(2,1)S(1)} %pad_maximum_fusion.refs_4_), channel_id=1, source_target_pairs={{0,1},{1,0},{2,3},{3,2},{4,5},{5,4},{6,7},{7,6},{8,9},{9,8},{10,11... | collective-permute-start | bytes 1671176 | tf_op jit(solution)/shard_map/ppermute | solution.py:24
  59.4 11.7 %collective-permute-start.13 = (bf16[64,4352]{1,0:T(8,128)(2,1)S(1)}, bf16[64,4352]{1,0:T(8,128)(2,1)S(1)}, u32[]{:S(2)}, u32[]{:S(2)}) collective-permute-start(bf16[64,4352]{1,0:T(8,128)(2,1)S(1)} %collective-permute-done.8.refs_6_), channel_id=1, source_target_pairs={{0,1},{1,0},{2,3},{3,2},{4,5},{5,4},{6,7},{7,6},{8,9},{9,8},{10,11... | collective-permute-start | bytes 1671176 | tf_op jit(solution)/shard_map/ppermute | solution.py:24
  59.9 11.2 %collective-permute-start.9 = (bf16[64,4096]{1,0:T(8,128)(2,1)S(1)}, bf16[64,4096]{1,0:T(8,128)(2,1)S(1)}, u32[]{:S(2)}, u32[]{:S(2)}) collective-permute-start(bf16[64,4096]{1,0:T(8,128)(2,1)S(1)} %forward_2.1.refs_0_), channel_id=1, source_target_pairs={{0,1},{1,0},{2,3},{3,2},{4,5},{5,4},{6,7},{7,6},{8,9},{9,8},{10,11... | collective-permute-start | bytes 1572872 | tf_op jit(solution)/shard_map/ppermute | solution.py:24
  71.1 1.9 %collective-permute-start.11 = (bf16[64,4096]{1,0:T(8,128)(2,1)S(1)}, bf16[64,4096]{1,0:T(8,128)(2,1)S(1)}, u32[]{:S(2)}, u32[]{:S(2)}) collective-permute-start(bf16[64,4096]{1,0:T(8,128)(2,1)S(1)} %collective-permute-done.10.refs_2_), channel_id=1, source_target_pairs={{0,1},{1,0},{2,3},{3,2},{4,5},{5,4},{6,7},{7,6},{8,9},{9,8},{10,11... | collective-permute-start | bytes 1572872 | tf_op jit(solution)/shard_map/ppermute | solution.py:24
  76.4 6.7 %collective-permute-start.16 = (f32[64,256]{1,0:T(8,128)S(1)}, f32[64,256]{1,0:T(8,128)S(1)}, u32[]{:S(2)}, u32[]{:S(2)}) collective-permute-start(f32[64,256]{1,0:T(8,128)S(1)} %get-tuple-element.74), channel_id=1, source_target_pairs={{0,24},{4,28},{8,16},{12,20},{16,8},{20,12},{24,0},{28,4},{32,56},... | collective-permute-start | bytes 196616 | tf_op jit(solution)/shard_map/ppermute | solution.py:24
  76.4 6.7 %collective-permute-start.15 = (f32[64,256]{1,0:T(8,128)S(1)}, f32[64,256]{1,0:T(8,128)S(1)}, u32[]{:S(2)}, u32[]{:S(2)}) collective-permute-start(f32[64,256]{1,0:T(8,128)S(1)} %get-tuple-element.74), channel_id=1, source_target_pairs={{0,16},{4,20},{8,24},{12,28},{16,0},{20,4},{24,8},{28,12},{32,48},... | collective-permute-start | bytes 196616 | tf_op jit(solution)/shard_map/ppermute | solution.py:24
  77.6 6.0 %collective-permute-start.14 = (f32[64,256]{1,0:T(8,128)S(1)}, f32[64,256]{1,0:T(8,128)S(1)}, u32[]{:S(2)}, u32[]{:S(2)}) collective-permute-start(f32[64,256]{1,0:T(8,128)S(1)} %get-tuple-element.74), channel_id=1, source_target_pairs={{0,8},{4,12},{8,0},{12,4},{16,24},{20,28},{24,16},{28,20},{32,40},... | collective-permute-start | bytes 196616 | tf_op jit(solution)/shard_map/ppermute | solution.py:24
  83.7 16.7 %collective-permute-start.17 = (bf16[64,4096]{1,0:T(8,128)(2,1)S(1)}, bf16[64,4096]{1,0:T(8,128)(2,1)S(1)}, u32[]{:S(2)}, u32[]{:S(2)}) collective-permute-start(bf16[64,4096]{1,0:T(8,128)(2,1)S(1)} %get-tuple-element.75), channel_id=1, source_target_pairs={{0,4},{4,0},{8,12},{12,8},{16,20},{20,16},{24,28},{28,24},{32,36},... | collective-permute-start | bytes 1572872 | tf_op jit(solution)/shard_map/ppermute | solution.py:24
  85.6 17.5 %collective-permute-start.18 = (bf16[64,4096]{1,0:T(8,128)(2,1)S(1)}, bf16[64,4096]{1,0:T(8,128)(2,1)S(1)}, u32[]{:S(2)}, u32[]{:S(2)}) collective-permute-start(bf16[64,4096]{1,0:T(8,128)(2,1)S(1)} %get-tuple-element.76), channel_id=1, source_target_pairs={{248,0},{12,4},{0,8},{20,12},{8,16},{28,20},{16,24},{36,28},{24,32... | collective-permute-start | bytes 1572872 | tf_op jit(solution)/shard_map/ppermute | solution.py:20
  86.6 16.5 %collective-permute-start.19 = (bf16[64,4096]{1,0:T(8,128)(2,1)S(1)}, bf16[64,4096]{1,0:T(8,128)(2,1)S(1)}, u32[]{:S(2)}, u32[]{:S(2)}) collective-permute-start(bf16[64,4096]{1,0:T(8,128)(2,1)S(1)} %get-tuple-element.77), channel_id=1, source_target_pairs={{8,0},{252,4},{16,8},{4,12},{24,16},{12,20},{32,24},{20,28},{40,32... | collective-permute-start | bytes 1572872 | tf_op jit(solution)/shard_map/ppermute | solution.py:20
  91.8 8.6 %collective-permute-start.20 = (f32[64,256]{1,0:T(8,128)S(1)}, f32[64,256]{1,0:T(8,128)S(1)}, u32[]{:S(2)}, u32[]{:S(2)}) collective-permute-start(f32[64,256]{1,0:T(8,128)S(1)} %add_add_fusion), channel_id=1, source_target_pairs={{0,32},{4,36},{8,40},{12,44},{16,48},{20,52},{24,56},{28,60},{32,0... | collective-permute-start | bytes 196616 | tf_op jit(solution)/shard_map/ppermute | solution.py:24
  103.1 7.4 %collective-permute-start.21 = (f32[64,256]{1,0:T(8,128)S(1)}, f32[64,256]{1,0:T(8,128)S(1)}, u32[]{:S(2)}, u32[]{:S(2)}) collective-permute-start(f32[64,256]{1,0:T(8,128)S(1)} %add.58), channel_id=1, source_target_pairs={{0,64},{4,68},{8,72},{12,76},{16,80},{20,84},{24,88},{28,92},{32,9... | collective-permute-start | bytes 196616 | tf_op jit(solution)/shard_map/ppermute | solution.py:24
  103.3 18.5 %collective-permute-start.22 = (bf16[64,4096]{1,0:T(8,128)(2,1)S(1)}, bf16[64,4096]{1,0:T(8,128)(2,1)S(1)}, u32[]{:S(2)}, u32[]{:S(2)}) collective-permute-start(bf16[64,4096]{1,0:T(8,128)(2,1)S(1)} %add_convert_fusion.4), channel_id=1, source_target_pairs={{248,0},{12,4},{0,8},{20,12},{8,16},{28,20},{16,24},{36,28},{24,32... | collective-permute-start | bytes 1572872 | tf_op jit(solution)/shard_map/ppermute | solution.py:20
  103.4 18.4 %collective-permute-start.23 = (bf16[64,4096]{1,0:T(8,128)(2,1)S(1)}, bf16[64,4096]{1,0:T(8,128)(2,1)S(1)}, u32[]{:S(2)}, u32[]{:S(2)}) collective-permute-start(bf16[64,4096]{1,0:T(8,128)(2,1)S(1)} %get-tuple-element.93), channel_id=1, source_target_pairs={{8,0},{252,4},{16,8},{4,12},{24,16},{12,20},{32,24},{20,28},{40,32... | collective-permute-start | bytes 1572872 | tf_op jit(solution)/shard_map/ppermute | solution.py:20
  110.5 11.3 %collective-permute-start.24 = (f32[64,256]{1,0:T(8,128)S(1)}, f32[64,256]{1,0:T(8,128)S(1)}, u32[]{:S(2)}, u32[]{:S(2)}) collective-permute-start(f32[64,256]{1,0:T(8,128)S(1)} %add.60), channel_id=1, source_target_pairs={{0,128},{4,132},{8,136},{12,140},{16,144},{20,148},{24,152},{28,15... | collective-permute-start | bytes 196616 | tf_op jit(solution)/shard_map/ppermute | solution.py:24
  119.8 16.8 %collective-permute-start.27 = (bf16[64,4096]{1,0:T(8,128)(2,1)S(1)}, bf16[64,4096]{1,0:T(8,128)(2,1)S(1)}, u32[]{:S(2)}, u32[]{:S(2)}) collective-permute-start(bf16[64,4096]{1,0:T(8,128)(2,1)S(1)} %add_convert_fusion.1), channel_id=1, source_target_pairs={{0,4},{4,0},{8,12},{12,8},{16,20},{20,16},{24,28},{28,24},{32,36},... | collective-permute-start | bytes 1572872 | tf_op jit(solution)/shard_map/ppermute | solution.py:24
  122.0 14.7 %collective-permute-start.26 = (bf16[64,4096]{1,0:T(8,128)(2,1)S(1)}, bf16[64,4096]{1,0:T(8,128)(2,1)S(1)}, u32[]{:S(2)}, u32[]{:S(2)}) collective-permute-start(bf16[64,4096]{1,0:T(8,128)(2,1)S(1)} %add_convert_fusion.2), channel_id=1, source_target_pairs={{8,0},{252,4},{16,8},{4,12},{24,16},{12,20},{32,24},{20,28},{40,32... | collective-permute-start | bytes 1572872 | tf_op jit(solution)/shard_map/ppermute | solution.py:20
  127.4 14.4 %collective-permute-start.25 = (bf16[64,4096]{1,0:T(8,128)(2,1)S(1)}, bf16[64,4096]{1,0:T(8,128)(2,1)S(1)}, u32[]{:S(2)}, u32[]{:S(2)}) collective-permute-start(bf16[64,4096]{1,0:T(8,128)(2,1)S(1)} %add_convert_fusion.3), channel_id=1, source_target_pairs={{248,0},{12,4},{0,8},{20,12},{8,16},{28,20},{16,24},{36,28},{24,32... | collective-permute-start | bytes 1572872 | tf_op jit(solution)/shard_map/ppermute | solution.py:20
  127.5 8.5 %collective-permute-start.28 = (f32[64,256]{1,0:T(8,128)S(1)}, f32[64,256]{1,0:T(8,128)S(1)}, u32[]{:S(2)}, u32[]{:S(2)}) collective-permute-start(f32[64,256]{1,0:T(8,128)S(1)} %add.68), channel_id=1, source_target_pairs={{0,4},{4,0},{8,12},{12,8},{16,20},{20,16},{24,28},{28,24},{32,36},... | collective-permute-start | bytes 196616 | tf_op jit(solution)/shard_map/ppermute | solution.py:24
  (5 other events, 33.6 us)

commit v8 on v7

--- a/solution.py
+++ b/solution.py
@@ -281,13 +281,14 @@
     ys = [y, flipped(y, "feat", 1), y_far, flipped(y_far, "feat", 1)]
     out_t, grad, wgrad = middle(place, ys, packed)
 
-    parts = [flipped(wgrad, "blk", bit) for bit in (2, 4, 6)]
     to_xu, to_xv, to_mx = backward(2, listed, tile_vals, grad, [bf16] * 3)
-    to_xu, to_xv, to_mx, parts, grad = fenced(to_xu, to_xv, to_mx, parts, grad)
+    to_xu, to_xv, to_mx, wgrad, grad = fenced(to_xu, to_xv, to_mx, wgrad, grad)
     from_mx, from_xu, from_xv = flipped(to_mx, "blk", 1), stepped(to_xu, False), stepped(to_xv, True)
-    wgrad = (wgrad + parts[0]) + (parts[1] + parts[2])
     part = flipped(wgrad, "blk", 8)
     to_x, to_m, to_n = backward(1, listed, tile_vals, grad, [f32, f32, bf16])
+    part, to_m, to_x = fenced(part, to_m, to_x)
+    wgrad = wgrad + part
+    part = flipped(wgrad, "blk", 2)
     from_mx, from_xu, from_xv, to_m, to_n, to_x, grad, part = fenced(
         from_mx, from_xu, from_xv, to_m, to_n, to_x, grad, part
     )
@@ -299,9 +300,10 @@
     part = flipped(wgrad, "blk", 16)
     total, to_u, to_v, part = fenced(total, to_u, to_v, part)
     wgrad = wgrad + part
-    part = flipped(wgrad, "blk", 32)
+    part = flipped(wgrad, "blk", 4)
     from_m, from_n, to_u, to_v, part = fenced(from_m, from_n, to_u, to_v, part)
     wgrad = wgrad + part
+    wgrad = wgrad + flipped(wgrad, "blk", 32)
     part = flipped(wgrad, "blk", 1)
     from_u = stepped((to_u + from_m.astype(f32)).astype(bf16), False)
     from_v = stepped((to_v + from_n.astype(f32)).astype(bf16), True)

time: 142 us -> 142 us (level)
  starting transfers between devices: 56 us -> 49.5 us
  waiting for transfers between devices: 58.2 us -> 64.2 us
    ppermute x17 -> x16, waiting for transfers between devices: 31.6 us -> 41 us  [flipped(): lax.ppermute(block, axis, [(i, i ^ bit) for i in range(lax.axis_size(axis...]
    ppermute x17 -> x16, starting transfers between devices: 23.2 us -> 17.8 us  [flipped(): lax.ppermute(block, axis, [(i, i ^ bit) for i in range(lax.axis_size(axis...]
    ppermute x12, waiting for transfers between devices: 26.6 us -> 23.3 us  [stepped(): return lax.ppermute(block, 'blk', route)]
  transfers between devices with their start and end apart: 29 -> 28, of which waited for: 16 -> 17; matrix products, arithmetic and copies ran while one was open for 3% -> 3% of each run, Pallas kernels for 8% -> 6%
where the time goes in v8:
time: 142 us
  waiting for transfers between devices  64.2 us (45%)
  starting transfers between devices  49.5 us (35%)
  Pallas kernels  15.8 us (11%)
  local copies, waits for them, and re-layouts  6.62 us (5%)
  other arithmetic  4.21 us (3%)
  between operations  1.53 us (1%)
    ppermute x16, waiting for transfers between devices, flipped(): lax.ppermute(block, axis, [(i, i ^ bit) for i in range(lax.axis_size(axis...  41 us
    ppermute x12, starting transfers between devices, stepped(): return lax.ppermute(block, 'blk', route)  31.7 us
    ppermute x12, waiting for transfers between devices, stepped(): return lax.ppermute(block, 'blk', route)  23.3 us
    ppermute x16, starting transfers between devices, flipped(): lax.ppermute(block, axis, [(i, i ^ bit) for i in range(lax.axis_size(axis...  17.8 us
    unnamed x16, local copies, waits for them, and re-layouts  5.74 us
    pallas_call x3, Pallas kernels, backward(): pl.pallas_call(functools.partial(backward_body, wave), out_shape=tuple((p...  5.3 us
    pallas_call x3, Pallas kernels, forward(): pl.pallas_call(functools.partial(forward_body, wave, seed is not None), o...  4.85 us
    pallas_call x1, Pallas kernels, middle(): pl.pallas_call(functools.partial(middle_body, factor), out_shape=(jax.Sha...  3.37 us
  transfers between devices with their start and end apart: 28, of which 17 were waited for; matrix products, arithmetic and copies ran while one was open for 3% of the time, Pallas kernels for 6%

profile of v8, /device:TPU:4, one launch (start us, length us, event | category | flops | bytes accessed | tf_op | source)
XLA Modules:
  0.0 141.9 jit_solution(2367485558103931341)
XLA Ops:
  0.6 8.4 %collective-permute-start.1 = (bf16[64,4096]{1,0:T(8,128)(2,1)}, bf16[64,4096]{1,0:T(8,128)(2,1)S(1)}, u32[]{:S(2)}, u32[]{:S(2)}) collective-permute-start(bf16[64,4096]{1,0:T(8,128)(2,1)} %refs_2_.1), channel_id=1, source_target_pairs={{8,0},{252,4},{16,8},{4,12},{24,16},{12,20},{32,24},{20,28},{40,32... | collective-permute-start | bytes 1572872 | tf_op jit(solution)/shard_map/ppermute | solution.py:20
  13.5 2.3 %plan.1.refs_0_ = s32[904]{0:T(1024)S(1)} custom-call(s32[288]{0:T(512)S(1)} %copy-done.2, s32[288]{0:T(512)S(1)} %copy-done.3, s32[288]{0:T(512)S(1)} %copy-done.4, s32[1]{0:T(128)S(6)} %copy.11.count_ref, s32[1]{0:T(128)} %bitcast.1.sign_ref), custom_call_target="tpu_custom_call" | custom-call | bytes 6000000 | tf_op jit(solution)/shard_map/plan/pallas_call | solution.py:81
  16.9 3.7 %collective-permute-done.1.refs_3_ = bf16[64,4096]{1,0:T(8,128)(2,1)S(1)} collective-permute-done((bf16[64,4096]{1,0:T(8,128)(2,1)}, bf16[64,4096]{1,0:T(8,128)(2,1)S(1)}, u32[]{:S(2)}, u32[]{:S(2)}) %collective-permute-start.1) | collective-permute-done | bytes 524320 | tf_op jit(solution)/shard_map/ppermute | solution.py:20
  20.5 2.1 %collective-permute-done.refs_2_ = bf16[64,4096]{1,0:T(8,128)(2,1)S(1)} collective-permute-done((bf16[64,4096]{1,0:T(8,128)(2,1)}, bf16[64,4096]{1,0:T(8,128)(2,1)S(1)}, u32[]{:S(2)}, u32[]{:S(2)}) %collective-permute-start) | collective-permute-done | bytes 524320 | tf_op jit(solution)/shard_map/ppermute | solution.py:24
  22.6 3.3 %collective-permute-done.2.refs_4_ = bf16[64,4096]{1,0:T(8,128)(2,1)S(1)} collective-permute-done((bf16[64,4096]{1,0:T(8,128)(2,1)}, bf16[64,4096]{1,0:T(8,128)(2,1)S(1)}, u32[]{:S(2)}, u32[]{:S(2)}) %collective-permute-start.2) | collective-permute-done | bytes 524320 | tf_op jit(solution)/shard_map/ppermute | solution.py:20
  26.2 1.7 %collective-permute-start.4 = (bf16[64,4096]{1,0:T(8,128)(2,1)S(1)}, bf16[64,4096]{1,0:T(8,128)(2,1)S(1)}, u32[]{:S(2)}, u32[]{:S(2)}) collective-permute-start(bf16[64,4096]{1,0:T(8,128)(2,1)S(1)} %collective-permute-done.2.refs_4_), channel_id=1, source_target_pairs={{248,0},{12,4},{0,8},{20,12},{8,16},{28,20},{16,24},{36,28},{24,32... | collective-permute-start | bytes 1572872 | tf_op jit(solution)/shard_map/ppermute | solution.py:20
  28.5 3.7 %copy-done = bf16[288,128,128]{2,1,0:T(8,128)(2,1)S(1)} copy-done((bf16[288,128,128]{2,1,0:T(8,128)(2,1)S(1)}, bf16[288,128,128]{2,1,0:T(8,128)(2,1)}, u32[]{:S(2)}) %copy-start) | copy-done | bytes 9437208
  32.2 1.8 %forward_0.1.refs_5_ = f32[64,4096]{1,0:T(8,128)S(1)} custom-call(s32[904]{0:T(1024)S(1)} %plan.1.refs_0_, bf16[288,128,128]{2,1,0:T(8,128)(2,1)S(1)} %copy-done, bf16[64,4096]{1,0:T(8,128)(2,1)S(1)} %copy-done.1, bf16[64,4096]{1,0:T(8,128)(2,1)S(1)} %collective-permute-done.1.refs_3_, bf16[64,4096]{1,0:T(8,128)(2,1)S(1)} %collective-permute-done.2.refs_4_), custom_call_target="tpu_custom_call" | custom-call | bytes 6000000 | tf_op jit(solution)/shard_map/forward_0/pallas_call | solution.py:154
  33.9 4.5 %collective-permute-done.3.refs_3_ = bf16[64,4096]{1,0:T(8,128)(2,1)S(1)} collective-permute-done((bf16[64,4096]{1,0:T(8,128)(2,1)S(1)}, bf16[64,4096]{1,0:T(8,128)(2,1)S(1)}, u32[]{:S(2)}, u32[]{:S(2)}) %collective-permute-start.3) | collective-permute-done | bytes 524320 | tf_op jit(solution)/shard_map/ppermute | solution.py:20
  38.4 3.6 %collective-permute-done.4.refs_4_ = bf16[64,4096]{1,0:T(8,128)(2,1)S(1)} collective-permute-done((bf16[64,4096]{1,0:T(8,128)(2,1)S(1)}, bf16[64,4096]{1,0:T(8,128)(2,1)S(1)}, u32[]{:S(2)}, u32[]{:S(2)}) %collective-permute-start.4) | collective-permute-done | bytes 524320 | tf_op jit(solution)/shard_map/ppermute | solution.py:20
  42.1 5.3 %collective-permute-start.5 = (bf16[64,4096]{1,0:T(8,128)(2,1)S(1)}, bf16[64,4096]{1,0:T(8,128)(2,1)S(1)}, u32[]{:S(2)}, u32[]{:S(2)}) collective-permute-start(bf16[64,4096]{1,0:T(8,128)(2,1)S(1)} %collective-permute-done.refs_2_), channel_id=1, source_target_pairs={{8,0},{252,4},{16,8},{4,12},{24,16},{12,20},{32,24},{20,28},{40,32... | collective-permute-start | bytes 1572872 | tf_op jit(solution)/shard_map/ppermute | solution.py:20
  49.0 4.7 %collective-permute-done.7.refs_4_ = bf16[64,4096]{1,0:T(8,128)(2,1)S(1)} collective-permute-done((bf16[64,4096]{1,0:T(8,128)(2,1)S(1)}, bf16[64,4096]{1,0:T(8,128)(2,1)S(1)}, u32[]{:S(2)}, u32[]{:S(2)}) %collective-permute-start.7) | collective-permute-done | bytes 524320 | tf_op jit(solution)/shard_map/ppermute | solution.py:24
  53.6 3.3 %collective-permute-done.6.refs_3_ = bf16[64,4096]{1,0:T(8,128)(2,1)S(1)} collective-permute-done((bf16[64,4096]{1,0:T(8,128)(2,1)S(1)}, bf16[64,4096]{1,0:T(8,128)(2,1)S(1)}, u32[]{:S(2)}, u32[]{:S(2)}) %collective-permute-start.6) | collective-permute-done | bytes 524320 | tf_op jit(solution)/shard_map/ppermute | solution.py:20
  59.7 11.2 %collective-permute-done.10.refs_2_ = bf16[64,4096]{1,0:T(8,128)(2,1)S(1)} collective-permute-done((bf16[64,4096]{1,0:T(8,128)(2,1)S(1)}, bf16[64,4096]{1,0:T(8,128)(2,1)S(1)}, u32[]{:S(2)}, u32[]{:S(2)}) %collective-permute-start.10) | collective-permute-done | bytes 524320 | tf_op jit(solution)/shard_map/ppermute | solution.py:24
  70.8 1.9 %collective-permute-done.11.refs_3_ = bf16[64,4096]{1,0:T(8,128)(2,1)S(1)} collective-permute-done((bf16[64,4096]{1,0:T(8,128)(2,1)S(1)}, bf16[64,4096]{1,0:T(8,128)(2,1)S(1)}, u32[]{:S(2)}, u32[]{:S(2)}) %collective-permute-start.11) | collective-permute-done | bytes 524320 | tf_op jit(solution)/shard_map/ppermute | solution.py:24
  72.7 3.4 %middle.1 = (bf16[64,4096]{1,0:T(8,128)(2,1)}, bf16[64,4096]{1,0:T(8,128)(2,1)S(1)}, f32[64,256]{1,0:T(8,128)S(1)}) custom-call(s32[1]{0:T(128)} %bitcast.place_ref, bf16[64,4096]{1,0:T(8,128)(2,1)S(1)} %forward_2.1.refs_0_, bf16[64,4096]{1,0:T(8,128)(2,1)S(1)} %collective-permute-done.9.refs_1_, bf16[64,4096]{1,0:T(8,128)(2,1)S(1)} %collective-permute-done.10.refs_2_, ...), custom_call_target="tpu_custom_call" | custom-call | bytes 6000000 | tf_op jit(solution)/shard_map/middle/pallas_call | solution.py:243
  76.1 1.7 %backward_2.1 = (bf16[64,4096]{1,0:T(8,128)(2,1)S(1)}, bf16[64,4096]{1,0:T(8,128)(2,1)S(1)}, bf16[64,4096]{1,0:T(8,128)(2,1)S(1)}) custom-call(s32[904]{0:T(1024)S(1)} %plan.1.refs_0_, bf16[288,128,128]{2,1,0:T(8,128)(2,1)S(1)} %bitcast.3, bf16[64,4096]{1,0:T(8,128)(2,1)S(1)} %get-tuple-element.87.refs_2_), custom_call_target="tpu_custom_call" | custom-call | bytes 6000000 | tf_op jit(solution)/shard_map/backward_2/pallas_call | solution.py:195
  77.8 5.6 %collective-permute-start.14 = (bf16[64,4096]{1,0:T(8,128)(2,1)S(1)}, bf16[64,4096]{1,0:T(8,128)(2,1)S(1)}, u32[]{:S(2)}, u32[]{:S(2)}) collective-permute-start(bf16[64,4096]{1,0:T(8,128)(2,1)S(1)} %get-tuple-element.76), channel_id=1, source_target_pairs={{0,4},{4,0},{8,12},{12,8},{16,20},{20,16},{24,28},{28,24},{32,36},... | collective-permute-start | bytes 1572872 | tf_op jit(solution)/shard_map/ppermute | solution.py:24
  83.4 5.3 %collective-permute-start.16 = (bf16[64,4096]{1,0:T(8,128)(2,1)S(1)}, bf16[64,4096]{1,0:T(8,128)(2,1)S(1)}, u32[]{:S(2)}, u32[]{:S(2)}) collective-permute-start(bf16[64,4096]{1,0:T(8,128)(2,1)S(1)} %get-tuple-element.78), channel_id=1, source_target_pairs={{8,0},{252,4},{16,8},{4,12},{24,16},{12,20},{32,24},{20,28},{40,32... | collective-permute-start | bytes 1572872 | tf_op jit(solution)/shard_map/ppermute | solution.py:20
  88.8 1.7 %backward_1.1 = (f32[64,4096]{1,0:T(8,128)S(1)}, f32[64,4096]{1,0:T(8,128)S(1)}, bf16[64,4096]{1,0:T(8,128)(2,1)S(1)}) custom-call(s32[904]{0:T(1024)S(1)} %plan.1.refs_0_, bf16[288,128,128]{2,1,0:T(8,128)(2,1)S(1)} %bitcast.3, bf16[64,4096]{1,0:T(8,128)(2,1)S(1)} %get-tuple-element.87.refs_2_), custom_call_target="tpu_custom_call" | custom-call | bytes 6000000 | tf_op jit(solution)/shard_map/backward_1/pallas_call | solution.py:195
  90.5 5.2 %collective-permute-done.17 = f32[64,256]{1,0:T(8,128)S(1)} collective-permute-done((f32[64,256]{1,0:T(8,128)S(1)}, f32[64,256]{1,0:T(8,128)S(1)}, u32[]{:S(2)}, u32[]{:S(2)}) %collective-permute-start.17) | collective-permute-done | bytes 65568 | tf_op jit(solution)/shard_map/ppermute | solution.py:24
  95.8 4.3 %collective-permute-done.18 = f32[64,256]{1,0:T(8,128)S(1)} collective-permute-done((f32[64,256]{1,0:T(8,128)S(1)}, f32[64,256]{1,0:T(8,128)S(1)}, u32[]{:S(2)}, u32[]{:S(2)}) %collective-permute-start.18) | collective-permute-done | bytes 65568 | tf_op jit(solution)/shard_map/ppermute | solution.py:24
  100.7 5.3 %collective-permute-start.21 = (bf16[64,4096]{1,0:T(8,128)(2,1)S(1)}, bf16[64,4096]{1,0:T(8,128)(2,1)S(1)}, u32[]{:S(2)}, u32[]{:S(2)}) collective-permute-start(bf16[64,4096]{1,0:T(8,128)(2,1)S(1)} %get-tuple-element.95), channel_id=1, source_target_pairs={{8,0},{252,4},{16,8},{4,12},{24,16},{12,20},{32,24},{20,28},{40,32... | collective-permute-start | bytes 1572872 | tf_op jit(solution)/shard_map/ppermute | solution.py:20
  106.1 1.9 %backward_0.1 = (f32[64,4096]{1,0:T(8,128)S(1)}, f32[64,4096]{1,0:T(8,128)S(1)}, f32[64,4096]{1,0:T(8,128)S(1)}) custom-call(s32[904]{0:T(1024)S(1)} %plan.1.refs_0_, bf16[288,128,128]{2,1,0:T(8,128)(2,1)S(1)} %bitcast.3, bf16[64,4096]{1,0:T(8,128)(2,1)S(1)} %get-tuple-element.87.refs_2_), custom_call_target="tpu_custom_call" | custom-call | bytes 6000000 | tf_op jit(solution)/shard_map/backward_0/pallas_call | solution.py:195
  108.4 2.2 %collective-permute-start.25 = (bf16[64,4096]{1,0:T(8,128)(2,1)S(1)}, bf16[64,4096]{1,0:T(8,128)(2,1)S(1)}, u32[]{:S(2)}, u32[]{:S(2)}) collective-permute-start(bf16[64,4096]{1,0:T(8,128)(2,1)S(1)} %add_convert_fusion.1), channel_id=1, source_target_pairs={{0,4},{4,0},{8,12},{12,8},{16,20},{20,16},{24,28},{28,24},{32,36},... | collective-permute-start | bytes 1572872 | tf_op jit(solution)/shard_map/ppermute | solution.py:24
  110.6 4.2 %collective-permute-done.22 = f32[64,256]{1,0:T(8,128)S(1)} collective-permute-done((f32[64,256]{1,0:T(8,128)S(1)}, f32[64,256]{1,0:T(8,128)S(1)}, u32[]{:S(2)}, u32[]{:S(2)}) %collective-permute-start.22) | collective-permute-done | bytes 65568 | tf_op jit(solution)/shard_map/ppermute | solution.py:24
  114.8 3.5 %collective-permute-done.20 = bf16[64,4096]{1,0:T(8,128)(2,1)S(1)} collective-permute-done((bf16[64,4096]{1,0:T(8,128)(2,1)S(1)}, bf16[64,4096]{1,0:T(8,128)(2,1)S(1)}, u32[]{:S(2)}, u32[]{:S(2)}) %collective-permute-start.20) | collective-permute-done | bytes 524320 | tf_op jit(solution)/shard_map/ppermute | solution.py:20
  118.4 5.1 %collective-permute-start.24 = (bf16[64,4096]{1,0:T(8,128)(2,1)S(1)}, bf16[64,4096]{1,0:T(8,128)(2,1)S(1)}, u32[]{:S(2)}, u32[]{:S(2)}) collective-permute-start(bf16[64,4096]{1,0:T(8,128)(2,1)S(1)} %add_convert_fusion.2), channel_id=1, source_target_pairs={{8,0},{252,4},{16,8},{4,12},{24,16},{12,20},{32,24},{20,28},{40,32... | collective-permute-start | bytes 1572872 | tf_op jit(solution)/shard_map/ppermute | solution.py:20
  123.7 3.0 %collective-permute-start.26 = (f32[64,256]{1,0:T(8,128)S(1)}, f32[64,256]{1,0:T(8,128)S(1)}, u32[]{:S(2)}, u32[]{:S(2)}) collective-permute-start(f32[64,256]{1,0:T(8,128)S(1)} %add.63), channel_id=1, source_target_pairs={{0,128},{4,132},{8,136},{12,140},{16,144},{20,148},{24,152},{28,15... | collective-permute-start | bytes 196616 | tf_op jit(solution)/shard_map/ppermute | solution.py:24
  126.8 5.2 %collective-permute-done.26 = f32[64,256]{1,0:T(8,128)S(1)} collective-permute-done((f32[64,256]{1,0:T(8,128)S(1)}, f32[64,256]{1,0:T(8,128)S(1)}, u32[]{:S(2)}, u32[]{:S(2)}) %collective-permute-start.26) | collective-permute-done | bytes 65568 | tf_op jit(solution)/shard_map/ppermute | solution.py:24
  132.0 5.0 %collective-permute-start.27 = (f32[64,256]{1,0:T(8,128)S(1)}, f32[64,256]{1,0:T(8,128)S(1)}, u32[]{:S(2)}, u32[]{:S(2)}) collective-permute-start(f32[64,256]{1,0:T(8,128)S(1)} %add.64), channel_id=1, source_target_pairs={{0,4},{4,0},{8,12},{12,8},{16,20},{20,16},{24,28},{28,24},{32,36},... | collective-permute-start | bytes 196616 | tf_op jit(solution)/shard_map/ppermute | solution.py:24
  137.0 2.2 %collective-permute-done.27 = f32[64,256]{1,0:T(8,128)S(1)} collective-permute-done((f32[64,256]{1,0:T(8,128)S(1)}, f32[64,256]{1,0:T(8,128)S(1)}, u32[]{:S(2)}, u32[]{:S(2)}) %collective-permute-start.27) | collective-permute-done | bytes 65568 | tf_op jit(solution)/shard_map/ppermute | solution.py:24
  (65 shorter events, 14.0 us)
Async XLA Ops:
  0.6 27.8 %copy-start.1 = (bf16[64,4096]{1,0:T(8,128)(2,1)S(1)}, bf16[64,4096]{1,0:T(8,128)(2,1)}, u32[]{:S(2)}) copy-start(bf16[64,4096]{1,0:T(8,128)(2,1)} %refs_2_.1) | copy-start | bytes 1572868
  0.6 19.9 %collective-permute-start.1 = (bf16[64,4096]{1,0:T(8,128)(2,1)}, bf16[64,4096]{1,0:T(8,128)(2,1)S(1)}, u32[]{:S(2)}, u32[]{:S(2)}) collective-permute-start(bf16[64,4096]{1,0:T(8,128)(2,1)} %refs_2_.1), channel_id=1, source_target_pairs={{8,0},{252,4},{16,8},{4,12},{24,16},{12,20},{32,24},{20,28},{40,32... | collective-permute-start | bytes 1572872 | tf_op jit(solution)/shard_map/ppermute | solution.py:20
  9.0 13.6 %collective-permute-start = (bf16[64,4096]{1,0:T(8,128)(2,1)}, bf16[64,4096]{1,0:T(8,128)(2,1)S(1)}, u32[]{:S(2)}, u32[]{:S(2)}) collective-permute-start(bf16[64,4096]{1,0:T(8,128)(2,1)} %refs_2_.1), channel_id=1, source_target_pairs={{0,4},{4,0},{8,12},{12,8},{16,20},{20,16},{24,28},{28,24},{32,36},... | collective-permute-start | bytes 1572872 | tf_op jit(solution)/shard_map/ppermute | solution.py:24
  9.0 16.9 %collective-permute-start.2 = (bf16[64,4096]{1,0:T(8,128)(2,1)}, bf16[64,4096]{1,0:T(8,128)(2,1)S(1)}, u32[]{:S(2)}, u32[]{:S(2)}) collective-permute-start(bf16[64,4096]{1,0:T(8,128)(2,1)} %refs_2_.1), channel_id=1, source_target_pairs={{248,0},{12,4},{0,8},{20,12},{8,16},{28,20},{16,24},{36,28},{24,32... | collective-permute-start | bytes 1572872 | tf_op jit(solution)/shard_map/ppermute | solution.py:20
  25.9 12.5 %collective-permute-start.3 = (bf16[64,4096]{1,0:T(8,128)(2,1)S(1)}, bf16[64,4096]{1,0:T(8,128)(2,1)S(1)}, u32[]{:S(2)}, u32[]{:S(2)}) collective-permute-start(bf16[64,4096]{1,0:T(8,128)(2,1)S(1)} %collective-permute-done.1.refs_3_), channel_id=1, source_target_pairs={{8,0},{252,4},{16,8},{4,12},{24,16},{12,20},{32,24},{20,28},{40,32... | collective-permute-start | bytes 1572872 | tf_op jit(solution)/shard_map/ppermute | solution.py:20
  26.2 15.8 %collective-permute-start.4 = (bf16[64,4096]{1,0:T(8,128)(2,1)S(1)}, bf16[64,4096]{1,0:T(8,128)(2,1)S(1)}, u32[]{:S(2)}, u32[]{:S(2)}) collective-permute-start(bf16[64,4096]{1,0:T(8,128)(2,1)S(1)} %collective-permute-done.2.refs_4_), channel_id=1, source_target_pairs={{248,0},{12,4},{0,8},{20,12},{8,16},{28,20},{16,24},{36,28},{24,32... | collective-permute-start | bytes 1572872 | tf_op jit(solution)/shard_map/ppermute | solution.py:20
  28.0 21.0 %collective-permute-start.8 = (bf16[64,4352]{1,0:T(8,128)(2,1)S(1)}, bf16[64,4352]{1,0:T(8,128)(2,1)S(1)}, u32[]{:S(2)}, u32[]{:S(2)}) collective-permute-start(bf16[64,4352]{1,0:T(8,128)(2,1)S(1)} %pad_maximum_fusion.refs_4_), channel_id=1, source_target_pairs={{0,2},{1,3},{2,0},{3,1},{4,6},{5,7},{6,4},{7,5},{8,10},{9,11},{10,... | collective-permute-start | bytes 1671176 | tf_op jit(solution)/shard_map/ppermute | solution.py:24
  42.1 11.6 %collective-permute-start.7 = (bf16[64,4096]{1,0:T(8,128)(2,1)S(1)}, bf16[64,4096]{1,0:T(8,128)(2,1)S(1)}, u32[]{:S(2)}, u32[]{:S(2)}) collective-permute-start(bf16[64,4096]{1,0:T(8,128)(2,1)S(1)} %collective-permute-done.3.refs_3_), channel_id=1, source_target_pairs={{0,4},{4,0},{8,12},{12,8},{16,20},{20,16},{24,28},{28,24},{32,36},... | collective-permute-start | bytes 1572872 | tf_op jit(solution)/shard_map/ppermute | solution.py:24
  42.1 14.9 %collective-permute-start.6 = (bf16[64,4096]{1,0:T(8,128)(2,1)S(1)}, bf16[64,4096]{1,0:T(8,128)(2,1)S(1)}, u32[]{:S(2)}, u32[]{:S(2)}) collective-permute-start(bf16[64,4096]{1,0:T(8,128)(2,1)S(1)} %collective-permute-done.refs_2_), channel_id=1, source_target_pairs={{248,0},{12,4},{0,8},{20,12},{8,16},{28,20},{16,24},{36,28},{24,32... | collective-permute-start | bytes 1572872 | tf_op jit(solution)/shard_map/ppermute | solution.py:20
  42.1 14.9 %collective-permute-start.5 = (bf16[64,4096]{1,0:T(8,128)(2,1)S(1)}, bf16[64,4096]{1,0:T(8,128)(2,1)S(1)}, u32[]{:S(2)}, u32[]{:S(2)}) collective-permute-start(bf16[64,4096]{1,0:T(8,128)(2,1)S(1)} %collective-permute-done.refs_2_), channel_id=1, source_target_pairs={{8,0},{252,4},{16,8},{4,12},{24,16},{12,20},{32,24},{20,28},{40,32... | collective-permute-start | bytes 1572872 | tf_op jit(solution)/shard_map/ppermute | solution.py:20
  47.4 28.7 %slice-start = ((s8[9437184]{0:T(1024)(128)(4,1)}), s8[4194304]{0:T(1024)(128)(4,1)S(1)}, s32[]{:S(2)}) async-start(s8[9437184]{0:T(1024)(128)(4,1)} %bitcast.2), calls=%async_computation | async-start | bytes 8388608
  47.4 28.7 %slice-start.1 = ((s8[9437184]{0:T(1024)(128)(4,1)}), s8[4194304]{0:T(1024)(128)(4,1)S(1)}, s32[]{:S(2)}) async-start(s8[9437184]{0:T(1024)(128)(4,1)} %bitcast.2), calls=%async_computation.1 | async-start | bytes 8388608
  48.9 27.2 %slice-start.2 = ((s8[9437184]{0:T(1024)(128)(4,1)}), s8[1048576]{0:T(1024)(128)(4,1)S(1)}, s32[]{:S(2)}) async-start(s8[9437184]{0:T(1024)(128)(4,1)} %bitcast.2), calls=%async_computation.2 | async-start | bytes 2097152
  58.6 12.3 %collective-permute-start.10 = (bf16[64,4096]{1,0:T(8,128)(2,1)S(1)}, bf16[64,4096]{1,0:T(8,128)(2,1)S(1)}, u32[]{:S(2)}, u32[]{:S(2)}) collective-permute-start(bf16[64,4096]{1,0:T(8,128)(2,1)S(1)} %forward_2.1.refs_0_), channel_id=1, source_target_pairs={{0,2},{1,3},{2,0},{3,1},{4,6},{5,7},{6,4},{7,5},{8,10},{9,11},{10,... | collective-permute-start | bytes 1572872 | tf_op jit(solution)/shard_map/ppermute | solution.py:24
  59.1 11.7 %collective-permute-start.12 = (bf16[64,4352]{1,0:T(8,128)(2,1)S(1)}, bf16[64,4352]{1,0:T(8,128)(2,1)S(1)}, u32[]{:S(2)}, u32[]{:S(2)}) collective-permute-start(bf16[64,4352]{1,0:T(8,128)(2,1)S(1)} %pad_maximum_fusion.refs_4_), channel_id=1, source_target_pairs={{0,1},{1,0},{2,3},{3,2},{4,5},{5,4},{6,7},{7,6},{8,9},{9,8},{10,11... | collective-permute-start | bytes 1671176 | tf_op jit(solution)/shard_map/ppermute | solution.py:24
  59.1 11.7 %collective-permute-start.13 = (bf16[64,4352]{1,0:T(8,128)(2,1)S(1)}, bf16[64,4352]{1,0:T(8,128)(2,1)S(1)}, u32[]{:S(2)}, u32[]{:S(2)}) collective-permute-start(bf16[64,4352]{1,0:T(8,128)(2,1)S(1)} %collective-permute-done.8.refs_6_), channel_id=1, source_target_pairs={{0,1},{1,0},{2,3},{3,2},{4,5},{5,4},{6,7},{7,6},{8,9},{9,8},{10,11... | collective-permute-start | bytes 1671176 | tf_op jit(solution)/shard_map/ppermute | solution.py:24
  59.7 11.2 %collective-permute-start.9 = (bf16[64,4096]{1,0:T(8,128)(2,1)S(1)}, bf16[64,4096]{1,0:T(8,128)(2,1)S(1)}, u32[]{:S(2)}, u32[]{:S(2)}) collective-permute-start(bf16[64,4096]{1,0:T(8,128)(2,1)S(1)} %forward_2.1.refs_0_), channel_id=1, source_target_pairs={{0,1},{1,0},{2,3},{3,2},{4,5},{5,4},{6,7},{7,6},{8,9},{9,8},{10,11... | collective-permute-start | bytes 1572872 | tf_op jit(solution)/shard_map/ppermute | solution.py:24
  70.8 1.9 %collective-permute-start.11 = (bf16[64,4096]{1,0:T(8,128)(2,1)S(1)}, bf16[64,4096]{1,0:T(8,128)(2,1)S(1)}, u32[]{:S(2)}, u32[]{:S(2)}) collective-permute-start(bf16[64,4096]{1,0:T(8,128)(2,1)S(1)} %collective-permute-done.10.refs_2_), channel_id=1, source_target_pairs={{0,1},{1,0},{2,3},{3,2},{4,5},{5,4},{6,7},{7,6},{8,9},{9,8},{10,11... | collective-permute-start | bytes 1572872 | tf_op jit(solution)/shard_map/ppermute | solution.py:24
  77.8 22.2 %collective-permute-start.14 = (bf16[64,4096]{1,0:T(8,128)(2,1)S(1)}, bf16[64,4096]{1,0:T(8,128)(2,1)S(1)}, u32[]{:S(2)}, u32[]{:S(2)}) collective-permute-start(bf16[64,4096]{1,0:T(8,128)(2,1)S(1)} %get-tuple-element.76), channel_id=1, source_target_pairs={{0,4},{4,0},{8,12},{12,8},{16,20},{20,16},{24,28},{28,24},{32,36},... | collective-permute-start | bytes 1572872 | tf_op jit(solution)/shard_map/ppermute | solution.py:24
  83.4 17.0 %collective-permute-start.15 = (bf16[64,4096]{1,0:T(8,128)(2,1)S(1)}, bf16[64,4096]{1,0:T(8,128)(2,1)S(1)}, u32[]{:S(2)}, u32[]{:S(2)}) collective-permute-start(bf16[64,4096]{1,0:T(8,128)(2,1)S(1)} %get-tuple-element.77), channel_id=1, source_target_pairs={{248,0},{12,4},{0,8},{20,12},{8,16},{28,20},{16,24},{36,28},{24,32... | collective-permute-start | bytes 1572872 | tf_op jit(solution)/shard_map/ppermute | solution.py:20
  83.4 17.0 %collective-permute-start.16 = (bf16[64,4096]{1,0:T(8,128)(2,1)S(1)}, bf16[64,4096]{1,0:T(8,128)(2,1)S(1)}, u32[]{:S(2)}, u32[]{:S(2)}) collective-permute-start(bf16[64,4096]{1,0:T(8,128)(2,1)S(1)} %get-tuple-element.78), channel_id=1, source_target_pairs={{8,0},{252,4},{16,8},{4,12},{24,16},{12,20},{32,24},{20,28},{40,32... | collective-permute-start | bytes 1572872 | tf_op jit(solution)/shard_map/ppermute | solution.py:20
  88.8 6.9 %collective-permute-start.17 = (f32[64,256]{1,0:T(8,128)S(1)}, f32[64,256]{1,0:T(8,128)S(1)}, u32[]{:S(2)}, u32[]{:S(2)}) collective-permute-start(f32[64,256]{1,0:T(8,128)S(1)} %get-tuple-element.79), channel_id=1, source_target_pairs={{0,32},{4,36},{8,40},{12,44},{16,48},{20,52},{24,56},{28,60},{32,0... | collective-permute-start | bytes 196616 | tf_op jit(solution)/shard_map/ppermute | solution.py:24
  95.7 4.4 %collective-permute-start.18 = (f32[64,256]{1,0:T(8,128)S(1)}, f32[64,256]{1,0:T(8,128)S(1)}, u32[]{:S(2)}, u32[]{:S(2)}) collective-permute-start(f32[64,256]{1,0:T(8,128)S(1)} %add.52), channel_id=1, source_target_pairs={{0,8},{4,12},{8,0},{12,4},{16,24},{20,28},{24,16},{28,20},{32,40},... | collective-permute-start | bytes 196616 | tf_op jit(solution)/shard_map/ppermute | solution.py:24
  100.4 7.6 %collective-permute-start.19 = (f32[64,256]{1,0:T(8,128)S(1)}, f32[64,256]{1,0:T(8,128)S(1)}, u32[]{:S(2)}, u32[]{:S(2)}) collective-permute-start(f32[64,256]{1,0:T(8,128)S(1)} %add.53), channel_id=1, source_target_pairs={{0,64},{4,68},{8,72},{12,76},{16,80},{20,84},{24,88},{28,92},{32,9... | collective-permute-start | bytes 196616 | tf_op jit(solution)/shard_map/ppermute | solution.py:24
  100.6 17.6 %collective-permute-start.20 = (bf16[64,4096]{1,0:T(8,128)(2,1)S(1)}, bf16[64,4096]{1,0:T(8,128)(2,1)S(1)}, u32[]{:S(2)}, u32[]{:S(2)}) collective-permute-start(bf16[64,4096]{1,0:T(8,128)(2,1)S(1)} %add_convert_fusion.4), channel_id=1, source_target_pairs={{248,0},{12,4},{0,8},{20,12},{8,16},{28,20},{16,24},{36,28},{24,32... | collective-permute-start | bytes 1572872 | tf_op jit(solution)/shard_map/ppermute | solution.py:20
  100.7 17.5 %collective-permute-start.21 = (bf16[64,4096]{1,0:T(8,128)(2,1)S(1)}, bf16[64,4096]{1,0:T(8,128)(2,1)S(1)}, u32[]{:S(2)}, u32[]{:S(2)}) collective-permute-start(bf16[64,4096]{1,0:T(8,128)(2,1)S(1)} %get-tuple-element.95), channel_id=1, source_target_pairs={{8,0},{252,4},{16,8},{4,12},{24,16},{12,20},{32,24},{20,28},{40,32... | collective-permute-start | bytes 1572872 | tf_op jit(solution)/shard_map/ppermute | solution.py:20
  108.0 6.7 %collective-permute-start.22 = (f32[64,256]{1,0:T(8,128)S(1)}, f32[64,256]{1,0:T(8,128)S(1)}, u32[]{:S(2)}, u32[]{:S(2)}) collective-permute-start(f32[64,256]{1,0:T(8,128)S(1)} %add.55), channel_id=1, source_target_pairs={{0,16},{4,20},{8,24},{12,28},{16,0},{20,4},{24,8},{28,12},{32,48},... | collective-permute-start | bytes 196616 | tf_op jit(solution)/shard_map/ppermute | solution.py:24
  108.4 31.5 %collective-permute-start.25 = (bf16[64,4096]{1,0:T(8,128)(2,1)S(1)}, bf16[64,4096]{1,0:T(8,128)(2,1)S(1)}, u32[]{:S(2)}, u32[]{:S(2)}) collective-permute-start(bf16[64,4096]{1,0:T(8,128)(2,1)S(1)} %add_convert_fusion.1), channel_id=1, source_target_pairs={{0,4},{4,0},{8,12},{12,8},{16,20},{20,16},{24,28},{28,24},{32,36},... | collective-permute-start | bytes 1572872 | tf_op jit(solution)/shard_map/ppermute | solution.py:24
  118.4 21.5 %collective-permute-start.24 = (bf16[64,4096]{1,0:T(8,128)(2,1)S(1)}, bf16[64,4096]{1,0:T(8,128)(2,1)S(1)}, u32[]{:S(2)}, u32[]{:S(2)}) collective-permute-start(bf16[64,4096]{1,0:T(8,128)(2,1)S(1)} %add_convert_fusion.2), channel_id=1, source_target_pairs={{8,0},{252,4},{16,8},{4,12},{24,16},{12,20},{32,24},{20,28},{40,32... | collective-permute-start | bytes 1572872 | tf_op jit(solution)/shard_map/ppermute | solution.py:20
  123.6 17.2 %collective-permute-start.23 = (bf16[64,4096]{1,0:T(8,128)(2,1)S(1)}, bf16[64,4096]{1,0:T(8,128)(2,1)S(1)}, u32[]{:S(2)}, u32[]{:S(2)}) collective-permute-start(bf16[64,4096]{1,0:T(8,128)(2,1)S(1)} %add_convert_fusion.3), channel_id=1, source_target_pairs={{248,0},{12,4},{0,8},{20,12},{8,16},{28,20},{16,24},{36,28},{24,32... | collective-permute-start | bytes 1572872 | tf_op jit(solution)/shard_map/ppermute | solution.py:20
  123.7 8.3 %collective-permute-start.26 = (f32[64,256]{1,0:T(8,128)S(1)}, f32[64,256]{1,0:T(8,128)S(1)}, u32[]{:S(2)}, u32[]{:S(2)}) collective-permute-start(f32[64,256]{1,0:T(8,128)S(1)} %add.63), channel_id=1, source_target_pairs={{0,128},{4,132},{8,136},{12,140},{16,144},{20,148},{24,152},{28,15... | collective-permute-start | bytes 196616 | tf_op jit(solution)/shard_map/ppermute | solution.py:24
  132.0 7.2 %collective-permute-start.27 = (f32[64,256]{1,0:T(8,128)S(1)}, f32[64,256]{1,0:T(8,128)S(1)}, u32[]{:S(2)}, u32[]{:S(2)}) collective-permute-start(f32[64,256]{1,0:T(8,128)S(1)} %add.64), channel_id=1, source_target_pairs={{0,4},{4,0},{8,12},{12,8},{16,20},{20,16},{24,28},{28,24},{32,36},... | collective-permute-start | bytes 196616 | tf_op jit(solution)/shard_map/ppermute | solution.py:24
  (4 other events, 5.7 us)

commit v9 on v3

--- a/solution.py
+++ b/solution.py
@@ -10,7 +10,7 @@
 
 REACH = 4
 GROUP = 8
-WAVES = [[0, 1, 2, -2], [4, -4], [3, -1, -3]]
+WAVES = [[0, 2, -2], [1, 4, -4], [3, -1, -3]]
 MIB = 1 << 20
 
 
@@ -270,10 +270,10 @@
     listed = plan(tile_row, tile_col, tile_off, tile_count, sign)
     x, u, v, listed, own = fenced(x, u, v, listed, own)
     m, n, far = stepped(u, True), stepped(v, False), flipped(own, "feat", 2)
-    y = forward(0, listed, tile_vals, [x_t, x, u, v], None, f32)
+    y = forward(0, listed, tile_vals, [x_t, u, v], None, f32)
     m, n, y, x = fenced(m, n, y, x)
     mx, xu, xv = flipped(m, "blk", 1), stepped(x, True), stepped(x, False)
-    y = forward(1, listed, tile_vals, [m, n], y, f32)
+    y = forward(1, listed, tile_vals, [x, m, n], y, f32)
     xu, xv, mx, y, far, own = fenced(xu, xv, mx, y, far, own)
     packed = [own, flipped(own, "feat", 1), far, flipped(far, "feat", 1)]
     y = forward(2, listed, tile_vals, [xu, xv, mx], y, bf16)
@@ -287,11 +287,11 @@
     from_mx, from_xu, from_xv = flipped(to_mx, "blk", 1), stepped(to_xu, False), stepped(to_xv, True)
     wgrad = wgrad + part
     part = flipped(wgrad, "blk", 8)
-    to_m, to_n = backward(1, listed, tile_vals, grad, [f32, bf16])
+    to_x, to_m, to_n = backward(1, listed, tile_vals, grad, [f32, f32, bf16])
     part, to_m, grad = fenced(part, to_m, grad)
     wgrad = wgrad + part
     part = flipped(wgrad, "blk", 16)
-    total, to_x, to_u, to_v = backward(0, listed, tile_vals, grad, [f32] * 4)
+    total, to_u, to_v = backward(0, listed, tile_vals, grad, [f32] * 3)
     from_mx, from_xu, from_xv, to_m, to_n, total, to_x, to_u, to_v, part = fenced(
         from_mx, from_xu, from_xv, to_m, to_n, total, to_x, to_u, to_v, part
     )
@@ -299,10 +299,10 @@
     from_n = stepped(to_n, True)
     to_x = (to_x + from_xu.astype(f32) + from_xv.astype(f32)).astype(bf16)
     wgrad = wgrad + part
-    wgrad = wgrad + flipped(wgrad, "blk", 32)
+    wgrad = wgrad + flipped(wgrad, "blk", 48)
     wgrad = wgrad + flipped(wgrad, "blk", 1)
     from_m, from_n, to_x, to_u, to_v, wgrad = fenced(from_m, from_n, to_x, to_u, to_v, wgrad)
-    part = flipped(wgrad, "blk", 4)
+    part = flipped(wgrad, "blk", 6)
     from_u = stepped((to_u + from_m.astype(f32)).astype(bf16), False)
     from_v = stepped((to_v + from_n.astype(f32)).astype(bf16), True)
     from_x = flipped(to_x, "blk", 1)

time: 142 us -> 141 us (level); the launches traced: 144 us -> 139 us
  Pallas kernels: 31.7 us -> 21.1 us
  starting transfers between devices: 44.6 us -> 48.7 us
    ppermute x16, waiting for transfers between devices: 29.8 us -> 37.1 us  [flipped(): lax.ppermute(block, axis, [(i, i ^ bit) for i in range(lax.axis_size(axis...]
    ppermute x12, waiting for transfers between devices: 25.4 us -> 19.4 us  [stepped(): return lax.ppermute(block, 'blk', route)]
    ppermute x16, starting transfers between devices: 12.8 us -> 17.7 us  [flipped(): lax.ppermute(block, axis, [(i, i ^ bit) for i in range(lax.axis_size(axis...]
    pallas_call x3, Pallas kernels: 11.5 us -> 7.08 us  [forward(): pl.pallas_call(functools.partial(forward_body, wave, seed is not None), o...]
    pallas_call x3, Pallas kernels: 11.7 us -> 7.43 us  [backward(): pl.pallas_call(functools.partial(backward_body, wave), out_shape=tuple((p...]
    pallas_call x1, Pallas kernels: 5.11 us -> 3.22 us  [plan(): pl.pallas_call(functools.partial(plan_body, cap), out_shape=jax.ShapeDtyp...]
  transfers between devices with their start and end apart: 28 -> 28, of which waited for: 15 -> 15; matrix products, arithmetic and copies ran while one was open for 3% -> 3% of each run, Pallas kernels for 17% -> 11%
where the time goes in v9:
time: 141 us; the launch traced here: 139 us
  waiting for transfers between devices  56.4 us (40%)
  starting transfers between devices  48.7 us (35%)
  Pallas kernels  21.1 us (15%)
  local copies, waits for them, and re-layouts  6.62 us (5%)
  other arithmetic  4.15 us (3%)
  between operations  1.55 us (1%)
    ppermute x16, waiting for transfers between devices, flipped(): lax.ppermute(block, axis, [(i, i ^ bit) for i in range(lax.axis_size(axis...  37.1 us
    ppermute x12, starting transfers between devices, stepped(): return lax.ppermute(block, 'blk', route)  31.1 us
    ppermute x12, waiting for transfers between devices, stepped(): return lax.ppermute(block, 'blk', route)  19.4 us
    ppermute x16, starting transfers between devices, flipped(): lax.ppermute(block, axis, [(i, i ^ bit) for i in range(lax.axis_size(axis...  17.7 us
    pallas_call x3, Pallas kernels, backward(): pl.pallas_call(functools.partial(backward_body, wave), out_shape=tuple((p...  7.43 us
    pallas_call x3, Pallas kernels, forward(): pl.pallas_call(functools.partial(forward_body, wave, seed is not None), o...  7.08 us
    unnamed x16, local copies, waits for them, and re-layouts  5.74 us
    pallas_call x1, Pallas kernels, middle(): pl.pallas_call(functools.partial(middle_body, factor), out_shape=(jax.Sha...  3.37 us
  transfers between devices with their start and end apart: 28, of which 15 were waited for; matrix products, arithmetic and copies ran while one was open for 3% of the time, Pallas kernels for 11%

profile of v9, /device:TPU:4, one launch (start us, length us, event | category | flops | bytes accessed | tf_op | source)
XLA Modules:
  0.0 138.6 jit_solution(9328639502461749573)
XLA Ops:
  0.6 8.4 %collective-permute-start.1 = (bf16[64,4096]{1,0:T(8,128)(2,1)}, bf16[64,4096]{1,0:T(8,128)(2,1)S(1)}, u32[]{:S(2)}, u32[]{:S(2)}) collective-permute-start(bf16[64,4096]{1,0:T(8,128)(2,1)} %refs_2_.1), channel_id=1, source_target_pairs={{8,0},{252,4},{16,8},{4,12},{24,16},{12,20},{32,24},{20,28},{40,32... | collective-permute-start | bytes 1572872 | tf_op jit(solution)/shard_map/ppermute | solution.py:20
  13.5 3.2 %plan.1.refs_0_ = s32[904]{0:T(1024)S(1)} custom-call(s32[288]{0:T(512)S(1)} %copy-done.2, s32[288]{0:T(512)S(1)} %copy-done.3, s32[288]{0:T(512)S(1)} %copy-done.4, s32[1]{0:T(128)S(6)} %copy.11.count_ref, s32[1]{0:T(128)} %bitcast.1.sign_ref), custom_call_target="tpu_custom_call" | custom-call | bytes 6000000 | tf_op jit(solution)/shard_map/plan/pallas_call | solution.py:81
  17.8 2.7 %collective-permute-done.1.refs_3_ = bf16[64,4096]{1,0:T(8,128)(2,1)S(1)} collective-permute-done((bf16[64,4096]{1,0:T(8,128)(2,1)}, bf16[64,4096]{1,0:T(8,128)(2,1)S(1)}, u32[]{:S(2)}, u32[]{:S(2)}) %collective-permute-start.1) | collective-permute-done | bytes 524320 | tf_op jit(solution)/shard_map/ppermute | solution.py:20
  20.5 2.1 %collective-permute-done.refs_2_ = bf16[64,4096]{1,0:T(8,128)(2,1)S(1)} collective-permute-done((bf16[64,4096]{1,0:T(8,128)(2,1)}, bf16[64,4096]{1,0:T(8,128)(2,1)S(1)}, u32[]{:S(2)}, u32[]{:S(2)}) %collective-permute-start) | collective-permute-done | bytes 524320 | tf_op jit(solution)/shard_map/ppermute | solution.py:24
  22.6 3.3 %collective-permute-done.2.refs_4_ = bf16[64,4096]{1,0:T(8,128)(2,1)S(1)} collective-permute-done((bf16[64,4096]{1,0:T(8,128)(2,1)}, bf16[64,4096]{1,0:T(8,128)(2,1)S(1)}, u32[]{:S(2)}, u32[]{:S(2)}) %collective-permute-start.2) | collective-permute-done | bytes 524320 | tf_op jit(solution)/shard_map/ppermute | solution.py:20
  26.2 1.7 %collective-permute-start.4 = (bf16[64,4096]{1,0:T(8,128)(2,1)S(1)}, bf16[64,4096]{1,0:T(8,128)(2,1)S(1)}, u32[]{:S(2)}, u32[]{:S(2)}) collective-permute-start(bf16[64,4096]{1,0:T(8,128)(2,1)S(1)} %collective-permute-done.2.refs_4_), channel_id=1, source_target_pairs={{248,0},{12,4},{0,8},{20,12},{8,16},{28,20},{16,24},{36,28},{24,32... | collective-permute-start | bytes 1572872 | tf_op jit(solution)/shard_map/ppermute | solution.py:20
  28.5 3.7 %copy-done = bf16[288,128,128]{2,1,0:T(8,128)(2,1)S(1)} copy-done((bf16[288,128,128]{2,1,0:T(8,128)(2,1)S(1)}, bf16[288,128,128]{2,1,0:T(8,128)(2,1)}, u32[]{:S(2)}) %copy-start) | copy-done | bytes 9437208
  32.2 2.5 %forward_0.1.refs_5_ = f32[64,4096]{1,0:T(8,128)S(1)} custom-call(s32[904]{0:T(1024)S(1)} %plan.1.refs_0_, bf16[288,128,128]{2,1,0:T(8,128)(2,1)S(1)} %copy-done, bf16[64,4096]{1,0:T(8,128)(2,1)S(1)} %copy-done.1, bf16[64,4096]{1,0:T(8,128)(2,1)S(1)} %collective-permute-done.1.refs_3_, bf16[64,4096]{1,0:T(8,128)(2,1)S(1)} %collective-permute-done.2.refs_4_), custom_call_target="tpu_custom_call" | custom-call | bytes 6000000 | tf_op jit(solution)/shard_map/forward_0/pallas_call | solution.py:154
  34.7 3.7 %collective-permute-done.3.refs_3_ = bf16[64,4096]{1,0:T(8,128)(2,1)S(1)} collective-permute-done((bf16[64,4096]{1,0:T(8,128)(2,1)S(1)}, bf16[64,4096]{1,0:T(8,128)(2,1)S(1)}, u32[]{:S(2)}, u32[]{:S(2)}) %collective-permute-start.3) | collective-permute-done | bytes 524320 | tf_op jit(solution)/shard_map/ppermute | solution.py:20
  38.4 3.6 %collective-permute-done.4.refs_4_ = bf16[64,4096]{1,0:T(8,128)(2,1)S(1)} collective-permute-done((bf16[64,4096]{1,0:T(8,128)(2,1)S(1)}, bf16[64,4096]{1,0:T(8,128)(2,1)S(1)}, u32[]{:S(2)}, u32[]{:S(2)}) %collective-permute-start.4) | collective-permute-done | bytes 524320 | tf_op jit(solution)/shard_map/ppermute | solution.py:20
  42.1 5.3 %collective-permute-start.5 = (bf16[64,4096]{1,0:T(8,128)(2,1)S(1)}, bf16[64,4096]{1,0:T(8,128)(2,1)S(1)}, u32[]{:S(2)}, u32[]{:S(2)}) collective-permute-start(bf16[64,4096]{1,0:T(8,128)(2,1)S(1)} %collective-permute-done.refs_2_), channel_id=1, source_target_pairs={{8,0},{252,4},{16,8},{4,12},{24,16},{12,20},{32,24},{20,28},{40,32... | collective-permute-start | bytes 1572872 | tf_op jit(solution)/shard_map/ppermute | solution.py:20
  47.4 2.3 %forward_1.1.refs_5_ = f32[64,4096]{1,0:T(8,128)S(1)} custom-call(s32[904]{0:T(1024)S(1)} %plan.1.refs_0_, bf16[288,128,128]{2,1,0:T(8,128)(2,1)S(1)} %copy-done, bf16[64,4096]{1,0:T(8,128)(2,1)S(1)} %collective-permute-done.refs_2_, bf16[64,4096]{1,0:T(8,128)(2,1)S(1)} %collective-permute-done.3.refs_3_, ...), custom_call_target="tpu_custom_call" | custom-call | bytes 6000000 | tf_op jit(solution)/shard_map/forward_1/pallas_call | solution.py:154
  49.7 3.9 %collective-permute-done.7.refs_4_ = bf16[64,4096]{1,0:T(8,128)(2,1)S(1)} collective-permute-done((bf16[64,4096]{1,0:T(8,128)(2,1)S(1)}, bf16[64,4096]{1,0:T(8,128)(2,1)S(1)}, u32[]{:S(2)}, u32[]{:S(2)}) %collective-permute-start.7) | collective-permute-done | bytes 524320 | tf_op jit(solution)/shard_map/ppermute | solution.py:24
  53.6 3.3 %collective-permute-done.6.refs_3_ = bf16[64,4096]{1,0:T(8,128)(2,1)S(1)} collective-permute-done((bf16[64,4096]{1,0:T(8,128)(2,1)S(1)}, bf16[64,4096]{1,0:T(8,128)(2,1)S(1)}, u32[]{:S(2)}, u32[]{:S(2)}) %collective-permute-start.6) | collective-permute-done | bytes 524320 | tf_op jit(solution)/shard_map/ppermute | solution.py:20
  57.0 2.3 %forward_2.1.refs_0_ = bf16[64,4096]{1,0:T(8,128)(2,1)S(1)} custom-call(s32[904]{0:T(1024)S(1)} %plan.1.refs_0_, bf16[288,128,128]{2,1,0:T(8,128)(2,1)S(1)} %copy-done, bf16[64,4096]{1,0:T(8,128)(2,1)S(1)} %collective-permute-done.5.refs_2_, bf16[64,4096]{1,0:T(8,128)(2,1)S(1)} %collective-permute-done.6.refs_3_, ...), custom_call_target="tpu_custom_call" | custom-call | bytes 6000000 | tf_op jit(solution)/shard_map/forward_2/pallas_call | solution.py:154
  60.4 11.2 %collective-permute-done.10.refs_2_ = bf16[64,4096]{1,0:T(8,128)(2,1)S(1)} collective-permute-done((bf16[64,4096]{1,0:T(8,128)(2,1)S(1)}, bf16[64,4096]{1,0:T(8,128)(2,1)S(1)}, u32[]{:S(2)}, u32[]{:S(2)}) %collective-permute-start.10) | collective-permute-done | bytes 524320 | tf_op jit(solution)/shard_map/ppermute | solution.py:24
  71.6 1.9 %collective-permute-done.11.refs_3_ = bf16[64,4096]{1,0:T(8,128)(2,1)S(1)} collective-permute-done((bf16[64,4096]{1,0:T(8,128)(2,1)S(1)}, bf16[64,4096]{1,0:T(8,128)(2,1)S(1)}, u32[]{:S(2)}, u32[]{:S(2)}) %collective-permute-start.11) | collective-permute-done | bytes 524320 | tf_op jit(solution)/shard_map/ppermute | solution.py:24
  73.5 3.4 %middle.1 = (bf16[64,4096]{1,0:T(8,128)(2,1)}, bf16[64,4096]{1,0:T(8,128)(2,1)S(1)}, f32[64,256]{1,0:T(8,128)S(1)}) custom-call(s32[1]{0:T(128)} %bitcast.place_ref, bf16[64,4096]{1,0:T(8,128)(2,1)S(1)} %forward_2.1.refs_0_, bf16[64,4096]{1,0:T(8,128)(2,1)S(1)} %collective-permute-done.9.refs_1_, bf16[64,4096]{1,0:T(8,128)(2,1)S(1)} %collective-permute-done.10.refs_2_, ...), custom_call_target="tpu_custom_call" | custom-call | bytes 6000000 | tf_op jit(solution)/shard_map/middle/pallas_call | solution.py:243
  76.9 2.4 %backward_2.1 = (bf16[64,4096]{1,0:T(8,128)(2,1)S(1)}, bf16[64,4096]{1,0:T(8,128)(2,1)S(1)}, bf16[64,4096]{1,0:T(8,128)(2,1)S(1)}) custom-call(s32[904]{0:T(1024)S(1)} %plan.1.refs_0_, bf16[288,128,128]{2,1,0:T(8,128)(2,1)S(1)} %bitcast.3, bf16[64,4096]{1,0:T(8,128)(2,1)S(1)} %get-tuple-element.83.refs_2_), custom_call_target="tpu_custom_call" | custom-call | bytes 6000000 | tf_op jit(solution)/shard_map/backward_2/pallas_call | solution.py:195
  79.3 1.9 %collective-permute-done.14 = f32[64,256]{1,0:T(8,128)S(1)} collective-permute-done((f32[64,256]{1,0:T(8,128)S(1)}, f32[64,256]{1,0:T(8,128)S(1)}, u32[]{:S(2)}, u32[]{:S(2)}) %collective-permute-start.14) | collective-permute-done | bytes 65568 | tf_op jit(solution)/shard_map/ppermute | solution.py:24
  82.6 5.1 %collective-permute-start.17 = (bf16[64,4096]{1,0:T(8,128)(2,1)S(1)}, bf16[64,4096]{1,0:T(8,128)(2,1)S(1)}, u32[]{:S(2)}, u32[]{:S(2)}) collective-permute-start(bf16[64,4096]{1,0:T(8,128)(2,1)S(1)} %get-tuple-element.77), channel_id=1, source_target_pairs={{8,0},{252,4},{16,8},{4,12},{24,16},{12,20},{32,24},{20,28},{40,32... | collective-permute-start | bytes 1572872 | tf_op jit(solution)/shard_map/ppermute | solution.py:20
  87.8 2.4 %backward_1.1 = (f32[64,4096]{1,0:T(8,128)S(1)}, f32[64,4096]{1,0:T(8,128)S(1)}, bf16[64,4096]{1,0:T(8,128)(2,1)S(1)}) custom-call(s32[904]{0:T(1024)S(1)} %plan.1.refs_0_, bf16[288,128,128]{2,1,0:T(8,128)(2,1)S(1)} %bitcast.3, bf16[64,4096]{1,0:T(8,128)(2,1)S(1)} %get-tuple-element.83.refs_2_), custom_call_target="tpu_custom_call" | custom-call | bytes 6000000 | tf_op jit(solution)/shard_map/backward_1/pallas_call | solution.py:195
  90.2 5.3 %collective-permute-done.18 = f32[64,256]{1,0:T(8,128)S(1)} collective-permute-done((f32[64,256]{1,0:T(8,128)S(1)}, f32[64,256]{1,0:T(8,128)S(1)}, u32[]{:S(2)}, u32[]{:S(2)}) %collective-permute-start.18) | collective-permute-done | bytes 65568 | tf_op jit(solution)/shard_map/ppermute | solution.py:24
  95.5 3.7 %collective-permute-start.19 = (f32[64,256]{1,0:T(8,128)S(1)}, f32[64,256]{1,0:T(8,128)S(1)}, u32[]{:S(2)}, u32[]{:S(2)}) collective-permute-start(f32[64,256]{1,0:T(8,128)S(1)} %add.53), channel_id=1, source_target_pairs={{0,64},{4,68},{8,72},{12,76},{16,80},{20,84},{24,88},{28,92},{32,9... | collective-permute-start | bytes 196616 | tf_op jit(solution)/shard_map/ppermute | solution.py:24
  99.2 2.6 %backward_0.1 = (f32[64,4096]{1,0:T(8,128)S(1)}, f32[64,4096]{1,0:T(8,128)S(1)}, f32[64,4096]{1,0:T(8,128)S(1)}) custom-call(s32[904]{0:T(1024)S(1)} %plan.1.refs_0_, bf16[288,128,128]{2,1,0:T(8,128)(2,1)S(1)} %bitcast.3, bf16[64,4096]{1,0:T(8,128)(2,1)S(1)} %get-tuple-element.83.refs_2_), custom_call_target="tpu_custom_call" | custom-call | bytes 6000000 | tf_op jit(solution)/shard_map/backward_0/pallas_call | solution.py:195
  102.3 5.3 %collective-permute-start.21 = (bf16[64,4096]{1,0:T(8,128)(2,1)S(1)}, bf16[64,4096]{1,0:T(8,128)(2,1)S(1)}, u32[]{:S(2)}, u32[]{:S(2)}) collective-permute-start(bf16[64,4096]{1,0:T(8,128)(2,1)S(1)} %get-tuple-element.92), channel_id=1, source_target_pairs={{8,0},{252,4},{16,8},{4,12},{24,16},{12,20},{32,24},{20,28},{40,32... | collective-permute-start | bytes 1572872 | tf_op jit(solution)/shard_map/ppermute | solution.py:20
  108.5 5.1 %collective-permute-start.23 = (f32[64,256]{1,0:T(8,128)S(1)}, f32[64,256]{1,0:T(8,128)S(1)}, u32[]{:S(2)}, u32[]{:S(2)}) collective-permute-start(f32[64,256]{1,0:T(8,128)S(1)} %add.58), channel_id=1, source_target_pairs={{0,4},{4,0},{8,12},{12,8},{16,20},{20,16},{24,28},{28,24},{32,36},... | collective-permute-start | bytes 196616 | tf_op jit(solution)/shard_map/ppermute | solution.py:24
  113.7 2.1 %collective-permute-done.23 = f32[64,256]{1,0:T(8,128)S(1)} collective-permute-done((f32[64,256]{1,0:T(8,128)S(1)}, f32[64,256]{1,0:T(8,128)S(1)}, u32[]{:S(2)}, u32[]{:S(2)}) %collective-permute-start.23) | collective-permute-done | bytes 65568 | tf_op jit(solution)/shard_map/ppermute | solution.py:24
  115.8 2.6 %collective-permute-done.20 = bf16[64,4096]{1,0:T(8,128)(2,1)S(1)} collective-permute-done((bf16[64,4096]{1,0:T(8,128)(2,1)S(1)}, bf16[64,4096]{1,0:T(8,128)(2,1)S(1)}, u32[]{:S(2)}, u32[]{:S(2)}) %collective-permute-start.20) | collective-permute-done | bytes 524320 | tf_op jit(solution)/shard_map/ppermute | solution.py:20
  118.5 3.6 %collective-permute-start.25 = (bf16[64,4096]{1,0:T(8,128)(2,1)S(1)}, bf16[64,4096]{1,0:T(8,128)(2,1)S(1)}, u32[]{:S(2)}, u32[]{:S(2)}) collective-permute-start(bf16[64,4096]{1,0:T(8,128)(2,1)S(1)} %add_convert_fusion.1), channel_id=1, source_target_pairs={{8,0},{252,4},{16,8},{4,12},{24,16},{12,20},{32,24},{20,28},{40,32... | collective-permute-start | bytes 1572872 | tf_op jit(solution)/shard_map/ppermute | solution.py:20
  122.4 6.6 %collective-permute-start.26 = (bf16[64,4096]{1,0:T(8,128)(2,1)S(1)}, bf16[64,4096]{1,0:T(8,128)(2,1)S(1)}, u32[]{:S(2)}, u32[]{:S(2)}) collective-permute-start(bf16[64,4096]{1,0:T(8,128)(2,1)S(1)} %add_convert_fusion.3), channel_id=1, source_target_pairs={{0,4},{4,0},{8,12},{12,8},{16,20},{20,16},{24,28},{28,24},{32,36},... | collective-permute-start | bytes 1572872 | tf_op jit(solution)/shard_map/ppermute | solution.py:24
  129.0 7.9 %collective-permute-done.27 = f32[64,256]{1,0:T(8,128)S(1)} collective-permute-done((f32[64,256]{1,0:T(8,128)S(1)}, f32[64,256]{1,0:T(8,128)S(1)}, u32[]{:S(2)}, u32[]{:S(2)}) %collective-permute-start.27) | collective-permute-done | bytes 65568 | tf_op jit(solution)/shard_map/ppermute | solution.py:24
  (65 shorter events, 11.8 us)
Async XLA Ops:
  0.6 27.8 %copy-start.1 = (bf16[64,4096]{1,0:T(8,128)(2,1)S(1)}, bf16[64,4096]{1,0:T(8,128)(2,1)}, u32[]{:S(2)}) copy-start(bf16[64,4096]{1,0:T(8,128)(2,1)} %refs_2_.1) | copy-start | bytes 1572868
  0.6 19.9 %collective-permute-start.1 = (bf16[64,4096]{1,0:T(8,128)(2,1)}, bf16[64,4096]{1,0:T(8,128)(2,1)S(1)}, u32[]{:S(2)}, u32[]{:S(2)}) collective-permute-start(bf16[64,4096]{1,0:T(8,128)(2,1)} %refs_2_.1), channel_id=1, source_target_pairs={{8,0},{252,4},{16,8},{4,12},{24,16},{12,20},{32,24},{20,28},{40,32... | collective-permute-start | bytes 1572872 | tf_op jit(solution)/shard_map/ppermute | solution.py:20
  9.0 13.6 %collective-permute-start = (bf16[64,4096]{1,0:T(8,128)(2,1)}, bf16[64,4096]{1,0:T(8,128)(2,1)S(1)}, u32[]{:S(2)}, u32[]{:S(2)}) collective-permute-start(bf16[64,4096]{1,0:T(8,128)(2,1)} %refs_2_.1), channel_id=1, source_target_pairs={{0,4},{4,0},{8,12},{12,8},{16,20},{20,16},{24,28},{28,24},{32,36},... | collective-permute-start | bytes 1572872 | tf_op jit(solution)/shard_map/ppermute | solution.py:24
  9.0 16.9 %collective-permute-start.2 = (bf16[64,4096]{1,0:T(8,128)(2,1)}, bf16[64,4096]{1,0:T(8,128)(2,1)S(1)}, u32[]{:S(2)}, u32[]{:S(2)}) collective-permute-start(bf16[64,4096]{1,0:T(8,128)(2,1)} %refs_2_.1), channel_id=1, source_target_pairs={{248,0},{12,4},{0,8},{20,12},{8,16},{28,20},{16,24},{36,28},{24,32... | collective-permute-start | bytes 1572872 | tf_op jit(solution)/shard_map/ppermute | solution.py:20
  25.9 12.5 %collective-permute-start.3 = (bf16[64,4096]{1,0:T(8,128)(2,1)S(1)}, bf16[64,4096]{1,0:T(8,128)(2,1)S(1)}, u32[]{:S(2)}, u32[]{:S(2)}) collective-permute-start(bf16[64,4096]{1,0:T(8,128)(2,1)S(1)} %collective-permute-done.1.refs_3_), channel_id=1, source_target_pairs={{8,0},{252,4},{16,8},{4,12},{24,16},{12,20},{32,24},{20,28},{40,32... | collective-permute-start | bytes 1572872 | tf_op jit(solution)/shard_map/ppermute | solution.py:20
  26.2 15.8 %collective-permute-start.4 = (bf16[64,4096]{1,0:T(8,128)(2,1)S(1)}, bf16[64,4096]{1,0:T(8,128)(2,1)S(1)}, u32[]{:S(2)}, u32[]{:S(2)}) collective-permute-start(bf16[64,4096]{1,0:T(8,128)(2,1)S(1)} %collective-permute-done.2.refs_4_), channel_id=1, source_target_pairs={{248,0},{12,4},{0,8},{20,12},{8,16},{28,20},{16,24},{36,28},{24,32... | collective-permute-start | bytes 1572872 | tf_op jit(solution)/shard_map/ppermute | solution.py:20
  28.0 21.7 %collective-permute-start.8 = (bf16[64,4352]{1,0:T(8,128)(2,1)S(1)}, bf16[64,4352]{1,0:T(8,128)(2,1)S(1)}, u32[]{:S(2)}, u32[]{:S(2)}) collective-permute-start(bf16[64,4352]{1,0:T(8,128)(2,1)S(1)} %pad_maximum_fusion.refs_4_), channel_id=1, source_target_pairs={{0,2},{1,3},{2,0},{3,1},{4,6},{5,7},{6,4},{7,5},{8,10},{9,11},{10,... | collective-permute-start | bytes 1671176 | tf_op jit(solution)/shard_map/ppermute | solution.py:24
  42.1 11.6 %collective-permute-start.7 = (bf16[64,4096]{1,0:T(8,128)(2,1)S(1)}, bf16[64,4096]{1,0:T(8,128)(2,1)S(1)}, u32[]{:S(2)}, u32[]{:S(2)}) collective-permute-start(bf16[64,4096]{1,0:T(8,128)(2,1)S(1)} %collective-permute-done.3.refs_3_), channel_id=1, source_target_pairs={{0,4},{4,0},{8,12},{12,8},{16,20},{20,16},{24,28},{28,24},{32,36},... | collective-permute-start | bytes 1572872 | tf_op jit(solution)/shard_map/ppermute | solution.py:24
  42.1 14.9 %collective-permute-start.6 = (bf16[64,4096]{1,0:T(8,128)(2,1)S(1)}, bf16[64,4096]{1,0:T(8,128)(2,1)S(1)}, u32[]{:S(2)}, u32[]{:S(2)}) collective-permute-start(bf16[64,4096]{1,0:T(8,128)(2,1)S(1)} %collective-permute-done.refs_2_), channel_id=1, source_target_pairs={{248,0},{12,4},{0,8},{20,12},{8,16},{28,20},{16,24},{36,28},{24,32... | collective-permute-start | bytes 1572872 | tf_op jit(solution)/shard_map/ppermute | solution.py:20
  42.1 14.9 %collective-permute-start.5 = (bf16[64,4096]{1,0:T(8,128)(2,1)S(1)}, bf16[64,4096]{1,0:T(8,128)(2,1)S(1)}, u32[]{:S(2)}, u32[]{:S(2)}) collective-permute-start(bf16[64,4096]{1,0:T(8,128)(2,1)S(1)} %collective-permute-done.refs_2_), channel_id=1, source_target_pairs={{8,0},{252,4},{16,8},{4,12},{24,16},{12,20},{32,24},{20,28},{40,32... | collective-permute-start | bytes 1572872 | tf_op jit(solution)/shard_map/ppermute | solution.py:20
  47.4 29.4 %slice-start = ((s8[9437184]{0:T(1024)(128)(4,1)}), s8[4194304]{0:T(1024)(128)(4,1)S(1)}, s32[]{:S(2)}) async-start(s8[9437184]{0:T(1024)(128)(4,1)} %bitcast.2), calls=%async_computation | async-start | bytes 8388608
  47.4 29.4 %slice-start.1 = ((s8[9437184]{0:T(1024)(128)(4,1)}), s8[4194304]{0:T(1024)(128)(4,1)S(1)}, s32[]{:S(2)}) async-start(s8[9437184]{0:T(1024)(128)(4,1)} %bitcast.2), calls=%async_computation.1 | async-start | bytes 8388608
  49.7 27.2 %slice-start.2 = ((s8[9437184]{0:T(1024)(128)(4,1)}), s8[1048576]{0:T(1024)(128)(4,1)S(1)}, s32[]{:S(2)}) async-start(s8[9437184]{0:T(1024)(128)(4,1)} %bitcast.2), calls=%async_computation.2 | async-start | bytes 2097152
  59.3 12.3 %collective-permute-start.10 = (bf16[64,4096]{1,0:T(8,128)(2,1)S(1)}, bf16[64,4096]{1,0:T(8,128)(2,1)S(1)}, u32[]{:S(2)}, u32[]{:S(2)}) collective-permute-start(bf16[64,4096]{1,0:T(8,128)(2,1)S(1)} %forward_2.1.refs_0_), channel_id=1, source_target_pairs={{0,2},{1,3},{2,0},{3,1},{4,6},{5,7},{6,4},{7,5},{8,10},{9,11},{10,... | collective-permute-start | bytes 1572872 | tf_op jit(solution)/shard_map/ppermute | solution.py:24
  59.9 11.7 %collective-permute-start.12 = (bf16[64,4352]{1,0:T(8,128)(2,1)S(1)}, bf16[64,4352]{1,0:T(8,128)(2,1)S(1)}, u32[]{:S(2)}, u32[]{:S(2)}) collective-permute-start(bf16[64,4352]{1,0:T(8,128)(2,1)S(1)} %pad_maximum_fusion.refs_4_), channel_id=1, source_target_pairs={{0,1},{1,0},{2,3},{3,2},{4,5},{5,4},{6,7},{7,6},{8,9},{9,8},{10,11... | collective-permute-start | bytes 1671176 | tf_op jit(solution)/shard_map/ppermute | solution.py:24
  59.9 11.7 %collective-permute-start.13 = (bf16[64,4352]{1,0:T(8,128)(2,1)S(1)}, bf16[64,4352]{1,0:T(8,128)(2,1)S(1)}, u32[]{:S(2)}, u32[]{:S(2)}) collective-permute-start(bf16[64,4352]{1,0:T(8,128)(2,1)S(1)} %collective-permute-done.8.refs_6_), channel_id=1, source_target_pairs={{0,1},{1,0},{2,3},{3,2},{4,5},{5,4},{6,7},{7,6},{8,9},{9,8},{10,11... | collective-permute-start | bytes 1671176 | tf_op jit(solution)/shard_map/ppermute | solution.py:24
  60.4 11.2 %collective-permute-start.9 = (bf16[64,4096]{1,0:T(8,128)(2,1)S(1)}, bf16[64,4096]{1,0:T(8,128)(2,1)S(1)}, u32[]{:S(2)}, u32[]{:S(2)}) collective-permute-start(bf16[64,4096]{1,0:T(8,128)(2,1)S(1)} %forward_2.1.refs_0_), channel_id=1, source_target_pairs={{0,1},{1,0},{2,3},{3,2},{4,5},{5,4},{6,7},{7,6},{8,9},{9,8},{10,11... | collective-permute-start | bytes 1572872 | tf_op jit(solution)/shard_map/ppermute | solution.py:24
  71.6 1.9 %collective-permute-start.11 = (bf16[64,4096]{1,0:T(8,128)(2,1)S(1)}, bf16[64,4096]{1,0:T(8,128)(2,1)S(1)}, u32[]{:S(2)}, u32[]{:S(2)}) collective-permute-start(bf16[64,4096]{1,0:T(8,128)(2,1)S(1)} %collective-permute-done.10.refs_2_), channel_id=1, source_target_pairs={{0,1},{1,0},{2,3},{3,2},{4,5},{5,4},{6,7},{7,6},{8,9},{9,8},{10,11... | collective-permute-start | bytes 1572872 | tf_op jit(solution)/shard_map/ppermute | solution.py:24
  76.8 4.3 %collective-permute-start.14 = (f32[64,256]{1,0:T(8,128)S(1)}, f32[64,256]{1,0:T(8,128)S(1)}, u32[]{:S(2)}, u32[]{:S(2)}) collective-permute-start(f32[64,256]{1,0:T(8,128)S(1)} %get-tuple-element.74), channel_id=1, source_target_pairs={{0,8},{4,12},{8,0},{12,4},{16,24},{20,28},{24,16},{28,20},{32,40},... | collective-permute-start | bytes 196616 | tf_op jit(solution)/shard_map/ppermute | solution.py:24
  81.1 20.7 %collective-permute-start.15 = (bf16[64,4096]{1,0:T(8,128)(2,1)S(1)}, bf16[64,4096]{1,0:T(8,128)(2,1)S(1)}, u32[]{:S(2)}, u32[]{:S(2)}) collective-permute-start(bf16[64,4096]{1,0:T(8,128)(2,1)S(1)} %get-tuple-element.75), channel_id=1, source_target_pairs={{0,4},{4,0},{8,12},{12,8},{16,20},{20,16},{24,28},{28,24},{32,36},... | collective-permute-start | bytes 1572872 | tf_op jit(solution)/shard_map/ppermute | solution.py:24
  81.5 20.3 %collective-permute-start.16 = (bf16[64,4096]{1,0:T(8,128)(2,1)S(1)}, bf16[64,4096]{1,0:T(8,128)(2,1)S(1)}, u32[]{:S(2)}, u32[]{:S(2)}) collective-permute-start(bf16[64,4096]{1,0:T(8,128)(2,1)S(1)} %get-tuple-element.76), channel_id=1, source_target_pairs={{248,0},{12,4},{0,8},{20,12},{8,16},{28,20},{16,24},{36,28},{24,32... | collective-permute-start | bytes 1572872 | tf_op jit(solution)/shard_map/ppermute | solution.py:20
  82.6 19.2 %collective-permute-start.17 = (bf16[64,4096]{1,0:T(8,128)(2,1)S(1)}, bf16[64,4096]{1,0:T(8,128)(2,1)S(1)}, u32[]{:S(2)}, u32[]{:S(2)}) collective-permute-start(bf16[64,4096]{1,0:T(8,128)(2,1)S(1)} %get-tuple-element.77), channel_id=1, source_target_pairs={{8,0},{252,4},{16,8},{4,12},{24,16},{12,20},{32,24},{20,28},{40,32... | collective-permute-start | bytes 1572872 | tf_op jit(solution)/shard_map/ppermute | solution.py:20
  87.7 7.8 %collective-permute-start.18 = (f32[64,256]{1,0:T(8,128)S(1)}, f32[64,256]{1,0:T(8,128)S(1)}, u32[]{:S(2)}, u32[]{:S(2)}) collective-permute-start(f32[64,256]{1,0:T(8,128)S(1)} %add.52), channel_id=1, source_target_pairs={{0,32},{4,36},{8,40},{12,44},{16,48},{20,52},{24,56},{28,60},{32,0... | collective-permute-start | bytes 196616 | tf_op jit(solution)/shard_map/ppermute | solution.py:24
  95.5 6.3 %collective-permute-start.19 = (f32[64,256]{1,0:T(8,128)S(1)}, f32[64,256]{1,0:T(8,128)S(1)}, u32[]{:S(2)}, u32[]{:S(2)}) collective-permute-start(f32[64,256]{1,0:T(8,128)S(1)} %add.53), channel_id=1, source_target_pairs={{0,64},{4,68},{8,72},{12,76},{16,80},{20,84},{24,88},{28,92},{32,9... | collective-permute-start | bytes 196616 | tf_op jit(solution)/shard_map/ppermute | solution.py:24
  101.9 6.6 %collective-permute-start.22 = (f32[64,256]{1,0:T(8,128)S(1)}, f32[64,256]{1,0:T(8,128)S(1)}, u32[]{:S(2)}, u32[]{:S(2)}) collective-permute-start(f32[64,256]{1,0:T(8,128)S(1)} %add.57), channel_id=1, source_target_pairs={{0,192},{4,196},{8,200},{12,204},{16,208},{20,212},{24,216},{28,22... | collective-permute-start | bytes 196616 | tf_op jit(solution)/shard_map/ppermute | solution.py:24
  102.2 16.2 %collective-permute-start.20 = (bf16[64,4096]{1,0:T(8,128)(2,1)S(1)}, bf16[64,4096]{1,0:T(8,128)(2,1)S(1)}, u32[]{:S(2)}, u32[]{:S(2)}) collective-permute-start(bf16[64,4096]{1,0:T(8,128)(2,1)S(1)} %add_convert_fusion.4), channel_id=1, source_target_pairs={{248,0},{12,4},{0,8},{20,12},{8,16},{28,20},{16,24},{36,28},{24,32... | collective-permute-start | bytes 1572872 | tf_op jit(solution)/shard_map/ppermute | solution.py:20
  102.3 16.1 %collective-permute-start.21 = (bf16[64,4096]{1,0:T(8,128)(2,1)S(1)}, bf16[64,4096]{1,0:T(8,128)(2,1)S(1)}, u32[]{:S(2)}, u32[]{:S(2)}) collective-permute-start(bf16[64,4096]{1,0:T(8,128)(2,1)S(1)} %get-tuple-element.92), channel_id=1, source_target_pairs={{8,0},{252,4},{16,8},{4,12},{24,16},{12,20},{32,24},{20,28},{40,32... | collective-permute-start | bytes 1572872 | tf_op jit(solution)/shard_map/ppermute | solution.py:20
  108.5 7.3 %collective-permute-start.23 = (f32[64,256]{1,0:T(8,128)S(1)}, f32[64,256]{1,0:T(8,128)S(1)}, u32[]{:S(2)}, u32[]{:S(2)}) collective-permute-start(f32[64,256]{1,0:T(8,128)S(1)} %add.58), channel_id=1, source_target_pairs={{0,4},{4,0},{8,12},{12,8},{16,20},{20,16},{24,28},{28,24},{32,36},... | collective-permute-start | bytes 196616 | tf_op jit(solution)/shard_map/ppermute | solution.py:24
  118.5 19.1 %collective-permute-start.25 = (bf16[64,4096]{1,0:T(8,128)(2,1)S(1)}, bf16[64,4096]{1,0:T(8,128)(2,1)S(1)}, u32[]{:S(2)}, u32[]{:S(2)}) collective-permute-start(bf16[64,4096]{1,0:T(8,128)(2,1)S(1)} %add_convert_fusion.1), channel_id=1, source_target_pairs={{8,0},{252,4},{16,8},{4,12},{24,16},{12,20},{32,24},{20,28},{40,32... | collective-permute-start | bytes 1572872 | tf_op jit(solution)/shard_map/ppermute | solution.py:20
  122.3 15.3 %collective-permute-start.24 = (bf16[64,4096]{1,0:T(8,128)(2,1)S(1)}, bf16[64,4096]{1,0:T(8,128)(2,1)S(1)}, u32[]{:S(2)}, u32[]{:S(2)}) collective-permute-start(bf16[64,4096]{1,0:T(8,128)(2,1)S(1)} %add_convert_fusion.2), channel_id=1, source_target_pairs={{248,0},{12,4},{0,8},{20,12},{8,16},{28,20},{16,24},{36,28},{24,32... | collective-permute-start | bytes 1572872 | tf_op jit(solution)/shard_map/ppermute | solution.py:20
  122.4 15.2 %collective-permute-start.26 = (bf16[64,4096]{1,0:T(8,128)(2,1)S(1)}, bf16[64,4096]{1,0:T(8,128)(2,1)S(1)}, u32[]{:S(2)}, u32[]{:S(2)}) collective-permute-start(bf16[64,4096]{1,0:T(8,128)(2,1)S(1)} %add_convert_fusion.3), channel_id=1, source_target_pairs={{0,4},{4,0},{8,12},{12,8},{16,20},{20,16},{24,28},{28,24},{32,36},... | collective-permute-start | bytes 1572872 | tf_op jit(solution)/shard_map/ppermute | solution.py:24
  129.0 7.9 %collective-permute-start.27 = (f32[64,256]{1,0:T(8,128)S(1)}, f32[64,256]{1,0:T(8,128)S(1)}, u32[]{:S(2)}, u32[]{:S(2)}) collective-permute-start(f32[64,256]{1,0:T(8,128)S(1)} %add.59), channel_id=1, source_target_pairs={{0,24},{4,28},{8,16},{12,20},{16,8},{20,12},{24,0},{28,4},{32,56},... | collective-permute-start | bytes 196616 | tf_op jit(solution)/shard_map/ppermute | solution.py:24
  (4 other events, 5.7 us)

commit v10 on v9

--- a/solution.py
+++ b/solution.py
@@ -9,7 +9,7 @@
 from jax.sharding import PartitionSpec as P
 
 REACH = 4
-GROUP = 8
+GROUP = 16
 WAVES = [[0, 2, -2], [1, 4, -4], [3, -1, -3]]
 MIB = 1 << 20
 
@@ -66,7 +66,7 @@
     lax.fori_loop(0, count_ref[0], place, 0)
     for w in range(len(WAVES)):
         n = fill[w]
-        groups = (n + GROUP - 1) >> 3
+        groups = (n + GROUP - 1) >> 4
 
         def pad(i, c):
             list_ref[w * cap + i] = 32 << 9

time: 141 us -> 139 us (0.986)
  waiting for transfers between devices: 56.4 us -> 59.7 us
  starting transfers between devices: 48.7 us -> 46.6 us
  Pallas kernels: 21.1 us -> 19.1 us
    ppermute x16, starting transfers between devices: 17.7 us -> 15.5 us  [flipped(): lax.ppermute(block, axis, [(i, i ^ bit) for i in range(lax.axis_size(axis...]
    ppermute x12, waiting for transfers between devices: 19.4 us -> 21.2 us  [stepped(): return lax.ppermute(block, 'blk', route)]
  transfers between devices with their start and end apart: 28 -> 28, of which waited for: 15 -> 16; matrix products, arithmetic and copies ran while one was open for 3% -> 3% of each run, Pallas kernels for 11% -> 10%
where the time goes in v10:
time: 139 us; the launch traced here: 138 us
  waiting for transfers between devices  59.7 us (43%)
  starting transfers between devices  46.6 us (34%)
  Pallas kernels  19.1 us (14%)
  local copies, waits for them, and re-layouts  6.62 us (5%)
  other arithmetic  4.15 us (3%)
  between operations  1.52 us (1%)
    ppermute x16, waiting for transfers between devices, flipped(): lax.ppermute(block, axis, [(i, i ^ bit) for i in range(lax.axis_size(axis...  38.5 us
    ppermute x12, starting transfers between devices, stepped(): return lax.ppermute(block, 'blk', route)  31 us
    ppermute x12, waiting for transfers between devices, stepped(): return lax.ppermute(block, 'blk', route)  21.2 us
    ppermute x16, starting transfers between devices, flipped(): lax.ppermute(block, axis, [(i, i ^ bit) for i in range(lax.axis_size(axis...  15.5 us
    pallas_call x3, Pallas kernels, backward(): pl.pallas_call(functools.partial(backward_body, wave), out_shape=tuple((p...  6.4 us
    pallas_call x3, Pallas kernels, forward(): pl.pallas_call(functools.partial(forward_body, wave, seed is not None), o...  6.01 us
    unnamed x16, local copies, waits for them, and re-layouts  5.74 us
    pallas_call x1, Pallas kernels, middle(): pl.pallas_call(functools.partial(middle_body, factor), out_shape=(jax.Sha...  3.37 us
  transfers between devices with their start and end apart: 28, of which 16 were waited for; matrix products, arithmetic and copies ran while one was open for 3% of the time, Pallas kernels for 10%

profile of v10, /device:TPU:4, one launch (start us, length us, event | category | flops | bytes accessed | tf_op | source)
XLA Modules:
  0.0 137.7 jit_solution(952312076114353123)
XLA Ops:
  0.6 8.4 %collective-permute-start.1 = (bf16[64,4096]{1,0:T(8,128)(2,1)}, bf16[64,4096]{1,0:T(8,128)(2,1)S(1)}, u32[]{:S(2)}, u32[]{:S(2)}) collective-permute-start(bf16[64,4096]{1,0:T(8,128)(2,1)} %refs_2_.1), channel_id=1, source_target_pairs={{8,0},{252,4},{16,8},{4,12},{24,16},{12,20},{32,24},{20,28},{40,32... | collective-permute-start | bytes 1572872 | tf_op jit(solution)/shard_map/ppermute | solution.py:20
  13.5 3.4 %plan.1.refs_0_ = s32[928]{0:T(1024)S(1)} custom-call(s32[288]{0:T(512)S(1)} %copy-done.2, s32[288]{0:T(512)S(1)} %copy-done.3, s32[288]{0:T(512)S(1)} %copy-done.4, s32[1]{0:T(128)S(6)} %copy.11.count_ref, s32[1]{0:T(128)} %bitcast.1.sign_ref), custom_call_target="tpu_custom_call" | custom-call | bytes 6000000 | tf_op jit(solution)/shard_map/plan/pallas_call | solution.py:81
  18.0 2.6 %collective-permute-done.1.refs_3_ = bf16[64,4096]{1,0:T(8,128)(2,1)S(1)} collective-permute-done((bf16[64,4096]{1,0:T(8,128)(2,1)}, bf16[64,4096]{1,0:T(8,128)(2,1)S(1)}, u32[]{:S(2)}, u32[]{:S(2)}) %collective-permute-start.1) | collective-permute-done | bytes 524320 | tf_op jit(solution)/shard_map/ppermute | solution.py:20
  20.5 2.1 %collective-permute-done.refs_2_ = bf16[64,4096]{1,0:T(8,128)(2,1)S(1)} collective-permute-done((bf16[64,4096]{1,0:T(8,128)(2,1)}, bf16[64,4096]{1,0:T(8,128)(2,1)S(1)}, u32[]{:S(2)}, u32[]{:S(2)}) %collective-permute-start) | collective-permute-done | bytes 524320 | tf_op jit(solution)/shard_map/ppermute | solution.py:24
  22.6 3.3 %collective-permute-done.2.refs_4_ = bf16[64,4096]{1,0:T(8,128)(2,1)S(1)} collective-permute-done((bf16[64,4096]{1,0:T(8,128)(2,1)}, bf16[64,4096]{1,0:T(8,128)(2,1)S(1)}, u32[]{:S(2)}, u32[]{:S(2)}) %collective-permute-start.2) | collective-permute-done | bytes 524320 | tf_op jit(solution)/shard_map/ppermute | solution.py:20
  28.5 3.7 %copy-done = bf16[288,128,128]{2,1,0:T(8,128)(2,1)S(1)} copy-done((bf16[288,128,128]{2,1,0:T(8,128)(2,1)S(1)}, bf16[288,128,128]{2,1,0:T(8,128)(2,1)}, u32[]{:S(2)}) %copy-start) | copy-done | bytes 9437208
  32.2 2.1 %forward_0.1.refs_5_ = f32[64,4096]{1,0:T(8,128)S(1)} custom-call(s32[928]{0:T(1024)S(1)} %plan.1.refs_0_, bf16[288,128,128]{2,1,0:T(8,128)(2,1)S(1)} %copy-done, bf16[64,4096]{1,0:T(8,128)(2,1)S(1)} %copy-done.1, bf16[64,4096]{1,0:T(8,128)(2,1)S(1)} %collective-permute-done.1.refs_3_, bf16[64,4096]{1,0:T(8,128)(2,1)S(1)} %collective-permute-done.2.refs_4_), custom_call_target="tpu_custom_call" | custom-call | bytes 6000000 | tf_op jit(solution)/shard_map/forward_0/pallas_call | solution.py:154
  34.3 4.1 %collective-permute-done.3.refs_3_ = bf16[64,4096]{1,0:T(8,128)(2,1)S(1)} collective-permute-done((bf16[64,4096]{1,0:T(8,128)(2,1)S(1)}, bf16[64,4096]{1,0:T(8,128)(2,1)S(1)}, u32[]{:S(2)}, u32[]{:S(2)}) %collective-permute-start.3) | collective-permute-done | bytes 524320 | tf_op jit(solution)/shard_map/ppermute | solution.py:20
  38.4 3.6 %collective-permute-done.4.refs_4_ = bf16[64,4096]{1,0:T(8,128)(2,1)S(1)} collective-permute-done((bf16[64,4096]{1,0:T(8,128)(2,1)S(1)}, bf16[64,4096]{1,0:T(8,128)(2,1)S(1)}, u32[]{:S(2)}, u32[]{:S(2)}) %collective-permute-start.4) | collective-permute-done | bytes 524320 | tf_op jit(solution)/shard_map/ppermute | solution.py:20
  42.1 5.3 %collective-permute-start.5 = (bf16[64,4096]{1,0:T(8,128)(2,1)S(1)}, bf16[64,4096]{1,0:T(8,128)(2,1)S(1)}, u32[]{:S(2)}, u32[]{:S(2)}) collective-permute-start(bf16[64,4096]{1,0:T(8,128)(2,1)S(1)} %collective-permute-done.refs_2_), channel_id=1, source_target_pairs={{8,0},{252,4},{16,8},{4,12},{24,16},{12,20},{32,24},{20,28},{40,32... | collective-permute-start | bytes 1572872 | tf_op jit(solution)/shard_map/ppermute | solution.py:20
  47.4 2.1 %forward_1.1.refs_5_ = f32[64,4096]{1,0:T(8,128)S(1)} custom-call(s32[928]{0:T(1024)S(1)} %plan.1.refs_0_, bf16[288,128,128]{2,1,0:T(8,128)(2,1)S(1)} %copy-done, bf16[64,4096]{1,0:T(8,128)(2,1)S(1)} %collective-permute-done.refs_2_, bf16[64,4096]{1,0:T(8,128)(2,1)S(1)} %collective-permute-done.3.refs_3_, ...), custom_call_target="tpu_custom_call" | custom-call | bytes 6000000 | tf_op jit(solution)/shard_map/forward_1/pallas_call | solution.py:154
  49.5 4.1 %collective-permute-done.7.refs_4_ = bf16[64,4096]{1,0:T(8,128)(2,1)S(1)} collective-permute-done((bf16[64,4096]{1,0:T(8,128)(2,1)S(1)}, bf16[64,4096]{1,0:T(8,128)(2,1)S(1)}, u32[]{:S(2)}, u32[]{:S(2)}) %collective-permute-start.7) | collective-permute-done | bytes 524320 | tf_op jit(solution)/shard_map/ppermute | solution.py:24
  53.6 3.3 %collective-permute-done.6.refs_3_ = bf16[64,4096]{1,0:T(8,128)(2,1)S(1)} collective-permute-done((bf16[64,4096]{1,0:T(8,128)(2,1)S(1)}, bf16[64,4096]{1,0:T(8,128)(2,1)S(1)}, u32[]{:S(2)}, u32[]{:S(2)}) %collective-permute-start.6) | collective-permute-done | bytes 524320 | tf_op jit(solution)/shard_map/ppermute | solution.py:20
  59.9 11.1 %collective-permute-done.10.refs_2_ = bf16[64,4096]{1,0:T(8,128)(2,1)S(1)} collective-permute-done((bf16[64,4096]{1,0:T(8,128)(2,1)S(1)}, bf16[64,4096]{1,0:T(8,128)(2,1)S(1)}, u32[]{:S(2)}, u32[]{:S(2)}) %collective-permute-start.10) | collective-permute-done | bytes 524320 | tf_op jit(solution)/shard_map/ppermute | solution.py:24
  71.1 1.9 %collective-permute-done.11.refs_3_ = bf16[64,4096]{1,0:T(8,128)(2,1)S(1)} collective-permute-done((bf16[64,4096]{1,0:T(8,128)(2,1)S(1)}, bf16[64,4096]{1,0:T(8,128)(2,1)S(1)}, u32[]{:S(2)}, u32[]{:S(2)}) %collective-permute-start.11) | collective-permute-done | bytes 524320 | tf_op jit(solution)/shard_map/ppermute | solution.py:24
  73.0 3.4 %middle.1 = (bf16[64,4096]{1,0:T(8,128)(2,1)}, bf16[64,4096]{1,0:T(8,128)(2,1)S(1)}, f32[64,256]{1,0:T(8,128)S(1)}) custom-call(s32[1]{0:T(128)} %bitcast.place_ref, bf16[64,4096]{1,0:T(8,128)(2,1)S(1)} %forward_2.1.refs_0_, bf16[64,4096]{1,0:T(8,128)(2,1)S(1)} %collective-permute-done.9.refs_1_, bf16[64,4096]{1,0:T(8,128)(2,1)S(1)} %collective-permute-done.10.refs_2_, ...), custom_call_target="tpu_custom_call" | custom-call | bytes 6000000 | tf_op jit(solution)/shard_map/middle/pallas_call | solution.py:243
  76.4 1.9 %backward_2.1 = (bf16[64,4096]{1,0:T(8,128)(2,1)S(1)}, bf16[64,4096]{1,0:T(8,128)(2,1)S(1)}, bf16[64,4096]{1,0:T(8,128)(2,1)S(1)}) custom-call(s32[928]{0:T(1024)S(1)} %plan.1.refs_0_, bf16[288,128,128]{2,1,0:T(8,128)(2,1)S(1)} %bitcast.3, bf16[64,4096]{1,0:T(8,128)(2,1)S(1)} %get-tuple-element.83.refs_2_), custom_call_target="tpu_custom_call" | custom-call | bytes 6000000 | tf_op jit(solution)/shard_map/backward_2/pallas_call | solution.py:195
  78.3 2.3 %collective-permute-done.14 = f32[64,256]{1,0:T(8,128)S(1)} collective-permute-done((f32[64,256]{1,0:T(8,128)S(1)}, f32[64,256]{1,0:T(8,128)S(1)}, u32[]{:S(2)}, u32[]{:S(2)}) %collective-permute-start.14) | collective-permute-done | bytes 65568 | tf_op jit(solution)/shard_map/ppermute | solution.py:24
  80.6 2.5 %collective-permute-start.15 = (bf16[64,4096]{1,0:T(8,128)(2,1)S(1)}, bf16[64,4096]{1,0:T(8,128)(2,1)S(1)}, u32[]{:S(2)}, u32[]{:S(2)}) collective-permute-start(bf16[64,4096]{1,0:T(8,128)(2,1)S(1)} %get-tuple-element.75), channel_id=1, source_target_pairs={{0,4},{4,0},{8,12},{12,8},{16,20},{20,16},{24,28},{28,24},{32,36},... | collective-permute-start | bytes 1572872 | tf_op jit(solution)/shard_map/ppermute | solution.py:24
  83.8 4.6 %collective-permute-start.17 = (bf16[64,4096]{1,0:T(8,128)(2,1)S(1)}, bf16[64,4096]{1,0:T(8,128)(2,1)S(1)}, u32[]{:S(2)}, u32[]{:S(2)}) collective-permute-start(bf16[64,4096]{1,0:T(8,128)(2,1)S(1)} %get-tuple-element.77), channel_id=1, source_target_pairs={{8,0},{252,4},{16,8},{4,12},{24,16},{12,20},{32,24},{20,28},{40,32... | collective-permute-start | bytes 1572872 | tf_op jit(solution)/shard_map/ppermute | solution.py:20
  88.6 2.3 %backward_1.1 = (f32[64,4096]{1,0:T(8,128)S(1)}, f32[64,4096]{1,0:T(8,128)S(1)}, bf16[64,4096]{1,0:T(8,128)(2,1)S(1)}) custom-call(s32[928]{0:T(1024)S(1)} %plan.1.refs_0_, bf16[288,128,128]{2,1,0:T(8,128)(2,1)S(1)} %bitcast.3, bf16[64,4096]{1,0:T(8,128)(2,1)S(1)} %get-tuple-element.83.refs_2_), custom_call_target="tpu_custom_call" | custom-call | bytes 6000000 | tf_op jit(solution)/shard_map/backward_1/pallas_call | solution.py:195
  90.9 2.7 %collective-permute-done.18 = f32[64,256]{1,0:T(8,128)S(1)} collective-permute-done((f32[64,256]{1,0:T(8,128)S(1)}, f32[64,256]{1,0:T(8,128)S(1)}, u32[]{:S(2)}, u32[]{:S(2)}) %collective-permute-start.18) | collective-permute-done | bytes 65568 | tf_op jit(solution)/shard_map/ppermute | solution.py:24
  94.6 2.3 %backward_0.1 = (f32[64,4096]{1,0:T(8,128)S(1)}, f32[64,4096]{1,0:T(8,128)S(1)}, f32[64,4096]{1,0:T(8,128)S(1)}) custom-call(s32[928]{0:T(1024)S(1)} %plan.1.refs_0_, bf16[288,128,128]{2,1,0:T(8,128)(2,1)S(1)} %bitcast.3, bf16[64,4096]{1,0:T(8,128)(2,1)S(1)} %get-tuple-element.83.refs_2_), custom_call_target="tpu_custom_call" | custom-call | bytes 6000000 | tf_op jit(solution)/shard_map/backward_0/pallas_call | solution.py:195
  96.9 1.9 %collective-permute-done.19 = f32[64,256]{1,0:T(8,128)S(1)} collective-permute-done((f32[64,256]{1,0:T(8,128)S(1)}, f32[64,256]{1,0:T(8,128)S(1)}, u32[]{:S(2)}, u32[]{:S(2)}) %collective-permute-start.19) | collective-permute-done | bytes 65568 | tf_op jit(solution)/shard_map/ppermute | solution.py:24
  99.2 3.1 %collective-permute-start.22 = (f32[64,256]{1,0:T(8,128)S(1)}, f32[64,256]{1,0:T(8,128)S(1)}, u32[]{:S(2)}, u32[]{:S(2)}) collective-permute-start(f32[64,256]{1,0:T(8,128)S(1)} %add.57), channel_id=1, source_target_pairs={{0,192},{4,196},{8,200},{12,204},{16,208},{20,212},{24,216},{28,22... | collective-permute-start | bytes 196616 | tf_op jit(solution)/shard_map/ppermute | solution.py:24
  102.5 5.3 %collective-permute-start.21 = (bf16[64,4096]{1,0:T(8,128)(2,1)S(1)}, bf16[64,4096]{1,0:T(8,128)(2,1)S(1)}, u32[]{:S(2)}, u32[]{:S(2)}) collective-permute-start(bf16[64,4096]{1,0:T(8,128)(2,1)S(1)} %get-tuple-element.92), channel_id=1, source_target_pairs={{8,0},{252,4},{16,8},{4,12},{24,16},{12,20},{32,24},{20,28},{40,32... | collective-permute-start | bytes 1572872 | tf_op jit(solution)/shard_map/ppermute | solution.py:20
  107.8 3.3 %collective-permute-start.23 = (f32[64,256]{1,0:T(8,128)S(1)}, f32[64,256]{1,0:T(8,128)S(1)}, u32[]{:S(2)}, u32[]{:S(2)}) collective-permute-start(f32[64,256]{1,0:T(8,128)S(1)} %add.58), channel_id=1, source_target_pairs={{0,4},{4,0},{8,12},{12,8},{16,20},{20,16},{24,28},{28,24},{32,36},... | collective-permute-start | bytes 196616 | tf_op jit(solution)/shard_map/ppermute | solution.py:24
  111.3 2.1 %collective-permute-done.23 = f32[64,256]{1,0:T(8,128)S(1)} collective-permute-done((f32[64,256]{1,0:T(8,128)S(1)}, f32[64,256]{1,0:T(8,128)S(1)}, u32[]{:S(2)}, u32[]{:S(2)}) %collective-permute-start.23) | collective-permute-done | bytes 65568 | tf_op jit(solution)/shard_map/ppermute | solution.py:24
  113.4 3.8 %collective-permute-done.20 = bf16[64,4096]{1,0:T(8,128)(2,1)S(1)} collective-permute-done((bf16[64,4096]{1,0:T(8,128)(2,1)S(1)}, bf16[64,4096]{1,0:T(8,128)(2,1)S(1)}, u32[]{:S(2)}, u32[]{:S(2)}) %collective-permute-start.20) | collective-permute-done | bytes 524320 | tf_op jit(solution)/shard_map/ppermute | solution.py:20
  117.3 4.4 %collective-permute-start.25 = (bf16[64,4096]{1,0:T(8,128)(2,1)S(1)}, bf16[64,4096]{1,0:T(8,128)(2,1)S(1)}, u32[]{:S(2)}, u32[]{:S(2)}) collective-permute-start(bf16[64,4096]{1,0:T(8,128)(2,1)S(1)} %add_convert_fusion.1), channel_id=1, source_target_pairs={{8,0},{252,4},{16,8},{4,12},{24,16},{12,20},{32,24},{20,28},{40,32... | collective-permute-start | bytes 1572872 | tf_op jit(solution)/shard_map/ppermute | solution.py:20
  122.0 3.8 %collective-permute-start.26 = (bf16[64,4096]{1,0:T(8,128)(2,1)S(1)}, bf16[64,4096]{1,0:T(8,128)(2,1)S(1)}, u32[]{:S(2)}, u32[]{:S(2)}) collective-permute-start(bf16[64,4096]{1,0:T(8,128)(2,1)S(1)} %add_convert_fusion.3), channel_id=1, source_target_pairs={{0,4},{4,0},{8,12},{12,8},{16,20},{20,16},{24,28},{28,24},{32,36},... | collective-permute-start | bytes 1572872 | tf_op jit(solution)/shard_map/ppermute | solution.py:24
  125.8 10.2 %collective-permute-done.27 = f32[64,256]{1,0:T(8,128)S(1)} collective-permute-done((f32[64,256]{1,0:T(8,128)S(1)}, f32[64,256]{1,0:T(8,128)S(1)}, u32[]{:S(2)}, u32[]{:S(2)}) %collective-permute-start.27) | collective-permute-done | bytes 65568 | tf_op jit(solution)/shard_map/ppermute | solution.py:24
  (65 shorter events, 15.0 us)
Async XLA Ops:
  0.6 27.8 %copy-start.1 = (bf16[64,4096]{1,0:T(8,128)(2,1)S(1)}, bf16[64,4096]{1,0:T(8,128)(2,1)}, u32[]{:S(2)}) copy-start(bf16[64,4096]{1,0:T(8,128)(2,1)} %refs_2_.1) | copy-start | bytes 1572868
  0.6 19.9 %collective-permute-start.1 = (bf16[64,4096]{1,0:T(8,128)(2,1)}, bf16[64,4096]{1,0:T(8,128)(2,1)S(1)}, u32[]{:S(2)}, u32[]{:S(2)}) collective-permute-start(bf16[64,4096]{1,0:T(8,128)(2,1)} %refs_2_.1), channel_id=1, source_target_pairs={{8,0},{252,4},{16,8},{4,12},{24,16},{12,20},{32,24},{20,28},{40,32... | collective-permute-start | bytes 1572872 | tf_op jit(solution)/shard_map/ppermute | solution.py:20
  9.0 13.6 %collective-permute-start = (bf16[64,4096]{1,0:T(8,128)(2,1)}, bf16[64,4096]{1,0:T(8,128)(2,1)S(1)}, u32[]{:S(2)}, u32[]{:S(2)}) collective-permute-start(bf16[64,4096]{1,0:T(8,128)(2,1)} %refs_2_.1), channel_id=1, source_target_pairs={{0,4},{4,0},{8,12},{12,8},{16,20},{20,16},{24,28},{28,24},{32,36},... | collective-permute-start | bytes 1572872 | tf_op jit(solution)/shard_map/ppermute | solution.py:24
  9.0 16.9 %collective-permute-start.2 = (bf16[64,4096]{1,0:T(8,128)(2,1)}, bf16[64,4096]{1,0:T(8,128)(2,1)S(1)}, u32[]{:S(2)}, u32[]{:S(2)}) collective-permute-start(bf16[64,4096]{1,0:T(8,128)(2,1)} %refs_2_.1), channel_id=1, source_target_pairs={{248,0},{12,4},{0,8},{20,12},{8,16},{28,20},{16,24},{36,28},{24,32... | collective-permute-start | bytes 1572872 | tf_op jit(solution)/shard_map/ppermute | solution.py:20
  25.9 12.5 %collective-permute-start.3 = (bf16[64,4096]{1,0:T(8,128)(2,1)S(1)}, bf16[64,4096]{1,0:T(8,128)(2,1)S(1)}, u32[]{:S(2)}, u32[]{:S(2)}) collective-permute-start(bf16[64,4096]{1,0:T(8,128)(2,1)S(1)} %collective-permute-done.1.refs_3_), channel_id=1, source_target_pairs={{8,0},{252,4},{16,8},{4,12},{24,16},{12,20},{32,24},{20,28},{40,32... | collective-permute-start | bytes 1572872 | tf_op jit(solution)/shard_map/ppermute | solution.py:20
  26.2 15.8 %collective-permute-start.4 = (bf16[64,4096]{1,0:T(8,128)(2,1)S(1)}, bf16[64,4096]{1,0:T(8,128)(2,1)S(1)}, u32[]{:S(2)}, u32[]{:S(2)}) collective-permute-start(bf16[64,4096]{1,0:T(8,128)(2,1)S(1)} %collective-permute-done.2.refs_4_), channel_id=1, source_target_pairs={{248,0},{12,4},{0,8},{20,12},{8,16},{28,20},{16,24},{36,28},{24,32... | collective-permute-start | bytes 1572872 | tf_op jit(solution)/shard_map/ppermute | solution.py:20
  28.0 21.6 %collective-permute-start.8 = (bf16[64,4352]{1,0:T(8,128)(2,1)S(1)}, bf16[64,4352]{1,0:T(8,128)(2,1)S(1)}, u32[]{:S(2)}, u32[]{:S(2)}) collective-permute-start(bf16[64,4352]{1,0:T(8,128)(2,1)S(1)} %pad_maximum_fusion.refs_4_), channel_id=1, source_target_pairs={{0,2},{1,3},{2,0},{3,1},{4,6},{5,7},{6,4},{7,5},{8,10},{9,11},{10,... | collective-permute-start | bytes 1671176 | tf_op jit(solution)/shard_map/ppermute | solution.py:24
  42.1 11.6 %collective-permute-start.7 = (bf16[64,4096]{1,0:T(8,128)(2,1)S(1)}, bf16[64,4096]{1,0:T(8,128)(2,1)S(1)}, u32[]{:S(2)}, u32[]{:S(2)}) collective-permute-start(bf16[64,4096]{1,0:T(8,128)(2,1)S(1)} %collective-permute-done.3.refs_3_), channel_id=1, source_target_pairs={{0,4},{4,0},{8,12},{12,8},{16,20},{20,16},{24,28},{28,24},{32,36},... | collective-permute-start | bytes 1572872 | tf_op jit(solution)/shard_map/ppermute | solution.py:24
  42.1 14.9 %collective-permute-start.6 = (bf16[64,4096]{1,0:T(8,128)(2,1)S(1)}, bf16[64,4096]{1,0:T(8,128)(2,1)S(1)}, u32[]{:S(2)}, u32[]{:S(2)}) collective-permute-start(bf16[64,4096]{1,0:T(8,128)(2,1)S(1)} %collective-permute-done.refs_2_), channel_id=1, source_target_pairs={{248,0},{12,4},{0,8},{20,12},{8,16},{28,20},{16,24},{36,28},{24,32... | collective-permute-start | bytes 1572872 | tf_op jit(solution)/shard_map/ppermute | solution.py:20
  42.1 14.9 %collective-permute-start.5 = (bf16[64,4096]{1,0:T(8,128)(2,1)S(1)}, bf16[64,4096]{1,0:T(8,128)(2,1)S(1)}, u32[]{:S(2)}, u32[]{:S(2)}) collective-permute-start(bf16[64,4096]{1,0:T(8,128)(2,1)S(1)} %collective-permute-done.refs_2_), channel_id=1, source_target_pairs={{8,0},{252,4},{16,8},{4,12},{24,16},{12,20},{32,24},{20,28},{40,32... | collective-permute-start | bytes 1572872 | tf_op jit(solution)/shard_map/ppermute | solution.py:20
  47.4 28.9 %slice-start = ((s8[9437184]{0:T(1024)(128)(4,1)}), s8[4194304]{0:T(1024)(128)(4,1)S(1)}, s32[]{:S(2)}) async-start(s8[9437184]{0:T(1024)(128)(4,1)} %bitcast.2), calls=%async_computation | async-start | bytes 8388608
  47.4 28.9 %slice-start.1 = ((s8[9437184]{0:T(1024)(128)(4,1)}), s8[4194304]{0:T(1024)(128)(4,1)S(1)}, s32[]{:S(2)}) async-start(s8[9437184]{0:T(1024)(128)(4,1)} %bitcast.2), calls=%async_computation.1 | async-start | bytes 8388608
  49.5 26.8 %slice-start.2 = ((s8[9437184]{0:T(1024)(128)(4,1)}), s8[1048576]{0:T(1024)(128)(4,1)S(1)}, s32[]{:S(2)}) async-start(s8[9437184]{0:T(1024)(128)(4,1)} %bitcast.2), calls=%async_computation.2 | async-start | bytes 2097152
  58.8 12.3 %collective-permute-start.10 = (bf16[64,4096]{1,0:T(8,128)(2,1)S(1)}, bf16[64,4096]{1,0:T(8,128)(2,1)S(1)}, u32[]{:S(2)}, u32[]{:S(2)}) collective-permute-start(bf16[64,4096]{1,0:T(8,128)(2,1)S(1)} %forward_2.1.refs_0_), channel_id=1, source_target_pairs={{0,2},{1,3},{2,0},{3,1},{4,6},{5,7},{6,4},{7,5},{8,10},{9,11},{10,... | collective-permute-start | bytes 1572872 | tf_op jit(solution)/shard_map/ppermute | solution.py:24
  59.4 11.7 %collective-permute-start.12 = (bf16[64,4352]{1,0:T(8,128)(2,1)S(1)}, bf16[64,4352]{1,0:T(8,128)(2,1)S(1)}, u32[]{:S(2)}, u32[]{:S(2)}) collective-permute-start(bf16[64,4352]{1,0:T(8,128)(2,1)S(1)} %pad_maximum_fusion.refs_4_), channel_id=1, source_target_pairs={{0,1},{1,0},{2,3},{3,2},{4,5},{5,4},{6,7},{7,6},{8,9},{9,8},{10,11... | collective-permute-start | bytes 1671176 | tf_op jit(solution)/shard_map/ppermute | solution.py:24
  59.4 11.7 %collective-permute-start.13 = (bf16[64,4352]{1,0:T(8,128)(2,1)S(1)}, bf16[64,4352]{1,0:T(8,128)(2,1)S(1)}, u32[]{:S(2)}, u32[]{:S(2)}) collective-permute-start(bf16[64,4352]{1,0:T(8,128)(2,1)S(1)} %collective-permute-done.8.refs_6_), channel_id=1, source_target_pairs={{0,1},{1,0},{2,3},{3,2},{4,5},{5,4},{6,7},{7,6},{8,9},{9,8},{10,11... | collective-permute-start | bytes 1671176 | tf_op jit(solution)/shard_map/ppermute | solution.py:24
  59.9 11.1 %collective-permute-start.9 = (bf16[64,4096]{1,0:T(8,128)(2,1)S(1)}, bf16[64,4096]{1,0:T(8,128)(2,1)S(1)}, u32[]{:S(2)}, u32[]{:S(2)}) collective-permute-start(bf16[64,4096]{1,0:T(8,128)(2,1)S(1)} %forward_2.1.refs_0_), channel_id=1, source_target_pairs={{0,1},{1,0},{2,3},{3,2},{4,5},{5,4},{6,7},{7,6},{8,9},{9,8},{10,11... | collective-permute-start | bytes 1572872 | tf_op jit(solution)/shard_map/ppermute | solution.py:24
  71.0 1.9 %collective-permute-start.11 = (bf16[64,4096]{1,0:T(8,128)(2,1)S(1)}, bf16[64,4096]{1,0:T(8,128)(2,1)S(1)}, u32[]{:S(2)}, u32[]{:S(2)}) collective-permute-start(bf16[64,4096]{1,0:T(8,128)(2,1)S(1)} %collective-permute-done.10.refs_2_), channel_id=1, source_target_pairs={{0,1},{1,0},{2,3},{3,2},{4,5},{5,4},{6,7},{7,6},{8,9},{9,8},{10,11... | collective-permute-start | bytes 1572872 | tf_op jit(solution)/shard_map/ppermute | solution.py:24
  76.3 4.3 %collective-permute-start.14 = (f32[64,256]{1,0:T(8,128)S(1)}, f32[64,256]{1,0:T(8,128)S(1)}, u32[]{:S(2)}, u32[]{:S(2)}) collective-permute-start(f32[64,256]{1,0:T(8,128)S(1)} %get-tuple-element.74), channel_id=1, source_target_pairs={{0,8},{4,12},{8,0},{12,4},{16,24},{20,28},{24,16},{28,20},{32,40},... | collective-permute-start | bytes 196616 | tf_op jit(solution)/shard_map/ppermute | solution.py:24
  80.6 18.2 %collective-permute-start.15 = (bf16[64,4096]{1,0:T(8,128)(2,1)S(1)}, bf16[64,4096]{1,0:T(8,128)(2,1)S(1)}, u32[]{:S(2)}, u32[]{:S(2)}) collective-permute-start(bf16[64,4096]{1,0:T(8,128)(2,1)S(1)} %get-tuple-element.75), channel_id=1, source_target_pairs={{0,4},{4,0},{8,12},{12,8},{16,20},{20,16},{24,28},{28,24},{32,36},... | collective-permute-start | bytes 1572872 | tf_op jit(solution)/shard_map/ppermute | solution.py:24
  83.1 16.0 %collective-permute-start.16 = (bf16[64,4096]{1,0:T(8,128)(2,1)S(1)}, bf16[64,4096]{1,0:T(8,128)(2,1)S(1)}, u32[]{:S(2)}, u32[]{:S(2)}) collective-permute-start(bf16[64,4096]{1,0:T(8,128)(2,1)S(1)} %get-tuple-element.76), channel_id=1, source_target_pairs={{248,0},{12,4},{0,8},{20,12},{8,16},{28,20},{16,24},{36,28},{24,32... | collective-permute-start | bytes 1572872 | tf_op jit(solution)/shard_map/ppermute | solution.py:20
  83.8 15.3 %collective-permute-start.17 = (bf16[64,4096]{1,0:T(8,128)(2,1)S(1)}, bf16[64,4096]{1,0:T(8,128)(2,1)S(1)}, u32[]{:S(2)}, u32[]{:S(2)}) collective-permute-start(bf16[64,4096]{1,0:T(8,128)(2,1)S(1)} %get-tuple-element.77), channel_id=1, source_target_pairs={{8,0},{252,4},{16,8},{4,12},{24,16},{12,20},{32,24},{20,28},{40,32... | collective-permute-start | bytes 1572872 | tf_op jit(solution)/shard_map/ppermute | solution.py:20
  88.5 5.0 %collective-permute-start.18 = (f32[64,256]{1,0:T(8,128)S(1)}, f32[64,256]{1,0:T(8,128)S(1)}, u32[]{:S(2)}, u32[]{:S(2)}) collective-permute-start(f32[64,256]{1,0:T(8,128)S(1)} %add.52), channel_id=1, source_target_pairs={{0,32},{4,36},{8,40},{12,44},{16,48},{20,52},{24,56},{28,60},{32,0... | collective-permute-start | bytes 196616 | tf_op jit(solution)/shard_map/ppermute | solution.py:24
  93.5 5.3 %collective-permute-start.19 = (f32[64,256]{1,0:T(8,128)S(1)}, f32[64,256]{1,0:T(8,128)S(1)}, u32[]{:S(2)}, u32[]{:S(2)}) collective-permute-start(f32[64,256]{1,0:T(8,128)S(1)} %add.53), channel_id=1, source_target_pairs={{0,64},{4,68},{8,72},{12,76},{16,80},{20,84},{24,88},{28,92},{32,9... | collective-permute-start | bytes 196616 | tf_op jit(solution)/shard_map/ppermute | solution.py:24
  99.2 8.6 %collective-permute-start.22 = (f32[64,256]{1,0:T(8,128)S(1)}, f32[64,256]{1,0:T(8,128)S(1)}, u32[]{:S(2)}, u32[]{:S(2)}) collective-permute-start(f32[64,256]{1,0:T(8,128)S(1)} %add.57), channel_id=1, source_target_pairs={{0,192},{4,196},{8,200},{12,204},{16,208},{20,212},{24,216},{28,22... | collective-permute-start | bytes 196616 | tf_op jit(solution)/shard_map/ppermute | solution.py:24
  102.4 14.9 %collective-permute-start.20 = (bf16[64,4096]{1,0:T(8,128)(2,1)S(1)}, bf16[64,4096]{1,0:T(8,128)(2,1)S(1)}, u32[]{:S(2)}, u32[]{:S(2)}) collective-permute-start(bf16[64,4096]{1,0:T(8,128)(2,1)S(1)} %add_convert_fusion.4), channel_id=1, source_target_pairs={{248,0},{12,4},{0,8},{20,12},{8,16},{28,20},{16,24},{36,28},{24,32... | collective-permute-start | bytes 1572872 | tf_op jit(solution)/shard_map/ppermute | solution.py:20
  102.5 14.8 %collective-permute-start.21 = (bf16[64,4096]{1,0:T(8,128)(2,1)S(1)}, bf16[64,4096]{1,0:T(8,128)(2,1)S(1)}, u32[]{:S(2)}, u32[]{:S(2)}) collective-permute-start(bf16[64,4096]{1,0:T(8,128)(2,1)S(1)} %get-tuple-element.92), channel_id=1, source_target_pairs={{8,0},{252,4},{16,8},{4,12},{24,16},{12,20},{32,24},{20,28},{40,32... | collective-permute-start | bytes 1572872 | tf_op jit(solution)/shard_map/ppermute | solution.py:20
  107.8 5.6 %collective-permute-start.23 = (f32[64,256]{1,0:T(8,128)S(1)}, f32[64,256]{1,0:T(8,128)S(1)}, u32[]{:S(2)}, u32[]{:S(2)}) collective-permute-start(f32[64,256]{1,0:T(8,128)S(1)} %add.58), channel_id=1, source_target_pairs={{0,4},{4,0},{8,12},{12,8},{16,20},{20,16},{24,28},{28,24},{32,36},... | collective-permute-start | bytes 196616 | tf_op jit(solution)/shard_map/ppermute | solution.py:24
  117.3 19.3 %collective-permute-start.25 = (bf16[64,4096]{1,0:T(8,128)(2,1)S(1)}, bf16[64,4096]{1,0:T(8,128)(2,1)S(1)}, u32[]{:S(2)}, u32[]{:S(2)}) collective-permute-start(bf16[64,4096]{1,0:T(8,128)(2,1)S(1)} %add_convert_fusion.1), channel_id=1, source_target_pairs={{8,0},{252,4},{16,8},{4,12},{24,16},{12,20},{32,24},{20,28},{40,32... | collective-permute-start | bytes 1572872 | tf_op jit(solution)/shard_map/ppermute | solution.py:20
  121.9 14.7 %collective-permute-start.24 = (bf16[64,4096]{1,0:T(8,128)(2,1)S(1)}, bf16[64,4096]{1,0:T(8,128)(2,1)S(1)}, u32[]{:S(2)}, u32[]{:S(2)}) collective-permute-start(bf16[64,4096]{1,0:T(8,128)(2,1)S(1)} %add_convert_fusion.2), channel_id=1, source_target_pairs={{248,0},{12,4},{0,8},{20,12},{8,16},{28,20},{16,24},{36,28},{24,32... | collective-permute-start | bytes 1572872 | tf_op jit(solution)/shard_map/ppermute | solution.py:20
  122.0 14.6 %collective-permute-start.26 = (bf16[64,4096]{1,0:T(8,128)(2,1)S(1)}, bf16[64,4096]{1,0:T(8,128)(2,1)S(1)}, u32[]{:S(2)}, u32[]{:S(2)}) collective-permute-start(bf16[64,4096]{1,0:T(8,128)(2,1)S(1)} %add_convert_fusion.3), channel_id=1, source_target_pairs={{0,4},{4,0},{8,12},{12,8},{16,20},{20,16},{24,28},{28,24},{32,36},... | collective-permute-start | bytes 1572872 | tf_op jit(solution)/shard_map/ppermute | solution.py:24
  125.8 10.2 %collective-permute-start.27 = (f32[64,256]{1,0:T(8,128)S(1)}, f32[64,256]{1,0:T(8,128)S(1)}, u32[]{:S(2)}, u32[]{:S(2)}) collective-permute-start(f32[64,256]{1,0:T(8,128)S(1)} %add.59), channel_id=1, source_target_pairs={{0,24},{4,28},{8,16},{12,20},{16,8},{20,12},{24,0},{28,4},{32,56},... | collective-permute-start | bytes 196616 | tf_op jit(solution)/shard_map/ppermute | solution.py:24
  (4 other events, 5.7 us)
